TPU v7x, 32 devices: a whole 2x2x4 slice. The times are simulated.
32 devices in a mesh: dp: 16 (over z, y, x), mp: 2 (over core).
Axes of the slice: x: 2, y: 2, z: 4, core: 2. Of those that a mesh axis runs over, the one named last changes fastest.
Arguments:
- decoder_in: bfloat16 [16, 512, 768], P('dp'), may hold values from -6 to 6
- encoder_out: bfloat16 [16, 1024, 768], P(None, 'dp'), may hold values from -6 to 6
- lengths: int32 [16], replicated, may hold values from 256 to 1024, as said below
- key_mask: int32 [16, 1024], replicated, may hold values 0 or 1
- assign: int32 [16], replicated, may hold values from 0 to 15, each once
- buckets: int32 [512, 512], replicated, may hold values from 0 to 31, as said below
- norm_one: float32 [768], replicated, may hold values from 0.5 to 1.5
- norm_two: float32 [768], replicated, may hold values from 0.5 to 1.5
- norm_three: float32 [768], replicated, may hold values from 0.5 to 1.5
- self_query: float32 [768, 768], P('dp', 'mp'), may hold values from -0.109375 to 0.109375
- self_key: float32 [768, 768], P('dp', 'mp'), may hold values from -0.109375 to 0.109375
- self_value: float32 [768, 768], P('dp', 'mp'), may hold values from -0.21875 to 0.21875
- self_output: float32 [768, 768], P('mp', 'dp'), may hold values from -0.875 to 0.875
- cross_query: float32 [768, 768], P('dp', 'mp'), may hold values from -0.109375 to 0.109375
- cross_key: float32 [768, 768], P('dp', 'mp'), may hold values from -0.109375 to 0.109375
- cross_value: float32 [768, 768], P('dp', 'mp'), may hold values from -0.21875 to 0.21875
- cross_output: float32 [768, 768], P('mp', 'dp'), may hold values from -1.75 to 1.75
- ffn_gate: float32 [768, 2048], P('dp', 'mp'), may hold values from -0.21875 to 0.21875
- ffn_up: float32 [768, 2048], P('dp', 'mp'), may hold values from -0.21875 to 0.21875
- ffn_down: float32 [2048, 768], P('mp', 'dp'), may hold values from -0.125 to 0.125
- bias_table: float32 [32, 12], P(None, 'mp'), may hold values from -4 to 4
- cotangent: bfloat16 [16, 512, 768], P('dp'), may hold values from -6 to 6
Outputs:
- layer_out: bfloat16 [16, 512, 768], P('dp')
- decoder_grad: float32 [16, 512, 768], P('dp')
- encoder_grad: bfloat16 [16, 1024, 768], P(None, 'dp', 'mp')
- grad_norm_one: float32 [768], replicated
- grad_norm_two: float32 [768], replicated
- grad_norm_three: float32 [768], replicated
- grad_self_query: float32 [768, 768], P('dp', 'mp')
- grad_self_key: float32 [768, 768], P('dp', 'mp')
- grad_self_value: float32 [768, 768], P('dp', 'mp')
- grad_self_output: float32 [768, 768], P('mp', 'dp')
- grad_cross_query: float32 [768, 768], P('dp', 'mp')
- grad_cross_key: float32 [768, 768], P('dp', 'mp')
- grad_cross_value: float32 [768, 768], P('dp', 'mp')
- grad_cross_output: float32 [768, 768], P('mp', 'dp')
- grad_ffn_gate: float32 [768, 2048], P('dp', 'mp')
- grad_ffn_up: float32 [768, 2048], P('dp', 'mp')
- grad_ffn_down: float32 [2048, 768], P('mp', 'dp')
- grad_bias_table: float32 [32, 12], P(None, 'mp')
Inputs may be any that keep to these rules, and one draw needn't show every extreme that they name: `lengths`: every example's encoder length; the longest is exactly 1024. `assign`: each example is held by exactly one slot. `buckets`: entry (i, j) depends only on max(i - j, 0).
All inputs are finite; a program needn't handle non-finite values.
Results may differ from a plain program's by a relative error of at most 0.024.
The roundings to bfloat16 on the way count: a program that leaves them out, or rounds other values in their place, can miss the bound.
Values may be sent and summed in bfloat16 or wider, within the bound.
No kernel may reach another device: no remote copies, remote signals or barrier semaphores. Data moves between devices by JAX's collectives and lax.ppermute only.
A program may use at most 256 MiB of HBM per device.

v0:
```python
import jax
import jax.numpy as jnp
from jax import lax
from jax.sharding import PartitionSpec as P

HEAD_DIM = 64


EPS = 1e-06
NEGATIVE = -1000000000.0


def norm_apply(value, gain):
    return value * lax.rsqrt(jnp.mean(value * value, axis=-1, keepdims=True) + EPS) * gain


def norm_back(value, gain, grad_normed):
    unused, pull = jax.vjp(norm_apply, value, gain)
    return pull(grad_normed)


def mixer(gate, up):
    return jax.nn.gelu(gate, approximate=True) * up


def project(acts, weight):
    return jnp.einsum("etd,dh->eth", acts, weight, preferred_element_type=jnp.float32)


def project_back(grads, weight):
    return jnp.einsum("eth,dh->etd", grads, weight, preferred_element_type=jnp.float32)


def weight_grad(acts, grads):
    return jnp.einsum("etd,eth->dh", acts, grads, preferred_element_type=jnp.float32)


def head_sum(partial_value):
    return lax.psum(partial_value, "mp")


def head_scores(query_head, keys_head, extras, head, valid):
    scores = jnp.einsum("etd,esd->ets", query_head, keys_head, preferred_element_type=jnp.float32)
    if extras is not None:
        scores = scores + extras[head][None]
    return jnp.where(valid, scores, NEGATIVE)


def attend_forward(query, keys, values, extras, valid):
    heads = query.shape[2] // HEAD_DIM
    output = jnp.zeros(query.shape, jnp.bfloat16)
    totals = jnp.zeros((heads, query.shape[0], query.shape[1]), jnp.float32)

    def one_head(head, carry):
        output, totals = carry
        start = head * HEAD_DIM
        query_head = lax.dynamic_slice_in_dim(query, start, HEAD_DIM, 2)
        keys_head = lax.dynamic_slice_in_dim(keys, start, HEAD_DIM, 2)
        values_head = lax.dynamic_slice_in_dim(values, start, HEAD_DIM, 2)
        scores = head_scores(query_head, keys_head, extras, head, valid)
        top = jnp.max(scores, axis=2, keepdims=True)
        weights = jnp.exp(scores - top)
        total = jnp.sum(weights, axis=2, keepdims=True)
        probs = (weights / total).astype(jnp.bfloat16)
        mixed = jnp.einsum("ets,esd->etd", probs, values_head, preferred_element_type=jnp.float32)
        output = lax.dynamic_update_slice_in_dim(output, mixed.astype(jnp.bfloat16), start, 2)
        totals = totals.at[head].set((top + jnp.log(total))[:, :, 0])
        return (output, totals)

    return lax.fori_loop(0, heads, one_head, (output, totals))


def attend_backward(query, keys, values, extras, valid, totals, grad_out):
    heads = query.shape[2] // HEAD_DIM
    grad_query = jnp.zeros(query.shape, jnp.bfloat16)
    grad_keys = jnp.zeros(keys.shape, jnp.bfloat16)
    grad_values = jnp.zeros(values.shape, jnp.bfloat16)
    if extras is not None:
        grad_extra = jnp.zeros((heads, query.shape[1], keys.shape[1]), jnp.float32)
    else:
        grad_extra = jnp.zeros((1,), jnp.float32)

    def one_head(head, carry):
        grad_query, grad_keys, grad_values, grad_extra = carry
        start = head * HEAD_DIM
        query_head = lax.dynamic_slice_in_dim(query, start, HEAD_DIM, 2)
        keys_head = lax.dynamic_slice_in_dim(keys, start, HEAD_DIM, 2)
        values_head = lax.dynamic_slice_in_dim(values, start, HEAD_DIM, 2)
        grad_head = lax.dynamic_slice_in_dim(grad_out, start, HEAD_DIM, 2)
        scores = head_scores(query_head, keys_head, extras, head, valid)
        probs = jnp.exp(scores - totals[head][:, :, None])
        low_probs = probs.astype(jnp.bfloat16)
        value_step = jnp.einsum(
            "ets,etd->esd", low_probs, grad_head, preferred_element_type=jnp.float32
        )
        grad_probs = jnp.einsum(
            "etd,esd->ets", grad_head, values_head, preferred_element_type=jnp.float32
        )
        grad_scores = probs * (grad_probs - jnp.sum(grad_probs * probs, axis=2, keepdims=True))
        low_scores = grad_scores.astype(jnp.bfloat16)
        query_step = jnp.einsum(
            "ets,esd->etd", low_scores, keys_head, preferred_element_type=jnp.float32
        )
        key_step = jnp.einsum(
            "ets,etd->esd", low_scores, query_head, preferred_element_type=jnp.float32
        )
        grad_query = lax.dynamic_update_slice_in_dim(
            grad_query, query_step.astype(jnp.bfloat16), start, 2
        )
        grad_keys = lax.dynamic_update_slice_in_dim(
            grad_keys, key_step.astype(jnp.bfloat16), start, 2
        )
        grad_values = lax.dynamic_update_slice_in_dim(
            grad_values, value_step.astype(jnp.bfloat16), start, 2
        )
        if extras is not None:
            grad_extra = grad_extra.at[head].set(jnp.sum(grad_scores, axis=0))
        return (grad_query, grad_keys, grad_values, grad_extra)

    return lax.fori_loop(0, heads, one_head, (grad_query, grad_keys, grad_values, grad_extra))


def shards(
    decoder_in,
    encoder_out,
    lengths,
    key_mask,
    assign,
    buckets,
    norm_one,
    norm_two,
    norm_three,
    self_query,
    self_key,
    self_value,
    self_output,
    cross_query,
    cross_key,
    cross_value,
    cross_output,
    ffn_gate,
    ffn_up,
    ffn_down,
    bias_table,
    cotangent,
):
    bf16 = jnp.bfloat16
    f32 = jnp.float32
    (
        query_one,
        key_one,
        value_one,
        output_one,
        query_two,
        key_two,
        value_two,
        output_two,
        gate_low,
        up_low,
        down_low,
    ) = (
        lax.all_gather(self_query.astype(bf16), "dp", axis=0, tiled=True),
        lax.all_gather(self_key.astype(bf16), "dp", axis=0, tiled=True),
        lax.all_gather(self_value.astype(bf16), "dp", axis=0, tiled=True),
        lax.all_gather(self_output.astype(bf16), "dp", axis=1, tiled=True),
        lax.all_gather(cross_query.astype(bf16), "dp", axis=0, tiled=True),
        lax.all_gather(cross_key.astype(bf16), "dp", axis=0, tiled=True),
        lax.all_gather(cross_value.astype(bf16), "dp", axis=0, tiled=True),
        lax.all_gather(cross_output.astype(bf16), "dp", axis=1, tiled=True),
        lax.all_gather(ffn_gate.astype(bf16), "dp", axis=0, tiled=True),
        lax.all_gather(ffn_up.astype(bf16), "dp", axis=0, tiled=True),
        lax.all_gather(ffn_down.astype(bf16), "dp", axis=1, tiled=True),
    )
    count = decoder_in.shape[0]
    targets = decoder_in.shape[1]
    capacity = key_mask.shape[1]
    rank = lax.axis_index("dp")
    mine = lax.dynamic_slice_in_dim(assign, rank * count, count)
    inverse = jnp.zeros_like(assign).at[assign].set(jnp.arange(assign.shape[0], dtype=jnp.int32))
    positions = jnp.arange(capacity, dtype=jnp.int32)
    live = (positions[None, :] < lengths[mine][:, None]) & (
        (key_mask[mine] == 1) | (positions[None, :] == 0)
    )
    cross_valid = live[:, None, :]
    causal = (jnp.arange(targets)[:, None] >= jnp.arange(targets)[None, :])[None]
    onehot = (buckets.reshape(-1)[:, None] == jnp.arange(bias_table.shape[0])[None, :]).astype(f32)
    extras = jnp.einsum("xb,bh->hx", onehot, bias_table, precision=lax.Precision.HIGHEST)
    extras = extras.reshape(bias_table.shape[1], targets, targets)
    tokens = decoder_in.astype(f32)
    normed_one = norm_apply(tokens, norm_one).astype(bf16)
    query = project(normed_one, query_one).astype(bf16)
    keys = project(normed_one, key_one).astype(bf16)
    values = project(normed_one, value_one).astype(bf16)
    attended, totals_self = attend_forward(query, keys, values, extras, causal)
    h_one = tokens + head_sum(project(attended, output_one))
    normed_two = norm_apply(h_one, norm_two).astype(bf16)
    cross_q = project(normed_two, query_two).astype(bf16)
    keys_local = jnp.einsum("esd,dh->esh", encoder_out, key_two, preferred_element_type=f32).astype(
        bf16
    )
    values_local = jnp.einsum(
        "esd,dh->esh", encoder_out, value_two, preferred_element_type=f32
    ).astype(bf16)
    cross_k, cross_v = (
        lax.all_to_all(keys_local[assign], "dp", split_axis=0, concat_axis=1, tiled=True),
        lax.all_to_all(values_local[assign], "dp", split_axis=0, concat_axis=1, tiled=True),
    )
    cross_att, totals_cross = attend_forward(cross_q, cross_k, cross_v, None, cross_valid)
    h_two = h_one + head_sum(project(cross_att, output_two))
    normed_three = norm_apply(h_two, norm_three).astype(bf16)
    gate = project(normed_three, gate_low)
    up = project(normed_three, up_low)
    act = mixer(gate, up).astype(bf16)
    layer_out = (h_two + head_sum(project(act, down_low))).astype(bf16)
    grad_down = weight_grad(act, cotangent)
    grad_act = project_back(cotangent, down_low).astype(bf16)
    unused, pull_mixer = jax.vjp(mixer, gate, up)
    grad_gate, grad_up = pull_mixer(grad_act.astype(f32))
    grad_gate = grad_gate.astype(bf16)
    grad_up = grad_up.astype(bf16)
    grad_gate_w = weight_grad(normed_three, grad_gate)
    grad_up_w = weight_grad(normed_three, grad_up)
    grad_normed = head_sum(project_back(grad_gate, gate_low) + project_back(grad_up, up_low))
    grad_h_two, gain_three = norm_back(h_two, norm_three, grad_normed)
    g_two = cotangent.astype(f32) + grad_h_two
    low_two = g_two.astype(bf16)
    grad_output_two = weight_grad(cross_att, low_two)
    grad_cross_att = project_back(low_two, output_two).astype(bf16)
    grad_cross_q, grad_cross_k, grad_cross_v, unused_extra = attend_backward(
        cross_q, cross_k, cross_v, None, cross_valid, totals_cross, grad_cross_att
    )
    grad_query_two = weight_grad(normed_two, grad_cross_q)
    back_keys, back_values = (
        lax.all_to_all(grad_cross_k, "dp", split_axis=1, concat_axis=0, tiled=True),
        lax.all_to_all(grad_cross_v, "dp", split_axis=1, concat_axis=0, tiled=True),
    )
    back_keys = back_keys[inverse]
    back_values = back_values[inverse]
    grad_key_two = jnp.einsum("esd,esh->dh", encoder_out, back_keys, preferred_element_type=f32)
    grad_value_two = jnp.einsum("esd,esh->dh", encoder_out, back_values, preferred_element_type=f32)
    enc_terms = jnp.einsum(
        "esh,dh->esd", back_keys, key_two, preferred_element_type=f32
    ) + jnp.einsum("esh,dh->esd", back_values, value_two, preferred_element_type=f32)
    encoder_grad = (
        lax.psum_scatter(enc_terms.astype(jnp.bfloat16), "mp", scatter_dimension=2, tiled=True)
        .astype(jnp.float32)
        .astype(bf16)
    )
    grad_normed = head_sum(project_back(grad_cross_q, query_two))
    grad_h_one, gain_two = norm_back(h_one, norm_two, grad_normed)
    g_one = g_two + grad_h_one
    low_one = g_one.astype(bf16)
    grad_output_one = weight_grad(attended, low_one)
    grad_attended = project_back(low_one, output_one).astype(bf16)
    grad_query, grad_keys, grad_values, grad_extra = attend_backward(
        query, keys, values, extras, causal, totals_self, grad_attended
    )
    grad_table = jnp.einsum(
        "hx,xb->bh",
        grad_extra.reshape(grad_extra.shape[0], targets * targets),
        onehot,
        precision=lax.Precision.HIGHEST,
    )
    grad_query_one = weight_grad(normed_one, grad_query)
    grad_key_one = weight_grad(normed_one, grad_keys)
    grad_value_one = weight_grad(normed_one, grad_values)
    grad_normed = head_sum(
        project_back(grad_query, query_one)
        + project_back(grad_keys, key_one)
        + project_back(grad_values, value_one)
    )
    grad_tokens, gain_one = norm_back(tokens, norm_one, grad_normed)
    decoder_grad = g_one + grad_tokens
    (
        grad_self_query,
        grad_self_key,
        grad_self_value,
        grad_self_output,
        grad_cross_query,
        grad_cross_key,
        grad_cross_value,
        grad_cross_output,
        grad_ffn_gate,
        grad_ffn_up,
        grad_ffn_down,
    ) = (
        lax.psum_scatter(grad_query_one, "dp", scatter_dimension=0, tiled=True),
        lax.psum_scatter(grad_key_one, "dp", scatter_dimension=0, tiled=True),
        lax.psum_scatter(grad_value_one, "dp", scatter_dimension=0, tiled=True),
        lax.psum_scatter(grad_output_one, "dp", scatter_dimension=1, tiled=True),
        lax.psum_scatter(grad_query_two, "dp", scatter_dimension=0, tiled=True),
        lax.psum_scatter(grad_key_two, "dp", scatter_dimension=0, tiled=True),
        lax.psum_scatter(grad_value_two, "dp", scatter_dimension=0, tiled=True),
        lax.psum_scatter(grad_output_two, "dp", scatter_dimension=1, tiled=True),
        lax.psum_scatter(grad_gate_w, "dp", scatter_dimension=0, tiled=True),
        lax.psum_scatter(grad_up_w, "dp", scatter_dimension=0, tiled=True),
        lax.psum_scatter(grad_down, "dp", scatter_dimension=1, tiled=True),
    )
    grad_norm_one, grad_norm_two, grad_norm_three, grad_bias_table = lax.psum(
        (gain_one, gain_two, gain_three, grad_table), "dp"
    )
    return (
        layer_out,
        decoder_grad,
        encoder_grad,
        grad_norm_one,
        grad_norm_two,
        grad_norm_three,
        grad_self_query,
        grad_self_key,
        grad_self_value,
        grad_self_output,
        grad_cross_query,
        grad_cross_key,
        grad_cross_value,
        grad_cross_output,
        grad_ffn_gate,
        grad_ffn_up,
        grad_ffn_down,
        grad_bias_table,
    )


def solution(mesh):
    in_specs = (
        P("dp", None, None),
        P(None, "dp", None),
        P(),
        P(),
        P(),
        P(),
        P(),
        P(),
        P(),
        P("dp", "mp"),
        P("dp", "mp"),
        P("dp", "mp"),
        P("mp", "dp"),
        P("dp", "mp"),
        P("dp", "mp"),
        P("dp", "mp"),
        P("mp", "dp"),
        P("dp", "mp"),
        P("dp", "mp"),
        P("mp", "dp"),
        P(None, "mp"),
        P("dp", None, None),
    )
    out_specs = (
        P("dp", None, None),
        P("dp", None, None),
        P(None, "dp", "mp"),
        P(),
        P(),
        P(),
        P("dp", "mp"),
        P("dp", "mp"),
        P("dp", "mp"),
        P("mp", "dp"),
        P("dp", "mp"),
        P("dp", "mp"),
        P("dp", "mp"),
        P("mp", "dp"),
        P("dp", "mp"),
        P("dp", "mp"),
        P("mp", "dp"),
        P(None, "mp"),
    )
    return jax.shard_map(shards, mesh=mesh, in_specs=in_specs, out_specs=out_specs, check_vma=False)
```

profile of v0, /device:TPU:0, one launch (start us, length us, event | category | flops | bytes accessed | tf_op | source)
XLA Modules:
  0.0 2386.3 jit_solution(3226060433992575100)
XLA Ops:
  13.2 48.5 %all_gather.36 = bf16[384,768]{0,1:T(8,128)(2,1)} all-gather(bf16[384,48]{0,1:T(8,128)(2,1)S(1)} %convert_element_type.261), channel_id=1, replica_groups=mesh['dp'=16,'mp'=2] {'dp'}, dimensions={1}, use_global_device_ids=true | all-gather | bytes 626688 | tf_op jit(solution)/shard_map/all_gather | solution.py:165
  61.7 39.0 %all_gather.35 = bf16[768,384]{1,0:T(8,128)(2,1)S(1)} all-gather(bf16[48,384]{1,0:T(8,128)(2,1)S(1)} %convert_element_type.258), channel_id=1, replica_groups=mesh['dp'=16,'mp'=2] {'dp'}, dimensions={0}, use_global_device_ids=true | all-gather | bytes 626688 | tf_op jit(solution)/shard_map/all_gather | solution.py:164
  100.7 41.6 %all_gather.34 = bf16[768,384]{1,0:T(8,128)(2,1)S(1)} all-gather(bf16[48,384]{1,0:T(8,128)(2,1)S(1)} %convert_element_type.255), channel_id=1, replica_groups=mesh['dp'=16,'mp'=2] {'dp'}, dimensions={0}, use_global_device_ids=true | all-gather | bytes 626688 | tf_op jit(solution)/shard_map/all_gather | solution.py:163
  144.3 39.1 %all_gather.33 = bf16[768,384]{1,0:T(8,128)(2,1)S(1)} all-gather(bf16[48,384]{1,0:T(8,128)(2,1)S(1)} %convert_element_type.252), channel_id=1, replica_groups=mesh['dp'=16,'mp'=2] {'dp'}, dimensions={0}, use_global_device_ids=true | all-gather | bytes 626688 | tf_op jit(solution)/shard_map/all_gather | solution.py:162
  185.0 10.5 fusion.98
  195.5 6.3 copy.89
  201.8 6.6 copy.58
  208.4 26.8 %while.75 = (s32[]{:T(128)}, bf16[1,512,384]{1,2,0:T(8,128)(2,1)S(1)}, f32[6,1,512]{2,1,0:T(1,128)S(1)}, bf16[1,512,384]{2,1,0:T(8,128)(2,1)S(1)}, bf16[1,512,38...) while((s32[]{:T(128)}, ...), condition=%wide.region_5.0_spmd.clone, body=%wide.region_1.5_spmd.clone.sunk | while | flops 69500944 | bytes 4677841 | solution.py:70
  237.2 41.6 %all_gather.38 = bf16[768,384]{1,0:T(8,128)(2,1)S(1)} all-gather(bf16[48,384]{1,0:T(8,128)(2,1)S(1)} %convert_element_type.266), channel_id=1, replica_groups=mesh['dp'=16,'mp'=2] {'dp'}, dimensions={0}, use_global_device_ids=true | all-gather | bytes 626688 | tf_op jit(solution)/shard_map/all_gather | solution.py:167
  281.4 13.0 all-to-all-start
  294.4 45.5 %all_gather.39 = bf16[768,384]{1,0:T(8,128)(2,1)S(1)} all-gather(bf16[48,384]{1,0:T(8,128)(2,1)S(1)} %convert_element_type.268), channel_id=1, replica_groups=mesh['dp'=16,'mp'=2] {'dp'}, dimensions={0}, use_global_device_ids=true | all-gather | bytes 626688 | tf_op jit(solution)/shard_map/all_gather | solution.py:168
  352.9 47.3 %all_gather.40 = bf16[384,768]{0,1:T(8,128)(2,1)} all-gather(bf16[384,48]{0,1:T(8,128)(2,1)S(1)} %convert_element_type.270), channel_id=1, replica_groups=mesh['dp'=16,'mp'=2] {'dp'}, dimensions={1}, use_global_device_ids=true | all-gather | bytes 626688 | tf_op jit(solution)/shard_map/all_gather | solution.py:169
  400.2 41.4 %all_gather.37 = bf16[768,384]{1,0:T(8,128)(2,1)} all-gather(bf16[48,384]{1,0:T(8,128)(2,1)S(1)} %convert_element_type.263), channel_id=1, replica_groups=mesh['dp'=16,'mp'=2] {'dp'}, dimensions={0}, use_global_device_ids=true | all-gather | bytes 626688 | tf_op jit(solution)/shard_map/all_gather | solution.py:166
  446.2 42.6 %while.73 = (s32[]{:T(128)}, bf16[1,512,384]{1,2,0:T(8,128)(2,1)}, f32[6,1,512]{2,1,0:T(1,128)}, pred[1,1,1024]{2,1,0:T(4,128)(4,1)S(1)}, bf16[1,512,384]{2,1,0:...) while((s32[]{:T(128)}, bf16[1,512,384]{1,2,0:T(8,128)(2,1)}, ...), condition=%wide.region_12.13_spmd, body=%wide.region_8.12_spmd.sunk | while | flops 138969104 | bytes 7043281 | solution.py:70
  498.8 10.9 all-reduce.10.cloned.1.call-done
  513.7 37.5 %all-gather.6.cloned.1.call-done = bf16[768,1024]{1,0:T(8,128)(2,1)} async-done(((bf16[48,1024]{1,0:T(8,128)(2,1)}), bf16[768,1024]{1,0:T(8,128)(2,1)}) %all-gather.6.cloned.1.call-update) | async-done | bytes 1572880 | tf_op jit(solution)/shard_map/all_gather | solution.py:171
  555.2 55.9 %all-gather.4.cloned.1.call-done = bf16[768,1024]{1,0:T(8,128)(2,1)} async-done(((bf16[48,1024]{1,0:T(8,128)(2,1)}), bf16[768,1024]{1,0:T(8,128)(2,1)}) %all-gather.4.cloned.1.call-update) | async-done | bytes 1572880 | tf_op jit(solution)/shard_map/all_gather | solution.py:170
  611.1 6.1 fusion.108
  622.9 19.1 all-reduce.12.cloned.1.call-done
  650.8 50.1 %while.74 = (s32[]{:T(128)}, bf16[1,512,384]{1,2,0:T(8,128)(2,1)}, bf16[1,1024,384]{1,2,0:T(8,128)(2,1)}, bf16[1,1024,384]{1,2,0:T(8,128)(2,1)}, pred[1,1,1024]{...) while((s32[]{:T(128)}, bf16[1,512,384]{1,2,0:T(8,128)(2,1)}, ...), condition=%wide.region_20.21_spmd, body=%wide.region_18.20_spmd.sunk | while | flops 339901952 | bytes 18958564 | solution.py:120
  701.0 4.8 copy.61
  706.3 7.3 reduce.68
  716.4 7.3 all-to-all-start.3
  723.6 4.8 copy.60
  728.5 7.3 reduce.67
  738.6 5.1 all-to-all-done.3
  743.8 5.1 all-to-all-start.2
  756.5 5.4 reshape.919
  767.7 5.3 reshape.917
  785.4 5.2 copy.65
  790.6 5.4 reshape.906
  806.8 113.1 %while.76 = (s32[]{:T(128)}, bf16[1,512,384]{1,2,0:T(8,128)(2,1)}, bf16[1,512,384]{1,2,0:T(8,128)(2,1)}, bf16[1,512,384]{1,2,0:T(8,128)(2,1)}, f32[6,512,512]{2,...) while((s32[]{:T(128)}, bf16[1,512,384]{1,2,0:T(8,128)(2,1)}, ...), condition=%wide.region_26.27_spmd.clone, body=%wide.region_23.26_spmd.clone.sunk | while | flops 170753568 | bytes 27869508 | solution.py:120
  946.7 4.7 fusion.171
  959.6 6.7 copy.87
  966.3 15.9 fusion.97
  988.9 75.7 %all-reduce = (f32[768]{0:T(1024)}, f32[768]{0:T(1024)}, f32[768]{0:T(1024)}, f32[32,6]{0,1:T(8,128)}) all-reduce(f32[768]{0:T(1024)S(1)} %get-tuple-element.943, f32[768]{0:T(1024)S(1)} %copy-done.77, f32[768]{0:T(1024)S(1)} %copy-done.76, f32[32,6]{0,1:T(8,128)S(1)} %fusion.97), channel_id=1, replica_groups=mesh['dp'=16,'mp'=2] {'dp'}, use_global_device_ids=true, to_apply=%region_32.33 | all-reduce | flops 2496 | bytes 19968 | tf_op jit(solution)/shard_map/psum | solution.py:299
  1064.6 4.6 fusion.115
  1069.2 8.4 reduce-scatter.29.cloned.1.call-done
  1077.7 128.0 %reduce-scatter.27.cloned.1.call-done = f32[48,384]{1,0:T(8,128)} async-done(((f32[768,384]{1,0:T(8,128)}), f32[48,384]{1,0:T(8,128)}) %reduce-scatter.27.cloned.1.call-update) | async-done | bytes 73744 | tf_op jit(solution)/shard_map/reduce_scatter | solution.py:291
  1205.6 128.0 %reduce-scatter.41.cloned.1.call-done = f32[48,384]{1,0:T(8,128)} async-done(((f32[768,384]{1,0:T(8,128)}), f32[48,384]{1,0:T(8,128)}) %reduce-scatter.41.cloned.1.call-update) | async-done | bytes 73744
  1333.6 127.8 %reduce-scatter.39.cloned.1.call-done = f32[48,384]{1,0:T(8,128)} async-done(((f32[768,384]{1,0:T(8,128)}), f32[48,384]{1,0:T(8,128)}) %reduce-scatter.39.cloned.1.call-update) | async-done | bytes 73744
  1461.4 128.0 %reduce-scatter.25.cloned.1.call-done = f32[384,48]{0,1:T(8,128)} async-done(((f32[384,768]{0,1:T(8,128)}), f32[384,48]{0,1:T(8,128)}) %reduce-scatter.25.cloned.1.call-update) | async-done | bytes 73744 | tf_op jit(solution)/shard_map/reduce_scatter | solution.py:290
  1589.4 127.8 %reduce-scatter.19.cloned.1.call-done = f32[48,384]{1,0:T(8,128)} async-done(((f32[768,384]{1,0:T(8,128)}), f32[48,384]{1,0:T(8,128)}) %reduce-scatter.19.cloned.1.call-update) | async-done | bytes 73744 | tf_op jit(solution)/shard_map/reduce_scatter | solution.py:287
  1717.1 128.0 %reduce-scatter.23.cloned.1.call-done = f32[48,384]{1,0:T(8,128)} async-done(((f32[768,384]{1,0:T(8,128)}), f32[48,384]{1,0:T(8,128)}) %reduce-scatter.23.cloned.1.call-update) | async-done | bytes 73744 | tf_op jit(solution)/shard_map/reduce_scatter | solution.py:289
  1845.1 127.8 %reduce-scatter.21.cloned.1.call-done = f32[48,384]{1,0:T(8,128)} async-done(((f32[768,384]{1,0:T(8,128)}), f32[48,384]{1,0:T(8,128)}) %reduce-scatter.21.cloned.1.call-update) | async-done | bytes 73744 | tf_op jit(solution)/shard_map/reduce_scatter | solution.py:288
  1972.9 135.3 %reduce-scatter.33.cloned.1.call-done = f32[48,1024]{1,0:T(8,128)} async-done(((f32[768,1024]{1,0:T(8,128)}), f32[48,1024]{1,0:T(8,128)}) %reduce-scatter.33.cloned.1.call-update) | async-done | bytes 196624 | tf_op jit(solution)/shard_map/reduce_scatter | solution.py:296
  2108.2 135.2 %reduce-scatter.31.cloned.1.call-done = f32[48,1024]{1,0:T(8,128)} async-done(((f32[768,1024]{1,0:T(8,128)}), f32[48,1024]{1,0:T(8,128)}) %reduce-scatter.31.cloned.1.call-update) | async-done | bytes 196624 | tf_op jit(solution)/shard_map/reduce_scatter | solution.py:295
  2243.4 135.4 %reduce-scatter.35.cloned.1.call-done = f32[1024,48]{0,1:T(8,128)} async-done(((f32[1024,768]{0,1:T(8,128)}), f32[1024,48]{0,1:T(8,128)}) %reduce-scatter.35.cloned.1.call-update) | async-done | bytes 196624 | tf_op jit(solution)/shard_map/reduce_scatter | solution.py:297
  (546 shorter events, 376.6 us)
Async XLA Ops:
  8.0 270.8 %copy-start = (bf16[16,64,768]{2,1,0:T(8,128)(2,1)S(1)}, bf16[16,64,768]{2,1,0:T(8,128)(2,1)}, u32[]{:S(2)}) copy-start(bf16[16,64,768]{2,1,0:T(8,128)(2,1)} %param.37) | copy-start | bytes 4718596
  8.0 134.3 %copy-start.7 = (bf16[1,512,768]{2,1,0:T(8,128)(2,1)S(1)}, bf16[1,512,768]{2,1,0:T(8,128)(2,1)}, u32[]{:S(2)}) copy-start(bf16[1,512,768]{2,1,0:T(8,128)(2,1)} %param.36) | copy-start | bytes 2359300
  8.0 134.3 %copy-start.55 = (f32[768]{0:T(1024)S(1)}, f32[768]{0:T(1024)}, u32[]{:S(2)}) copy-start(f32[768]{0:T(1024)} %param.42) | copy-start | bytes 9220
  8.1 433.6 %all-reduce.8.cloned.1.call-start = ((), (), s32[]{:S(2)}) async-start(), calls=%async_computation.16 | async-start | bytes 3145728 | tf_op jit(solution)/shard_map/psum | solution.py:39
  9.6 132.7 %copy-start.72 = (f32[512]{0:T(512)}, f32[512]{0:T(512)S(1)}, u32[]{:S(2)}) copy-start(f32[512]{0:T(512)S(1)} %fusion.116) | copy-start | bytes 6148
  9.6 173.8 %copy-start.62 = (f32[512]{0:T(512)}, f32[512]{0:T(512)S(1)}, u32[]{:S(2)}) copy-start(f32[512]{0:T(512)S(1)} %fusion.164) | copy-start | bytes 6148
  100.7 43.0 %copy-start.47 = (bf16[768,384]{1,0:T(8,128)(2,1)}, bf16[768,384]{1,0:T(8,128)(2,1)S(1)}, u32[]{:S(2)}) copy-start(bf16[768,384]{1,0:T(8,128)(2,1)S(1)} %all_gather.35) | copy-start | bytes 1769476
  144.3 39.9 %copy-start.51 = (s32[512,512]{1,0:T(8,128)S(1)}, s32[512,512]{1,0:T(8,128)}, u32[]{:S(2)}) copy-start(s32[512,512]{1,0:T(8,128)} %param.41) | copy-start | bytes 3145732
  184.5 10.9 copy-start.29
  201.8 6.6 copy-start.54
  208.4 26.9 %copy-start.25 = (bf16[384,768]{0,1:T(8,128)(2,1)S(1)}, bf16[384,768]{0,1:T(8,128)(2,1)}, u32[]{:S(2)}) copy-start(bf16[384,768]{0,1:T(8,128)(2,1)} %all_gather.36) | copy-start | bytes 1769476
  237.2 42.6 %copy-start.79 = (s32[16]{0:T(128)}, s32[16]{0:T(128)S(1)}, u32[]{:S(2)}) copy-start(s32[16]{0:T(128)S(1)} %compare_select_fusion.1) | copy-start | bytes 196
  279.8 14.6 copy-start.59
  281.4 61.9 %all-to-all-start = ((bf16[16,64,384]{2,1,0:T(8,128)(2,1)}), bf16[16,64,384]{2,1,0:T(8,128)(2,1)S(1)}, u32[]{:S(2)}, u32[]{:S(2)}) async-start(bf16[16,64,384]{2,1,0:T(8,128)(2,1)} %gather_fusion), calls=%async_computation | async-start | bytes 1572864 | tf_op jit(solution)/shard_map/all_to_all | solution.py:205
  341.7 5.9 copy-start.53
  341.7 8.6 copy-start.60
  341.7 8.6 copy-start.61
  341.7 9.2 copy-start.83
  343.2 98.4 %copy-start.9 = (bf16[16,64,384]{2,1,0:T(8,128)(2,1)}, bf16[16,64,384]{2,1,0:T(8,128)(2,1)S(1)}, u32[]{:S(2)}) copy-start(bf16[16,64,384]{2,1,0:T(8,128)(2,1)S(1)} %all-to-all-done) | copy-start | bytes 2359300
  343.2 101.6 %all-to-all-start.1 = ((bf16[16,64,384]{2,1,0:T(8,128)(2,1)}), bf16[16,64,384]{2,1,0:T(8,128)(2,1)}, u32[]{:S(2)}, u32[]{:S(2)}) async-start(bf16[16,64,384]{2,1,0:T(8,128)(2,1)} %gather_fusion.1), calls=%async_computation.1 | async-start | bytes 1572864 | tf_op jit(solution)/shard_map/all_to_all | solution.py:206
  347.5 147.6 %all-gather.8.cloned.1.call-start = ((), (), s32[]{:S(2)}) async-start(), calls=%async_computation.20 | async-start | bytes 1671168 | tf_op jit(solution)/shard_map/all_gather | solution.py:172
  348.3 161.5 %all-reduce.10.cloned.1.call-start = ((), (), s32[]{:S(2)}) async-start(), calls=%async_computation.17 | async-start | bytes 3145728 | tf_op jit(solution)/shard_map/psum | solution.py:39
  443.6 355.7 %copy-start.2 = (f32[1,512,768]{2,1,0:T(8,128)}, f32[1,512,768]{2,1,0:T(8,128)S(1)}, u32[]{:S(2)}) copy-start(f32[1,512,768]{2,1,0:T(8,128)S(1)} %get-tuple-element.1024) | copy-start | bytes 4718596
  491.8 59.4 %all-gather.6.cloned.1.call-start = ((), (), s32[]{:S(2)}) async-start(), calls=%async_computation.19 | async-start | bytes 1671168 | tf_op jit(solution)/shard_map/all_gather | solution.py:171
  493.4 117.7 %all-gather.4.cloned.1.call-start = ((), (), s32[]{:S(2)}) async-start(), calls=%async_computation.18 | async-start | bytes 1671168 | tf_op jit(solution)/shard_map/all_gather | solution.py:170
  495.1 146.9 %all-reduce.12.cloned.1.call-start = ((), (), s32[]{:S(2)}) async-start(), calls=%async_computation.21 | async-start | bytes 3145728 | tf_op jit(solution)/shard_map/psum | solution.py:39
  498.8 13.8 copy-start.67
  611.1 6.1 copy-start.81
  716.4 27.4 %all-to-all-start.3 = ((bf16[16,2,12288]{2,1,0:T(2,128)(2,1)}), bf16[16,2,12288]{2,1,0:T(2,128)(2,1)}, u32[]{:S(2)}, u32[]{:S(2)}) async-start(bf16[16,2,12288]{2,1,0:T(2,128)(2,1)} %reshape.918), calls=%async_computation.3 | async-start | bytes 1572864 | tf_op jit(solution)/shard_map/all_to_all | solution.py:235
  735.8 13.1 copy-start.38
  743.8 23.9 %all-to-all-start.2 = ((bf16[16,2,12288]{2,1,0:T(2,128)(2,1)}), bf16[16,2,12288]{2,1,0:T(2,128)(2,1)}, u32[]{:S(2)}, u32[]{:S(2)}) async-start(bf16[16,2,12288]{2,1,0:T(2,128)(2,1)} %reshape.916), calls=%async_computation.2 | async-start | bytes 1572864 | tf_op jit(solution)/shard_map/all_to_all | solution.py:234
  748.9 47.2 %all-reduce.14.cloned.1.call-start = ((), (), s32[]{:S(2)}) async-start(), calls=%async_computation.22 | async-start | bytes 3145728 | tf_op jit(solution)/shard_map/psum | solution.py:39
  751.8 230.4 %reduce-scatter.37.cloned.1.call-start = ((), (), s32[]{:S(2)}) async-start(), calls=%async_computation.32 | async-start | bytes 2359296
  796.0 190.5 %all-reduce.16.cloned.1.call-start = ((), (), s32[]{:S(2)}) async-start(), calls=%async_computation.35 | async-start | bytes 6291456 | tf_op jit(solution)/shard_map/psum | solution.py:39
  924.7 153.0 %reduce-scatter.29.cloned.1.call-start = ((), (), s32[]{:S(2)}) async-start(), calls=%async_computation.28 | async-start | bytes 1253376 | tf_op jit(solution)/shard_map/reduce_scatter | solution.py:294
  928.7 276.9 %reduce-scatter.27.cloned.1.call-start = ((), (), s32[]{:S(2)}) async-start(), calls=%async_computation.27 | async-start | bytes 1253376 | tf_op jit(solution)/shard_map/reduce_scatter | solution.py:291
  931.8 401.8 %reduce-scatter.41.cloned.1.call-start = ((), (), s32[]{:S(2)}) async-start(), calls=%async_computation.34 | async-start | bytes 1253376
  935.3 526.1 %reduce-scatter.39.cloned.1.call-start = ((), (), s32[]{:S(2)}) async-start(), calls=%async_computation.33 | async-start | bytes 1253376
  937.6 651.7 %reduce-scatter.25.cloned.1.call-start = ((), (), s32[]{:S(2)}) async-start(), calls=%async_computation.26 | async-start | bytes 1253376 | tf_op jit(solution)/shard_map/reduce_scatter | solution.py:290
  941.0 776.2 %reduce-scatter.19.cloned.1.call-start = ((), (), s32[]{:S(2)}) async-start(), calls=%async_computation.23 | async-start | bytes 1253376 | tf_op jit(solution)/shard_map/reduce_scatter | solution.py:287
  942.9 902.2 %reduce-scatter.23.cloned.1.call-start = ((), (), s32[]{:S(2)}) async-start(), calls=%async_computation.25 | async-start | bytes 1253376 | tf_op jit(solution)/shard_map/reduce_scatter | solution.py:289
  944.8 1028.1 %reduce-scatter.21.cloned.1.call-start = ((), (), s32[]{:S(2)}) async-start(), calls=%async_computation.24 | async-start | bytes 1253376 | tf_op jit(solution)/shard_map/reduce_scatter | solution.py:288
  946.6 1161.6 %reduce-scatter.33.cloned.1.call-start = ((), (), s32[]{:S(2)}) async-start(), calls=%async_computation.30 | async-start | bytes 3342336 | tf_op jit(solution)/shard_map/reduce_scatter | solution.py:296
  951.4 1291.9 %reduce-scatter.31.cloned.1.call-start = ((), (), s32[]{:S(2)}) async-start(), calls=%async_computation.29 | async-start | bytes 3342336 | tf_op jit(solution)/shard_map/reduce_scatter | solution.py:295
  955.4 1423.3 %reduce-scatter.35.cloned.1.call-start = ((), (), s32[]{:S(2)}) async-start(), calls=%async_computation.31 | async-start | bytes 3342336 | tf_op jit(solution)/shard_map/reduce_scatter | solution.py:297
  959.5 6.7 copy-start.30
  986.6 78.0 %copy-start.73 = (f32[512]{0:T(512)S(1)}, f32[512]{0:T(512)}, u32[]{:S(2)}) copy-start(f32[512]{0:T(512)} %copy-done.72) | copy-start | bytes 6148
  986.6 78.1 %copy-start.6 = (f32[1,512,768]{2,1,0:T(8,128)S(1)}, f32[1,512,768]{2,1,0:T(8,128)}, u32[]{:S(2)}) copy-start(f32[1,512,768]{2,1,0:T(8,128)} %copy-done.4) | copy-start | bytes 4718596
  (80 other events, 173.7 us)
Sparse Core Ops, SparseCore 0:
  237.3 17.8 all-reduce.7
  491.9 17.8 all-reduce.9
  623.0 18.9 all-reduce.11
  751.9 21.6 all-reduce.13
  796.1 8.4 reduce-scatter.36
  924.8 22.6 all-reduce.15
  952.8 124.8 reduce-scatter.28
  1083.0 122.6 reduce-scatter.26
  1211.0 122.5 reduce-scatter.40
  1338.8 122.5 reduce-scatter.38
  1466.7 122.5 reduce-scatter.24
  1594.5 122.5 reduce-scatter.18
  1722.5 122.5 reduce-scatter.22
  1850.3 122.5 reduce-scatter.20
  1978.3 129.8 reduce-scatter.32
  2113.6 129.7 reduce-scatter.30
  2248.8 129.9 reduce-scatter.34
Sparse Core Ops, SparseCore 1:
  351.4 60.6 all-gather.7
  495.6 55.5 all-gather.5
  554.4 56.6 all-gather.3
where the time goes:
time: 2390 us
  waiting for transfers between devices  1440 us (60%)
  blocking collectives  420 us (18%)
  matrix products  230 us (10%)
  local copies, waits for them, and re-layouts  153 us (6%)
  other arithmetic  91 us (4%)
  starting transfers between devices  31.1 us (1%)
    unnamed x23, waiting for transfers between devices  256 us
    reduce_scatter x1, waiting for transfers between devices, shards(): lax.psum_scatter(grad_down, 'dp', scatter_dimension=1, tiled=True)  135 us
    reduce_scatter x1, waiting for transfers between devices, shards(): lax.psum_scatter(grad_up_w, 'dp', scatter_dimension=0, tiled=True)  135 us
    reduce_scatter x1, waiting for transfers between devices, shards(): lax.psum_scatter(grad_gate_w, 'dp', scatter_dimension=0, tiled=True)  135 us
    reduce_scatter x1, waiting for transfers between devices, shards(): lax.psum_scatter(grad_query_two, 'dp', scatter_dimension=0, tiled=True)  128 us
    reduce_scatter x1, waiting for transfers between devices, shards(): lax.psum_scatter(grad_output_one, 'dp', scatter_dimension=1, tiled=True)  128 us
    reduce_scatter x1, waiting for transfers between devices, shards(): lax.psum_scatter(grad_value_one, 'dp', scatter_dimension=0, tiled=True)  128 us
    reduce_scatter x1, waiting for transfers between devices, shards(): lax.psum_scatter(grad_key_one, 'dp', scatter_dimension=0, tiled=True)  128 us
  transfers between devices with their start and end apart: 24, of which 17 were waited for; matrix products, arithmetic and copies ran while one was open for 13% of the time, Pallas kernels for 0%

commit v1 on v0

v1 whole, which is shorter than its diff:
```python
import functools

import jax
import jax.numpy as jnp
from jax import lax
from jax.experimental import pallas as pl
from jax.experimental.pallas import tpu as pltpu
from jax.sharding import PartitionSpec as P

HEAD_DIM = 64
PAIR = 2 * HEAD_DIM
QUERIES = 256
KEYS = 1024
TILE = 128

EPS = 1e-06
NEGATIVE = -1000000000.0
BF16 = jnp.bfloat16
F32 = jnp.float32


def norm_apply(value, gain):
    return value * lax.rsqrt(jnp.mean(value * value, axis=-1, keepdims=True) + EPS) * gain


def mixer(gate, up):
    return jax.nn.gelu(gate, approximate=True) * up


def dot(left, right, dims):
    return lax.dot_general(left, right, (dims, ((), ())), preferred_element_type=F32)


def nn(left, right):
    return dot(left, right, ((1,), (0,)))


def nt(left, right):
    return dot(left, right, ((1,), (1,)))


def tn(left, right):
    return dot(left, right, ((0,), (0,)))


def swap(value, mask, size):
    return lax.ppermute(value, "dp", [(i, i ^ mask) for i in range(size)])


def swap_cores(value):
    return lax.ppermute(value, "mp", [(0, 1), (1, 0)])


def cut_of(columns):
    return (columns // TILE + 1) // 2 * TILE


def gather_rows(shard, size):
    outer = size // 4
    cut = cut_of(shard.shape[1])
    if outer <= 4:
        rows = jnp.concatenate([shard] + [swap(shard, 4 * k, size) for k in range(1, outer)])
    else:
        rows, mask = shard, 4
        while mask < size:
            rows = jnp.concatenate([rows, swap(rows, mask, size)])
            mask *= 2
    quarter = rows.shape[0]
    left, right = rows[:, :cut], rows[:, cut:]
    left = jnp.concatenate([left, swap(left, 2, size)])
    right = jnp.concatenate([right, swap(right, 1, size)])
    left_more, right_more = swap(left, 1, size), swap(right, 2, size)
    left = jnp.concatenate([left, left_more])
    right = jnp.concatenate(
        [right[:quarter], right_more[:quarter], right[quarter:], right_more[quarter:]]
    )
    return jnp.concatenate([left, right], axis=1)


def scatter_rows(grad, size):
    outer = size // 4
    quarter = grad.shape[0] // 4
    half = 2 * quarter
    cut = cut_of(grad.shape[1])
    low = grad.astype(BF16)
    left, right = low[:, :cut], low[:, cut:]
    left_in = swap(left[half:], 1, size)
    right_out = jnp.concatenate([right[quarter:half], right[half + quarter :]])
    right_in = swap(right_out, 2, size)
    left = left[:half].astype(F32) + left_in.astype(F32)
    right = jnp.concatenate([right[:quarter], right[half : half + quarter]]).astype(
        F32
    ) + right_in.astype(F32)
    left_in = swap(left[quarter:].astype(BF16), 2, size)
    right_in = swap(right[quarter:].astype(BF16), 1, size)
    left = left[:quarter] + left_in.astype(F32)
    right = right[:quarter] + right_in.astype(F32)
    rows = jnp.concatenate([left, right], axis=1)
    if outer <= 4:
        count = quarter // outer
        total = rows[:count]
        for k in range(1, outer):
            total = total + swap(
                rows[k * count : (k + 1) * count].astype(BF16), 4 * k, size
            ).astype(F32)
        return total
    mask = size // 2
    while mask >= 4:
        count = rows.shape[0] // 2
        rows = rows[:count] + swap(rows[count:].astype(BF16), mask, size).astype(F32)
        mask //= 2
    return rows


def sum_devices(value, size):
    value = value + swap_cores(value)
    value = value + swap(value, 1, size)
    value = value + swap(value, 2, size)
    if size <= 16:
        total = value
        for k in range(1, size // 4):
            total = total + swap(value, 4 * k, size)
        return total
    mask = 4
    while mask < size:
        value = value + swap(value, mask, size)
        mask *= 2
    return value


def each_chunk(count, size, body):
    if count == 1:
        body(0)
    else:
        pl.loop(0, count)(lambda step: body(pl.multiple_of(step * size, size)))


def of_head(value, head):
    lane = lax.broadcasted_iota(jnp.int32, value.shape, 1)
    return jnp.where(lane // HEAD_DIM == head, value, jnp.zeros_like(value))


def cross_forward_kernel(q_ref, k_ref, v_ref, dead_ref, out_ref, lse_ref, s_ref, acc_ref):
    targets, capacity = q_ref.shape[0], k_ref.shape[0]
    size = min(capacity, KEYS)
    count = capacity // size
    for head in range(2):
        rows = slice(head * HEAD_DIM, (head + 1) * HEAD_DIM)
        for start in range(0, targets, QUERIES):
            cols = slice(start, start + QUERIES)
            query = of_head(q_ref[cols, :], head)
            top = jnp.full((1, QUERIES), NEGATIVE * 2, F32)
            lse_ref[0, head : head + 1, cols] = top

            def scores(base):
                keys = pl.ds(base, size)
                score = nt(k_ref[keys, :], query) + dead_ref[keys, 0:1]
                s_ref[keys, :] = score
                lse_ref[0, head : head + 1, cols] = jnp.maximum(
                    lse_ref[0, head : head + 1, cols], jnp.max(score, axis=0, keepdims=True)
                )

            each_chunk(count, size, scores)
            top = lse_ref[0, head : head + 1, cols]
            lse_ref[0, head : head + 1, cols] = jnp.zeros((1, QUERIES), F32)

            def weights(base):
                keys = pl.ds(base, size)
                weight = jnp.exp(s_ref[keys, :] - top)
                s_ref[keys, :] = weight
                lse_ref[0, head : head + 1, cols] += jnp.sum(weight, axis=0, keepdims=True)

            each_chunk(count, size, weights)
            total = lse_ref[0, head : head + 1, cols]
            lse_ref[0, head : head + 1, cols] = top + jnp.log(total)
            scale = 1.0 / total
            acc_ref[rows, cols] = jnp.zeros((HEAD_DIM, QUERIES), F32)

            def mix(base):
                keys = pl.ds(base, size)
                probs = (s_ref[keys, :] * scale).astype(BF16)
                acc_ref[rows, cols] += tn(v_ref[keys, :], probs)[rows]

            each_chunk(count, size, mix)
    out_ref[...] = acc_ref[...].T.astype(BF16)


def cross_backward_kernel(
    q_ref, k_ref, v_ref, dead_ref, lse_ref, go_ref, dq_ref, dk_ref, dv_ref,
    p_ref, dp_ref, dqt_ref, dk_acc, dv_acc, delta_ref,
):
    targets, capacity = q_ref.shape[0], k_ref.shape[0]
    size = min(capacity, KEYS)
    count = capacity // size
    dk_acc[...] = jnp.zeros_like(dk_acc)
    dv_acc[...] = jnp.zeros_like(dv_acc)
    for head in range(2):
        rows = slice(head * HEAD_DIM, (head + 1) * HEAD_DIM)
        for start in range(0, targets, QUERIES):
            cols = slice(start, start + QUERIES)
            query = of_head(q_ref[cols, :], head)
            grad = of_head(go_ref[cols, :], head)
            lse = lse_ref[0, head : head + 1, cols]
            delta_ref[...] = jnp.zeros_like(delta_ref)

            def first(base):
                keys = pl.ds(base, size)
                probs = jnp.exp(nt(k_ref[keys, :], query) + dead_ref[keys, 0:1] - lse)
                grad_probs = nt(v_ref[keys, :], grad)
                p_ref[keys, :] = probs
                dp_ref[keys, :] = grad_probs
                delta_ref[...] += jnp.sum(probs * grad_probs, axis=0, keepdims=True)

            each_chunk(count, size, first)
            delta = delta_ref[...]
            dqt_ref[rows, cols] = jnp.zeros((HEAD_DIM, QUERIES), F32)

            def second(base):
                keys = pl.ds(base, size)
                probs = p_ref[keys, :]
                dv_acc[keys, :] += nn(probs.astype(BF16), grad)
                low = (probs * (dp_ref[keys, :] - delta)).astype(BF16)
                dk_acc[keys, :] += nn(low, query)
                dqt_ref[rows, cols] += tn(k_ref[keys, :], low)[rows]

            each_chunk(count, size, second)
    dq_ref[...] = dqt_ref[...].T.astype(BF16)
    dk_ref[...] = dk_acc[...].astype(BF16)
    dv_ref[...] = dv_acc[...].astype(BF16)


def skewed(row, block):
    low = row[:, (block - 1) * TILE : block * TILE] if block else jnp.zeros((1, TILE), F32)
    both = jnp.concatenate([low, row[:, block * TILE : (block + 1) * TILE]], axis=1)
    both = jnp.broadcast_to(both, (TILE, 2 * TILE))
    return pltpu.roll(both, 0, 1, stride=1, stride_axis=0)[:, TILE:]


def unskewed(tile):
    both = jnp.concatenate([jnp.zeros_like(tile), tile], axis=1)
    total = both[:8]
    for base in range(8, TILE, 8):
        total = total + pltpu.roll(both[base : base + 8], 2 * TILE - base, 1)
    row = lax.broadcasted_iota(jnp.int32, total.shape, 0)
    for bit in (1, 2, 4):
        total = jnp.where(row & bit != 0, pltpu.roll(total, 2 * TILE - bit, 1), total)
    return jnp.sum(total, axis=0, keepdims=True)


def self_scores(k_ref, query, tiles, start):
    keys = start + QUERIES
    columns = []
    for i in range(start // TILE, keys // TILE):
        columns.append(
            jnp.concatenate([tiles[max(i - j, 0)] for j in range(keys // TILE)], axis=0)
        )
    score = nt(k_ref[:keys, :], query) + jnp.concatenate(columns, axis=1)
    key = lax.broadcasted_iota(jnp.int32, score.shape, 0)
    spot = lax.broadcasted_iota(jnp.int32, score.shape, 1) + start
    return jnp.where(key <= spot, score, NEGATIVE)


def self_forward_kernel(q_ref, k_ref, v_ref, bias_ref, out_ref, lse_ref, acc_ref):
    targets = q_ref.shape[0]
    for head in range(2):
        rows = slice(head * HEAD_DIM, (head + 1) * HEAD_DIM)
        row = bias_ref[0, head : head + 1, :]
        tiles = [skewed(row, block) for block in range(targets // TILE)]
        for start in range(0, targets, QUERIES):
            cols = slice(start, start + QUERIES)
            query = of_head(q_ref[cols, :], head)
            score = self_scores(k_ref, query, tiles, start)
            top = jnp.max(score, axis=0, keepdims=True)
            weight = jnp.exp(score - top)
            total = jnp.sum(weight, axis=0, keepdims=True)
            lse_ref[0, head : head + 1, cols] = top + jnp.log(total)
            probs = (weight * (1.0 / total)).astype(BF16)
            acc_ref[rows, cols] = tn(v_ref[: start + QUERIES, :], probs)[rows]
    out_ref[...] = acc_ref[...].T.astype(BF16)


def self_backward_kernel(
    q_ref, k_ref, v_ref, bias_ref, lse_ref, go_ref, dq_ref, dk_ref, dv_ref, dbias_ref,
    dqt_ref, dk_acc, dv_acc,
):
    targets = q_ref.shape[0]
    dk_acc[...] = jnp.zeros_like(dk_acc)
    dv_acc[...] = jnp.zeros_like(dv_acc)
    blocks = targets // TILE
    for head in range(2):
        rows = slice(head * HEAD_DIM, (head + 1) * HEAD_DIM)
        row = bias_ref[0, head : head + 1, :]
        tiles = [skewed(row, block) for block in range(blocks)]
        sums = [jnp.zeros((TILE, TILE), F32) for block in range(blocks)]
        for start in range(0, targets, QUERIES):
            cols = slice(start, start + QUERIES)
            keys = start + QUERIES
            query = of_head(q_ref[cols, :], head)
            grad = of_head(go_ref[cols, :], head)
            score = self_scores(k_ref, query, tiles, start)
            probs = jnp.exp(score - lse_ref[0, head : head + 1, cols])
            grad_probs = nt(v_ref[:keys, :], grad)
            delta = jnp.sum(probs * grad_probs, axis=0, keepdims=True)
            dv_acc[:keys, :] += nn(probs.astype(BF16), grad)
            grad_scores = probs * (grad_probs - delta)
            for i in range(start // TILE, keys // TILE):
                for j in range(i + 1):
                    sums[i - j] = sums[i - j] + grad_scores[
                        j * TILE : (j + 1) * TILE, i * TILE - start : (i + 1) * TILE - start
                    ]
            low = grad_scores.astype(BF16)
            dk_acc[:keys, :] += nn(low, query)
            dqt_ref[rows, cols] = tn(k_ref[:keys, :], low)[rows]
        lines = [unskewed(tile) for tile in sums]
        parts = []
        for block in range(blocks):
            part = lines[block][:, TILE:]
            if block + 1 < blocks:
                part = part + lines[block + 1][:, :TILE]
            parts.append(part)
        dbias_ref[0, head : head + 1, :] = jnp.concatenate(parts, axis=1)
    dq_ref[...] = dqt_ref[...].T.astype(BF16)
    dk_ref[...] = dk_acc[...].astype(BF16)
    dv_ref[...] = dv_acc[...].astype(BF16)


def pair_call(kernel, ins, outs, scratch, flops):
    def spec(shape, whole=False):
        if whole:
            return pl.BlockSpec(shape, lambda pair: (0, 0))
        if len(shape) == 3:
            return pl.BlockSpec((1,) + shape[1:], lambda pair: (pair, 0, 0))
        return pl.BlockSpec((shape[0], PAIR), lambda pair: (0, pair))

    pairs = ins[0].shape[1] // PAIR
    size = sum(value.size * value.dtype.itemsize for value in ins)
    return pl.pallas_call(
        kernel,
        grid=(pairs,),
        in_specs=[spec(value.shape, value.dtype == F32 and value.ndim == 2) for value in ins],
        out_specs=[spec(value.shape) for value in outs],
        out_shape=outs,
        scratch_shapes=scratch,
        compiler_params=pltpu.CompilerParams(vmem_limit_bytes=60 * 1024 * 1024),
        cost_estimate=pl.CostEstimate(flops=flops, bytes_accessed=size, transcendentals=flops // 256),
    )(*ins)


def struct(shape, dtype):
    return jax.ShapeDtypeStruct(shape, dtype)


def cross_forward(query, keys, values, dead):
    targets, width = query.shape
    capacity = keys.shape[0]
    return pair_call(
        cross_forward_kernel,
        [query, keys, values, dead],
        [struct(query.shape, BF16), struct((width // PAIR, 8, targets), F32)],
        [pltpu.VMEM((capacity, QUERIES), F32), pltpu.VMEM((PAIR, targets), F32)],
        4 * targets * capacity * width,
    )


def cross_backward(query, keys, values, dead, lse, grad):
    targets, width = query.shape
    capacity = keys.shape[0]
    return pair_call(
        cross_backward_kernel,
        [query, keys, values, dead, lse, grad],
        [struct(query.shape, BF16), struct(keys.shape, BF16), struct(keys.shape, BF16)],
        [
            pltpu.VMEM((capacity, QUERIES), F32),
            pltpu.VMEM((capacity, QUERIES), F32),
            pltpu.VMEM((PAIR, targets), F32),
            pltpu.VMEM((capacity, PAIR), F32),
            pltpu.VMEM((capacity, PAIR), F32),
            pltpu.VMEM((1, QUERIES), F32),
        ],
        10 * targets * capacity * width,
    )


def self_forward(query, keys, values, bias):
    targets, width = query.shape
    return pair_call(
        self_forward_kernel,
        [query, keys, values, bias],
        [struct(query.shape, BF16), struct((width // PAIR, 8, targets), F32)],
        [pltpu.VMEM((PAIR, targets), F32)],
        3 * targets * targets * width,
    )


def self_backward(query, keys, values, bias, lse, grad):
    targets, width = query.shape
    return pair_call(
        self_backward_kernel,
        [query, keys, values, bias, lse, grad],
        [
            struct(query.shape, BF16),
            struct(query.shape, BF16),
            struct(query.shape, BF16),
            struct((width // PAIR, 8, targets), F32),
        ],
        [
            pltpu.VMEM((PAIR, targets), F32),
            pltpu.VMEM((targets, PAIR), F32),
            pltpu.VMEM((targets, PAIR), F32),
        ],
        8 * targets * targets * width,
    )


def norm_back(value, gain, grad):
    root = lax.rsqrt(jnp.mean(value * value, axis=-1, keepdims=True) + EPS)
    scaled = grad * gain
    inner = jnp.mean(value * scaled, axis=-1, keepdims=True)
    return root * scaled - value * (root * root * root * inner)


def gain_grad(value, grad):
    root = lax.rsqrt(jnp.mean(value * value, axis=-1, keepdims=True) + EPS)
    return jnp.sum(grad * value * root, axis=0)


def shards(
    decoder_in,
    encoder_out,
    lengths,
    key_mask,
    assign,
    buckets,
    norm_one,
    norm_two,
    norm_three,
    self_query,
    self_key,
    self_value,
    self_output,
    cross_query,
    cross_key,
    cross_value,
    cross_output,
    ffn_gate,
    ffn_up,
    ffn_down,
    bias_table,
    cotangent,
    *,
    size,
):
    rank = lax.axis_index("dp")
    core = lax.axis_index("mp")
    targets, width = decoder_in.shape[1:]
    capacity = key_mask.shape[1]
    block = width // size
    outer = size // 4
    half = width // 2
    heads = bias_table.shape[1]

    spots = jnp.arange(size, dtype=jnp.int32)
    masks = spots // (2 * outer) + 2 * (spots // outer % 2) + 4 * (spots % outer)
    owner = rank ^ masks
    other = rank ^ spots
    place = (other % 2) * (2 * outer) + (other // 2 % 2) * outer + other // 4
    source = (owner[:, None] * block + jnp.arange(block, dtype=jnp.int32)[None, :]).reshape(-1)
    order = (jnp.arange(width, dtype=jnp.int32)[:, None] == source[None, :]).astype(BF16)

    def true_rows(value):
        return value.reshape(size, block, -1)[place].reshape(width, -1)

    def own_rows(value):
        return value.reshape(size, block, -1)[owner].reshape(width, -1)

    def low(*shards):
        return jnp.concatenate([value.astype(BF16) for value in shards], axis=1)

    qkv = gather_rows(low(self_query, self_key, self_value), size)
    part = self_query.shape[1]
    attend = gather_rows(
        low(self_output.T, cross_query, cross_output.T, cross_key, cross_value), size
    )
    ffn = gather_rows(low(ffn_gate, ffn_up), size)
    down = gather_rows(ffn_down.T.astype(BF16), size)
    output_one, query_two, output_two = (
        attend[:, i * part : (i + 1) * part] for i in range(3)
    )
    key_value = true_rows(attend[:, 3 * part :])
    hidden = ffn_gate.shape[1]

    mine = assign[rank]
    sent = lax.dynamic_slice_in_dim(encoder_out, core * half, half, 2)[assign]
    own = lax.all_to_all(sent, "dp", split_axis=0, concat_axis=0, tiled=True)
    own = own.reshape(capacity, half)
    peer = swap_cores(own)
    encoded = jnp.where(
        core == 0, jnp.concatenate([own, peer], axis=1), jnp.concatenate([peer, own], axis=1)
    )
    cross_kv = nn(encoded, key_value).astype(BF16)
    cross_k, cross_v = cross_kv[:, :part], cross_kv[:, part:]

    positions = jnp.arange(capacity, dtype=jnp.int32)
    live = (positions < lengths[mine]) & ((key_mask[mine] == 1) | (positions == 0))
    dead = jnp.broadcast_to(jnp.where(live, 0.0, NEGATIVE)[:, None], (capacity, TILE))
    labels = buckets[:, 0]
    which = labels[None, :] == jnp.arange(bias_table.shape[0], dtype=jnp.int32)[:, None]
    bias = jnp.sum(jnp.where(which[None], bias_table.T[:, :, None], 0.0), axis=1)
    bias = jnp.pad(bias.reshape(heads // 2, 2, targets), ((0, 0), (0, 6), (0, 0)))

    gains = jnp.stack([norm_one, norm_two, norm_three]).reshape(3, size, block)
    gain_one, gain_two, gain_three = gains[:, owner].reshape(3, width)
    tokens = nn(decoder_in[0], order)
    cot = nn(cotangent[0], order).astype(BF16)

    normed_one = norm_apply(tokens, gain_one).astype(BF16)
    mixed = nn(normed_one, qkv).astype(BF16)
    query, keys, values = (mixed[:, i * part : (i + 1) * part] for i in range(3))
    attended, lse_self = self_forward(query, keys, values, bias)
    partial = nt(attended, output_one)
    h_one = tokens + (partial + swap_cores(partial))
    normed_two = norm_apply(h_one, gain_two).astype(BF16)
    cross_q = nn(normed_two, query_two).astype(BF16)
    cross_att, lse_cross = cross_forward(cross_q, cross_k, cross_v, dead)
    partial = nt(cross_att, output_two)
    h_two = h_one + (partial + swap_cores(partial))
    normed_three = norm_apply(h_two, gain_three).astype(BF16)
    gate_up = nn(normed_three, ffn)
    gate, up = gate_up[:, :hidden], gate_up[:, hidden:]
    act, pull_mixer = jax.vjp(mixer, gate, up)
    act = act.astype(BF16)
    partial = nt(act, down)
    layer_out = (h_two + (partial + swap_cores(partial))).astype(BF16)
    layer_out = nt(layer_out, order).astype(BF16)

    grad_act = nn(cot, down).astype(BF16)
    grad_gate, grad_up = pull_mixer(grad_act.astype(F32))
    grad_gate_up = jnp.concatenate([grad_gate.astype(BF16), grad_up.astype(BF16)], axis=1)
    grad_down = tn(cot, act)
    grad_ffn = tn(normed_three, grad_gate_up)
    sum_down = scatter_rows(grad_down, size)
    sum_ffn = scatter_rows(grad_ffn, size)
    partial = nt(grad_gate_up, ffn)
    grad_normed = partial + swap_cores(partial)
    g_two = cot.astype(F32) + norm_back(h_two, gain_three, grad_normed)
    gain_grad_three = gain_grad(h_two, partial)

    low_two = g_two.astype(BF16)
    grad_cross_att = nn(low_two, output_two).astype(BF16)
    grad_cross_q, grad_cross_k, grad_cross_v = cross_backward(
        cross_q, cross_k, cross_v, dead, lse_cross, grad_cross_att
    )
    grad_cross_kv = jnp.concatenate([grad_cross_k, grad_cross_v], axis=1)
    partial = nt(grad_cross_q, query_two)
    grad_normed = partial + swap_cores(partial)
    g_one = g_two + norm_back(h_one, gain_two, grad_normed)
    gain_grad_two = gain_grad(h_one, partial)
    low_one = g_one.astype(BF16)
    grad_kv = own_rows(tn(encoded, grad_cross_kv).astype(BF16))
    grad_attend = jnp.concatenate(
        [
            tn(low_one, attended).astype(BF16),
            tn(normed_two, grad_cross_q).astype(BF16),
            tn(low_two, cross_att).astype(BF16),
            grad_kv,
        ],
        axis=1,
    )
    sum_attend = scatter_rows(grad_attend, size)

    terms = nt(grad_cross_kv, key_value)
    kept = lax.dynamic_slice_in_dim(terms, core * half, half, 1)
    given = lax.dynamic_slice_in_dim(terms, half - core * half, half, 1).astype(BF16)
    terms = (kept + swap_cores(given).astype(F32)).astype(BF16)
    back = lax.all_to_all(
        terms.reshape(size, capacity // size, half), "dp", split_axis=0, concat_axis=0, tiled=True
    )
    inverse = jnp.zeros_like(assign).at[assign].set(jnp.arange(size, dtype=jnp.int32))
    encoder_grad = back[inverse]

    grad_attended = nn(low_one, output_one).astype(BF16)
    grad_query, grad_keys, grad_values, diagonals = self_backward(
        query, keys, values, bias, lse_self, grad_attended
    )
    grad_mixed = jnp.concatenate([grad_query, grad_keys, grad_values], axis=1)
    sum_mixed = scatter_rows(tn(normed_one, grad_mixed), size)
    partial = nt(grad_mixed, qkv)
    grad_normed = partial + swap_cores(partial)
    decoder_grad = g_one + norm_back(tokens, gain_one, grad_normed)
    decoder_grad = lax.dot_general(
        decoder_grad,
        order.astype(F32),
        (((1,), (1,)), ((), ())),
        precision=lax.Precision.HIGHEST,
        preferred_element_type=F32,
    )
    gain_grad_one = gain_grad(tokens, partial)

    diagonals = diagonals[:, :2].reshape(heads, targets)
    grad_table = jnp.sum(jnp.where(which[:, None], diagonals[None], 0.0), axis=2)
    grad_gains = jnp.stack([gain_grad_one, gain_grad_two, gain_grad_three])
    grad_gains = grad_gains.reshape(3, size, block)[:, place].reshape(-1)
    table = jnp.where(
        jnp.arange(2)[:, None] == core, grad_table.reshape(1, -1), 0.0
    ).reshape(-1)
    small = jnp.concatenate([grad_gains, table])
    small = jnp.pad(small, (0, -small.size % (8 * TILE))).reshape(-1, TILE)
    small = sum_devices(small, size).reshape(-1)
    grad_gains = small[: 3 * width].reshape(3, width)
    grad_table = lax.dynamic_slice_in_dim(
        small, 3 * width + core * grad_table.size, grad_table.size
    ).reshape(grad_table.shape)

    def parts(value, count):
        step = value.shape[1] // count
        return [value[:, i * step : (i + 1) * step] for i in range(count)]

    grad_self_query, grad_self_key, grad_self_value = parts(sum_mixed, 3)
    grad_output_one, grad_cross_query, grad_output_two, grad_cross_key, grad_cross_value = parts(
        sum_attend, 5
    )
    grad_ffn_gate, grad_ffn_up = parts(sum_ffn, 2)
    return (
        layer_out[None],
        decoder_grad[None],
        encoder_grad,
        grad_gains[0],
        grad_gains[1],
        grad_gains[2],
        grad_self_query,
        grad_self_key,
        grad_self_value,
        grad_output_one.T,
        grad_cross_query,
        grad_cross_key,
        grad_cross_value,
        grad_output_two.T,
        grad_ffn_gate,
        grad_ffn_up,
        sum_down.T,
        grad_table,
    )


def solution(mesh):
    in_specs = (
        P("dp", None, None),
        P(None, "dp", None),
        P(),
        P(),
        P(),
        P(),
        P(),
        P(),
        P(),
        P("dp", "mp"),
        P("dp", "mp"),
        P("dp", "mp"),
        P("mp", "dp"),
        P("dp", "mp"),
        P("dp", "mp"),
        P("dp", "mp"),
        P("mp", "dp"),
        P("dp", "mp"),
        P("dp", "mp"),
        P("mp", "dp"),
        P(None, "mp"),
        P("dp", None, None),
    )
    out_specs = (
        P("dp", None, None),
        P("dp", None, None),
        P(None, "dp", "mp"),
        P(),
        P(),
        P(),
        P("dp", "mp"),
        P("dp", "mp"),
        P("dp", "mp"),
        P("mp", "dp"),
        P("dp", "mp"),
        P("dp", "mp"),
        P("dp", "mp"),
        P("mp", "dp"),
        P("dp", "mp"),
        P("dp", "mp"),
        P("mp", "dp"),
        P(None, "mp"),
    )
    body = functools.partial(shards, size=mesh.shape["dp"])
    return jax.shard_map(body, mesh=mesh, in_specs=in_specs, out_specs=out_specs, check_vma=False)
```

time: 2390 us -> 522 us (0.22)
  waiting for transfers between devices: 1440 us -> 184 us
  blocking collectives: 420 us -> 0 us
  matrix products: 230 us -> 71.6 us
  local copies, waits for them, and re-layouts: 153 us -> 53.9 us
  starting transfers between devices: 31.1 us -> 101 us
  Pallas kernels: 0 us -> 39.8 us
  other arithmetic: 91 us -> 61.9 us
    reduce_scatter x9 -> x0, waiting for transfers between devices: 1050 us -> none  [the longest x1 135 us: shards(): lax.psum_scatter(grad_down, 'dp', scatter_dimension=1, tiled=True)]
    all_gather x8 -> x0, blocking collectives: 344 us -> none  [the longest x1 48.5 us: shards(): lax.all_gather(self_output.astype(bf16), 'dp', axis=1, tiled=True)]
    unnamed x23 -> x0, waiting for transfers between devices: 256 us -> none
    ppermute x0 -> x70, waiting for transfers between devices: none -> 184 us  [the longest x61 184 us: swap(): return lax.ppermute(value, 'dp', [(i, i ^ mask) for i in range(size)])]
    dot_general x119 -> x25, matrix products: 230 us -> 71.6 us  [the longest x24 63.8 us: dot(): lax.dot_general(left, right, (dims, ((), ())), preferred_element_type=F32)]
    all_gather x3 -> x0, waiting for transfers between devices: 93.4 us -> none  [the longest x1 55.9 us: shards(): lax.all_gather(ffn_gate.astype(bf16), 'dp', axis=0, tiled=True)]
    ppermute x0 -> x70, starting transfers between devices: none -> 88.6 us  [the longest x61 87.4 us: swap(): return lax.ppermute(value, 'dp', [(i, i ^ mask) for i in range(size)])]
    psum x1 -> x0, blocking collectives: 75.7 us -> none  [shards(): lax.psum((gain_one, gain_two, gain_three, grad_table), 'dp')]
  transfers between devices with their start and end apart: 24 -> 72, of which waited for: 17 -> 25; matrix products, arithmetic and copies ran while one was open for 13% -> 32% of each run, Pallas kernels for 0% -> 8%
where the time goes in v1:
time: 522 us; the launch traced here: 517 us
  waiting for transfers between devices  184 us (35%)
  starting transfers between devices  101 us (19%)
  matrix products  71.6 us (14%)
  other arithmetic  61.9 us (12%)
  local copies, waits for them, and re-layouts  53.9 us (10%)
  Pallas kernels  39.8 us (8%)
    ppermute x61, waiting for transfers between devices, swap(): return lax.ppermute(value, 'dp', [(i, i ^ mask) for i in range(size)])  184 us
    ppermute x61, starting transfers between devices, swap(): return lax.ppermute(value, 'dp', [(i, i ^ mask) for i in range(size)])  87.4 us
    dot_general x24, matrix products, dot(): lax.dot_general(left, right, (dims, ((), ())), preferred_element_type=F32)  63.8 us
    pallas_call x4, Pallas kernels, pair_call(): pl.pallas_call(kernel, grid=(pairs,), in_specs=[spec(value.shape, value.d...  39.8 us
    unnamed x205, local copies, waits for them, and re-layouts  13.6 us
  transfers between devices with their start and end apart: 72, of which 25 were waited for; matrix products, arithmetic and copies ran while one was open for 32% of the time, Pallas kernels for 8%

profile of v1, /device:TPU:0, one launch (start us, length us, event | category | flops | bytes accessed | tf_op | source)
XLA Modules:
  0.0 516.6 jit_solution(5737254511300145802)
XLA Ops:
  4.1 5.0 collective-permute-start.2
  14.2 3.9 collective-permute-start.9
  21.0 6.2 %all-to-all-start = ((bf16[16,64,384]{2,1,0:T(8,128)(2,1)}), bf16[16,64,384]{2,1,0:T(8,128)(2,1)}, u32[]{:S(2)}, u32[]{:S(2)}) async-start(bf16[16,64,384]{2,1,0:T(8,128)(2,1)} %gather_fusion.1), calls=%async_computation | async-start | bytes 1572864 | tf_op jit(solution)/shard_map/all_to_all | solution.py:494
  36.0 3.0 fusion.30
  59.9 3.5 collective-permute-start.19
  72.2 2.6 collective-permute-done.6
  80.1 6.4 %shard_map.349 = (bf16[512,384]{1,0:T(8,128)(2,1)}, f32[3,8,512]{2,1,0:T(8,128)}) custom-call(bf16[512,384]{1,0:T(8,128)(2,1)} %get-tuple-element.147.q_ref, bf16[512,384]{1,0:T(8,128)(2,1)} %get-tuple-element.146.k_ref, bf16[512,384]{1,0:T(8,128)(2,1)} %get-tuple-element.145.v_ref, f32[3,8,512]{2,1,0:T(8,128)} %pad.8.bias_ref), custom_call_target="tpu_custom_call" | custom-call | flops 301989888 | bytes 1228800 | tf_op jit(solution)/shard_map/pallas_call | solution.py:337
  86.5 6.4 %collective-permute-done.11 = bf16[384,1024]{1,0:T(8,128)(2,1)S(1)} collective-permute-done((bf16[384,1024]{1,0:T(8,128)(2,1)}, bf16[384,1024]{1,0:T(8,128)(2,1)S(1)}, u32[]{:S(2)}, u32[]{:S(2)}) %collective-permute-start.11) | collective-permute-done | bytes 786464 | tf_op jit(solution)/shard_map/ppermute | solution.py:47
  93.0 3.0 fusion.111
  102.7 2.9 gather_fusion.2
  107.5 3.3 convolution_convert_fusion.4
  117.0 12.7 %shard_map.350 = (bf16[512,384]{1,0:T(8,128)(2,1)}, f32[3,8,512]{2,1,0:T(8,128)}) custom-call(bf16[512,384]{1,0:T(8,128)(2,1)} %convolution_convert_fusion.12.q_ref, bf16[1024,384]{1,0:T(8,128)(2,1)} %get-tuple-element.144.k_ref, bf16[1024,384]{1,0:T(8,128)(2,1)} %get-tuple-element.143.v_ref, f32[1024,128]{1,0:T(8,128)} %broadcast_in_dim.121.dead_ref), custom_call_target="tpu_custom_call" | custom-call | flops 805306368 | bytes 2490368 | tf_op jit(solution)/shard_map/pallas_call | solution.py:337
  145.6 4.3 collective-permute-done.20
  152.6 21.8 %collective-permute-done.30 = bf16[384,512]{1,0:T(8,128)(2,1)} collective-permute-done((bf16[384,512]{1,0:T(8,128)(2,1)}, bf16[384,512]{1,0:T(8,128)(2,1)}, u32[]{:S(2)}, u32[]{:S(2)}) %collective-permute-start.30) | collective-permute-done | bytes 393248 | tf_op jit(solution)/shard_map/ppermute | solution.py:47
  178.6 4.0 fusion.108
  182.6 3.5 fusion.10
  187.2 3.2 fusion.113
  192.3 3.2 fusion.36
  200.1 24.0 %collective-permute-done.63 = bf16[384,512]{1,0:T(8,128)(2,1)S(1)} collective-permute-done((bf16[384,512]{1,0:T(8,128)(2,1)S(1)}, bf16[384,512]{1,0:T(8,128)(2,1)S(1)}, u32[]{:S(2)}, u32[]{:S(2)}) %collective-permute-start.63) | collective-permute-done | bytes 393248 | tf_op jit(solution)/shard_map/ppermute | solution.py:47
  226.5 20.4 %collective-permute-done.64 = bf16[192,512]{1,0:T(8,128)(2,1)S(1)} collective-permute-done((bf16[192,512]{1,0:T(8,128)(2,1)S(1)}, bf16[192,512]{1,0:T(8,128)(2,1)S(1)}, u32[]{:S(2)}, u32[]{:S(2)}) %collective-permute-start.64) | collective-permute-done | bytes 196640 | tf_op jit(solution)/shard_map/ppermute | solution.py:47
  248.5 4.1 collective-permute-done.66
  256.8 3.1 collective-permute-start.69
  261.4 3.9 collective-permute-start.68
  268.4 6.9 %collective-permute-done.68 = bf16[48,1024]{1,0:T(8,128)(2,1)S(1)} collective-permute-done((bf16[48,1024]{1,0:T(8,128)(2,1)S(1)}, bf16[48,1024]{1,0:T(8,128)(2,1)S(1)}, u32[]{:S(2)}, u32[]{:S(2)}) %collective-permute-start.68) | collective-permute-done | bytes 98336 | tf_op jit(solution)/shard_map/ppermute | solution.py:47
  275.3 3.2 collective-permute-start.60
  279.2 5.9 %collective-permute-done.61 = bf16[48,2048]{1,0:T(8,128)(2,1)S(1)} collective-permute-done((bf16[48,2048]{1,0:T(8,128)(2,1)S(1)}, bf16[48,2048]{1,0:T(8,128)(2,1)S(1)}, u32[]{:S(2)}, u32[]{:S(2)}) %collective-permute-start.61) | collective-permute-done | bytes 196640 | tf_op jit(solution)/shard_map/ppermute | solution.py:47
  289.8 13.3 %shard_map.351 = (bf16[512,384]{1,0:T(8,128)(2,1)}, bf16[1024,384]{1,0:T(8,128)(2,1)}, bf16[1024,384]{1,0:T(8,128)(2,1)}) custom-call(bf16[512,384]{1,0:T(8,128)(2,1)} %convolution_convert_fusion.12.q_ref, bf16[1024,384]{1,0:T(8,128)(2,1)} %get-tuple-element.144.k_ref, bf16[1024,384]{1,0:T(8,128)(2,1)} %get-tuple-element.143.v_ref, ...), custom_call_target="tpu_custom_call" | custom-call | flops 2013265920 | bytes 2932736 | tf_op jit(solution)/shard_map/pallas_call | solution.py:337
  303.1 3.0 fusion.112
  307.4 4.9 convolution_convert_fusion.5
  312.3 3.0 gather_fusion.5
  325.4 4.0 fusion.37
  329.4 7.8 %collective-permute-done.51 = bf16[384,896]{0,1:T(8,128)(2,1)S(1)} collective-permute-done((bf16[384,896]{0,1:T(8,128)(2,1)S(1)}, bf16[384,896]{0,1:T(8,128)(2,1)S(1)}, u32[]{:S(2)}, u32[]{:S(2)}) %collective-permute-start.51) | collective-permute-done | bytes 688160 | tf_op jit(solution)/shard_map/ppermute | solution.py:47
  341.3 2.7 add_convert_fusion
  344.0 5.8 %all-to-all-start.1 = ((bf16[16,64,384]{2,1,0:T(8,128)(2,1)}), bf16[16,64,384]{2,1,0:T(8,128)(2,1)}, u32[]{:S(2)}, u32[]{:S(2)}) async-start(bf16[16,64,384]{2,1,0:T(8,128)(2,1)} %bitcast.103), calls=%async_computation.1 | async-start | bytes 1572864 | tf_op jit(solution)/shard_map/all_to_all | solution.py:575
  351.9 3.1 multiply_reduce_fusion.1
  358.8 7.5 %shard_map.352 = (bf16[512,384]{1,0:T(8,128)(2,1)}, bf16[512,384]{1,0:T(8,128)(2,1)}, bf16[512,384]{1,0:T(8,128)(2,1)}, f32[3,8,512]{2,1,0:T(8,128)}) custom-call(bf16[512,384]{1,0:T(8,128)(2,1)} %get-tuple-element.147.q_ref, bf16[512,384]{1,0:T(8,128)(2,1)} %get-tuple-element.146.k_ref, bf16[512,384]{1,0:T(8,128)(2,1)} %get-tuple-element.145.v_ref, ...), custom_call_target="tpu_custom_call" | custom-call | flops 805306368 | bytes 1671168 | tf_op jit(solution)/shard_map/pallas_call | solution.py:337
  373.3 11.4 %fusion.114 = f32[512,768]{0,1:T(8,128)} fusion(bf16[512,1152]{1,0:T(8,128)(2,1)S(1)} %constant_dynamic-update-slice_fusion, bf16[192,512]{1,0:T(8,128)(2,1)S(1)} %copy-done.61, bf16[192,512]{1,0:T(8,128)(2,1)S(1)} %copy-done.57, bf16[192,512]{1,0:T(8,128)(2,1)S(1)} %copy-done.59, bf16[192,512]{1,0:T(8,128)(2,1)S(1)} %copy-done.41, ...), kind=kOutput, calls=%fused_computation.317 | convolution fusion | flops 918355968 | bytes 4521984 | tf_op jit(solution)/shard_map/dot_general | solution.py:31
  394.9 3.6 collective-permute-done.44
  405.9 17.9 %collective-permute-done.45 = bf16[192,512]{1,0:T(8,128)(2,1)S(1)} collective-permute-done((bf16[192,512]{1,0:T(8,128)(2,1)S(1)}, bf16[192,512]{1,0:T(8,128)(2,1)S(1)}, u32[]{:S(2)}, u32[]{:S(2)}) %collective-permute-start.45) | collective-permute-done | bytes 196640 | tf_op jit(solution)/shard_map/ppermute | solution.py:47
  423.9 2.8 gather_fusion.3
  428.0 3.3 collective-permute-start.48
  435.7 4.7 collective-permute-done.47
  441.2 5.2 %collective-permute-done.50 = bf16[192,1024]{0,1:T(8,128)(2,1)S(1)} collective-permute-done((bf16[192,1024]{0,1:T(8,128)(2,1)S(1)}, bf16[192,1024]{0,1:T(8,128)(2,1)S(1)}, u32[]{:S(2)}, u32[]{:S(2)}) %collective-permute-start.50) | collective-permute-done | bytes 393248 | tf_op jit(solution)/shard_map/ppermute | solution.py:47
  448.2 3.3 collective-permute-start.55
  456.2 8.3 %collective-permute-done.55 = bf16[48,1920]{0,1:T(8,128)(2,1)S(1)} collective-permute-done((bf16[48,1920]{0,1:T(8,128)(2,1)}, bf16[48,1920]{0,1:T(8,128)(2,1)S(1)}, u32[]{:S(2)}, u32[]{:S(2)}) %collective-permute-start.55) | collective-permute-done | bytes 184352 | tf_op jit(solution)/shard_map/ppermute | solution.py:47
  464.5 27.3 %collective-permute-done.54 = bf16[48,1920]{0,1:T(8,128)(2,1)} collective-permute-done((bf16[48,1920]{0,1:T(8,128)(2,1)}, bf16[48,1920]{0,1:T(8,128)(2,1)}, u32[]{:S(2)}, u32[]{:S(2)}) %collective-permute-start.54) | collective-permute-done | bytes 184352 | tf_op jit(solution)/shard_map/ppermute | solution.py:47
  499.3 3.1 collective-permute-done.38
  506.9 7.8 %fusion.27 = f32[1,512,768]{2,1,0:T(8,128)} fusion(f32[512,768]{0,1:T(8,128)S(1)} %subtract_add_fusion, f32[768,512]{1,0:T(8,128)} %copy-done.8, s32[768]{0:T(1024)S(1)} %copy-done.68, f32[512]{0:T(512)S(1)} %fusion.81, f32[512]{0:T(512)S(1)} %copy-done.80, f32[512,768]{0,1:T(8,128)} %fusion.114, f32[512,768]{0,1:T(8,128)} %collective-permute-done.34, ...), kind=kOutput, calls=%fused_computation.87 | convolution fusion | flops 3626827776 | bytes 7874560 | tf_op jit(solution)/shard_map/dot_general | solution.py:590
  (497 shorter events, 187.3 us)
Async XLA Ops:
  4.1 38.9 %collective-permute-start.2 = (bf16[48,1152]{1,0:T(8,128)(2,1)}, bf16[48,1152]{1,0:T(8,128)(2,1)}, u32[]{:S(2)}, u32[]{:S(2)}) collective-permute-start(bf16[48,1152]{1,0:T(8,128)(2,1)} %pad_maximum_fusion.38), channel_id=1, source_target_pairs={{0,24},{2,26},{4,28},{6,30},{8,16},{10,18},{12,20},{14,22},{16,8},... | collective-permute-start | bytes 331784 | tf_op jit(solution)/shard_map/ppermute | solution.py:47
  9.2 35.8 %collective-permute-start.1 = (bf16[48,1152]{1,0:T(8,128)(2,1)}, bf16[48,1152]{1,0:T(8,128)(2,1)}, u32[]{:S(2)}, u32[]{:S(2)}) collective-permute-start(bf16[48,1152]{1,0:T(8,128)(2,1)} %pad_maximum_fusion.38), channel_id=1, source_target_pairs={{0,16},{2,18},{4,20},{6,22},{8,24},{10,26},{12,28},{14,30},{16,0},... | collective-permute-start | bytes 331784 | tf_op jit(solution)/shard_map/ppermute | solution.py:47
  9.2 38.2 %collective-permute-start = (bf16[48,1152]{1,0:T(8,128)(2,1)}, bf16[48,1152]{1,0:T(8,128)(2,1)}, u32[]{:S(2)}, u32[]{:S(2)}) collective-permute-start(bf16[48,1152]{1,0:T(8,128)(2,1)} %pad_maximum_fusion.38), channel_id=1, source_target_pairs={{0,8},{2,10},{4,12},{6,14},{8,0},{10,2},{12,4},{14,6},{16,24},{18,... | collective-permute-start | bytes 331784 | tf_op jit(solution)/shard_map/ppermute | solution.py:47
  14.2 35.3 %collective-permute-start.9 = (bf16[48,1920]{1,0:T(8,128)(2,1)S(1)}, bf16[48,1920]{1,0:T(8,128)(2,1)S(1)}, u32[]{:S(2)}, u32[]{:S(2)}) collective-permute-start(bf16[48,1920]{1,0:T(8,128)(2,1)S(1)} %convert_dynamic-update-slice_fusion), channel_id=1, source_target_pairs={{0,24},{2,26},{4,28},{6,30},{8,16},{10,18},{12,20},{14,22},{16,8},... | collective-permute-start | bytes 552968 | tf_op jit(solution)/shard_map/ppermute | solution.py:47
  18.1 33.4 %collective-permute-start.8 = (bf16[48,1920]{1,0:T(8,128)(2,1)S(1)}, bf16[48,1920]{1,0:T(8,128)(2,1)}, u32[]{:S(2)}, u32[]{:S(2)}) collective-permute-start(bf16[48,1920]{1,0:T(8,128)(2,1)S(1)} %convert_dynamic-update-slice_fusion), channel_id=1, source_target_pairs={{0,16},{2,18},{4,20},{6,22},{8,24},{10,26},{12,28},{14,30},{16,0},... | collective-permute-start | bytes 552968 | tf_op jit(solution)/shard_map/ppermute | solution.py:47
  21.0 75.0 %all-to-all-start = ((bf16[16,64,384]{2,1,0:T(8,128)(2,1)}), bf16[16,64,384]{2,1,0:T(8,128)(2,1)}, u32[]{:S(2)}, u32[]{:S(2)}) async-start(bf16[16,64,384]{2,1,0:T(8,128)(2,1)} %gather_fusion.1), calls=%async_computation | async-start | bytes 1572864 | tf_op jit(solution)/shard_map/all_to_all | solution.py:494
  45.0 12.7 %collective-permute-start.26 = (bf16[48,1024]{1,0:T(8,128)(2,1)S(1)}, bf16[48,1024]{1,0:T(8,128)(2,1)S(1)}, u32[]{:S(2)}, u32[]{:S(2)}) collective-permute-start(bf16[48,1024]{1,0:T(8,128)(2,1)S(1)} %convert_bitcast_fusion), channel_id=1, source_target_pairs={{0,24},{2,26},{4,28},{6,30},{8,16},{10,18},{12,20},{14,22},{16,8},... | collective-permute-start | bytes 294920 | tf_op jit(solution)/shard_map/ppermute | solution.py:47
  47.4 12.5 %collective-permute-start.25 = (bf16[48,1024]{1,0:T(8,128)(2,1)S(1)}, bf16[48,1024]{1,0:T(8,128)(2,1)S(1)}, u32[]{:S(2)}, u32[]{:S(2)}) collective-permute-start(bf16[48,1024]{1,0:T(8,128)(2,1)S(1)} %convert_bitcast_fusion), channel_id=1, source_target_pairs={{0,16},{2,18},{4,20},{6,22},{8,24},{10,26},{12,28},{14,30},{16,0},... | collective-permute-start | bytes 294920 | tf_op jit(solution)/shard_map/ppermute | solution.py:47
  49.5 13.9 %collective-permute-start.24 = (bf16[48,1024]{1,0:T(8,128)(2,1)S(1)}, bf16[48,1024]{1,0:T(8,128)(2,1)S(1)}, u32[]{:S(2)}, u32[]{:S(2)}) collective-permute-start(bf16[48,1024]{1,0:T(8,128)(2,1)S(1)} %convert_bitcast_fusion), channel_id=1, source_target_pairs={{0,8},{2,10},{4,12},{6,14},{8,0},{10,2},{12,4},{14,6},{16,24},{18,... | collective-permute-start | bytes 294920 | tf_op jit(solution)/shard_map/ppermute | solution.py:47
  57.8 11.6 %collective-permute-start.10 = (bf16[192,1024]{1,0:T(8,128)(2,1)S(1)}, bf16[192,1024]{1,0:T(8,128)(2,1)S(1)}, u32[]{:S(2)}, u32[]{:S(2)}) collective-permute-start(bf16[192,1024]{1,0:T(8,128)(2,1)S(1)} %slice.475), channel_id=1, source_target_pairs={{0,4},{2,6},{4,0},{6,2},{8,12},{10,14},{12,8},{14,10},{16,20},{18,... | collective-permute-start | bytes 1179656 | tf_op jit(solution)/shard_map/ppermute | solution.py:47
  59.9 36.1 %collective-permute-start.19 = (bf16[48,2048]{1,0:T(8,128)(2,1)}, bf16[48,2048]{1,0:T(8,128)(2,1)}, u32[]{:S(2)}, u32[]{:S(2)}) collective-permute-start(bf16[48,2048]{1,0:T(8,128)(2,1)} %pad_maximum_fusion.37), channel_id=1, source_target_pairs={{0,24},{2,26},{4,28},{6,30},{8,16},{10,18},{12,20},{14,22},{16,8},... | collective-permute-start | bytes 589832 | tf_op jit(solution)/shard_map/ppermute | solution.py:47
  65.0 31.5 %collective-permute-start.18 = (bf16[48,2048]{1,0:T(8,128)(2,1)}, bf16[48,2048]{1,0:T(8,128)(2,1)}, u32[]{:S(2)}, u32[]{:S(2)}) collective-permute-start(bf16[48,2048]{1,0:T(8,128)(2,1)} %pad_maximum_fusion.37), channel_id=1, source_target_pairs={{0,16},{2,18},{4,20},{6,22},{8,24},{10,26},{12,28},{14,30},{16,0},... | collective-permute-start | bytes 589832 | tf_op jit(solution)/shard_map/ppermute | solution.py:47
  69.4 27.1 %collective-permute-start.17 = (bf16[48,2048]{1,0:T(8,128)(2,1)}, bf16[48,2048]{1,0:T(8,128)(2,1)}, u32[]{:S(2)}, u32[]{:S(2)}) collective-permute-start(bf16[48,2048]{1,0:T(8,128)(2,1)} %pad_maximum_fusion.37), channel_id=1, source_target_pairs={{0,8},{2,10},{4,12},{6,14},{8,0},{10,2},{12,4},{14,6},{16,24},{18,... | collective-permute-start | bytes 589832 | tf_op jit(solution)/shard_map/ppermute | solution.py:47
  74.8 25.5 %collective-permute-start.15 = (bf16[384,896]{1,0:T(8,128)(2,1)}, bf16[384,896]{1,0:T(8,128)(2,1)}, u32[]{:S(2)}, u32[]{:S(2)}) collective-permute-start(bf16[384,896]{1,0:T(8,128)(2,1)} %pad_maximum_fusion.18), channel_id=1, source_target_pairs={{0,4},{2,6},{4,0},{6,2},{8,12},{10,14},{12,8},{14,10},{16,20},{18,... | collective-permute-start | bytes 2064392 | tf_op jit(solution)/shard_map/ppermute | solution.py:47
  76.3 16.7 %collective-permute-start.11 = (bf16[384,1024]{1,0:T(8,128)(2,1)}, bf16[384,1024]{1,0:T(8,128)(2,1)S(1)}, u32[]{:S(2)}, u32[]{:S(2)}) collective-permute-start(bf16[384,1024]{1,0:T(8,128)(2,1)} %pad_maximum_fusion.12), channel_id=1, source_target_pairs={{0,2},{2,0},{4,6},{6,4},{8,10},{10,8},{12,14},{14,12},{16,18},{18,... | collective-permute-start | bytes 2359304 | tf_op jit(solution)/shard_map/ppermute | solution.py:47
  96.0 16.1 %collective-permute-start.12 = (f32[512,768]{0,1:T(8,128)}, f32[512,768]{0,1:T(8,128)}, u32[]{:S(2)}, u32[]{:S(2)}) collective-permute-start(f32[512,768]{0,1:T(8,128)} %fusion.111), channel_id=1, source_target_pairs={{0,1},{1,0},{2,3},{3,2},{4,5},{5,4},{6,7},{7,6},{8,9},{9,8},{10,11... | collective-permute-start | bytes 4718600 | tf_op jit(solution)/shard_map/ppermute | solution.py:51
  98.8 36.6 %collective-permute-start.22 = (bf16[192,1024]{1,0:T(8,128)(2,1)}, bf16[192,1024]{1,0:T(8,128)(2,1)}, u32[]{:S(2)}, u32[]{:S(2)}) collective-permute-start(bf16[192,1024]{1,0:T(8,128)(2,1)} %get-tuple-element.160), channel_id=1, source_target_pairs={{0,2},{2,0},{4,6},{6,4},{8,10},{10,8},{12,14},{14,12},{16,18},{18,... | collective-permute-start | bytes 1179656 | tf_op jit(solution)/shard_map/ppermute | solution.py:47
  131.5 45.1 %collective-permute-start.16 = (f32[512,768]{0,1:T(8,128)S(1)}, f32[512,768]{0,1:T(8,128)}, u32[]{:S(2)}, u32[]{:S(2)}) collective-permute-start(f32[512,768]{0,1:T(8,128)S(1)} %fusion.132), channel_id=1, source_target_pairs={{0,1},{1,0},{2,3},{3,2},{4,5},{5,4},{6,7},{7,6},{8,9},{9,8},{10,11... | collective-permute-start | bytes 4718600 | tf_op jit(solution)/shard_map/ppermute | solution.py:51
  134.9 15.0 %collective-permute-start.20 = (bf16[192,1024]{1,0:T(8,128)(2,1)}, bf16[192,1024]{1,0:T(8,128)(2,1)}, u32[]{:S(2)}, u32[]{:S(2)}) collective-permute-start(bf16[192,1024]{1,0:T(8,128)(2,1)} %get-tuple-element.159), channel_id=1, source_target_pairs={{0,4},{2,6},{4,0},{6,2},{8,12},{10,14},{12,8},{14,10},{16,20},{18,... | collective-permute-start | bytes 1179656 | tf_op jit(solution)/shard_map/ppermute | solution.py:47
  137.5 38.0 %collective-permute-start.23 = (bf16[384,1024]{1,0:T(8,128)(2,1)}, bf16[384,1024]{1,0:T(8,128)(2,1)}, u32[]{:S(2)}, u32[]{:S(2)}) collective-permute-start(bf16[384,1024]{1,0:T(8,128)(2,1)} %pad_maximum_fusion.15), channel_id=1, source_target_pairs={{0,4},{2,6},{4,0},{6,2},{8,12},{10,14},{12,8},{14,10},{16,20},{18,... | collective-permute-start | bytes 2359304 | tf_op jit(solution)/shard_map/ppermute | solution.py:47
  140.5 34.0 %collective-permute-start.30 = (bf16[384,512]{1,0:T(8,128)(2,1)}, bf16[384,512]{1,0:T(8,128)(2,1)}, u32[]{:S(2)}, u32[]{:S(2)}) collective-permute-start(bf16[384,512]{1,0:T(8,128)(2,1)} %pad_maximum_fusion.32), channel_id=1, source_target_pairs={{0,4},{2,6},{4,0},{6,2},{8,12},{10,14},{12,8},{14,10},{16,20},{18,... | collective-permute-start | bytes 1179656 | tf_op jit(solution)/shard_map/ppermute | solution.py:47
  145.0 37.6 %collective-permute-start.28 = (bf16[384,512]{1,0:T(8,128)(2,1)S(1)}, bf16[384,512]{1,0:T(8,128)(2,1)S(1)}, u32[]{:S(2)}, u32[]{:S(2)}) collective-permute-start(bf16[384,512]{1,0:T(8,128)(2,1)S(1)} %pad_maximum_fusion.31), channel_id=1, source_target_pairs={{0,2},{2,0},{4,6},{6,4},{8,10},{10,8},{12,14},{14,12},{16,18},{18,... | collective-permute-start | bytes 1179656 | tf_op jit(solution)/shard_map/ppermute | solution.py:47
  151.1 27.5 %collective-permute-start.21 = (bf16[384,1024]{1,0:T(8,128)(2,1)S(1)}, bf16[384,1024]{1,0:T(8,128)(2,1)S(1)}, u32[]{:S(2)}, u32[]{:S(2)}) collective-permute-start(bf16[384,1024]{1,0:T(8,128)(2,1)S(1)} %pad_maximum_fusion.14), channel_id=1, source_target_pairs={{0,2},{2,0},{4,6},{6,4},{8,10},{10,8},{12,14},{14,12},{16,18},{18,... | collective-permute-start | bytes 2359304 | tf_op jit(solution)/shard_map/ppermute | solution.py:47
  190.5 133.4 %collective-permute-start.31 = (f32[512,768]{0,1:T(8,128)}, f32[512,768]{0,1:T(8,128)}, u32[]{:S(2)}, u32[]{:S(2)}) collective-permute-start(f32[512,768]{0,1:T(8,128)} %fusion.113), channel_id=1, source_target_pairs={{0,1},{1,0},{2,3},{3,2},{4,5},{5,4},{6,7},{7,6},{8,9},{9,8},{10,11... | collective-permute-start | bytes 4718600 | tf_op jit(solution)/shard_map/ppermute | solution.py:51
  195.5 90.6 %collective-permute-start.32 = (f32[512,768]{0,1:T(8,128)S(1)}, f32[512,768]{0,1:T(8,128)S(1)}, u32[]{:S(2)}, u32[]{:S(2)}) collective-permute-start(f32[512,768]{0,1:T(8,128)S(1)} %fusion.36), channel_id=1, source_target_pairs={{0,1},{1,0},{2,3},{3,2},{4,5},{5,4},{6,7},{7,6},{8,9},{9,8},{10,11... | collective-permute-start | bytes 4718600 | tf_op jit(solution)/shard_map/ppermute | solution.py:51
  196.2 56.6 %collective-permute-start.56 = (bf16[384,1024]{1,0:T(8,128)(2,1)S(1)}, bf16[384,1024]{1,0:T(8,128)(2,1)S(1)}, u32[]{:S(2)}, u32[]{:S(2)}) collective-permute-start(bf16[384,1024]{1,0:T(8,128)(2,1)S(1)} %slice.532), channel_id=1, source_target_pairs={{0,2},{2,0},{4,6},{6,4},{8,10},{10,8},{12,14},{14,12},{16,18},{18,... | collective-permute-start | bytes 2359304 | tf_op jit(solution)/shard_map/ppermute | solution.py:47
  197.7 26.4 %collective-permute-start.63 = (bf16[384,512]{1,0:T(8,128)(2,1)S(1)}, bf16[384,512]{1,0:T(8,128)(2,1)S(1)}, u32[]{:S(2)}, u32[]{:S(2)}) collective-permute-start(bf16[384,512]{1,0:T(8,128)(2,1)S(1)} %slice.549), channel_id=1, source_target_pairs={{0,2},{2,0},{4,6},{6,4},{8,10},{10,8},{12,14},{14,12},{16,18},{18,... | collective-permute-start | bytes 1179656 | tf_op jit(solution)/shard_map/ppermute | solution.py:47
  198.3 27.5 %collective-permute-start.65 = (bf16[384,512]{1,0:T(8,128)(2,1)S(1)}, bf16[384,512]{1,0:T(8,128)(2,1)S(1)}, u32[]{:S(2)}, u32[]{:S(2)}) collective-permute-start(bf16[384,512]{1,0:T(8,128)(2,1)S(1)} %pad_maximum_fusion.34), channel_id=1, source_target_pairs={{0,4},{2,6},{4,0},{6,2},{8,12},{10,14},{12,8},{14,10},{16,20},{18,... | collective-permute-start | bytes 1179656 | tf_op jit(solution)/shard_map/ppermute | solution.py:47
  224.1 30.7 %collective-permute-start.58 = (bf16[384,1024]{1,0:T(8,128)(2,1)S(1)}, bf16[384,1024]{1,0:T(8,128)(2,1)S(1)}, u32[]{:S(2)}, u32[]{:S(2)}) collective-permute-start(bf16[384,1024]{1,0:T(8,128)(2,1)S(1)} %pad_maximum_fusion.16), channel_id=1, source_target_pairs={{0,4},{2,6},{4,0},{6,2},{8,12},{10,14},{12,8},{14,10},{16,20},{18,... | collective-permute-start | bytes 2359304 | tf_op jit(solution)/shard_map/ppermute | solution.py:47
  225.8 21.1 %collective-permute-start.64 = (bf16[192,512]{1,0:T(8,128)(2,1)S(1)}, bf16[192,512]{1,0:T(8,128)(2,1)S(1)}, u32[]{:S(2)}, u32[]{:S(2)}) collective-permute-start(bf16[192,512]{1,0:T(8,128)(2,1)S(1)} %slice.675), channel_id=1, source_target_pairs={{0,4},{2,6},{4,0},{6,2},{8,12},{10,14},{12,8},{14,10},{16,20},{18,... | collective-permute-start | bytes 589832 | tf_op jit(solution)/shard_map/ppermute | solution.py:47
  261.4 13.8 %collective-permute-start.68 = (bf16[48,1024]{1,0:T(8,128)(2,1)S(1)}, bf16[48,1024]{1,0:T(8,128)(2,1)S(1)}, u32[]{:S(2)}, u32[]{:S(2)}) collective-permute-start(bf16[48,1024]{1,0:T(8,128)(2,1)S(1)} %get-tuple-element.170), channel_id=1, source_target_pairs={{0,16},{2,18},{4,20},{6,22},{8,24},{10,26},{12,28},{14,30},{16,0},... | collective-permute-start | bytes 294920 | tf_op jit(solution)/shard_map/ppermute | solution.py:47
  265.9 13.3 %collective-permute-start.62 = (bf16[48,2048]{1,0:T(8,128)(2,1)S(1)}, bf16[48,2048]{1,0:T(8,128)(2,1)S(1)}, u32[]{:S(2)}, u32[]{:S(2)}) collective-permute-start(bf16[48,2048]{1,0:T(8,128)(2,1)S(1)} %get-tuple-element.157), channel_id=1, source_target_pairs={{0,24},{2,26},{4,28},{6,30},{8,16},{10,18},{12,20},{14,22},{16,8},... | collective-permute-start | bytes 589832 | tf_op jit(solution)/shard_map/ppermute | solution.py:47
  306.1 45.8 %collective-permute-start.33 = (f32[512,768]{0,1:T(8,128)}, f32[512,768]{0,1:T(8,128)}, u32[]{:S(2)}, u32[]{:S(2)}) collective-permute-start(f32[512,768]{0,1:T(8,128)} %fusion.112), channel_id=1, source_target_pairs={{0,1},{1,0},{2,3},{3,2},{4,5},{5,4},{6,7},{7,6},{8,9},{9,8},{10,11... | collective-permute-start | bytes 4718600 | tf_op jit(solution)/shard_map/ppermute | solution.py:51
  320.3 16.9 %collective-permute-start.51 = (bf16[384,896]{0,1:T(8,128)(2,1)S(1)}, bf16[384,896]{0,1:T(8,128)(2,1)S(1)}, u32[]{:S(2)}, u32[]{:S(2)}) collective-permute-start(bf16[384,896]{0,1:T(8,128)(2,1)S(1)} %fusion.53), channel_id=1, source_target_pairs={{0,4},{2,6},{4,0},{6,2},{8,12},{10,14},{12,8},{14,10},{16,20},{18,... | collective-permute-start | bytes 2064392 | tf_op jit(solution)/shard_map/ppermute | solution.py:47
  323.9 17.5 %collective-permute-start.35 = (bf16[1024,384]{1,0:T(8,128)(2,1)}, bf16[1024,384]{1,0:T(8,128)(2,1)}, u32[]{:S(2)}, u32[]{:S(2)}) collective-permute-start(bf16[1024,384]{1,0:T(8,128)(2,1)} %dynamic-slice_convert_fusion), channel_id=1, source_target_pairs={{0,1},{1,0},{2,3},{3,2},{4,5},{5,4},{6,7},{7,6},{8,9},{9,8},{10,11... | collective-permute-start | bytes 2359304 | tf_op jit(solution)/shard_map/ppermute | solution.py:51
  344.0 79.9 %all-to-all-start.1 = ((bf16[16,64,384]{2,1,0:T(8,128)(2,1)}), bf16[16,64,384]{2,1,0:T(8,128)(2,1)}, u32[]{:S(2)}, u32[]{:S(2)}) async-start(bf16[16,64,384]{2,1,0:T(8,128)(2,1)} %bitcast.103), calls=%async_computation.1 | async-start | bytes 1572864 | tf_op jit(solution)/shard_map/all_to_all | solution.py:575
  384.6 68.0 %collective-permute-start.34 = (f32[512,768]{0,1:T(8,128)}, f32[512,768]{0,1:T(8,128)}, u32[]{:S(2)}, u32[]{:S(2)}) collective-permute-start(f32[512,768]{0,1:T(8,128)} %fusion.114), channel_id=1, source_target_pairs={{0,1},{1,0},{2,3},{3,2},{4,5},{5,4},{6,7},{7,6},{8,9},{9,8},{10,11... | collective-permute-start | bytes 4718600 | tf_op jit(solution)/shard_map/ppermute | solution.py:51
  386.3 12.1 %collective-permute-start.44 = (bf16[384,512]{1,0:T(8,128)(2,1)}, bf16[384,512]{1,0:T(8,128)(2,1)}, u32[]{:S(2)}, u32[]{:S(2)}) collective-permute-start(bf16[384,512]{1,0:T(8,128)(2,1)} %pad_maximum_fusion.33), channel_id=1, source_target_pairs={{0,4},{2,6},{4,0},{6,2},{8,12},{10,14},{12,8},{14,10},{16,20},{18,... | collective-permute-start | bytes 1179656 | tf_op jit(solution)/shard_map/ppermute | solution.py:47
  389.2 14.4 %collective-permute-start.42 = (bf16[384,640]{1,0:T(8,128)(2,1)}, bf16[384,640]{1,0:T(8,128)(2,1)}, u32[]{:S(2)}, u32[]{:S(2)}) collective-permute-start(bf16[384,640]{1,0:T(8,128)(2,1)} %slice.494), channel_id=1, source_target_pairs={{0,2},{2,0},{4,6},{6,4},{8,10},{10,8},{12,14},{14,12},{16,18},{18,... | collective-permute-start | bytes 1474568 | tf_op jit(solution)/shard_map/ppermute | solution.py:47
  394.3 38.1 %collective-permute-start.49 = (bf16[384,1024]{0,1:T(8,128)(2,1)}, bf16[384,1024]{0,1:T(8,128)(2,1)}, u32[]{:S(2)}, u32[]{:S(2)}) collective-permute-start(bf16[384,1024]{0,1:T(8,128)(2,1)} %pad_maximum_fusion.10), channel_id=1, source_target_pairs={{0,2},{2,0},{4,6},{6,4},{8,10},{10,8},{12,14},{14,12},{16,18},{18,... | collective-permute-start | bytes 2359304 | tf_op jit(solution)/shard_map/ppermute | solution.py:47
  399.6 24.3 %collective-permute-start.45 = (bf16[192,512]{1,0:T(8,128)(2,1)S(1)}, bf16[192,512]{1,0:T(8,128)(2,1)S(1)}, u32[]{:S(2)}, u32[]{:S(2)}) collective-permute-start(bf16[192,512]{1,0:T(8,128)(2,1)S(1)} %slice.676), channel_id=1, source_target_pairs={{0,2},{2,0},{4,6},{6,4},{8,10},{10,8},{12,14},{14,12},{16,18},{18,... | collective-permute-start | bytes 589832 | tf_op jit(solution)/shard_map/ppermute | solution.py:47
  405.7 21.0 %collective-permute-start.43 = (bf16[192,640]{1,0:T(8,128)(2,1)}, bf16[192,640]{1,0:T(8,128)(2,1)S(1)}, u32[]{:S(2)}, u32[]{:S(2)}) collective-permute-start(bf16[192,640]{1,0:T(8,128)(2,1)} %slice.673), channel_id=1, source_target_pairs={{0,4},{2,6},{4,0},{6,2},{8,12},{10,14},{12,8},{14,10},{16,20},{18,... | collective-permute-start | bytes 737288 | tf_op jit(solution)/shard_map/ppermute | solution.py:47
  434.0 12.4 %collective-permute-start.50 = (bf16[192,1024]{0,1:T(8,128)(2,1)S(1)}, bf16[192,1024]{0,1:T(8,128)(2,1)S(1)}, u32[]{:S(2)}, u32[]{:S(2)}) collective-permute-start(bf16[192,1024]{0,1:T(8,128)(2,1)S(1)} %slice.669), channel_id=1, source_target_pairs={{0,4},{2,6},{4,0},{6,2},{8,12},{10,14},{12,8},{14,10},{16,20},{18,... | collective-permute-start | bytes 1179656 | tf_op jit(solution)/shard_map/ppermute | solution.py:47
  448.2 16.3 %collective-permute-start.55 = (bf16[48,1920]{0,1:T(8,128)(2,1)}, bf16[48,1920]{0,1:T(8,128)(2,1)S(1)}, u32[]{:S(2)}, u32[]{:S(2)}) collective-permute-start(bf16[48,1920]{0,1:T(8,128)(2,1)} %get-tuple-element.154), channel_id=1, source_target_pairs={{0,24},{2,26},{4,28},{6,30},{8,16},{10,18},{12,20},{14,22},{16,8},... | collective-permute-start | bytes 552968 | tf_op jit(solution)/shard_map/ppermute | solution.py:47
  451.5 40.3 %collective-permute-start.54 = (bf16[48,1920]{0,1:T(8,128)(2,1)}, bf16[48,1920]{0,1:T(8,128)(2,1)}, u32[]{:S(2)}, u32[]{:S(2)}) collective-permute-start(bf16[48,1920]{0,1:T(8,128)(2,1)} %get-tuple-element.155), channel_id=1, source_target_pairs={{0,16},{2,18},{4,20},{6,22},{8,24},{10,26},{12,28},{14,30},{16,0},... | collective-permute-start | bytes 552968 | tf_op jit(solution)/shard_map/ppermute | solution.py:47
  451.5 40.3 %collective-permute-start.53 = (bf16[48,1920]{0,1:T(8,128)(2,1)}, bf16[48,1920]{0,1:T(8,128)(2,1)}, u32[]{:S(2)}, u32[]{:S(2)}) collective-permute-start(bf16[48,1920]{0,1:T(8,128)(2,1)} %get-tuple-element.153), channel_id=1, source_target_pairs={{0,8},{2,10},{4,12},{6,14},{8,0},{10,2},{12,4},{14,6},{16,24},{18,... | collective-permute-start | bytes 552968 | tf_op jit(solution)/shard_map/ppermute | solution.py:47
  456.1 37.2 %collective-permute-start.36 = (f32[24,128]{1,0:T(8,128)S(1)}, f32[24,128]{1,0:T(8,128)S(1)}, u32[]{:S(2)}, u32[]{:S(2)}) collective-permute-start(f32[24,128]{1,0:T(8,128)S(1)} %fusion.75), channel_id=1, source_target_pairs={{0,1},{1,0},{2,3},{3,2},{4,5},{5,4},{6,7},{7,6},{8,9},{9,8},{10,11... | collective-permute-start | bytes 36872 | tf_op jit(solution)/shard_map/ppermute | solution.py:51
  502.5 12.2 %collective-permute-start.41 = (f32[24,128]{1,0:T(8,128)S(1)}, f32[24,128]{1,0:T(8,128)S(1)}, u32[]{:S(2)}, u32[]{:S(2)}) collective-permute-start(f32[24,128]{1,0:T(8,128)S(1)} %add.448), channel_id=1, source_target_pairs={{0,24},{2,26},{4,28},{6,30},{8,16},{10,18},{12,20},{14,22},{16,8},... | collective-permute-start | bytes 36872 | tf_op jit(solution)/shard_map/ppermute | solution.py:47
  (122 other events, 1136.1 us)

commit v2 on v1

v2 whole, which is shorter than its diff:
```python
import functools

import jax
import jax.numpy as jnp
from jax import lax
from jax.experimental import pallas as pl
from jax.experimental.pallas import tpu as pltpu
from jax.sharding import PartitionSpec as P

HEAD_DIM = 64
PAIR = 2 * HEAD_DIM
QUERIES = 256
KEYS = 1024
TILE = 128
WIDE = 256
ROWS = 64

EPS = 1e-06
NEGATIVE = -1000000000.0
GELU_ROOT = 0.7978845608028654
GELU_CUBE = 0.044715
BF16 = jnp.bfloat16
F32 = jnp.float32


def dot(left, right, dims):
    return lax.dot_general(left, right, (dims, ((), ())), preferred_element_type=F32)


def nn(left, right):
    return dot(left, right, ((1,), (0,)))


def nt(left, right):
    return dot(left, right, ((1,), (1,)))


def tn(left, right):
    return dot(left, right, ((0,), (0,)))


def struct(shape, dtype):
    return jax.ShapeDtypeStruct(shape, dtype)


def thirds(value):
    high = lax.reduce_precision(value, 8, 7)
    middle = lax.reduce_precision(value - high, 8, 7)
    return [part.astype(BF16) for part in (high, middle, value - high - middle)]


def swap(value, mask, size):
    return lax.ppermute(value, "dp", [(i, i ^ mask) for i in range(size)])


def swap_cores(value):
    return lax.ppermute(value, "mp", [(0, 1), (1, 0)])


def after(values, *others):
    return lax.optimization_barrier((values, others))[0]


def gather_outer(shard, size):
    if size <= 16:
        return [shard] + [swap(shard, mask, size) for mask in range(4, size, 4)]
    mask = 4
    while mask < size:
        shard = jnp.concatenate([shard, swap(shard, mask, size)])
        mask *= 2
    return [shard]


def gather_first(pieces, size):
    rows, columns = sum(piece.shape[0] for piece in pieces), pieces[0].shape[1]
    left, right = kernel_call(
        stack_kernel, pieces, [struct((rows, columns // 2), BF16)] * 2, []
    )
    return left, right


def gather_second(state, size):
    left = state[0]
    return kernel_call(
        join_kernel, list(state), [struct((2 * left.shape[0], left.shape[1]), BF16)] * 2, []
    )


def send_first(halves, size):
    left, right = halves
    return left, swap(left, 2, size), right, swap(right, 1, size)


def send_second(halves, size):
    left, right = halves
    return [left, swap(left, 1, size)], [right, swap(right, 2, size)]


def scatter_first(grads, size):
    left, left_out, right, right_out = grads
    return left, right, swap(left_out, 1, size), swap(right_out, 2, size)


def scatter_second_parts(state):
    return add_call(scatter_second_kernel, state, 0.5)


def scatter_second_send(parts, size):
    keep, left_out, right_out = parts
    return keep, swap(left_out, 2, size), swap(right_out, 1, size)


def scatter_outer_parts(state):
    return add_call(scatter_outer_kernel, state, 0.25)


def scatter_outer_send(parts, size):
    keep, *outs = parts
    if size == 16:
        return [keep] + [swap(out, 4 * (k + 1), size) for k, out in enumerate(outs)]
    rows = jnp.concatenate([keep] + [out.astype(F32) for out in outs])
    mask = size // 2
    while mask >= 4:
        count = rows.shape[0] // 2
        rows = rows[:count] + swap(rows[count:].astype(BF16), mask, size).astype(F32)
        mask //= 2
    return [rows]


def scatter_last(state):
    total = state[0]
    for value in state[1:]:
        total = total + value.astype(F32)
    return total


def sum_devices(value, size):
    value = value + swap(value, 1, size)
    value = value + swap(value, 2, size)
    if size <= 16:
        return functools.reduce(
            lambda total, mask: total + swap(value, mask, size), range(4, size, 4), value
        )
    mask = 4
    while mask < size:
        value = value + swap(value, mask, size)
        mask *= 2
    return value


def kernel_call(kernel, ins, outs, scratch, time=2, grid=None, in_specs=None, out_specs=None):
    everywhere = pl.BlockSpec(memory_space=pltpu.VMEM)
    return pl.pallas_call(
        kernel,
        out_shape=outs,
        in_specs=in_specs or [everywhere] * len(ins),
        out_specs=out_specs or [everywhere] * len(outs),
        scratch_shapes=scratch,
        compiler_params=pltpu.CompilerParams(vmem_limit_bytes=58 * 1024 * 1024),
        cost_estimate=pl.CostEstimate(
            flops=time * 1000000000, bytes_accessed=1, transcendentals=0
        ),
        **({"grid": grid} if grid else {}),
    )(*ins)


IN_VMEM = pl.BlockSpec(memory_space=pltpu.VMEM)
IN_PLACE = pl.BlockSpec(memory_space=pl.ANY)
IN_SMEM = pl.BlockSpec(memory_space=pltpu.SMEM)


def stack_kernel(*refs):
    *in_refs, left_ref, right_ref = refs
    half = left_ref.shape[1]
    start = 0
    for ref in in_refs:
        rows = slice(start, start + ref.shape[0])
        left_ref[rows, :] = ref[:, :half]
        right_ref[rows, :] = ref[:, half:]
        start += ref.shape[0]


def join_kernel(left_ref, left_in_ref, right_ref, right_in_ref, left_out, right_out):
    count = left_ref.shape[0]
    left_out[:count, :] = left_ref[...]
    left_out[count:, :] = left_in_ref[...]
    right_out[:count, :] = right_ref[...]
    right_out[count:, :] = right_in_ref[...]


def scatter_second_kernel(left_ref, right_ref, left_in_ref, right_in_ref, keep_ref, *out_refs):
    count, half = keep_ref.shape[0], left_ref.shape[1]
    halves = ((left_ref, left_in_ref, out_refs[0]), (right_ref, right_in_ref, out_refs[1]))
    for i, (own_ref, in_ref, out_ref) in enumerate(halves):
        keep_ref[:, i * half : (i + 1) * half] = own_ref[:count, :].astype(F32) + in_ref[
            :count, :
        ].astype(F32)
        out_ref[...] = (
            own_ref[count:, :].astype(F32) + in_ref[count:, :].astype(F32)
        ).astype(BF16)


def scatter_outer_kernel(keep_ref, left_in_ref, right_in_ref, *out_refs):
    count, half = out_refs[0].shape[0], left_in_ref.shape[1]
    for k, out_ref in enumerate(out_refs):
        rows = slice(k * count, (k + 1) * count)
        for i, in_ref in enumerate((left_in_ref, right_in_ref)):
            cols = slice(i * half, (i + 1) * half)
            out_ref[:, cols] = (keep_ref[rows, cols] + in_ref[rows, :].astype(F32)).astype(
                out_ref.dtype
            )


def add_call(kernel, ins, share):
    rows, half = ins[-1].shape
    if share == 0.5:
        outs = [struct((rows // 2, 2 * half), F32)] + [struct((rows // 2, half), BF16)] * 2
    else:
        outs = [struct((rows // 4, 2 * half), dtype) for dtype in (F32, BF16, BF16, BF16)]
    return kernel_call(kernel, list(ins), outs, [])


def cast_kernel(*refs):
    *in_refs, out_ref = refs
    start = 0
    for ref in in_refs:
        out_ref[:, start : start + ref.shape[1]] = ref[...].astype(BF16)
        start += ref.shape[1]


def low(*values):
    width = sum(value.shape[1] for value in values)
    return kernel_call(
        cast_kernel, list(values), [struct((values[0].shape[0], width), BF16)], []
    )[0]


def each_rows(count, body):
    @pl.loop(0, count // ROWS)
    def step(i):
        body(pl.ds(pl.multiple_of(i * ROWS, ROWS), ROWS))


def each_tile(start, width, body):
    @pl.loop(0, width // WIDE)
    def step(i):
        body(pl.ds(pl.multiple_of(start + i * WIDE, WIDE), WIDE))


def fetch(left, right, weights_ref, sems, first=0):
    moves = []
    start = left[0].shape[1] if left else 0
    for i, ref in enumerate(left):
        count = ref.shape[0]
        moves.append((ref, weights_ref.at[i * count : (i + 1) * count, :start]))
    columns = weights_ref.shape[1] - start
    for i, ref in enumerate(right):
        count = ref.shape[0] // 2
        for x in range(2):
            place = (2 * x + i) * count
            moves.append(
                (
                    ref.at[x * count : (x + 1) * count, first : first + columns],
                    weights_ref.at[place : place + count, start:],
                )
            )
    copies = [pltpu.make_async_copy(*move, sems.at[i]) for i, move in enumerate(moves)]
    for copy in copies:
        copy.start()
    return copies


def deliver(grads_ref, out_refs, sems):
    left, left_out, right, right_out = out_refs
    rows, cols = left.shape[0] // 2, left.shape[1]
    moves = [
        (left.at[:, :], 0, 2, 0),
        (left_out.at[:, :], 2, 2, 0),
        (right.at[:rows, :], 0, 1, 1),
        (right.at[rows:, :], 2, 1, 1),
        (right_out.at[:rows, :], 1, 1, 1),
        (right_out.at[rows:, :], 3, 1, 1),
    ]
    copies = []
    for i, (target, place, count, side) in enumerate(moves):
        spot = grads_ref.at[
            place * rows : (place + count) * rows, side * cols : (side + 1) * cols
        ]
        copies.append(pltpu.make_async_copy(spot, target, sems.at[i]))
    for copy in copies:
        copy.start()
    for copy in copies:
        copy.wait()


def grad_structs(width, columns):
    return [struct((width // 2, columns // 2), BF16)] * 4


def root_of(value):
    return lax.rsqrt(jnp.mean(value * value, axis=-1, keepdims=True) + EPS)


def norm_back(value, gain, grad):
    root = root_of(value)
    scaled = grad * gain
    inner = jnp.mean(value * scaled, axis=-1, keepdims=True)
    back = root * scaled - value * (root * root * root * inner)
    return back, jnp.sum(grad * value * root, axis=0, keepdims=True)


def rows_kernel(
    tokens_ref, cot_ref, gains_ref, source_ref, tokens_out, cot_out, gains_out, order_ref, normed_ref
):
    width = tokens_ref.shape[1]
    spot = lax.broadcasted_iota(jnp.int32, (width, width), 0)
    order_ref[...] = jnp.where(spot == source_ref[0:1, :], 1.0, 0.0).astype(BF16)
    order = order_ref[...]
    high, middle, rest = (nn(value, order) for value in thirds(gains_ref[...]))
    gains_out[...] = high + (middle + rest)
    tokens_out[...] = nn(tokens_ref[...], order)
    cot_out[...] = nn(cot_ref[...], order).astype(BF16)
    gain = gains_out[0:1, :]

    def norm(rows):
        value = tokens_out[rows, :]
        normed_ref[rows, :] = (value * root_of(value) * gain).astype(BF16)

    each_rows(tokens_ref.shape[0], norm)


def queries_of(capacity):
    return QUERIES if capacity <= 2 * KEYS else TILE


def each_chunk(count, size, body):
    if count == 1:
        body(0)
    else:
        pl.loop(0, count)(lambda step: body(pl.multiple_of(step * size, size)))


def each_pair(pairs, body):
    @pl.loop(0, pairs)
    def step(pair):
        body(pair, lambda which: pl.ds(pl.multiple_of((which * pairs + pair) * PAIR, PAIR), PAIR))


def of_head(value, head):
    lane = lax.broadcasted_iota(jnp.int32, value.shape, 1)
    return jnp.where(lane // HEAD_DIM == head, value, jnp.zeros_like(value))


def cross_forward_pair(q_ref, k_ref, v_ref, dead_ref, out_ref, lse_ref, s_ref, acc_ref):
    targets, capacity = q_ref.shape[0], k_ref.shape[0]
    size = min(capacity, KEYS)
    count = capacity // size
    queries = s_ref.shape[1]
    for head in range(2):
        rows = slice(head * HEAD_DIM, (head + 1) * HEAD_DIM)
        line = slice(head, head + 1)
        for start in range(0, targets, queries):
            cols = slice(start, start + queries)
            query = of_head(q_ref[cols, :], head)
            lse_ref[line, cols] = jnp.full((1, queries), NEGATIVE * 2, F32)

            def scores(base):
                keys = pl.ds(base, size)
                score = nt(k_ref[keys, :], query) + dead_ref[keys, 0:1]
                s_ref[keys, :] = score
                lse_ref[line, cols] = jnp.maximum(
                    lse_ref[line, cols], jnp.max(score, axis=0, keepdims=True)
                )

            each_chunk(count, size, scores)
            top = lse_ref[line, cols]
            lse_ref[line, cols] = jnp.zeros((1, queries), F32)

            def weights(base):
                keys = pl.ds(base, size)
                weight = jnp.exp(s_ref[keys, :] - top)
                s_ref[keys, :] = weight
                lse_ref[line, cols] += jnp.sum(weight, axis=0, keepdims=True)

            each_chunk(count, size, weights)
            total = lse_ref[line, cols]
            lse_ref[line, cols] = top + jnp.log(total)
            scale = 1.0 / total
            acc_ref[rows, cols] = jnp.zeros((HEAD_DIM, queries), F32)

            def mix(base):
                keys = pl.ds(base, size)
                probs = (s_ref[keys, :] * scale).astype(BF16)
                acc_ref[rows, cols] += tn(v_ref[keys, :], probs)[rows]

            each_chunk(count, size, mix)
    out_ref[...] = acc_ref[...].T.astype(BF16)


def cross_backward_pair(
    q_ref, k_ref, v_ref, dead_ref, lse_ref, go_ref, dq_ref, dk_ref, dv_ref,
    p_ref, dp_ref, dqt_ref, dk_acc, dv_acc, delta_ref,
):
    targets, capacity = q_ref.shape[0], k_ref.shape[0]
    size = min(capacity, KEYS)
    count = capacity // size
    queries = p_ref.shape[1]
    dk_acc[...] = jnp.zeros_like(dk_acc)
    dv_acc[...] = jnp.zeros_like(dv_acc)
    for head in range(2):
        rows = slice(head * HEAD_DIM, (head + 1) * HEAD_DIM)
        for start in range(0, targets, queries):
            cols = slice(start, start + queries)
            query = of_head(q_ref[cols, :], head)
            grad = of_head(go_ref[cols, :], head)
            lse = lse_ref[head : head + 1, cols]
            delta_ref[...] = jnp.zeros_like(delta_ref)

            def first(base):
                keys = pl.ds(base, size)
                probs = jnp.exp(nt(k_ref[keys, :], query) + dead_ref[keys, 0:1] - lse)
                grad_probs = nt(v_ref[keys, :], grad)
                p_ref[keys, :] = probs
                dp_ref[keys, :] = grad_probs
                delta_ref[...] += jnp.sum(probs * grad_probs, axis=0, keepdims=True)

            each_chunk(count, size, first)
            delta = delta_ref[...]
            dqt_ref[rows, cols] = jnp.zeros((HEAD_DIM, queries), F32)

            def second(base):
                keys = pl.ds(base, size)
                probs = p_ref[keys, :]
                dv_acc[keys, :] += nn(probs.astype(BF16), grad)
                low = (probs * (dp_ref[keys, :] - delta)).astype(BF16)
                dk_acc[keys, :] += nn(low, query)
                dqt_ref[rows, cols] += tn(k_ref[keys, :], low)[rows]

            each_chunk(count, size, second)
    dq_ref[...] = dqt_ref[...].T.astype(BF16)
    dk_ref[...] = dk_acc[...].astype(BF16)
    dv_ref[...] = dv_acc[...].astype(BF16)


def skewed(row, block):
    before = row[:, (block - 1) * TILE : block * TILE] if block else jnp.zeros((1, TILE), F32)
    both = jnp.concatenate([before, row[:, block * TILE : (block + 1) * TILE]], axis=1)
    both = jnp.broadcast_to(both, (TILE, 2 * TILE))
    return pltpu.roll(both, 0, 1, stride=1, stride_axis=0)[:, TILE:]


def unskewed(tile):
    both = jnp.concatenate([jnp.zeros_like(tile), tile], axis=1)
    total = both[:8]
    for base in range(8, TILE, 8):
        total = total + pltpu.roll(both[base : base + 8], 2 * TILE - base, 1)
    row = lax.broadcasted_iota(jnp.int32, total.shape, 0)
    for bit in (1, 2, 4):
        total = jnp.where(row & bit != 0, pltpu.roll(total, 2 * TILE - bit, 1), total)
    return jnp.sum(total, axis=0, keepdims=True)


def self_scores(k_ref, query, tiles, start):
    keys = start + QUERIES
    columns = []
    for i in range(start // TILE, keys // TILE):
        columns.append(
            jnp.concatenate([tiles[max(i - j, 0)] for j in range(keys // TILE)], axis=0)
        )
    score = nt(k_ref[:keys, :], query) + jnp.concatenate(columns, axis=1)
    key = lax.broadcasted_iota(jnp.int32, score.shape, 0)
    spot = lax.broadcasted_iota(jnp.int32, score.shape, 1) + start
    return jnp.where(key <= spot, score, NEGATIVE)


def self_forward_pair(q_ref, k_ref, v_ref, bias_ref, out_ref, lse_ref, acc_ref):
    targets = q_ref.shape[0]
    for head in range(2):
        rows = slice(head * HEAD_DIM, (head + 1) * HEAD_DIM)
        row = bias_ref[head : head + 1, :]
        tiles = [skewed(row, block) for block in range(targets // TILE)]
        for start in range(0, targets, QUERIES):
            cols = slice(start, start + QUERIES)
            query = of_head(q_ref[cols, :], head)
            score = self_scores(k_ref, query, tiles, start)
            top = jnp.max(score, axis=0, keepdims=True)
            weight = jnp.exp(score - top)
            total = jnp.sum(weight, axis=0, keepdims=True)
            lse_ref[head : head + 1, cols] = top + jnp.log(total)
            probs = (weight * (1.0 / total)).astype(BF16)
            acc_ref[rows, cols] = tn(v_ref[: start + QUERIES, :], probs)[rows]
    out_ref[...] = acc_ref[...].T.astype(BF16)


def self_backward_pair(
    q_ref, k_ref, v_ref, bias_ref, lse_ref, go_ref, dq_ref, dk_ref, dv_ref, dbias_ref,
    dqt_ref, dk_acc, dv_acc,
):
    targets = q_ref.shape[0]
    dk_acc[...] = jnp.zeros_like(dk_acc)
    dv_acc[...] = jnp.zeros_like(dv_acc)
    blocks = targets // TILE
    for head in range(2):
        rows = slice(head * HEAD_DIM, (head + 1) * HEAD_DIM)
        row = bias_ref[head : head + 1, :]
        tiles = [skewed(row, block) for block in range(blocks)]
        sums = [jnp.zeros((TILE, TILE), F32) for block in range(blocks)]
        for start in range(0, targets, QUERIES):
            cols = slice(start, start + QUERIES)
            keys = start + QUERIES
            query = of_head(q_ref[cols, :], head)
            grad = of_head(go_ref[cols, :], head)
            score = self_scores(k_ref, query, tiles, start)
            probs = jnp.exp(score - lse_ref[head : head + 1, cols])
            grad_probs = nt(v_ref[:keys, :], grad)
            delta = jnp.sum(probs * grad_probs, axis=0, keepdims=True)
            dv_acc[:keys, :] += nn(probs.astype(BF16), grad)
            grad_scores = probs * (grad_probs - delta)
            for i in range(start // TILE, keys // TILE):
                for j in range(i + 1):
                    sums[i - j] = sums[i - j] + grad_scores[
                        j * TILE : (j + 1) * TILE, i * TILE - start : (i + 1) * TILE - start
                    ]
            low_scores = grad_scores.astype(BF16)
            dk_acc[:keys, :] += nn(low_scores, query)
            dqt_ref[rows, cols] = tn(k_ref[:keys, :], low_scores)[rows]
        lines = [unskewed(tile) for tile in sums]
        parts = []
        for block in range(blocks):
            part = lines[block][:, TILE:]
            if block + 1 < blocks:
                part = part + lines[block + 1][:, :TILE]
            parts.append(part)
        dbias_ref[head : head + 1, :] = jnp.concatenate(parts, axis=1)
    dq_ref[...] = dqt_ref[...].T.astype(BF16)
    dk_ref[...] = dk_acc[...].astype(BF16)
    dv_ref[...] = dv_acc[...].astype(BF16)


def self_forward_kernel(
    normed_ref, bias_ref, *refs
):
    mixed_ref, attended_ref, lse_ref, partial_ref, weights_ref, acc_ref, sems = refs[2:]
    copies = fetch(refs[:2], [], weights_ref, sems)
    for copy in copies:
        copy.wait()
    part = attended_ref.shape[1]
    pairs = part // PAIR
    normed = normed_ref[...]

    @pl.loop(0, 3 * part // TILE)
    def project(i):
        cols = pl.ds(pl.multiple_of(i * TILE, TILE), TILE)
        mixed_ref[:, cols] = nn(normed, weights_ref[:, cols]).astype(BF16)

    def attend(pair, cols):
        self_forward_pair(
            *(mixed_ref.at[:, cols(i)] for i in range(3)),
            bias_ref.at[pair], attended_ref.at[:, cols(0)], lse_ref.at[pair], acc_ref,
        )

    each_pair(pairs, attend)
    partial_ref[...] = nt(attended_ref[...], weights_ref[:, 3 * part :])


def self_forward(normed, bias, quarters):
    targets, width = normed.shape
    columns = quarters[0].shape[1]
    part = columns // 4
    pairs = part // PAIR
    return kernel_call(
        self_forward_kernel,
        [normed, bias, *quarters],
        [
            struct((targets, 3 * part), BF16),
            struct((targets, part), BF16),
            struct((pairs, 8, targets), F32),
            struct((targets, width), F32),
        ],
        [
            pltpu.VMEM((width, columns), BF16),
            pltpu.VMEM((PAIR, targets), F32),
            pltpu.SemaphoreType.DMA((6,)),
        ],
        in_specs=[IN_VMEM] * 2 + [IN_PLACE] * 2,
        time=12,
    )


def encoder_kernel(core_ref, own_ref, peer_ref, order_ref, *refs):
    encoded_ref, out_ref, weights_ref, sems = refs[2:]

    @pl.when(pl.program_id(0) == 0)
    def load():
        for copy in fetch([], refs[:2], weights_ref, sems, weights_ref.shape[1]):
            copy.wait()

    core, half = core_ref[0], own_ref.shape[1]
    own_rows = pl.ds(pl.multiple_of(core * half, half), half)
    peer_rows = pl.ds(pl.multiple_of(half - core * half, half), half)
    encoded = nn(own_ref[...], order_ref[own_rows, :]) + nn(peer_ref[...], order_ref[peer_rows, :])
    encoded_ref[...] = encoded.astype(BF16)
    encoded = encoded_ref[...]

    def project(cols):
        out_ref[:, cols] = nn(encoded, weights_ref[:, cols]).astype(BF16)

    each_tile(0, out_ref.shape[1], project)


def encoder_call(core, own, peer, order, quarters):
    capacity, half = own.shape
    width = 2 * half
    columns = quarters[0].shape[1] // 2
    size = min(capacity, KEYS)
    block = lambda cols: pl.BlockSpec((size, cols), lambda i: (i, 0))
    return kernel_call(
        encoder_kernel,
        [core, own, peer, order, *quarters],
        [struct((capacity, width), BF16), struct((capacity, columns), BF16)],
        [pltpu.VMEM((width, columns), BF16), pltpu.SemaphoreType.DMA((4,))],
        grid=(capacity // size,),
        in_specs=[IN_SMEM, block(half), block(half), IN_VMEM] + [IN_PLACE] * 2,
        out_specs=[block(width), block(columns)],
        time=8,
    )


def cross_forward_kernel(tokens_ref, partial_ref, peer_ref, gains_ref, kv_ref, dead_ref, *refs):
    (
        h_ref, normed_ref, query_ref, att_ref, lse_ref, out_ref, more_ref,
        weights_ref, s_ref, acc_ref, sems,
    ) = refs[2:]
    copies = fetch([], refs[:2], weights_ref, sems)
    gain = gains_ref[1:2, :]

    def norm(rows):
        value = tokens_ref[rows, :] + (partial_ref[rows, :] + peer_ref[rows, :])
        h_ref[rows, :] = value
        normed_ref[rows, :] = (value * root_of(value) * gain).astype(BF16)

    each_rows(h_ref.shape[0], norm)
    for copy in copies:
        copy.wait()
    part = query_ref.shape[1]
    pairs = part // PAIR
    query_ref[...] = nn(normed_ref[...], weights_ref[:, :part]).astype(BF16)

    def attend(pair, cols):
        cross_forward_pair(
            query_ref.at[:, cols(0)], kv_ref.at[:, cols(0)], kv_ref.at[:, cols(1)], dead_ref,
            att_ref.at[:, cols(0)], lse_ref.at[pair], s_ref, acc_ref,
        )

    each_pair(pairs, attend)
    count = out_ref.shape[0]
    out_ref[...] = nt(att_ref[:count, :], weights_ref[:, part:])
    more_ref[...] = nt(att_ref[count:, :], weights_ref[:, part:])


def cross_forward(tokens, partial, peer, gains, key_value, dead, quarters):
    targets, width = tokens.shape
    capacity, columns = key_value.shape
    part = columns // 2
    pairs = part // PAIR
    return kernel_call(
        cross_forward_kernel,
        [tokens, partial, peer, gains, key_value, dead, *quarters],
        [
            struct((targets, width), F32),
            struct((targets, width), BF16),
            struct((targets, part), BF16),
            struct((targets, part), BF16),
            struct((pairs, 8, targets), F32),
            struct((targets // 2, width), F32),
            struct((targets // 2, width), F32),
        ],
        [
            pltpu.VMEM((width, columns), BF16),
            pltpu.VMEM((capacity, queries_of(capacity)), F32),
            pltpu.VMEM((PAIR, targets), F32),
            pltpu.SemaphoreType.DMA((4,)),
        ],
        in_specs=[IN_VMEM] * 6 + [IN_PLACE] * 2,
        time=16,
    )


def ffn_kernel(
    before_ref, first_ref, second_ref, first_in_ref, second_in_ref, gains_ref, cot_ref, *refs
):
    h_ref, down_ref, back_ref, *outs = refs[4:11]
    weights_ref, grads_ref, normed_ref, normed_t, cot_t, in_sems, out_sems = refs[11:]
    copies = fetch(refs[:2], refs[2:4], weights_ref, in_sems)
    gain = gains_ref[2:3, :]
    count = first_ref.shape[0]
    halves = ((first_ref, first_in_ref), (second_ref, second_in_ref))
    for i, (partial_ref, peer_ref) in enumerate(halves):

        def norm(rows):
            own = pl.ds(pl.multiple_of(rows.start + i * count, ROWS), ROWS)
            value = before_ref[own, :] + (partial_ref[rows, :] + peer_ref[rows, :])
            h_ref[own, :] = value
            normed_ref[own, :] = (value * root_of(value) * gain).astype(BF16)

        each_rows(count, norm)
    normed_t[...] = normed_ref[...].T
    cot_t[...] = cot_ref[...].T
    down_ref[...] = jnp.zeros_like(down_ref)
    back_ref[...] = jnp.zeros_like(back_ref)
    for copy in copies:
        copy.wait()
    hidden = weights_ref.shape[1] // 3

    @pl.loop(0, hidden // WIDE)
    def tile(i):
        gates, ups, downs = (
            pl.ds(pl.multiple_of(k * hidden + i * WIDE, WIDE), WIDE) for k in range(3)
        )
        normed = normed_ref[...]
        gate = nn(normed, weights_ref[:, gates])
        up = nn(normed, weights_ref[:, ups])
        grad_act = nn(cot_ref[...], weights_ref[:, downs]).astype(BF16).astype(F32)
        square = gate * gate
        curve = jnp.tanh(GELU_ROOT * (gate + GELU_CUBE * (square * gate)))
        share = 0.5 * (1.0 + curve)
        gelu = gate * share
        slope = share + (0.5 * gate) * (1.0 - curve * curve) * (
            GELU_ROOT * (1.0 + (3.0 * GELU_CUBE) * square)
        )
        act = (gelu * up).astype(BF16)
        grad_gate = (grad_act * up * slope).astype(BF16)
        grad_up = (grad_act * gelu).astype(BF16)
        back_ref[...] += nt(grad_gate, weights_ref[:, gates]) + nt(grad_up, weights_ref[:, ups])
        down_ref[...] += nt(act, weights_ref[:, downs])
        grads_ref[:, gates] = nn(normed_t[...], grad_gate).astype(BF16)
        grads_ref[:, ups] = nn(normed_t[...], grad_up).astype(BF16)
        grads_ref[:, downs] = nn(cot_t[...], act).astype(BF16)

    deliver(grads_ref, outs, out_sems)


def ffn_call(before, partials, peers, gains, cot, quarters):
    targets, width = before.shape
    columns = 2 * quarters[0].shape[1]
    return kernel_call(
        ffn_kernel,
        [before, *partials, *peers, gains, cot, *quarters],
        [struct((targets, width), F32)] * 3 + grad_structs(width, columns),
        [
            pltpu.VMEM((width, columns), BF16),
            pltpu.VMEM((width, columns), BF16),
            pltpu.VMEM((targets, width), BF16),
            pltpu.VMEM((width, targets), BF16),
            pltpu.VMEM((width, targets), BF16),
            pltpu.SemaphoreType.DMA((6,)),
            pltpu.SemaphoreType.DMA((6,)),
        ],
        in_specs=[IN_VMEM] * 7 + [IN_PLACE] * 4,
        out_specs=[IN_VMEM] * 3 + [IN_PLACE] * 4,
        time=20,
    )


def cross_backward_kernel(
    cot_ref, partial_ref, peer_ref, h_ref, gains_ref, query_ref, kv_ref, dead_ref, lse_ref, *refs
):
    (
        g_ref, low_ref, dq_ref, dkv_ref, back_ref, gain_grad_ref,
        weights_ref, go_ref, p_ref, dp_ref, dqt_ref, dk_acc, dv_acc, delta_ref, sems,
    ) = refs[2:]
    copies = fetch([], refs[:2], weights_ref, sems)
    gain = gains_ref[2:3, :]
    gain_grad_ref[...] = jnp.zeros_like(gain_grad_ref)

    def norm(rows):
        back, gain_grad = norm_back(h_ref[rows, :], gain, partial_ref[rows, :] + peer_ref[rows, :])
        gain_grad_ref[0:1, :] += gain_grad
        value = cot_ref[rows, :].astype(F32) + back
        g_ref[rows, :] = value
        low_ref[rows, :] = value.astype(BF16)

    each_rows(h_ref.shape[0], norm)
    for copy in copies:
        copy.wait()
    part = query_ref.shape[1]
    pairs = part // PAIR
    go_ref[...] = nn(low_ref[...], weights_ref[:, part:]).astype(BF16)

    def attend(pair, cols):
        cross_backward_pair(
            query_ref.at[:, cols(0)], kv_ref.at[:, cols(0)], kv_ref.at[:, cols(1)], dead_ref,
            lse_ref.at[pair], go_ref.at[:, cols(0)],
            dq_ref.at[:, cols(0)], dkv_ref.at[:, cols(0)], dkv_ref.at[:, cols(1)],
            p_ref, dp_ref, dqt_ref, dk_acc, dv_acc, delta_ref,
        )

    each_pair(pairs, attend)
    back_ref[...] = nt(dq_ref[...], weights_ref[:, :part])


def cross_backward(cot, partial, peer, before, gains, query, key_value, dead, lse, quarters):
    targets, width = cot.shape
    capacity, columns = key_value.shape
    return kernel_call(
        cross_backward_kernel,
        [cot, partial, peer, before, gains, query, key_value, dead, lse, *quarters],
        [
            struct((targets, width), F32),
            struct((targets, width), BF16),
            struct(query.shape, BF16),
            struct(key_value.shape, BF16),
            struct((targets, width), F32),
            struct((8, width), F32),
        ],
        [
            pltpu.VMEM((width, columns), BF16),
            pltpu.VMEM(query.shape, BF16),
            pltpu.VMEM((capacity, queries_of(capacity)), F32),
            pltpu.VMEM((capacity, queries_of(capacity)), F32),
            pltpu.VMEM((PAIR, targets), F32),
            pltpu.VMEM((capacity, PAIR), F32),
            pltpu.VMEM((capacity, PAIR), F32),
            pltpu.VMEM((1, queries_of(capacity)), F32),
            pltpu.SemaphoreType.DMA((4,)),
        ],
        in_specs=[IN_VMEM] * 9 + [IN_PLACE] * 2,
        time=18,
    )


def cross_grads_kernel(
    core_ref, normed_ref, dq_ref, low_ref, att_ref, order_ref, encoded_ref, dkv_ref, *refs
):
    kept_ref, given_ref, *outs = refs[2:8]
    weights_ref, acc_ref, grads_ref, in_sems, out_sems = refs[8:]
    step = pl.program_id(0)
    part = dq_ref.shape[1]

    @pl.when(step == 0)
    def load():
        copies = fetch([], refs[:2], weights_ref, in_sems, weights_ref.shape[1])
        grads_ref[:, :part] = tn(normed_ref[...], dq_ref[...]).astype(BF16)
        grads_ref[:, part : 2 * part] = tn(low_ref[...], att_ref[...]).astype(BF16)
        acc_ref[...] = jnp.zeros_like(acc_ref)
        for copy in copies:
            copy.wait()

    encoded_t = encoded_ref[...].T

    def project(cols):
        acc_ref[:, cols] += nn(encoded_t, dkv_ref[:, cols])

    each_tile(0, acc_ref.shape[1], project)
    core, half = core_ref[0], kept_ref.shape[1]
    terms = nt(dkv_ref[...], weights_ref[...]).astype(BF16)
    own_rows = pl.ds(pl.multiple_of(core * half, half), half)
    peer_rows = pl.ds(pl.multiple_of(half - core * half, half), half)
    kept_ref[...] = nt(terms, order_ref[own_rows, :]).astype(BF16)
    given_ref[...] = nt(terms, order_ref[peer_rows, :]).astype(BF16)

    @pl.when(step == pl.num_programs(0) - 1)
    def store():
        grads_ref[:, 2 * part :] = acc_ref[...].astype(BF16)
        deliver(grads_ref, outs, out_sems)


def cross_grads(core, normed, dq, low_two, attended, order, encoded, dkv, quarters):
    capacity, width = encoded.shape
    columns = dkv.shape[1]
    size = min(capacity, KEYS)
    block = lambda cols: pl.BlockSpec((size, cols), lambda i: (i, 0))
    return kernel_call(
        cross_grads_kernel,
        [core, normed, dq, low_two, attended, order, encoded, dkv, *quarters],
        [struct((capacity, width // 2), BF16)] * 2 + grad_structs(width, 2 * columns),
        [
            pltpu.VMEM((width, columns), BF16),
            pltpu.VMEM((width, columns), F32),
            pltpu.VMEM((width, 2 * columns), BF16),
            pltpu.SemaphoreType.DMA((4,)),
            pltpu.SemaphoreType.DMA((6,)),
        ],
        grid=(capacity // size,),
        in_specs=[IN_SMEM] + [IN_VMEM] * 5 + [block(width), block(columns)] + [IN_PLACE] * 2,
        out_specs=[block(width // 2)] * 2 + [IN_PLACE] * 4,
        time=12,
    )


def self_backward_kernel(
    core_ref, g_in_ref, partial_ref, peer_ref, h_ref, gains_ref, mixed_ref, bias_ref, lse_ref,
    attended_ref, normed_ref, tokens_ref, gain_three_ref, order_ref, labels_ref, *refs
):
    g_ref, back_ref, small_ref, *outs = refs[2:9]
    (
        weights_ref, grads_ref, low_ref, go_ref, dmixed_ref, dbias_ref,
        dqt_ref, dk_acc, dv_acc, gain_ref, in_sems, out_sems,
    ) = refs[9:]
    copies = fetch(refs[:2], [], weights_ref, in_sems)
    gain = gains_ref[1:2, :]
    gain_ref[...] = jnp.zeros_like(gain_ref)

    def norm(rows):
        back, gain_grad = norm_back(h_ref[rows, :], gain, partial_ref[rows, :] + peer_ref[rows, :])
        gain_ref[1:2, :] += gain_grad
        value = g_in_ref[rows, :] + back
        g_ref[rows, :] = value
        low_ref[rows, :] = value.astype(BF16)

    each_rows(h_ref.shape[0], norm)
    for copy in copies:
        copy.wait()
    part = attended_ref.shape[1]
    pairs = part // PAIR
    go_ref[...] = nn(low_ref[...], weights_ref[:, 3 * part :]).astype(BF16)
    dbias_ref[...] = jnp.zeros_like(dbias_ref)

    def attend(pair, cols):
        self_backward_pair(
            *(mixed_ref.at[:, cols(i)] for i in range(3)),
            bias_ref.at[pair], lse_ref.at[pair], go_ref.at[:, cols(0)],
            *(dmixed_ref.at[:, cols(i)] for i in range(3)),
            dbias_ref.at[pair], dqt_ref, dk_acc, dv_acc,
        )

    each_pair(pairs, attend)
    back_ref[...] = nt(dmixed_ref[...], weights_ref[:, : 3 * part])
    normed_t = normed_ref[...].T

    @pl.loop(0, 3 * part // TILE)
    def project(i):
        cols = pl.ds(pl.multiple_of(i * TILE, TILE), TILE)
        grads_ref[:, cols] = nn(normed_t, dmixed_ref[:, cols]).astype(BF16)

    grads_ref[:, 3 * part :] = tn(low_ref[...], attended_ref[...]).astype(BF16)

    def sums(rows):
        value = tokens_ref[rows, :]
        gain_ref[0:1, :] += jnp.sum(back_ref[rows, :] * value * root_of(value), axis=0, keepdims=True)

    each_rows(h_ref.shape[0], sums)
    core = core_ref[0]
    first = jnp.where(core == 0, 1.0, 0.0)
    line = lax.broadcasted_iota(jnp.int32, gain_ref.shape, 0)
    gains = gain_ref[...] + jnp.where(line == 2, gain_three_ref[0:1, :], 0.0)
    gains = gains * jnp.where(line == 0, 1.0, first)
    high, middle, rest = (nt(value, order_ref[...]) for value in thirds(gains))
    small_ref[...] = jnp.zeros_like(small_ref)
    small_ref[0:8, :] = high + (middle + rest)
    bucket = lax.broadcasted_iota(jnp.int32, (labels_ref.shape[0], TILE), 1)
    which = jnp.where(labels_ref[:, 0:1] == bucket, 1.0, 0.0).astype(BF16)
    for pair in range(pairs):
        high, middle, rest = (nn(value, which) for value in thirds(dbias_ref[pair]))
        table = high + (middle + rest)
        for side in range(2):
            spot = side * pairs + pair
            small_ref[8:, spot * TILE : (spot + 1) * TILE] = table * jnp.where(
                core == side, 1.0, 0.0
            )
    deliver(grads_ref, outs, out_sems)


def self_backward(
    core, g_in, partial, peer, before, gains, mixed, bias, lse, attended, normed, tokens,
    gain_three, order, labels, quarters,
):
    targets, width = g_in.shape
    part = attended.shape[1]
    pairs = part // PAIR
    return kernel_call(
        self_backward_kernel,
        [
            core, g_in, partial, peer, before, gains, mixed, bias, lse, attended, normed, tokens,
            gain_three, order, labels, *quarters,
        ],
        [
            struct((targets, width), F32),
            struct((targets, width), F32),
            struct((16, width), F32),
        ]
        + grad_structs(width, 4 * part),
        [
            pltpu.VMEM((width, 4 * part), BF16),
            pltpu.VMEM((width, 4 * part), BF16),
            pltpu.VMEM((targets, width), BF16),
            pltpu.VMEM((targets, part), BF16),
            pltpu.VMEM((targets, 3 * part), BF16),
            pltpu.VMEM((pairs, 8, targets), F32),
            pltpu.VMEM((PAIR, targets), F32),
            pltpu.VMEM((targets, PAIR), F32),
            pltpu.VMEM((targets, PAIR), F32),
            pltpu.VMEM((8, width), F32),
            pltpu.SemaphoreType.DMA((6,)),
            pltpu.SemaphoreType.DMA((6,)),
        ],
        in_specs=[IN_SMEM] + [IN_VMEM] * 14 + [IN_PLACE] * 2,
        out_specs=[IN_VMEM] * 3 + [IN_PLACE] * 4,
        time=22,
    )


def last_kernel(
    g_ref, partial_ref, peer_ref, tokens_ref, gains_ref, h_ref, down_ref, down_in_ref, order_ref,
    grad_ref, out_ref,
):
    gain = gains_ref[0:1, :]
    order = order_ref[...]

    def finish(rows):
        back, unused = norm_back(
            tokens_ref[rows, :], gain, partial_ref[rows, :] + peer_ref[rows, :]
        )
        high, middle, rest = (nt(value, order) for value in thirds(g_ref[rows, :] + back))
        grad_ref[rows, :] = high + (middle + rest)
        value = h_ref[rows, :] + (down_ref[rows, :] + down_in_ref[rows, :])
        out_ref[rows, :] = nt(value.astype(BF16), order).astype(BF16)

    count = 4 * ROWS

    @pl.loop(0, g_ref.shape[0] // count)
    def step(i):
        finish(pl.ds(pl.multiple_of(i * count, count), count))


def shards(
    decoder_in,
    encoder_out,
    lengths,
    key_mask,
    assign,
    buckets,
    norm_one,
    norm_two,
    norm_three,
    self_query,
    self_key,
    self_value,
    self_output,
    cross_query,
    cross_key,
    cross_value,
    cross_output,
    ffn_gate,
    ffn_up,
    ffn_down,
    bias_table,
    cotangent,
    *,
    size,
):
    rank = lax.axis_index("dp")
    core = lax.axis_index("mp")
    targets, width = decoder_in.shape[1:]
    capacity = key_mask.shape[1]
    block = width // size
    outer = size // 4
    half = width // 2
    heads = bias_table.shape[1]
    which_core = core.reshape(1)

    spots = jnp.arange(width, dtype=jnp.int32)
    spot = spots // block
    masks = spot // (2 * outer) + 2 * (spot // outer % 2) + 4 * (spot % outer)
    source = jnp.broadcast_to(((rank ^ masks) * block + spots % block)[None], (8, width))

    weights = gather_outer(
        low(
            self_query, self_key, self_value, self_output.T,
            cross_query, cross_output.T, cross_key, cross_value,
        ),
        size,
    )
    gains = jnp.concatenate(
        [norm_one[None], norm_two[None], norm_three[None], jnp.zeros((5, width), F32)]
    )
    tokens, cot, gains, order, normed_one = kernel_call(
        rows_kernel,
        [decoder_in[0], cotangent[0], gains, source],
        [
            struct((targets, width), F32),
            struct((targets, width), BF16),
            struct((8, width), F32),
            struct((width, width), BF16),
            struct((targets, width), BF16),
        ],
        [],
    )
    ffn = low(ffn_gate, ffn_up, ffn_down.T)

    sent = lax.dynamic_slice_in_dim(encoder_out, core * half, half, 2)[assign]
    weights, ffn, normed_one, sent = after((weights, ffn, normed_one, sent))
    weights = gather_first(weights, size)
    weights, ffn, sent = after((weights, ffn, sent))
    weights = send_first(weights, size)
    own = lax.all_to_all(sent, "dp", split_axis=0, concat_axis=0, tiled=True)
    own = own.reshape(capacity, half)
    labels, bias_table, lengths = after((buckets[:, :TILE], bias_table, lengths), weights[0])
    mine = assign[rank]
    positions = jnp.arange(capacity, dtype=jnp.int32)
    live = (positions < lengths[mine]) & ((key_mask[mine] == 1) | (positions == 0))
    dead = jnp.broadcast_to(jnp.where(live, 0.0, NEGATIVE)[:, None], (capacity, TILE))
    which = labels[None, :, 0] == jnp.arange(bias_table.shape[0], dtype=jnp.int32)[:, None]
    bias = jnp.sum(jnp.where(which[None], bias_table.T[:, :, None], 0.0), axis=1)
    bias = jnp.pad(bias.reshape(heads // 2, 2, targets), ((0, 0), (0, 6), (0, 0)))

    weights, own, ffn, bias, dead = after((weights, own, ffn, bias, dead))
    weights = gather_second(weights, size)
    weights, ffn = after((weights, ffn))
    weights = send_second(weights, size)
    ffn = gather_outer(ffn, size)

    weights, own, ffn = after((weights, own, ffn))
    ffn = gather_first(ffn, size)
    ffn, weights, own = after((ffn, weights, own))
    ffn = send_first(ffn, size)
    own_peer = swap_cores(own)
    left, right = weights
    mixed, attended, lse_self, partial_one = self_forward(normed_one, bias, left)
    ffn, mixed, attended, lse_self, partial_one, own, own_peer = after(
        (ffn, mixed, attended, lse_self, partial_one, own, own_peer)
    )
    ffn = gather_second(ffn, size)
    ffn, partial_one, own = after((ffn, partial_one, own))
    ffn = send_second(ffn, size)
    peer_one = swap_cores(partial_one)
    encoded, key_value = encoder_call(which_core, own, own_peer, order, right)
    h_one, normed_two, cross_q, cross_att, lse_cross, *partial_two = cross_forward(
        tokens, partial_one, peer_one, gains, key_value, dead, right
    )
    peer_two = [swap_cores(value) for value in partial_two]
    h_two, partial_down, partial_three, *grads = ffn_call(
        h_one, partial_two, peer_two, gains, cot, ffn[0] + ffn[1]
    )

    ffn = scatter_first(grads, size)
    peer_three = swap_cores(partial_three)
    g_two, low_two, dq, dkv, partial_four, gain_three = cross_backward(
        cot, partial_three, peer_three, h_two, gains, cross_q, key_value, dead, lse_cross, right
    )
    ffn, dq, dkv, low_two, partial_four = after((ffn, dq, dkv, low_two, partial_four))
    ffn = scatter_second_parts(ffn)
    ffn, dq, dkv, low_two, partial_four = after((ffn, dq, dkv, low_two, partial_four))
    ffn = scatter_second_send(ffn, size)
    peer_four = swap_cores(partial_four)
    kept, given, *grads = cross_grads(
        which_core, normed_two, dq, low_two, cross_att, order, encoded, dkv, right
    )
    ffn, kept, given, grads, peer_four = after((ffn, kept, given, grads, peer_four))
    ffn = scatter_outer_parts(ffn)
    ffn, kept, given, grads, peer_four = after((ffn, kept, given, grads, peer_four))
    cross = scatter_first(grads, size)
    ffn = scatter_outer_send(ffn, size)
    taken = swap_cores(given)
    g_one, partial_five, small, *grads = self_backward(
        which_core, g_two, partial_four, peer_four, h_one, gains, mixed, bias, lse_self, attended,
        normed_one, tokens, gain_three, order, labels, left,
    )
    ffn, cross, kept, taken, g_one, partial_five, small, grads = after(
        (ffn, cross, kept, taken, g_one, partial_five, small, grads)
    )
    last = scatter_first(grads, size)
    peer_five = swap_cores(partial_five)
    peer_down = swap_cores(partial_down)
    terms = (kept.astype(F32) + taken.astype(F32)).astype(BF16)
    cross = scatter_second_send(scatter_second_parts(cross), size)
    back = lax.all_to_all(
        terms.reshape(size, capacity // size, half), "dp", split_axis=0, concat_axis=0, tiled=True
    )
    sum_ffn = scatter_last(ffn)
    decoder_grad, layer_out = kernel_call(
        last_kernel,
        [g_one, partial_five, peer_five, tokens, gains, h_two, partial_down, peer_down, order],
        [struct((targets, width), F32), struct((targets, width), BF16)],
        [],
        time=10,
    )
    last, cross, layer_out, sum_ffn, small = after((last, cross, layer_out, sum_ffn, small))
    last, cross = scatter_second_parts(last), scatter_outer_parts(cross)
    last, cross, back = after((last, cross, back))
    last = scatter_second_send(last, size)
    cross = scatter_outer_send(cross, size)
    small = small + swap_cores(small)
    last, small = after((last, small))
    last = scatter_outer_parts(last)
    last, small, back = after((last, small, back))
    last = scatter_outer_send(last, size)
    small = sum_devices(small, size)
    inverse = jnp.zeros_like(assign).at[assign].set(jnp.arange(size, dtype=jnp.int32))
    encoder_grad = back[inverse]
    sum_cross, sum_self = scatter_last(cross), scatter_last(last)

    table = small[8:10].reshape(2, 2, heads // 2, TILE)[:, :, :, : bias_table.shape[0]]
    table = lax.dynamic_index_in_dim(table, core, 1, keepdims=False)
    grad_table = table.transpose(1, 0, 2).reshape(heads, -1).T

    def parts(value, count):
        step = value.shape[1] // count
        return [value[:, i * step : (i + 1) * step] for i in range(count)]

    grad_self_query, grad_self_key, grad_self_value, grad_output_one = parts(sum_self, 4)
    grad_cross_query, grad_output_two, grad_cross_key, grad_cross_value = parts(sum_cross, 4)
    grad_ffn_gate, grad_ffn_up, grad_ffn_down = parts(sum_ffn, 3)
    return (
        layer_out[None],
        decoder_grad[None],
        encoder_grad,
        small[0],
        small[1],
        small[2],
        grad_self_query,
        grad_self_key,
        grad_self_value,
        grad_output_one.T,
        grad_cross_query,
        grad_cross_key,
        grad_cross_value,
        grad_output_two.T,
        grad_ffn_gate,
        grad_ffn_up,
        grad_ffn_down.T,
        grad_table,
    )


def solution(mesh):
    in_specs = (
        P("dp", None, None),
        P(None, "dp", None),
        P(),
        P(),
        P(),
        P(),
        P(),
        P(),
        P(),
        P("dp", "mp"),
        P("dp", "mp"),
        P("dp", "mp"),
        P("mp", "dp"),
        P("dp", "mp"),
        P("dp", "mp"),
        P("dp", "mp"),
        P("mp", "dp"),
        P("dp", "mp"),
        P("dp", "mp"),
        P("mp", "dp"),
        P(None, "mp"),
        P("dp", None, None),
    )
    out_specs = (
        P("dp", None, None),
        P("dp", None, None),
        P(None, "dp", "mp"),
        P(),
        P(),
        P(),
        P("dp", "mp"),
        P("dp", "mp"),
        P("dp", "mp"),
        P("mp", "dp"),
        P("dp", "mp"),
        P("dp", "mp"),
        P("dp", "mp"),
        P("mp", "dp"),
        P("dp", "mp"),
        P("dp", "mp"),
        P("mp", "dp"),
        P(None, "mp"),
    )
    body = functools.partial(shards, size=mesh.shape["dp"])
    return jax.shard_map(body, mesh=mesh, in_specs=in_specs, out_specs=out_specs, check_vma=False)
```

time: 522 us -> 357 us (0.68)
  Pallas kernels: 39.8 us -> 159 us
  waiting for transfers between devices: 184 us -> 98.1 us
  matrix products: 71.6 us -> 0 us
  other arithmetic: 61.9 us -> 3.66 us
  local copies, waits for them, and re-layouts: 53.9 us -> 20.8 us
  starting transfers between devices: 101 us -> 68.6 us
    pallas_call x4 -> x21, Pallas kernels: 39.8 us -> 159 us  [kernel_call(): pl.pallas_call(kernel, out_shape=outs, in_specs=in_specs or [everywhere]...]
    ppermute x61 -> x40, waiting for transfers between devices: 184 us -> 93.7 us  [swap(): return lax.ppermute(value, 'dp', [(i, i ^ mask) for i in range(size)])]
    dot_general x25 -> x0, matrix products: 71.6 us -> none  [the longest x24 63.8 us: dot(): lax.dot_general(left, right, (dims, ((), ())), preferred_element_type=F32)]
    ppermute x61 -> x40, starting transfers between devices: 87.4 us -> 52.5 us  [swap(): return lax.ppermute(value, 'dp', [(i, i ^ mask) for i in range(size)])]
    concatenate x23 -> x1, other arithmetic: 19.6 us -> 0.68 us  [shards(): jnp.concatenate([norm_one[None], norm_two[None], norm_three[None], jnp.ze...]
    slice x32 -> x4, local copies, waits for them, and re-layouts: 15.9 us -> 1.74 us  [the longest x1 0.97 us: shards(): buckets[:, :TILE]]
    add x24 -> x6, other arithmetic: 13 us -> 0.29 us  [the longest x3 0.24 us: scatter_last(): total = total + value.astype(F32)]
    reduce_sum x6 -> x0, other arithmetic: 11.2 us -> none  [the longest x3 6.8 us: gain_grad(): return jnp.sum(grad * value * root, axis=0)]
  transfers between devices with their start and end apart: 72 -> 52, of which waited for: 25 -> 28; matrix products, arithmetic and copies ran while one was open for 32% -> 4% of each run, Pallas kernels for 8% -> 33%
where the time goes in v2:
time: 357 us; the launch traced here: 354 us
  Pallas kernels  159 us (45%)
  waiting for transfers between devices  98.1 us (27%)
  starting transfers between devices  68.6 us (19%)
  local copies, waits for them, and re-layouts  20.8 us (6%)
  other arithmetic  3.66 us (1%)
    pallas_call x21, Pallas kernels, kernel_call(): pl.pallas_call(kernel, out_shape=outs, in_specs=in_specs or [everywhere]...  159 us
    ppermute x40, waiting for transfers between devices, swap(): return lax.ppermute(value, 'dp', [(i, i ^ mask) for i in range(size)])  93.7 us
    ppermute x40, starting transfers between devices, swap(): return lax.ppermute(value, 'dp', [(i, i ^ mask) for i in range(size)])  52.5 us
    all_to_all x1, starting transfers between devices, shards(): own = lax.all_to_all(sent, 'dp', split_axis=0, concat_axis=0, tiled=True)  10.3 us
    unnamed x116, local copies, waits for them, and re-layouts  8.81 us
  transfers between devices with their start and end apart: 52, of which 28 were waited for; matrix products, arithmetic and copies ran while one was open for 4% of the time, Pallas kernels for 33%

profile of v2, /device:TPU:0, one launch (start us, length us, event | category | flops | bytes accessed | tf_op | source)
XLA Modules:
  0.0 353.8 jit_solution(9938589879786988030)
XLA Ops:
  0.7 2.0 shard_map.350.refs_0_
  2.7 3.0 collective-permute-start
  5.7 2.6 collective-permute-start.1
  10.2 1.9 shard_map.351.refs_0_
  13.4 6.3 %shard_map.349 = (f32[512,768]{1,0:T(8,128)}, bf16[512,768]{1,0:T(8,128)(2,1)}, f32[8,768]{1,0:T(8,128)}, bf16[768,768]{1,0:T(8,128)(2,1)}, bf16[512,768]{1,0:T(8,128)(2,1)}) custom-call(bf16[512,768]{1,0:T(8,128)(2,1)} %bitcast.32, bf16[512,768]{1,0:T(8,128)(2,1)} %bitcast.33, f32[8,768]{1,0:T(8,128)} %maximum_maximum_fusion.gains_ref, ...), custom_call_target="tpu_custom_call" | custom-call | flops 2000000000 | bytes 1 | tf_op jit(solution)/shard_map/pallas_call | solution.py:153
  19.7 9.7 %collective-permute-done.1.refs_2_ = bf16[48,3072]{1,0:T(8,128)(2,1)S(1)} collective-permute-done((bf16[48,3072]{1,0:T(8,128)(2,1)}, bf16[48,3072]{1,0:T(8,128)(2,1)S(1)}, u32[]{:S(2)}, u32[]{:S(2)}) %collective-permute-start.1) | collective-permute-done | bytes 294944 | tf_op jit(solution)/shard_map/ppermute | solution.py:53
  30.2 2.3 shard_map.352
  32.6 10.3 %all-to-all-start = ((bf16[16,64,384]{2,1,0:T(8,128)(2,1)}), bf16[16,64,384]{2,1,0:T(8,128)(2,1)S(1)}, u32[]{:S(2)}, u32[]{:S(2)}) async-start(bf16[16,64,384]{2,1,0:T(8,128)(2,1)} %gather_fusion), calls=%async_computation | async-start | bytes 1572864 | tf_op jit(solution)/shard_map/all_to_all | solution.py:1096
  47.2 2.1 collective-permute-start.3
  52.9 13.0 %collective-permute-done.3.left_in_ref = bf16[192,1536]{1,0:T(8,128)(2,1)S(1)} collective-permute-done((bf16[192,1536]{1,0:T(8,128)(2,1)S(1)}, bf16[192,1536]{1,0:T(8,128)(2,1)S(1)}, u32[]{:S(2)}, u32[]{:S(2)}) %collective-permute-start.3) | collective-permute-done | bytes 589856 | tf_op jit(solution)/shard_map/ppermute | solution.py:53
  66.0 2.2 collective-permute-done.4.right_in_ref
  69.3 3.1 shard_map.353
  78.6 8.7 %collective-permute-done.7.refs_1_ = bf16[48,3072]{1,0:T(8,128)(2,1)S(1)} collective-permute-done((bf16[48,3072]{1,0:T(8,128)(2,1)S(1)}, bf16[48,3072]{1,0:T(8,128)(2,1)S(1)}, u32[]{:S(2)}, u32[]{:S(2)}) %collective-permute-start.7) | collective-permute-done | bytes 294944 | tf_op jit(solution)/shard_map/ppermute | solution.py:53
  87.4 11.3 %collective-permute-done.8.refs_2_ = bf16[48,3072]{1,0:T(8,128)(2,1)S(1)} collective-permute-done((bf16[48,3072]{1,0:T(8,128)(2,1)S(1)}, bf16[48,3072]{1,0:T(8,128)(2,1)S(1)}, u32[]{:S(2)}, u32[]{:S(2)}) %collective-permute-start.8) | collective-permute-done | bytes 294944 | tf_op jit(solution)/shard_map/ppermute | solution.py:53
  100.9 2.3 shard_map.354
  104.4 12.7 %shard_map.355 = (bf16[512,1152]{1,0:T(8,128)(2,1)}, bf16[512,384]{1,0:T(8,128)(2,1)}, f32[3,8,512]{2,1,0:T(8,128)}, f32[512,768]{1,0:T(8,128)}) custom-call(bf16[512,768]{1,0:T(8,128)(2,1)} %get-tuple-element.270.normed_ref, f32[3,8,512]{2,1,0:T(8,128)} %pad.4.bias_ref, bf16[384,1536]{1,0:T(8,128)(2,1)} %get-tuple-element.272.refs_0_, ...), custom_call_target="tpu_custom_call" | custom-call | flops 12000000000 | bytes 1 | tf_op jit(solution)/shard_map/pallas_call | solution.py:153
  117.1 2.1 collective-permute-done.10.left_in_ref
  120.3 3.3 shard_map.356
  125.8 7.7 %shard_map.357 = (bf16[1024,768]{1,0:T(8,128)(2,1)}, bf16[1024,768]{1,0:T(8,128)(2,1)}) custom-call(s32[1]{0:T(128)} %bitcast.9.core_ref, bf16[1024,384]{1,0:T(8,128)(2,1)} %bitcast.27, bf16[1024,384]{1,0:T(8,128)(2,1)} %copy-done.24, bf16[768,768]{1,0:T(8,128)(2,1)} %get-tuple-element.291.order_ref, bf16[384,1536]{1,0:T(8,128)(2,1)} %get-tuple-element.292.refs_0_, ...), custom_call_target="tpu_custom_call" | custom-call | flops 8000000000 | bytes 1 | tf_op jit(solution)/shard_map/pallas_call | solution.py:153
  134.7 16.5 %shard_map.358 = (f32[512,768]{1,0:T(8,128)}, bf16[512,768]{1,0:T(8,128)(2,1)}, bf16[512,384]{1,0:T(8,128)(2,1)}, bf16[512,384]{1,0:T(8,128)(2,1)}, f32[3,8,512]...) custom-call(f32[512,768]{1,0:T(8,128)} %get-tuple-element.229.tokens_ref, ...), custom_call_target="tpu_custom_call" | custom-call | flops 16000000000 | bytes 1 | tf_op jit(solution)/shard_map/pallas_call | solution.py:153
  155.7 20.0 %shard_map.359 = (f32[512,768]{1,0:T(8,128)}, f32[512,768]{1,0:T(8,128)}, f32[512,768]{1,0:T(8,128)}, bf16[384,1536]{1,0:T(8,128)(2,1)}, bf16[384,1536]{1,0:T(8,...) custom-call(f32[512,768]{1,0:T(8,128)} %get-tuple-element.296.before_ref.h_ref, ...), custom_call_target="tpu_custom_call" | custom-call | flops 20000000000 | bytes 1 | tf_op jit(solution)/shard_map/pallas_call | solution.py:153
  180.6 18.1 %shard_map.360 = (f32[512,768]{1,0:T(8,128)}, bf16[512,768]{1,0:T(8,128)(2,1)}, bf16[512,384]{1,0:T(8,128)(2,1)}, bf16[1024,768]{1,0:T(8,128)(2,1)}, f32[512,768]{1,0:T(8,128)}, /*index=5*/f32[8,768]{1,0:T(8,128)}) custom-call(bf16[512,768]{1,0:T(8,128)(2,1)} %get-tuple-element.299.cot_ref, f32[512,768]{1,0:T(8,128)} %get-tuple-element.306.partial_ref, ...), custom_call_target="tpu_custom_call" | custom-call | flops 17999998976 | bytes 1 | tf_op jit(solution)/shard_map/pallas_call | solution.py:153
  198.7 5.7 %collective-permute-done.18.left_in_ref = bf16[384,1536]{1,0:T(8,128)(2,1)S(1)} collective-permute-done((bf16[384,1536]{1,0:T(8,128)(2,1)}, bf16[384,1536]{1,0:T(8,128)(2,1)S(1)}, u32[]{:S(2)}, u32[]{:S(2)}) %collective-permute-start.18) | collective-permute-done | bytes 1179680 | tf_op jit(solution)/shard_map/ppermute | solution.py:53
  206.6 4.4 %shard_map.361 = (f32[192,3072]{1,0:T(8,128)}, bf16[192,1536]{1,0:T(8,128)(2,1)}, bf16[192,1536]{1,0:T(8,128)(2,1)}) custom-call(bf16[384,1536]{1,0:T(8,128)(2,1)} %get-tuple-element.314.left_ref, bf16[384,1536]{1,0:T(8,128)(2,1)} %get-tuple-element.315.right_ref, bf16[384,1536]{1,0:T(8,128)(2,1)} %copy-done.21, bf16[384,1536]{1,0:T(8,128)(2,1)} %copy-done.22), custom_call_target="tpu_custom_call" | custom-call | flops 2000000000 | bytes 1 | tf_op jit(solution)/shard_map/pallas_call | solution.py:153
  212.2 12.4 %shard_map.362 = (bf16[1024,384]{1,0:T(8,128)(2,1)}, bf16[1024,384]{1,0:T(8,128)(2,1)}, bf16[384,768]{1,0:T(8,128)(2,1)}, bf16[384,768]{1,0:T(8,128)(2,1)}, bf16...) custom-call(s32[1]{0:T(128)} %bitcast.9.core_ref, bf16[512,768]{1,0:T(8,128)(2,1)} %get-tuple-element.328.normed_ref, ...), custom_call_target="tpu_custom_call" | custom-call | flops 12000000000 | bytes 1 | tf_op jit(solution)/shard_map/pallas_call | solution.py:153
  224.7 2.3 collective-permute-done.21.left_in_ref
  228.0 3.3 shard_map.363
  231.3 3.3 collective-permute-start.24
  237.3 8.5 %collective-permute-done.24 = bf16[48,3072]{1,0:T(8,128)(2,1)S(1)} collective-permute-done((bf16[48,3072]{1,0:T(8,128)(2,1)}, bf16[48,3072]{1,0:T(8,128)(2,1)S(1)}, u32[]{:S(2)}, u32[]{:S(2)}) %collective-permute-start.24) | collective-permute-done | bytes 294944 | tf_op jit(solution)/shard_map/ppermute | solution.py:53
  246.8 21.7 %shard_map.364 = (f32[512,768]{1,0:T(8,128)}, f32[512,768]{1,0:T(8,128)}, f32[16,768]{1,0:T(8,128)}, bf16[384,768]{1,0:T(8,128)(2,1)}, bf16[384,768]{1,0:T(8,128...) custom-call(s32[1]{0:T(128)} %bitcast.9.core_ref, f32[512,768]{1,0:T(8,128)} %get-tuple-element.365.g_in_ref, ...), custom_call_target="tpu_custom_call" | custom-call | flops 22000001024 | bytes 1 | tf_op jit(solution)/shard_map/pallas_call | solution.py:153
  271.9 4.4 %all-to-all-start.1 = ((bf16[16,64,384]{2,1,0:T(8,128)(2,1)}), bf16[16,64,384]{2,1,0:T(8,128)(2,1)S(1)}, u32[]{:S(2)}, u32[]{:S(2)}) async-start(bf16[16,64,384]{2,1,0:T(8,128)(2,1)} %bitcast.12), calls=%async_computation.1 | async-start | bytes 1572864 | tf_op jit(solution)/shard_map/all_to_all | solution.py:1167
  276.4 3.0 shard_map.365
  279.4 2.0 collective-permute-start.32
  283.7 10.0 %shard_map.366 = (f32[512,768]{1,0:T(8,128)}, bf16[512,768]{1,0:T(8,128)(2,1)}) custom-call(f32[512,768]{1,0:T(8,128)} %get-tuple-element.389.g_ref, f32[512,768]{1,0:T(8,128)} %get-tuple-element.390.partial_ref, f32[512,768]{1,0:T(8,128)} %collective-permute-done.34.peer_ref, f32[512,768]{1,0:T(8,128)} %get-tuple-element.229.tokens_ref, ...), custom_call_target="tpu_custom_call" | custom-call | flops 10000000000 | bytes 1 | tf_op jit(solution)/shard_map/pallas_call | solution.py:153
  293.6 3.7 %collective-permute-done.33.right_in_ref = bf16[192,768]{1,0:T(8,128)(2,1)S(1)} collective-permute-done((bf16[192,768]{1,0:T(8,128)(2,1)}, bf16[192,768]{1,0:T(8,128)(2,1)S(1)}, u32[]{:S(2)}, u32[]{:S(2)}) %collective-permute-start.33) | collective-permute-done | bytes 294944 | tf_op jit(solution)/shard_map/ppermute | solution.py:53
  297.3 11.2 %collective-permute-done.30.left_in_ref = bf16[384,768]{1,0:T(8,128)(2,1)S(1)} collective-permute-done((bf16[384,768]{1,0:T(8,128)(2,1)S(1)}, bf16[384,768]{1,0:T(8,128)(2,1)S(1)}, u32[]{:S(2)}, u32[]{:S(2)}) %collective-permute-start.30) | collective-permute-done | bytes 589856 | tf_op jit(solution)/shard_map/ppermute | solution.py:53
  308.6 2.7 shard_map.368
  311.3 3.0 shard_map.367
  316.1 1.6 collective-permute-start.47
  323.6 2.3 shard_map.369
  327.2 2.2 collective-permute-done.48
  329.5 3.3 collective-permute-start.44
  333.6 1.6 collective-permute-start.46
  335.3 1.7 collective-permute-start.40
  340.5 1.7 collective-permute-start.42
  342.3 1.6 collective-permute-start.43
  343.9 4.6 %collective-permute-done.45 = bf16[48,1536]{1,0:T(8,128)(2,1)S(1)} collective-permute-done((bf16[48,1536]{1,0:T(8,128)(2,1)}, bf16[48,1536]{1,0:T(8,128)(2,1)S(1)}, u32[]{:S(2)}, u32[]{:S(2)}) %collective-permute-start.45) | collective-permute-done | bytes 147488 | tf_op jit(solution)/shard_map/ppermute | solution.py:53
  349.3 2.9 collective-permute-done.42
  (238 shorter events, 63.6 us)
Async XLA Ops:
  2.7 17.0 %collective-permute-start = (bf16[48,3072]{1,0:T(8,128)(2,1)}, bf16[48,3072]{1,0:T(8,128)(2,1)S(1)}, u32[]{:S(2)}, u32[]{:S(2)}) collective-permute-start(bf16[48,3072]{1,0:T(8,128)(2,1)} %shard_map.350.refs_0_), channel_id=1, source_target_pairs={{0,8},{2,10},{4,12},{6,14},{8,0},{10,2},{12,4},{14,6},{16,24},{18,... | collective-permute-start | bytes 884744 | tf_op jit(solution)/shard_map/ppermute | solution.py:53
  5.7 23.7 %collective-permute-start.1 = (bf16[48,3072]{1,0:T(8,128)(2,1)}, bf16[48,3072]{1,0:T(8,128)(2,1)S(1)}, u32[]{:S(2)}, u32[]{:S(2)}) collective-permute-start(bf16[48,3072]{1,0:T(8,128)(2,1)} %shard_map.350.refs_0_), channel_id=1, source_target_pairs={{0,16},{2,18},{4,20},{6,22},{8,24},{10,26},{12,28},{14,30},{16,0},... | collective-permute-start | bytes 884744 | tf_op jit(solution)/shard_map/ppermute | solution.py:53
  8.3 21.1 %collective-permute-start.2 = (bf16[48,3072]{1,0:T(8,128)(2,1)}, bf16[48,3072]{1,0:T(8,128)(2,1)S(1)}, u32[]{:S(2)}, u32[]{:S(2)}) collective-permute-start(bf16[48,3072]{1,0:T(8,128)(2,1)} %shard_map.350.refs_0_), channel_id=1, source_target_pairs={{0,24},{2,26},{4,28},{6,30},{8,16},{10,18},{12,20},{14,22},{16,8},... | collective-permute-start | bytes 884744 | tf_op jit(solution)/shard_map/ppermute | solution.py:53
  32.6 35.6 %all-to-all-start = ((bf16[16,64,384]{2,1,0:T(8,128)(2,1)}), bf16[16,64,384]{2,1,0:T(8,128)(2,1)S(1)}, u32[]{:S(2)}, u32[]{:S(2)}) async-start(bf16[16,64,384]{2,1,0:T(8,128)(2,1)} %gather_fusion), calls=%async_computation | async-start | bytes 1572864 | tf_op jit(solution)/shard_map/all_to_all | solution.py:1096
  47.2 18.8 %collective-permute-start.3 = (bf16[192,1536]{1,0:T(8,128)(2,1)S(1)}, bf16[192,1536]{1,0:T(8,128)(2,1)S(1)}, u32[]{:S(2)}, u32[]{:S(2)}) collective-permute-start(bf16[192,1536]{1,0:T(8,128)(2,1)S(1)} %copy-done.33), channel_id=1, source_target_pairs={{0,4},{2,6},{4,0},{6,2},{8,12},{10,14},{12,8},{14,10},{16,20},{18,... | collective-permute-start | bytes 1769480 | tf_op jit(solution)/shard_map/ppermute | solution.py:53
  49.3 18.9 %collective-permute-start.4 = (bf16[192,1536]{1,0:T(8,128)(2,1)S(1)}, bf16[192,1536]{1,0:T(8,128)(2,1)}, u32[]{:S(2)}, u32[]{:S(2)}) collective-permute-start(bf16[192,1536]{1,0:T(8,128)(2,1)S(1)} %copy-done.34), channel_id=1, source_target_pairs={{0,2},{2,0},{4,6},{6,4},{8,10},{10,8},{12,14},{14,12},{16,18},{18,... | collective-permute-start | bytes 1769480 | tf_op jit(solution)/shard_map/ppermute | solution.py:53
  72.4 26.9 %collective-permute-start.5 = (bf16[384,1536]{1,0:T(8,128)(2,1)}, bf16[384,1536]{1,0:T(8,128)(2,1)S(1)}, u32[]{:S(2)}, u32[]{:S(2)}) collective-permute-start(bf16[384,1536]{1,0:T(8,128)(2,1)} %get-tuple-element.272.refs_0_), channel_id=1, source_target_pairs={{0,2},{2,0},{4,6},{6,4},{8,10},{10,8},{12,14},{14,12},{16,18},{18,... | collective-permute-start | bytes 3538952 | tf_op jit(solution)/shard_map/ppermute | solution.py:53
  73.8 27.1 %collective-permute-start.6 = (bf16[384,1536]{1,0:T(8,128)(2,1)}, bf16[384,1536]{1,0:T(8,128)(2,1)}, u32[]{:S(2)}, u32[]{:S(2)}) collective-permute-start(bf16[384,1536]{1,0:T(8,128)(2,1)} %get-tuple-element.292.refs_0_), channel_id=1, source_target_pairs={{0,4},{2,6},{4,0},{6,2},{8,12},{10,14},{12,8},{14,10},{16,20},{18,... | collective-permute-start | bytes 3538952 | tf_op jit(solution)/shard_map/ppermute | solution.py:53
  74.2 13.1 %collective-permute-start.7 = (bf16[48,3072]{1,0:T(8,128)(2,1)S(1)}, bf16[48,3072]{1,0:T(8,128)(2,1)S(1)}, u32[]{:S(2)}, u32[]{:S(2)}) collective-permute-start(bf16[48,3072]{1,0:T(8,128)(2,1)S(1)} %copy-done.42), channel_id=1, source_target_pairs={{0,8},{2,10},{4,12},{6,14},{8,0},{10,2},{12,4},{14,6},{16,24},{18,... | collective-permute-start | bytes 884744 | tf_op jit(solution)/shard_map/ppermute | solution.py:53
  75.5 23.2 %collective-permute-start.8 = (bf16[48,3072]{1,0:T(8,128)(2,1)S(1)}, bf16[48,3072]{1,0:T(8,128)(2,1)S(1)}, u32[]{:S(2)}, u32[]{:S(2)}) collective-permute-start(bf16[48,3072]{1,0:T(8,128)(2,1)S(1)} %copy-done.42), channel_id=1, source_target_pairs={{0,16},{2,18},{4,20},{6,22},{8,24},{10,26},{12,28},{14,30},{16,0},... | collective-permute-start | bytes 884744 | tf_op jit(solution)/shard_map/ppermute | solution.py:53
  77.0 21.7 %collective-permute-start.9 = (bf16[48,3072]{1,0:T(8,128)(2,1)S(1)}, bf16[48,3072]{1,0:T(8,128)(2,1)S(1)}, u32[]{:S(2)}, u32[]{:S(2)}) collective-permute-start(bf16[48,3072]{1,0:T(8,128)(2,1)S(1)} %copy-done.42), channel_id=1, source_target_pairs={{0,24},{2,26},{4,28},{6,30},{8,16},{10,18},{12,20},{14,22},{16,8},... | collective-permute-start | bytes 884744 | tf_op jit(solution)/shard_map/ppermute | solution.py:53
  103.2 16.2 %collective-permute-start.12 = (bf16[1024,384]{1,0:T(8,128)(2,1)S(1)}, bf16[1024,384]{1,0:T(8,128)(2,1)S(1)}, u32[]{:S(2)}, u32[]{:S(2)}) collective-permute-start(bf16[1024,384]{1,0:T(8,128)(2,1)S(1)} %bitcast.26), channel_id=1, source_target_pairs={{0,1},{1,0},{2,3},{3,2},{4,5},{5,4},{6,7},{7,6},{8,9},{9,8},{10,11... | collective-permute-start | bytes 2359304 | tf_op jit(solution)/shard_map/ppermute | solution.py:57
  103.3 16.0 %collective-permute-start.10 = (bf16[192,1536]{1,0:T(8,128)(2,1)}, bf16[192,1536]{1,0:T(8,128)(2,1)S(1)}, u32[]{:S(2)}, u32[]{:S(2)}) collective-permute-start(bf16[192,1536]{1,0:T(8,128)(2,1)} %get-tuple-element.279.left_ref), channel_id=1, source_target_pairs={{0,4},{2,6},{4,0},{6,2},{8,12},{10,14},{12,8},{14,10},{16,20},{18,... | collective-permute-start | bytes 1769480 | tf_op jit(solution)/shard_map/ppermute | solution.py:53
  103.8 15.6 %collective-permute-start.11 = (bf16[192,1536]{1,0:T(8,128)(2,1)}, bf16[192,1536]{1,0:T(8,128)(2,1)S(1)}, u32[]{:S(2)}, u32[]{:S(2)}) collective-permute-start(bf16[192,1536]{1,0:T(8,128)(2,1)} %get-tuple-element.281.right_ref), channel_id=1, source_target_pairs={{0,2},{2,0},{4,6},{6,4},{8,10},{10,8},{12,14},{14,12},{16,18},{18,... | collective-permute-start | bytes 1769480 | tf_op jit(solution)/shard_map/ppermute | solution.py:53
  123.6 9.9 %collective-permute-start.13 = (f32[512,768]{1,0:T(8,128)S(1)}, f32[512,768]{1,0:T(8,128)S(1)}, u32[]{:S(2)}, u32[]{:S(2)}) collective-permute-start(f32[512,768]{1,0:T(8,128)S(1)} %copy-done.15), channel_id=1, source_target_pairs={{0,1},{1,0},{2,3},{3,2},{4,5},{5,4},{6,7},{7,6},{8,9},{9,8},{10,11... | collective-permute-start | bytes 4718600 | tf_op jit(solution)/shard_map/ppermute | solution.py:57
  123.6 28.6 %collective-permute-start.16 = (bf16[384,1536]{1,0:T(8,128)(2,1)}, bf16[384,1536]{1,0:T(8,128)(2,1)S(1)}, u32[]{:S(2)}, u32[]{:S(2)}) collective-permute-start(bf16[384,1536]{1,0:T(8,128)(2,1)} %get-tuple-element.300.refs_0_), channel_id=1, source_target_pairs={{0,2},{2,0},{4,6},{6,4},{8,10},{10,8},{12,14},{14,12},{16,18},{18,... | collective-permute-start | bytes 3538952 | tf_op jit(solution)/shard_map/ppermute | solution.py:53
  124.2 28.2 %collective-permute-start.17 = (bf16[384,1536]{1,0:T(8,128)(2,1)}, bf16[384,1536]{1,0:T(8,128)(2,1)S(1)}, u32[]{:S(2)}, u32[]{:S(2)}) collective-permute-start(bf16[384,1536]{1,0:T(8,128)(2,1)} %get-tuple-element.301.refs_2_), channel_id=1, source_target_pairs={{0,4},{2,6},{4,0},{6,2},{8,12},{10,14},{12,8},{14,10},{16,20},{18,... | collective-permute-start | bytes 3538952 | tf_op jit(solution)/shard_map/ppermute | solution.py:53
  175.9 28.5 %collective-permute-start.18 = (bf16[384,1536]{1,0:T(8,128)(2,1)}, bf16[384,1536]{1,0:T(8,128)(2,1)S(1)}, u32[]{:S(2)}, u32[]{:S(2)}) collective-permute-start(bf16[384,1536]{1,0:T(8,128)(2,1)} %get-tuple-element.304), channel_id=1, source_target_pairs={{0,2},{2,0},{4,6},{6,4},{8,10},{10,8},{12,14},{14,12},{16,18},{18,... | collective-permute-start | bytes 3538952 | tf_op jit(solution)/shard_map/ppermute | solution.py:53
  177.4 28.2 %collective-permute-start.19 = (bf16[384,1536]{1,0:T(8,128)(2,1)}, bf16[384,1536]{1,0:T(8,128)(2,1)S(1)}, u32[]{:S(2)}, u32[]{:S(2)}) collective-permute-start(bf16[384,1536]{1,0:T(8,128)(2,1)} %get-tuple-element.305), channel_id=1, source_target_pairs={{0,4},{2,6},{4,0},{6,2},{8,12},{10,14},{12,8},{14,10},{16,20},{18,... | collective-permute-start | bytes 3538952 | tf_op jit(solution)/shard_map/ppermute | solution.py:53
  211.0 16.2 %collective-permute-start.23 = (f32[512,768]{1,0:T(8,128)S(1)}, f32[512,768]{1,0:T(8,128)S(1)}, u32[]{:S(2)}, u32[]{:S(2)}) collective-permute-start(f32[512,768]{1,0:T(8,128)S(1)} %copy-done.13), channel_id=1, source_target_pairs={{0,1},{1,0},{2,3},{3,2},{4,5},{5,4},{6,7},{7,6},{8,9},{9,8},{10,11... | collective-permute-start | bytes 4718600 | tf_op jit(solution)/shard_map/ppermute | solution.py:57
  211.0 16.0 %collective-permute-start.21 = (bf16[192,1536]{1,0:T(8,128)(2,1)}, bf16[192,1536]{1,0:T(8,128)(2,1)S(1)}, u32[]{:S(2)}, u32[]{:S(2)}) collective-permute-start(bf16[192,1536]{1,0:T(8,128)(2,1)} %get-tuple-element.326), channel_id=1, source_target_pairs={{0,4},{2,6},{4,0},{6,2},{8,12},{10,14},{12,8},{14,10},{16,20},{18,... | collective-permute-start | bytes 1769480 | tf_op jit(solution)/shard_map/ppermute | solution.py:53
  211.6 15.6 %collective-permute-start.22 = (bf16[192,1536]{1,0:T(8,128)(2,1)}, bf16[192,1536]{1,0:T(8,128)(2,1)S(1)}, u32[]{:S(2)}, u32[]{:S(2)}) collective-permute-start(bf16[192,1536]{1,0:T(8,128)(2,1)} %get-tuple-element.327), channel_id=1, source_target_pairs={{0,2},{2,0},{4,6},{6,4},{8,10},{10,8},{12,14},{14,12},{16,18},{18,... | collective-permute-start | bytes 1769480 | tf_op jit(solution)/shard_map/ppermute | solution.py:53
  231.3 14.5 %collective-permute-start.24 = (bf16[48,3072]{1,0:T(8,128)(2,1)}, bf16[48,3072]{1,0:T(8,128)(2,1)S(1)}, u32[]{:S(2)}, u32[]{:S(2)}) collective-permute-start(bf16[48,3072]{1,0:T(8,128)(2,1)} %get-tuple-element.356), channel_id=1, source_target_pairs={{0,8},{2,10},{4,12},{6,14},{8,0},{10,2},{12,4},{14,6},{16,24},{18,... | collective-permute-start | bytes 884744 | tf_op jit(solution)/shard_map/ppermute | solution.py:53
  234.6 34.1 %collective-permute-start.29 = (bf16[1024,384]{1,0:T(8,128)(2,1)S(1)}, bf16[1024,384]{1,0:T(8,128)(2,1)S(1)}, u32[]{:S(2)}, u32[]{:S(2)}) collective-permute-start(bf16[1024,384]{1,0:T(8,128)(2,1)S(1)} %copy-done.23), channel_id=1, source_target_pairs={{0,1},{1,0},{2,3},{3,2},{4,5},{5,4},{6,7},{7,6},{8,9},{9,8},{10,11... | collective-permute-start | bytes 2359304 | tf_op jit(solution)/shard_map/ppermute | solution.py:57
  234.6 34.0 %collective-permute-start.27 = (bf16[384,768]{1,0:T(8,128)(2,1)S(1)}, bf16[384,768]{1,0:T(8,128)(2,1)S(1)}, u32[]{:S(2)}, u32[]{:S(2)}) collective-permute-start(bf16[384,768]{1,0:T(8,128)(2,1)S(1)} %copy-done.30), channel_id=1, source_target_pairs={{0,2},{2,0},{4,6},{6,4},{8,10},{10,8},{12,14},{14,12},{16,18},{18,... | collective-permute-start | bytes 1769480 | tf_op jit(solution)/shard_map/ppermute | solution.py:53
  235.4 33.3 %collective-permute-start.28 = (bf16[384,768]{1,0:T(8,128)(2,1)S(1)}, bf16[384,768]{1,0:T(8,128)(2,1)S(1)}, u32[]{:S(2)}, u32[]{:S(2)}) collective-permute-start(bf16[384,768]{1,0:T(8,128)(2,1)S(1)} %copy-done.29), channel_id=1, source_target_pairs={{0,4},{2,6},{4,0},{6,2},{8,12},{10,14},{12,8},{14,10},{16,20},{18,... | collective-permute-start | bytes 1769480 | tf_op jit(solution)/shard_map/ppermute | solution.py:53
  235.9 32.7 %collective-permute-start.25 = (bf16[48,3072]{1,0:T(8,128)(2,1)}, bf16[48,3072]{1,0:T(8,128)(2,1)S(1)}, u32[]{:S(2)}, u32[]{:S(2)}) collective-permute-start(bf16[48,3072]{1,0:T(8,128)(2,1)} %get-tuple-element.357), channel_id=1, source_target_pairs={{0,16},{2,18},{4,20},{6,22},{8,24},{10,26},{12,28},{14,30},{16,0},... | collective-permute-start | bytes 884744 | tf_op jit(solution)/shard_map/ppermute | solution.py:53
  245.8 22.9 %collective-permute-start.26 = (bf16[48,3072]{1,0:T(8,128)(2,1)}, bf16[48,3072]{1,0:T(8,128)(2,1)S(1)}, u32[]{:S(2)}, u32[]{:S(2)}) collective-permute-start(bf16[48,3072]{1,0:T(8,128)(2,1)} %get-tuple-element.358), channel_id=1, source_target_pairs={{0,24},{2,26},{4,28},{6,30},{8,16},{10,18},{12,20},{14,22},{16,8},... | collective-permute-start | bytes 884744 | tf_op jit(solution)/shard_map/ppermute | solution.py:53
  268.6 15.0 %collective-permute-start.35 = (f32[512,768]{1,0:T(8,128)}, f32[512,768]{1,0:T(8,128)}, u32[]{:S(2)}, u32[]{:S(2)}) collective-permute-start(f32[512,768]{1,0:T(8,128)} %get-tuple-element.391.down_ref), channel_id=1, source_target_pairs={{0,1},{1,0},{2,3},{3,2},{4,5},{5,4},{6,7},{7,6},{8,9},{9,8},{10,11... | collective-permute-start | bytes 4718600 | tf_op jit(solution)/shard_map/ppermute | solution.py:57
  269.7 14.0 %collective-permute-start.34 = (f32[512,768]{1,0:T(8,128)}, f32[512,768]{1,0:T(8,128)}, u32[]{:S(2)}, u32[]{:S(2)}) collective-permute-start(f32[512,768]{1,0:T(8,128)} %get-tuple-element.390.partial_ref), channel_id=1, source_target_pairs={{0,1},{1,0},{2,3},{3,2},{4,5},{5,4},{6,7},{7,6},{8,9},{9,8},{10,11... | collective-permute-start | bytes 4718600 | tf_op jit(solution)/shard_map/ppermute | solution.py:57
  271.9 42.4 %all-to-all-start.1 = ((bf16[16,64,384]{2,1,0:T(8,128)(2,1)}), bf16[16,64,384]{2,1,0:T(8,128)(2,1)S(1)}, u32[]{:S(2)}, u32[]{:S(2)}) async-start(bf16[16,64,384]{2,1,0:T(8,128)(2,1)} %bitcast.12), calls=%async_computation.1 | async-start | bytes 1572864 | tf_op jit(solution)/shard_map/all_to_all | solution.py:1167
  279.4 14.3 %collective-permute-start.32 = (bf16[192,768]{1,0:T(8,128)(2,1)}, bf16[192,768]{1,0:T(8,128)(2,1)S(1)}, u32[]{:S(2)}, u32[]{:S(2)}) collective-permute-start(bf16[192,768]{1,0:T(8,128)(2,1)} %get-tuple-element.387), channel_id=1, source_target_pairs={{0,4},{2,6},{4,0},{6,2},{8,12},{10,14},{12,8},{14,10},{16,20},{18,... | collective-permute-start | bytes 884744 | tf_op jit(solution)/shard_map/ppermute | solution.py:53
  281.4 15.9 %collective-permute-start.33 = (bf16[192,768]{1,0:T(8,128)(2,1)}, bf16[192,768]{1,0:T(8,128)(2,1)S(1)}, u32[]{:S(2)}, u32[]{:S(2)}) collective-permute-start(bf16[192,768]{1,0:T(8,128)(2,1)} %get-tuple-element.388), channel_id=1, source_target_pairs={{0,2},{2,0},{4,6},{6,4},{8,10},{10,8},{12,14},{14,12},{16,18},{18,... | collective-permute-start | bytes 884744 | tf_op jit(solution)/shard_map/ppermute | solution.py:53
  282.8 25.7 %collective-permute-start.30 = (bf16[384,768]{1,0:T(8,128)(2,1)S(1)}, bf16[384,768]{1,0:T(8,128)(2,1)S(1)}, u32[]{:S(2)}, u32[]{:S(2)}) collective-permute-start(bf16[384,768]{1,0:T(8,128)(2,1)S(1)} %copy-done.28), channel_id=1, source_target_pairs={{0,2},{2,0},{4,6},{6,4},{8,10},{10,8},{12,14},{14,12},{16,18},{18,... | collective-permute-start | bytes 1769480 | tf_op jit(solution)/shard_map/ppermute | solution.py:53
  283.6 25.0 %collective-permute-start.31 = (bf16[384,768]{1,0:T(8,128)(2,1)S(1)}, bf16[384,768]{1,0:T(8,128)(2,1)S(1)}, u32[]{:S(2)}, u32[]{:S(2)}) collective-permute-start(bf16[384,768]{1,0:T(8,128)(2,1)S(1)} %copy-done.27), channel_id=1, source_target_pairs={{0,4},{2,6},{4,0},{6,2},{8,12},{10,14},{12,8},{14,10},{16,20},{18,... | collective-permute-start | bytes 1769480 | tf_op jit(solution)/shard_map/ppermute | solution.py:53
  314.3 7.8 %collective-permute-start.36 = (bf16[192,768]{1,0:T(8,128)(2,1)}, bf16[192,768]{1,0:T(8,128)(2,1)S(1)}, u32[]{:S(2)}, u32[]{:S(2)}) collective-permute-start(bf16[192,768]{1,0:T(8,128)(2,1)} %get-tuple-element.417), channel_id=1, source_target_pairs={{0,4},{2,6},{4,0},{6,2},{8,12},{10,14},{12,8},{14,10},{16,20},{18,... | collective-permute-start | bytes 884744 | tf_op jit(solution)/shard_map/ppermute | solution.py:53
  314.8 7.9 %collective-permute-start.37 = (bf16[192,768]{1,0:T(8,128)(2,1)}, bf16[192,768]{1,0:T(8,128)(2,1)S(1)}, u32[]{:S(2)}, u32[]{:S(2)}) collective-permute-start(bf16[192,768]{1,0:T(8,128)(2,1)} %get-tuple-element.418), channel_id=1, source_target_pairs={{0,2},{2,0},{4,6},{6,4},{8,10},{10,8},{12,14},{14,12},{16,18},{18,... | collective-permute-start | bytes 884744 | tf_op jit(solution)/shard_map/ppermute | solution.py:53
  316.1 11.1 %collective-permute-start.47 = (bf16[48,1536]{1,0:T(8,128)(2,1)S(1)}, bf16[48,1536]{1,0:T(8,128)(2,1)S(1)}, u32[]{:S(2)}, u32[]{:S(2)}) collective-permute-start(bf16[48,1536]{1,0:T(8,128)(2,1)S(1)} %copy-done.55), channel_id=1, source_target_pairs={{0,8},{2,10},{4,12},{6,14},{8,0},{10,2},{12,4},{14,6},{16,24},{18,... | collective-permute-start | bytes 442376 | tf_op jit(solution)/shard_map/ppermute | solution.py:53
  317.7 11.7 %collective-permute-start.48 = (bf16[48,1536]{1,0:T(8,128)(2,1)S(1)}, bf16[48,1536]{1,0:T(8,128)(2,1)S(1)}, u32[]{:S(2)}, u32[]{:S(2)}) collective-permute-start(bf16[48,1536]{1,0:T(8,128)(2,1)S(1)} %copy-done.54), channel_id=1, source_target_pairs={{0,16},{2,18},{4,20},{6,22},{8,24},{10,26},{12,28},{14,30},{16,0},... | collective-permute-start | bytes 442376 | tf_op jit(solution)/shard_map/ppermute | solution.py:53
  320.2 9.2 %collective-permute-start.49 = (bf16[48,1536]{1,0:T(8,128)(2,1)S(1)}, bf16[48,1536]{1,0:T(8,128)(2,1)S(1)}, u32[]{:S(2)}, u32[]{:S(2)}) collective-permute-start(bf16[48,1536]{1,0:T(8,128)(2,1)S(1)} %copy-done.53), channel_id=1, source_target_pairs={{0,24},{2,26},{4,28},{6,30},{8,16},{10,18},{12,20},{14,22},{16,8},... | collective-permute-start | bytes 442376 | tf_op jit(solution)/shard_map/ppermute | solution.py:53
  325.9 9.4 %collective-permute-start.39 = (f32[16,768]{1,0:T(8,128)S(1)}, f32[16,768]{1,0:T(8,128)S(1)}, u32[]{:S(2)}, u32[]{:S(2)}) collective-permute-start(f32[16,768]{1,0:T(8,128)S(1)} %add.147), channel_id=1, source_target_pairs={{0,2},{2,0},{4,6},{6,4},{8,10},{10,8},{12,14},{14,12},{16,18},{18,... | collective-permute-start | bytes 147464 | tf_op jit(solution)/shard_map/ppermute | solution.py:53
  329.5 12.7 %collective-permute-start.44 = (bf16[48,1536]{1,0:T(8,128)(2,1)}, bf16[48,1536]{1,0:T(8,128)(2,1)S(1)}, u32[]{:S(2)}, u32[]{:S(2)}) collective-permute-start(bf16[48,1536]{1,0:T(8,128)(2,1)} %get-tuple-element.432), channel_id=1, source_target_pairs={{0,8},{2,10},{4,12},{6,14},{8,0},{10,2},{12,4},{14,6},{16,24},{18,... | collective-permute-start | bytes 442376 | tf_op jit(solution)/shard_map/ppermute | solution.py:53
  332.8 15.7 %collective-permute-start.45 = (bf16[48,1536]{1,0:T(8,128)(2,1)}, bf16[48,1536]{1,0:T(8,128)(2,1)S(1)}, u32[]{:S(2)}, u32[]{:S(2)}) collective-permute-start(bf16[48,1536]{1,0:T(8,128)(2,1)} %get-tuple-element.433), channel_id=1, source_target_pairs={{0,16},{2,18},{4,20},{6,22},{8,24},{10,26},{12,28},{14,30},{16,0},... | collective-permute-start | bytes 442376 | tf_op jit(solution)/shard_map/ppermute | solution.py:53
  333.6 14.9 %collective-permute-start.46 = (bf16[48,1536]{1,0:T(8,128)(2,1)}, bf16[48,1536]{1,0:T(8,128)(2,1)S(1)}, u32[]{:S(2)}, u32[]{:S(2)}) collective-permute-start(bf16[48,1536]{1,0:T(8,128)(2,1)} %get-tuple-element.434), channel_id=1, source_target_pairs={{0,24},{2,26},{4,28},{6,30},{8,16},{10,18},{12,20},{14,22},{16,8},... | collective-permute-start | bytes 442376 | tf_op jit(solution)/shard_map/ppermute | solution.py:53
  335.3 4.2 %collective-permute-start.40 = (f32[16,768]{1,0:T(8,128)S(1)}, f32[16,768]{1,0:T(8,128)S(1)}, u32[]{:S(2)}, u32[]{:S(2)}) collective-permute-start(f32[16,768]{1,0:T(8,128)S(1)} %add.149), channel_id=1, source_target_pairs={{0,4},{2,6},{4,0},{6,2},{8,12},{10,14},{12,8},{14,10},{16,20},{18,... | collective-permute-start | bytes 147464 | tf_op jit(solution)/shard_map/ppermute | solution.py:53
  339.4 9.9 %collective-permute-start.41 = (f32[16,768]{1,0:T(8,128)S(1)}, f32[16,768]{1,0:T(8,128)S(1)}, u32[]{:S(2)}, u32[]{:S(2)}) collective-permute-start(f32[16,768]{1,0:T(8,128)S(1)} %add.150), channel_id=1, source_target_pairs={{0,8},{2,10},{4,12},{6,14},{8,0},{10,2},{12,4},{14,6},{16,24},{18,... | collective-permute-start | bytes 147464 | tf_op jit(solution)/shard_map/ppermute | solution.py:53
  340.5 11.6 %collective-permute-start.42 = (f32[16,768]{1,0:T(8,128)S(1)}, f32[16,768]{1,0:T(8,128)S(1)}, u32[]{:S(2)}, u32[]{:S(2)}) collective-permute-start(f32[16,768]{1,0:T(8,128)S(1)} %add.150), channel_id=1, source_target_pairs={{0,16},{2,18},{4,20},{6,22},{8,24},{10,26},{12,28},{14,30},{16,0},... | collective-permute-start | bytes 147464 | tf_op jit(solution)/shard_map/ppermute | solution.py:53
  342.3 9.9 %collective-permute-start.43 = (f32[16,768]{1,0:T(8,128)S(1)}, f32[16,768]{1,0:T(8,128)S(1)}, u32[]{:S(2)}, u32[]{:S(2)}) collective-permute-start(f32[16,768]{1,0:T(8,128)S(1)} %add.150), channel_id=1, source_target_pairs={{0,24},{2,26},{4,28},{6,30},{8,16},{10,18},{12,20},{14,22},{16,8},... | collective-permute-start | bytes 147464 | tf_op jit(solution)/shard_map/ppermute | solution.py:53
  (62 other events, 424.3 us)

commit v3 on v2

--- a/solution.py
+++ b/solution.py
@@ -13,6 +13,7 @@
 KEYS = 1024
 TILE = 128
 WIDE = 256
+HIDDEN = 512
 ROWS = 64
 
 EPS = 1e-06
@@ -43,10 +44,9 @@
     return jax.ShapeDtypeStruct(shape, dtype)
 
 
-def thirds(value):
-    high = lax.reduce_precision(value, 8, 7)
-    middle = lax.reduce_precision(value - high, 8, 7)
-    return [part.astype(BF16) for part in (high, middle, value - high - middle)]
+def halves(value):
+    high = value.astype(BF16)
+    return high, (value - high.astype(F32)).astype(BF16)
 
 
 def swap(value, mask, size):
@@ -61,9 +61,12 @@
     return lax.optimization_barrier((values, others))[0]
 
 
-def gather_outer(shard, size):
+def gather_outer(shard, size, late=()):
     if size <= 16:
-        return [shard] + [swap(shard, mask, size) for mask in range(4, size, 4)]
+        held = after(shard, late)
+        ins = [swap(held if mask + 4 == size else shard, mask, size) for mask in range(4, size, 4)]
+        return [shard] + ins
+    shard = after(shard, late)
     mask = 4
     while mask < size:
         shard = jnp.concatenate([shard, swap(shard, mask, size)])
@@ -72,18 +75,14 @@
 
 
 def gather_first(pieces, size):
-    rows, columns = sum(piece.shape[0] for piece in pieces), pieces[0].shape[1]
-    left, right = kernel_call(
-        stack_kernel, pieces, [struct((rows, columns // 2), BF16)] * 2, []
-    )
-    return left, right
-
-
-def gather_second(state, size):
-    left = state[0]
-    return kernel_call(
-        join_kernel, list(state), [struct((2 * left.shape[0], left.shape[1]), BF16)] * 2, []
-    )
+    rows, half = sum(piece.shape[0] for piece in pieces), pieces[0].shape[1] // 2
+    return kernel_call(stack_kernel, list(pieces), [struct((rows, half), BF16)] * 2, [])
+
+
+def gather_second(state, size, time=2):
+    rows, half = state[0].shape
+    outs = [struct((2 * rows, half), BF16)] * 2
+    return kernel_call(join_kernel, list(state), outs, [], time=time)
 
 
 def send_first(halves, size):
@@ -101,17 +100,40 @@
     return left, right, swap(left_out, 1, size), swap(right_out, 2, size)
 
 
-def scatter_second_parts(state):
-    return add_call(scatter_second_kernel, state, 0.5)
+def scatter_second_parts(state, time=2):
+    left = state[0]
+    rows, half = left.shape[0] // 2, left.shape[1]
+    outs = kernel_call(
+        scatter_second_kernel,
+        list(state),
+        [struct((rows, half), BF16)] * 2,
+        [],
+        time=time,
+        grid=(1,),
+        in_specs=[pl.BlockSpec((rows, half), lambda i: (1, 0))] * 4,
+        out_specs=[pl.BlockSpec((rows, half), lambda i: (0, 0))] * 2,
+    )
+    return (*state, *outs)
 
 
 def scatter_second_send(parts, size):
-    keep, left_out, right_out = parts
-    return keep, swap(left_out, 2, size), swap(right_out, 1, size)
-
-
-def scatter_outer_parts(state):
-    return add_call(scatter_outer_kernel, state, 0.25)
+    *state, left_out, right_out = parts
+    return (*state, swap(left_out, 2, size), swap(right_out, 1, size))
+
+
+def scatter_outer_parts(state, *sides):
+    rows, half = state[-1].shape
+    ins = [value for side in sides for value in state[side::2]]
+    width = len(sides) * half
+    return kernel_call(
+        scatter_outer_kernel,
+        ins,
+        [struct((rows // 4, width), dtype) for dtype in (F32, BF16, BF16, BF16)],
+        [],
+        grid=(1,),
+        in_specs=[pl.BlockSpec((rows, half), lambda i: (0, 0))] * len(ins),
+        out_specs=[pl.BlockSpec((rows // 4, width), lambda i: (0, 0))] * 4,
+    )
 
 
 def scatter_outer_send(parts, size):
@@ -132,20 +154,6 @@
     for value in state[1:]:
         total = total + value.astype(F32)
     return total
-
-
-def sum_devices(value, size):
-    value = value + swap(value, 1, size)
-    value = value + swap(value, 2, size)
-    if size <= 16:
-        return functools.reduce(
-            lambda total, mask: total + swap(value, mask, size), range(4, size, 4), value
-        )
-    mask = 4
-    while mask < size:
-        value = value + swap(value, mask, size)
-        mask *= 2
-    return value
 
 
 def kernel_call(kernel, ins, outs, scratch, time=2, grid=None, in_specs=None, out_specs=None):
@@ -188,36 +196,22 @@
     right_out[count:, :] = right_in_ref[...]
 
 
-def scatter_second_kernel(left_ref, right_ref, left_in_ref, right_in_ref, keep_ref, *out_refs):
-    count, half = keep_ref.shape[0], left_ref.shape[1]
-    halves = ((left_ref, left_in_ref, out_refs[0]), (right_ref, right_in_ref, out_refs[1]))
-    for i, (own_ref, in_ref, out_ref) in enumerate(halves):
-        keep_ref[:, i * half : (i + 1) * half] = own_ref[:count, :].astype(F32) + in_ref[
-            :count, :
-        ].astype(F32)
-        out_ref[...] = (
-            own_ref[count:, :].astype(F32) + in_ref[count:, :].astype(F32)
-        ).astype(BF16)
-
-
-def scatter_outer_kernel(keep_ref, left_in_ref, right_in_ref, *out_refs):
-    count, half = out_refs[0].shape[0], left_in_ref.shape[1]
-    for k, out_ref in enumerate(out_refs):
-        rows = slice(k * count, (k + 1) * count)
-        for i, in_ref in enumerate((left_in_ref, right_in_ref)):
-            cols = slice(i * half, (i + 1) * half)
-            out_ref[:, cols] = (keep_ref[rows, cols] + in_ref[rows, :].astype(F32)).astype(
-                out_ref.dtype
-            )
-
-
-def add_call(kernel, ins, share):
-    rows, half = ins[-1].shape
-    if share == 0.5:
-        outs = [struct((rows // 2, 2 * half), F32)] + [struct((rows // 2, half), BF16)] * 2
-    else:
-        outs = [struct((rows // 4, 2 * half), dtype) for dtype in (F32, BF16, BF16, BF16)]
-    return kernel_call(kernel, list(ins), outs, [])
+def scatter_second_kernel(left_ref, right_ref, left_in_ref, right_in_ref, left_out, right_out):
+    left_out[...] = (left_ref[...].astype(F32) + left_in_ref[...].astype(F32)).astype(BF16)
+    right_out[...] = (right_ref[...].astype(F32) + right_in_ref[...].astype(F32)).astype(BF16)
+
+
+def scatter_outer_kernel(*refs):
+    *in_refs, keep_ref, first_ref, second_ref, third_ref = refs
+    count = keep_ref.shape[0]
+    for side in range(len(in_refs) // 3):
+        own_ref, in_ref, more_ref = in_refs[3 * side : 3 * side + 3]
+        half = own_ref.shape[1]
+        cols = slice(side * half, (side + 1) * half)
+        for k, out_ref in enumerate((keep_ref, first_ref, second_ref, third_ref)):
+            rows = slice(k * count, (k + 1) * count)
+            total = own_ref[rows, :].astype(F32) + in_ref[rows, :].astype(F32)
+            out_ref[:, cols] = (total + more_ref[rows, :].astype(F32)).astype(out_ref.dtype)
 
 
 def cast_kernel(*refs):
@@ -270,25 +264,35 @@
     return copies
 
 
-def deliver(grads_ref, out_refs, sems):
+def deliver(grads_ref, out_refs, sems, columns, first=0):
     left, left_out, right, right_out = out_refs
-    rows, cols = left.shape[0] // 2, left.shape[1]
-    moves = [
-        (left.at[:, :], 0, 2, 0),
-        (left_out.at[:, :], 2, 2, 0),
-        (right.at[:rows, :], 0, 1, 1),
-        (right.at[rows:, :], 2, 1, 1),
-        (right_out.at[:rows, :], 1, 1, 1),
-        (right_out.at[rows:, :], 3, 1, 1),
-    ]
+    rows, half = left.shape[0] // 2, left.shape[1]
+    side = columns.start // half
+    if side == 0:
+        moves = [(left, 0, 0, 2), (left_out, 0, 2, 2)]
+    else:
+        moves = [(right, 0, 0, 1), (right, 1, 2, 1), (right_out, 0, 1, 1), (right_out, 1, 3, 1)]
     copies = []
-    for i, (target, place, count, side) in enumerate(moves):
-        spot = grads_ref.at[
-            place * rows : (place + count) * rows, side * cols : (side + 1) * cols
-        ]
-        copies.append(pltpu.make_async_copy(spot, target, sems.at[i]))
+    for target, spot, place, count in moves:
+        copies.append(
+            pltpu.make_async_copy(
+                grads_ref.at[place * rows : (place + count) * rows, columns],
+                target.at[
+                    spot * rows : (spot + count) * rows,
+                    columns.start - side * half : columns.stop - side * half,
+                ],
+                sems.at[first + len(copies)],
+            )
+        )
     for copy in copies:
         copy.start()
+    return copies
+
+
+def deliver_all(grads_ref, out_refs, sems):
+    half = out_refs[0].shape[1]
+    copies = deliver(grads_ref, out_refs, sems, slice(0, half))
+    copies += deliver(grads_ref, out_refs, sems, slice(half, 2 * half), 2)
     for copy in copies:
         copy.wait()
 
@@ -310,16 +314,20 @@
 
 
 def rows_kernel(
-    tokens_ref, cot_ref, gains_ref, source_ref, tokens_out, cot_out, gains_out, order_ref, normed_ref
+    tokens_ref, cot_ref, gains_ref, source_ref,
+    tokens_out, cot_out, cot_t_out, gains_out, order_ref, turned_ref, normed_ref,
 ):
     width = tokens_ref.shape[1]
     spot = lax.broadcasted_iota(jnp.int32, (width, width), 0)
     order_ref[...] = jnp.where(spot == source_ref[0:1, :], 1.0, 0.0).astype(BF16)
     order = order_ref[...]
-    high, middle, rest = (nn(value, order) for value in thirds(gains_ref[...]))
-    gains_out[...] = high + (middle + rest)
+    turned_ref[...] = order.T
+    high = gains_ref[...].astype(BF16)
+    middle, rest = halves(gains_ref[...] - high.astype(F32))
+    gains_out[...] = nn(high, order) + (nn(middle, order) + nn(rest, order))
     tokens_out[...] = nn(tokens_ref[...], order)
     cot_out[...] = nn(cot_ref[...], order).astype(BF16)
+    cot_t_out[...] = cot_out[...].T
     gain = gains_out[0:1, :]
 
     def norm(rows):
@@ -687,10 +695,11 @@
 
 
 def ffn_kernel(
-    before_ref, first_ref, second_ref, first_in_ref, second_in_ref, gains_ref, cot_ref, *refs
+    before_ref, first_ref, second_ref, first_in_ref, second_in_ref, gains_ref, cot_ref, cot_t_ref,
+    *refs
 ):
-    h_ref, down_ref, back_ref, *outs = refs[4:11]
-    weights_ref, grads_ref, normed_ref, normed_t, cot_t, in_sems, out_sems = refs[11:]
+    h_out, down_ref, back_ref, *outs = refs[4:11]
+    weights_ref, grads_ref, h_ref, normed_ref, normed_t, in_sems, out_sems = refs[11:]
     copies = fetch(refs[:2], refs[2:4], weights_ref, in_sems)
     gain = gains_ref[2:3, :]
     count = first_ref.shape[0]
@@ -704,18 +713,20 @@
             normed_ref[own, :] = (value * root_of(value) * gain).astype(BF16)
 
         each_rows(count, norm)
+    h_copy = pltpu.make_async_copy(h_ref, h_out, out_sems.at[18])
+    h_copy.start()
     normed_t[...] = normed_ref[...].T
-    cot_t[...] = cot_ref[...].T
     down_ref[...] = jnp.zeros_like(down_ref)
     back_ref[...] = jnp.zeros_like(back_ref)
     for copy in copies:
         copy.wait()
     hidden = weights_ref.shape[1] // 3
-
-    @pl.loop(0, hidden // WIDE)
-    def tile(i):
+    half = outs[0].shape[1]
+    sent = []
+
+    def tile(start):
         gates, ups, downs = (
-            pl.ds(pl.multiple_of(k * hidden + i * WIDE, WIDE), WIDE) for k in range(3)
+            slice(k * hidden + start, k * hidden + start + HIDDEN) for k in range(3)
         )
         normed = normed_ref[...]
         gate = nn(normed, weights_ref[:, gates])
@@ -731,34 +742,40 @@
         act = (gelu * up).astype(BF16)
         grad_gate = (grad_act * up * slope).astype(BF16)
         grad_up = (grad_act * gelu).astype(BF16)
+        grads_ref[:, gates] = nn(normed_t[...], grad_gate).astype(BF16)
+        grads_ref[:, ups] = nn(normed_t[...], grad_up).astype(BF16)
+        grads_ref[:, downs] = nn(cot_t_ref[...], act).astype(BF16)
+        for columns in (gates, ups, downs):
+            sent.extend(deliver(grads_ref, outs, out_sems, columns, len(sent)))
         back_ref[...] += nt(grad_gate, weights_ref[:, gates]) + nt(grad_up, weights_ref[:, ups])
         down_ref[...] += nt(act, weights_ref[:, downs])
-        grads_ref[:, gates] = nn(normed_t[...], grad_gate).astype(BF16)
-        grads_ref[:, ups] = nn(normed_t[...], grad_up).astype(BF16)
-        grads_ref[:, downs] = nn(cot_t[...], act).astype(BF16)
-
-    deliver(grads_ref, outs, out_sems)
-
-
-def ffn_call(before, partials, peers, gains, cot, quarters):
+
+    for start in range(0, hidden, HIDDEN):
+        tile(start)
+    for copy in sent:
+        copy.wait()
+    h_copy.wait()
+
+
+def ffn_call(before, partials, peers, gains, cot, cot_t, quarters):
     targets, width = before.shape
     columns = 2 * quarters[0].shape[1]
     return kernel_call(
         ffn_kernel,
-        [before, *partials, *peers, gains, cot, *quarters],
+        [before, *partials, *peers, gains, cot, cot_t, *quarters],
         [struct((targets, width), F32)] * 3 + grad_structs(width, columns),
         [
             pltpu.VMEM((width, columns), BF16),
             pltpu.VMEM((width, columns), BF16),
+            pltpu.VMEM((targets, width), F32),
             pltpu.VMEM((targets, width), BF16),
             pltpu.VMEM((width, targets), BF16),
-            pltpu.VMEM((width, targets), BF16),
             pltpu.SemaphoreType.DMA((6,)),
-            pltpu.SemaphoreType.DMA((6,)),
+            pltpu.SemaphoreType.DMA((19,)),
         ],
-        in_specs=[IN_VMEM] * 7 + [IN_PLACE] * 4,
-        out_specs=[IN_VMEM] * 3 + [IN_PLACE] * 4,
         time=20,
+        in_specs=[IN_VMEM] * 8 + [IN_PLACE] * 4,
+        out_specs=[IN_PLACE] + [IN_VMEM] * 2 + [IN_PLACE] * 4,
     )
 
 
@@ -854,15 +871,15 @@
     each_tile(0, acc_ref.shape[1], project)
     core, half = core_ref[0], kept_ref.shape[1]
     terms = nt(dkv_ref[...], weights_ref[...]).astype(BF16)
-    own_rows = pl.ds(pl.multiple_of(core * half, half), half)
-    peer_rows = pl.ds(pl.multiple_of(half - core * half, half), half)
-    kept_ref[...] = nt(terms, order_ref[own_rows, :]).astype(BF16)
-    given_ref[...] = nt(terms, order_ref[peer_rows, :]).astype(BF16)
+    own_cols = pl.ds(pl.multiple_of(core * half, half), half)
+    peer_cols = pl.ds(pl.multiple_of(half - core * half, half), half)
+    kept_ref[...] = nn(terms, order_ref[:, own_cols]).astype(BF16)
+    given_ref[...] = nn(terms, order_ref[:, peer_cols]).astype(BF16)
 
     @pl.when(step == pl.num_programs(0) - 1)
     def store():
         grads_ref[:, 2 * part :] = acc_ref[...].astype(BF16)
-        deliver(grads_ref, outs, out_sems)
+        deliver_all(grads_ref, outs, out_sems)
 
 
 def cross_grads(core, normed, dq, low_two, attended, order, encoded, dkv, quarters):
@@ -889,13 +906,13 @@
 
 
 def self_backward_kernel(
-    core_ref, g_in_ref, partial_ref, peer_ref, h_ref, gains_ref, mixed_ref, bias_ref, lse_ref,
+    g_in_ref, partial_ref, peer_ref, h_ref, gains_ref, mixed_ref, bias_ref, lse_ref,
     attended_ref, normed_ref, tokens_ref, gain_three_ref, order_ref, labels_ref, *refs
 ):
     g_ref, back_ref, small_ref, *outs = refs[2:9]
     (
         weights_ref, grads_ref, low_ref, go_ref, dmixed_ref, dbias_ref,
-        dqt_ref, dk_acc, dv_acc, gain_ref, in_sems, out_sems,
+        dqt_ref, dk_acc, dv_acc, gain_ref, pack_ref, in_sems, out_sems,
     ) = refs[9:]
     copies = fetch(refs[:2], [], weights_ref, in_sems)
     gain = gains_ref[1:2, :]
@@ -940,29 +957,24 @@
         gain_ref[0:1, :] += jnp.sum(back_ref[rows, :] * value * root_of(value), axis=0, keepdims=True)
 
     each_rows(h_ref.shape[0], sums)
-    core = core_ref[0]
-    first = jnp.where(core == 0, 1.0, 0.0)
-    line = lax.broadcasted_iota(jnp.int32, gain_ref.shape, 0)
-    gains = gain_ref[...] + jnp.where(line == 2, gain_three_ref[0:1, :], 0.0)
-    gains = gains * jnp.where(line == 0, 1.0, first)
-    high, middle, rest = (nt(value, order_ref[...]) for value in thirds(gains))
-    small_ref[...] = jnp.zeros_like(small_ref)
-    small_ref[0:8, :] = high + (middle + rest)
+    gain_ref[2:3, :] = gain_three_ref[0:1, :]
+    high, rest = halves(gain_ref[...])
+    gain_ref[...] = nn(high, order_ref[...]) + nn(rest, order_ref[...])
+    half = pack_ref.shape[1]
+    pack_ref[0:3, :] = gain_ref[0:3, :half]
+    pack_ref[3:6, :] = gain_ref[0:3, half:]
     bucket = lax.broadcasted_iota(jnp.int32, (labels_ref.shape[0], TILE), 1)
     which = jnp.where(labels_ref[:, 0:1] == bucket, 1.0, 0.0).astype(BF16)
     for pair in range(pairs):
-        high, middle, rest = (nn(value, which) for value in thirds(dbias_ref[pair]))
-        table = high + (middle + rest)
-        for side in range(2):
-            spot = side * pairs + pair
-            small_ref[8:, spot * TILE : (spot + 1) * TILE] = table * jnp.where(
-                core == side, 1.0, 0.0
-            )
-    deliver(grads_ref, outs, out_sems)
+        high, rest = halves(dbias_ref[pair])
+        table = nn(high, which) + nn(rest, which)
+        pack_ref[6:8, pair * TILE : (pair + 1) * TILE] = table[0:2]
+    small_ref[...] = jnp.concatenate(halves(pack_ref[...]), axis=0)
+    deliver_all(grads_ref, outs, out_sems)
 
 
 def self_backward(
-    core, g_in, partial, peer, before, gains, mixed, bias, lse, attended, normed, tokens,
+    g_in, partial, peer, before, gains, mixed, bias, lse, attended, normed, tokens,
     gain_three, order, labels, quarters,
 ):
     targets, width = g_in.shape
@@ -971,13 +983,13 @@
     return kernel_call(
         self_backward_kernel,
         [
-            core, g_in, partial, peer, before, gains, mixed, bias, lse, attended, normed, tokens,
+            g_in, partial, peer, before, gains, mixed, bias, lse, attended, normed, tokens,
             gain_three, order, labels, *quarters,
         ],
         [
             struct((targets, width), F32),
             struct((targets, width), F32),
-            struct((16, width), F32),
+            struct((16, width // 2), BF16),
         ]
         + grad_structs(width, 4 * part),
         [
@@ -991,36 +1003,41 @@
             pltpu.VMEM((targets, PAIR), F32),
             pltpu.VMEM((targets, PAIR), F32),
             pltpu.VMEM((8, width), F32),
+            pltpu.VMEM((8, width // 2), F32),
             pltpu.SemaphoreType.DMA((6,)),
             pltpu.SemaphoreType.DMA((6,)),
         ],
-        in_specs=[IN_SMEM] + [IN_VMEM] * 14 + [IN_PLACE] * 2,
+        in_specs=[IN_VMEM] * 14 + [IN_PLACE] * 2,
         out_specs=[IN_VMEM] * 3 + [IN_PLACE] * 4,
         time=22,
     )
 
 
 def last_kernel(
-    g_ref, partial_ref, peer_ref, tokens_ref, gains_ref, h_ref, down_ref, down_in_ref, order_ref,
+    g_ref, partial_ref, peer_ref, tokens_ref, h_ref, down_ref, down_in_ref, gains_ref, order_ref,
     grad_ref, out_ref,
 ):
-    gain = gains_ref[0:1, :]
     order = order_ref[...]
-
-    def finish(rows):
-        back, unused = norm_back(
-            tokens_ref[rows, :], gain, partial_ref[rows, :] + peer_ref[rows, :]
-        )
-        high, middle, rest = (nt(value, order) for value in thirds(g_ref[rows, :] + back))
-        grad_ref[rows, :] = high + (middle + rest)
-        value = h_ref[rows, :] + (down_ref[rows, :] + down_in_ref[rows, :])
-        out_ref[rows, :] = nt(value.astype(BF16), order).astype(BF16)
-
-    count = 4 * ROWS
-
-    @pl.loop(0, g_ref.shape[0] // count)
-    def step(i):
-        finish(pl.ds(pl.multiple_of(i * count, count), count))
+    value = h_ref[...] + (down_ref[...] + down_in_ref[...])
+    out_ref[...] = nn(value.astype(BF16), order).astype(BF16)
+    back, unused = norm_back(tokens_ref[...], gains_ref[0:1, :], partial_ref[...] + peer_ref[...])
+    high, rest = halves(g_ref[...] + back)
+    grad_ref[...] = nn(high, order) + nn(rest, order)
+
+
+def last_call(*ins):
+    targets, width = ins[0].shape
+    block = pl.BlockSpec((WIDE, width), lambda i: (i, 0))
+    return kernel_call(
+        last_kernel,
+        list(ins),
+        [struct((targets, width), F32), struct((targets, width), BF16)],
+        [],
+        time=8,
+        grid=(targets // WIDE,),
+        in_specs=[block] * 7 + [IN_VMEM] * 2,
+        out_specs=[block] * 2,
+    )
 
 
 def shards(
@@ -1074,13 +1091,15 @@
     gains = jnp.concatenate(
         [norm_one[None], norm_two[None], norm_three[None], jnp.zeros((5, width), F32)]
     )
-    tokens, cot, gains, order, normed_one = kernel_call(
+    tokens, cot, cot_t, gains, order, turned, normed_one = kernel_call(
         rows_kernel,
         [decoder_in[0], cotangent[0], gains, source],
         [
             struct((targets, width), F32),
             struct((targets, width), BF16),
+            struct((width, targets), BF16),
             struct((8, width), F32),
+            struct((width, width), BF16),
             struct((width, width), BF16),
             struct((targets, width), BF16),
         ],
@@ -1104,11 +1123,11 @@
     bias = jnp.sum(jnp.where(which[None], bias_table.T[:, :, None], 0.0), axis=1)
     bias = jnp.pad(bias.reshape(heads // 2, 2, targets), ((0, 0), (0, 6), (0, 0)))
 
-    weights, own, ffn, bias, dead = after((weights, own, ffn, bias, dead))
-    weights = gather_second(weights, size)
+    weights, ffn, bias, dead = after((weights, ffn, bias, dead))
+    weights = gather_second(weights, size, time=40)
     weights, ffn = after((weights, ffn))
     weights = send_second(weights, size)
-    ffn = gather_outer(ffn, size)
+    ffn = gather_outer(ffn, size, own)
 
     weights, own, ffn = after((weights, own, ffn))
     ffn = gather_first(ffn, size)
@@ -1130,68 +1149,68 @@
     )
     peer_two = [swap_cores(value) for value in partial_two]
     h_two, partial_down, partial_three, *grads = ffn_call(
-        h_one, partial_two, peer_two, gains, cot, ffn[0] + ffn[1]
+        h_one, partial_two, peer_two, gains, cot, cot_t, ffn[0] + ffn[1]
     )
 
     ffn = scatter_first(grads, size)
     peer_three = swap_cores(partial_three)
+    peer_down = swap_cores(partial_down)
     g_two, low_two, dq, dkv, partial_four, gain_three = cross_backward(
         cot, partial_three, peer_three, h_two, gains, cross_q, key_value, dead, lse_cross, right
     )
-    ffn, dq, dkv, low_two, partial_four = after((ffn, dq, dkv, low_two, partial_four))
+    ffn, dq, dkv, low_two, partial_four, peer_down = after(
+        (ffn, dq, dkv, low_two, partial_four, peer_down)
+    )
     ffn = scatter_second_parts(ffn)
     ffn, dq, dkv, low_two, partial_four = after((ffn, dq, dkv, low_two, partial_four))
     ffn = scatter_second_send(ffn, size)
     peer_four = swap_cores(partial_four)
     kept, given, *grads = cross_grads(
-        which_core, normed_two, dq, low_two, cross_att, order, encoded, dkv, right
+        which_core, normed_two, dq, low_two, cross_att, turned, encoded, dkv, right
     )
     ffn, kept, given, grads, peer_four = after((ffn, kept, given, grads, peer_four))
-    ffn = scatter_outer_parts(ffn)
+    ffn = scatter_outer_parts(ffn, 0, 1)
     ffn, kept, given, grads, peer_four = after((ffn, kept, given, grads, peer_four))
     cross = scatter_first(grads, size)
     ffn = scatter_outer_send(ffn, size)
-    taken = swap_cores(given)
     g_one, partial_five, small, *grads = self_backward(
-        which_core, g_two, partial_four, peer_four, h_one, gains, mixed, bias, lse_self, attended,
-        normed_one, tokens, gain_three, order, labels, left,
-    )
-    ffn, cross, kept, taken, g_one, partial_five, small, grads = after(
-        (ffn, cross, kept, taken, g_one, partial_five, small, grads)
+        g_two, partial_four, peer_four, h_one, gains, mixed, bias, lse_self, attended,
+        normed_one, tokens, gain_three, turned, labels, left,
+    )
+    ffn, cross, given, partial_five, small, grads = after(
+        (ffn, cross, given, partial_five, small, grads)
     )
     last = scatter_first(grads, size)
     peer_five = swap_cores(partial_five)
-    peer_down = swap_cores(partial_down)
-    terms = (kept.astype(F32) + taken.astype(F32)).astype(BF16)
+    taken = swap_cores(given)
     cross = scatter_second_send(scatter_second_parts(cross), size)
-    back = lax.all_to_all(
-        terms.reshape(size, capacity // size, half), "dp", split_axis=0, concat_axis=0, tiled=True
-    )
-    sum_ffn = scatter_last(ffn)
-    decoder_grad, layer_out = kernel_call(
-        last_kernel,
-        [g_one, partial_five, peer_five, tokens, gains, h_two, partial_down, peer_down, order],
-        [struct((targets, width), F32), struct((targets, width), BF16)],
-        [],
-        time=10,
-    )
-    last, cross, layer_out, sum_ffn, small = after((last, cross, layer_out, sum_ffn, small))
-    last, cross = scatter_second_parts(last), scatter_outer_parts(cross)
-    last, cross, back = after((last, cross, back))
+
+    terms = (kept.astype(F32) + taken.astype(F32)).astype(BF16).reshape(size, -1, half)
+    count = terms.shape[1]
+    terms = jnp.concatenate(
+        [terms, jnp.broadcast_to(small[None], (size, *small.shape))], axis=1
+    )
+    back = lax.all_to_all(terms, "dp", split_axis=0, concat_axis=0, tiled=True)
+    decoder_grad, layer_out = last_call(
+        g_one, partial_five, peer_five, tokens, h_two, partial_down, peer_down, gains, turned
+    )
+    cross, layer_out = after((cross, layer_out))
+    cross = scatter_outer_parts(cross, 0, 1)
+    cross, last = after((cross, last))
+    cross = scatter_outer_send(cross, size)
+    last = scatter_second_parts(last, time=40)
     last = scatter_second_send(last, size)
-    cross = scatter_outer_send(cross, size)
-    small = small + swap_cores(small)
-    last, small = after((last, small))
-    last = scatter_outer_parts(last)
-    last, small, back = after((last, small, back))
+    last, ffn = after((last, ffn))
+    last = scatter_outer_parts(last, 0, 1)
+    last, back, ffn = after((last, back, ffn))
     last = scatter_outer_send(last, size)
-    small = sum_devices(small, size)
     inverse = jnp.zeros_like(assign).at[assign].set(jnp.arange(size, dtype=jnp.int32))
-    encoder_grad = back[inverse]
-    sum_cross, sum_self = scatter_last(cross), scatter_last(last)
-
-    table = small[8:10].reshape(2, 2, heads // 2, TILE)[:, :, :, : bias_table.shape[0]]
-    table = lax.dynamic_index_in_dim(table, core, 1, keepdims=False)
+    encoder_grad = back[:, :count][inverse]
+    small = jnp.sum(back[:, count:].astype(F32), axis=0)
+    small = small[:8] + small[8:]
+    both = small + swap_cores(small)
+    sum_ffn, sum_cross, sum_self = scatter_last(ffn), scatter_last(cross), scatter_last(last)
+    table = small[6:8].reshape(2, heads // 2, TILE)[:, :, : bias_table.shape[0]]
     grad_table = table.transpose(1, 0, 2).reshape(heads, -1).T
 
     def parts(value, count):
@@ -1205,9 +1224,9 @@
         layer_out[None],
         decoder_grad[None],
         encoder_grad,
-        small[0],
-        small[1],
-        small[2],
+        both[0:4:3].reshape(-1),
+        small[1:5:3].reshape(-1),
+        small[2:6:3].reshape(-1),
         grad_self_query,
         grad_self_key,
         grad_self_value,

time: 357 us -> 320 us (0.90)
  waiting for transfers between devices: 98.1 us -> 57.1 us
  Pallas kernels: 159 us -> 149 us
  starting transfers between devices: 68.6 us -> 78.2 us
    ppermute x40 -> x35, waiting for transfers between devices: 93.7 us -> 54.8 us  [swap(): return lax.ppermute(value, 'dp', [(i, i ^ mask) for i in range(size)])]
    pallas_call x21, Pallas kernels: 159 us -> 149 us  [kernel_call(): pl.pallas_call(kernel, out_shape=outs, in_specs=in_specs or [everywhere]...]
    ppermute x40 -> x35, starting transfers between devices: 52.5 us -> 62 us  [swap(): return lax.ppermute(value, 'dp', [(i, i ^ mask) for i in range(size)])]
    unnamed x116 -> x108, local copies, waits for them, and re-layouts: 8.81 us -> 10.2 us
  transfers between devices with their start and end apart: 52 -> 47, of which waited for: 28 -> 20; matrix products, arithmetic and copies ran while one was open for 4% -> 5% of each run, Pallas kernels for 33% -> 37%
where the time goes in v3:
time: 320 us; the launch traced here: 316 us
  Pallas kernels  149 us (47%)
  starting transfers between devices  78.2 us (24%)
  waiting for transfers between devices  57.1 us (18%)
  local copies, waits for them, and re-layouts  23.6 us (7%)
  other arithmetic  3.88 us (1%)
  between operations  3.56 us (1%)
    pallas_call x21, Pallas kernels, kernel_call(): pl.pallas_call(kernel, out_shape=outs, in_specs=in_specs or [everywhere]...  149 us
    ppermute x35, starting transfers between devices, swap(): return lax.ppermute(value, 'dp', [(i, i ^ mask) for i in range(size)])  62 us
    ppermute x35, waiting for transfers between devices, swap(): return lax.ppermute(value, 'dp', [(i, i ^ mask) for i in range(size)])  54.8 us
    unnamed x108, local copies, waits for them, and re-layouts  10.2 us
    all_to_all x1, starting transfers between devices, shards(): own = lax.all_to_all(sent, 'dp', split_axis=0, concat_axis=0, tiled=True)  8.26 us
  transfers between devices with their start and end apart: 47, of which 20 were waited for; matrix products, arithmetic and copies ran while one was open for 5% of the time, Pallas kernels for 37%

profile of v3, /device:TPU:0, one launch (start us, length us, event | category | flops | bytes accessed | tf_op | source)
XLA Modules:
  0.0 315.9 jit_solution(10718527084760191340)
XLA Ops:
  0.7 2.0 shard_map.350.refs_0_
  2.7 3.0 collective-permute-start
  5.7 2.6 collective-permute-start.1
  11.4 1.5 gather_fusion
  14.5 1.9 shard_map.351.refs_0_
  17.7 7.0 %shard_map.349 = (f32[512,768]{1,0:T(8,128)}, bf16[512,768]{1,0:T(8,128)(2,1)}, bf16[768,512]{1,0:T(8,128)(2,1)}, f32[8,768]{1,0:T(8,128)}, bf16[768,768]{1,0:T(...) custom-call(bf16[512,768]{1,0:T(8,128)(2,1)} %bitcast.29, bf16[512,768]{1,0:T(8,128)(2,1)} %bitcast.30, ...), custom_call_target="tpu_custom_call" | custom-call | flops 2000000000 | bytes 1 | tf_op jit(solution)/shard_map/pallas_call | solution.py:161
  24.7 4.7 %collective-permute-done.1.refs_2_ = bf16[48,3072]{1,0:T(8,128)(2,1)S(1)} collective-permute-done((bf16[48,3072]{1,0:T(8,128)(2,1)}, bf16[48,3072]{1,0:T(8,128)(2,1)S(1)}, u32[]{:S(2)}, u32[]{:S(2)}) %collective-permute-start.1) | collective-permute-done | bytes 294944 | tf_op jit(solution)/shard_map/ppermute | solution.py:53
  30.3 2.4 shard_map.352
  32.6 1.5 collective-permute-start.3
  34.1 1.5 collective-permute-start.4
  37.2 8.3 %all-to-all-start = ((bf16[16,64,384]{2,1,0:T(8,128)(2,1)}), bf16[16,64,384]{2,1,0:T(8,128)(2,1)S(1)}, u32[]{:S(2)}, u32[]{:S(2)}) async-start(bf16[16,64,384]{2,1,0:T(8,128)(2,1)} %gather_fusion), calls=%async_computation | async-start | bytes 1572864 | tf_op jit(solution)/shard_map/all_to_all | solution.py:1115
  48.0 3.2 %shard_map.353 = (bf16[384,1536]{1,0:T(8,128)(2,1)}, bf16[384,1536]{1,0:T(8,128)(2,1)}) custom-call(bf16[192,1536]{1,0:T(8,128)(2,1)} %get-tuple-element.255.left_ref, bf16[192,1536]{1,0:T(8,128)(2,1)} %copy-done.36, bf16[192,1536]{1,0:T(8,128)(2,1)} %get-tuple-element.257.right_ref, bf16[192,1536]{1,0:T(8,128)(2,1)} %copy-done.37), custom_call_target="tpu_custom_call" | custom-call | flops 40000000000 | bytes 1 | tf_op jit(solution)/shard_map/pallas_call | solution.py:161
  51.2 2.1 collective-permute-start.5
  54.0 10.8 %collective-permute-start.7 = (bf16[48,3072]{1,0:T(8,128)(2,1)S(1)}, bf16[48,3072]{1,0:T(8,128)(2,1)S(1)}, u32[]{:S(2)}, u32[]{:S(2)}) collective-permute-start(bf16[48,3072]{1,0:T(8,128)(2,1)S(1)} %copy-done.40), channel_id=1, source_target_pairs={{0,8},{2,10},{4,12},{6,14},{8,0},{10,2},{12,4},{14,6},{16,24},{18,... | collective-permute-start | bytes 884744 | tf_op jit(solution)/shard_map/ppermute | solution.py:53
  65.8 1.5 collective-permute-start.9
  67.3 8.5 %collective-permute-done.7.refs_1_ = bf16[48,3072]{1,0:T(8,128)(2,1)S(1)} collective-permute-done((bf16[48,3072]{1,0:T(8,128)(2,1)S(1)}, bf16[48,3072]{1,0:T(8,128)(2,1)S(1)}, u32[]{:S(2)}, u32[]{:S(2)}) %collective-permute-start.7) | collective-permute-done | bytes 294944 | tf_op jit(solution)/shard_map/ppermute | solution.py:53
  75.8 8.6 %collective-permute-done.8.refs_2_ = bf16[48,3072]{1,0:T(8,128)(2,1)S(1)} collective-permute-done((bf16[48,3072]{1,0:T(8,128)(2,1)S(1)}, bf16[48,3072]{1,0:T(8,128)(2,1)S(1)}, u32[]{:S(2)}, u32[]{:S(2)}) %collective-permute-start.8) | collective-permute-done | bytes 294944 | tf_op jit(solution)/shard_map/ppermute | solution.py:53
  85.2 2.3 shard_map.354
  87.5 1.5 collective-permute-start.10
  90.4 12.7 %shard_map.355 = (bf16[512,1152]{1,0:T(8,128)(2,1)}, bf16[512,384]{1,0:T(8,128)(2,1)}, f32[3,8,512]{2,1,0:T(8,128)}, f32[512,768]{1,0:T(8,128)}) custom-call(bf16[512,768]{1,0:T(8,128)(2,1)} %get-tuple-element.280.normed_ref, f32[3,8,512]{2,1,0:T(8,128)} %pad.4.bias_ref, bf16[384,1536]{1,0:T(8,128)(2,1)} %get-tuple-element.282.refs_0_, ...), custom_call_target="tpu_custom_call" | custom-call | flops 12000000000 | bytes 1 | tf_op jit(solution)/shard_map/pallas_call | solution.py:161
  105.5 3.2 %shard_map.356 = (bf16[384,1536]{1,0:T(8,128)(2,1)}, bf16[384,1536]{1,0:T(8,128)(2,1)}) custom-call(bf16[192,1536]{1,0:T(8,128)(2,1)} %get-tuple-element.289.left_ref, bf16[192,1536]{1,0:T(8,128)(2,1)} %copy-done.38, bf16[192,1536]{1,0:T(8,128)(2,1)} %get-tuple-element.291.right_ref, bf16[192,1536]{1,0:T(8,128)(2,1)} %copy-done.39), custom_call_target="tpu_custom_call" | custom-call | flops 2000000000 | bytes 1 | tf_op jit(solution)/shard_map/pallas_call | solution.py:161
  108.7 1.5 collective-permute-start.16
  110.7 7.7 %shard_map.357 = (bf16[1024,768]{1,0:T(8,128)(2,1)}, bf16[1024,768]{1,0:T(8,128)(2,1)}) custom-call(s32[1]{0:T(128)} %bitcast.9.core_ref, bf16[1024,384]{1,0:T(8,128)(2,1)} %bitcast.26, bf16[1024,384]{1,0:T(8,128)(2,1)} %copy-done.26, bf16[768,768]{1,0:T(8,128)(2,1)} %get-tuple-element.301.order_ref, bf16[384,1536]{1,0:T(8,128)(2,1)} %get-tuple-element.302.refs_0_, ...), custom_call_target="tpu_custom_call" | custom-call | flops 8000000000 | bytes 1 | tf_op jit(solution)/shard_map/pallas_call | solution.py:161
  119.6 16.5 %shard_map.358 = (f32[512,768]{1,0:T(8,128)}, bf16[512,768]{1,0:T(8,128)(2,1)}, bf16[512,384]{1,0:T(8,128)(2,1)}, bf16[512,384]{1,0:T(8,128)(2,1)}, f32[3,8,512]...) custom-call(f32[512,768]{1,0:T(8,128)} %get-tuple-element.239.tokens_ref, ...), custom_call_target="tpu_custom_call" | custom-call | flops 16000000000 | bytes 1 | tf_op jit(solution)/shard_map/pallas_call | solution.py:161
  140.7 15.7 %shard_map.359 = (f32[512,768]{1,0:T(8,128)}, f32[512,768]{1,0:T(8,128)}, f32[512,768]{1,0:T(8,128)}, bf16[384,1536]{1,0:T(8,128)(2,1)}, bf16[384,1536]{1,0:T(8,...) custom-call(f32[512,768]{1,0:T(8,128)} %get-tuple-element.306.before_ref.h_ref, ...), custom_call_target="tpu_custom_call" | custom-call | flops 20000000000 | bytes 1 | tf_op jit(solution)/shard_map/pallas_call | solution.py:161
  157.8 1.4 collective-permute-start.19
  161.3 18.4 %shard_map.360 = (f32[512,768]{1,0:T(8,128)}, bf16[512,768]{1,0:T(8,128)(2,1)}, bf16[512,384]{1,0:T(8,128)(2,1)}, bf16[1024,768]{1,0:T(8,128)(2,1)}, f32[512,768]{1,0:T(8,128)}, /*index=5*/f32[8,768]{1,0:T(8,128)}) custom-call(bf16[512,768]{1,0:T(8,128)(2,1)} %get-tuple-element.309.cot_ref, f32[512,768]{1,0:T(8,128)} %get-tuple-element.317.partial_ref, ...), custom_call_target="tpu_custom_call" | custom-call | flops 17999998976 | bytes 1 | tf_op jit(solution)/shard_map/pallas_call | solution.py:161
  179.7 5.5 %collective-permute-done.18.left_in_ref.refs_1_ = bf16[384,1536]{1,0:T(8,128)(2,1)S(1)} collective-permute-done((bf16[384,1536]{1,0:T(8,128)(2,1)}, bf16[384,1536]{1,0:T(8,128)(2,1)S(1)}, u32[]{:S(2)}, u32[]{:S(2)}) %collective-permute-start.18) | collective-permute-done | bytes 1179680 | tf_op jit(solution)/shard_map/ppermute | solution.py:53
  186.7 2.9 shard_map.361
  189.6 1.6 collective-permute-start.22
  192.5 12.2 %shard_map.362 = (bf16[1024,384]{1,0:T(8,128)(2,1)}, bf16[1024,384]{1,0:T(8,128)(2,1)}, bf16[384,768]{1,0:T(8,128)(2,1)}, bf16[384,768]{1,0:T(8,128)(2,1)}, bf16...) custom-call(s32[1]{0:T(128)} %bitcast.9.core_ref, bf16[512,768]{1,0:T(8,128)(2,1)} %get-tuple-element.342.normed_ref, ...), custom_call_target="tpu_custom_call" | custom-call | flops 12000000000 | bytes 1 | tf_op jit(solution)/shard_map/pallas_call | solution.py:161
  207.6 3.4 %shard_map.363 = (f32[48,3072]{1,0:T(8,128)}, bf16[48,3072]{1,0:T(8,128)(2,1)}, bf16[48,3072]{1,0:T(8,128)(2,1)}, bf16[48,3072]{1,0:T(8,128)(2,1)}) custom-call(bf16[384,1536]{1,0:T(8,128)(2,1)} %get-tuple-element.356.left_ref.refs_0_, bf16[384,1536]{1,0:T(8,128)(2,1)} %copy-done.21, bf16[192,1536]{1,0:T(8,128)(2,1)} %copy-done.34, ...), custom_call_target="tpu_custom_call" | custom-call | flops 2000000000 | bytes 1 | tf_op jit(solution)/shard_map/pallas_call | solution.py:161
  212.9 5.4 %collective-permute-start.25 = (bf16[48,3072]{1,0:T(8,128)(2,1)}, bf16[48,3072]{1,0:T(8,128)(2,1)S(1)}, u32[]{:S(2)}, u32[]{:S(2)}) collective-permute-start(bf16[48,3072]{1,0:T(8,128)(2,1)} %get-tuple-element.374), channel_id=1, source_target_pairs={{0,8},{2,10},{4,12},{6,14},{8,0},{10,2},{12,4},{14,6},{16,24},{18,... | collective-permute-start | bytes 884744 | tf_op jit(solution)/shard_map/ppermute | solution.py:53
  218.2 2.4 collective-permute-start.27
  220.6 21.9 %shard_map.364 = (f32[512,768]{1,0:T(8,128)}, f32[512,768]{1,0:T(8,128)}, bf16[16,384]{1,0:T(8,128)(2,1)}, bf16[384,768]{1,0:T(8,128)(2,1)}, bf16[384,768]{1,0:T...) custom-call(f32[512,768]{1,0:T(8,128)} %get-tuple-element.382.g_in_ref, ...), custom_call_target="tpu_custom_call" | custom-call | flops 22000001024 | bytes 1 | tf_op jit(solution)/shard_map/pallas_call | solution.py:161
  244.3 2.2 shard_map.365
  251.9 6.1 %all-to-all-start.1 = ((bf16[16,80,384]{2,1,0:T(8,128)(2,1)}), bf16[16,80,384]{2,1,0:T(8,128)(2,1)S(1)}, u32[]{:S(2)}, u32[]{:S(2)}) async-start(bf16[16,80,384]{2,1,0:T(8,128)(2,1)} %pad_maximum_fusion), calls=%async_computation.1 | async-start | bytes 1966080 | tf_op jit(solution)/shard_map/all_to_all | solution.py:1193
  258.0 7.1 %shard_map.366 = (f32[512,768]{1,0:T(8,128)}, bf16[512,768]{1,0:T(8,128)(2,1)}) custom-call(f32[512,768]{1,0:T(8,128)} %get-tuple-element.400.g_ref, f32[512,768]{1,0:T(8,128)} %get-tuple-element.401.partial_ref, f32[512,768]{1,0:T(8,128)} %collective-permute-done.32.peer_ref, f32[512,768]{1,0:T(8,128)} %get-tuple-element.239.tokens_ref, ...), custom_call_target="tpu_custom_call" | custom-call | flops 8000000000 | bytes 1 | tf_op jit(solution)/shard_map/pallas_call | solution.py:161
  265.8 2.4 shard_map.367
  268.2 8.1 %collective-permute-done.33.left_in_ref.refs_1_ = bf16[384,768]{1,0:T(8,128)(2,1)} collective-permute-done((bf16[384,768]{1,0:T(8,128)(2,1)}, bf16[384,768]{1,0:T(8,128)(2,1)}, u32[]{:S(2)}, u32[]{:S(2)}) %collective-permute-start.33) | collective-permute-done | bytes 589856 | tf_op jit(solution)/shard_map/ppermute | solution.py:53
  276.2 5.0 %collective-permute-start.42 = (bf16[48,1536]{1,0:T(8,128)(2,1)}, bf16[48,1536]{1,0:T(8,128)(2,1)S(1)}, u32[]{:S(2)}, u32[]{:S(2)}) collective-permute-start(bf16[48,1536]{1,0:T(8,128)(2,1)} %get-tuple-element.453), channel_id=1, source_target_pairs={{0,8},{2,10},{4,12},{6,14},{8,0},{10,2},{12,4},{14,6},{16,24},{18,... | collective-permute-start | bytes 442376 | tf_op jit(solution)/shard_map/ppermute | solution.py:53
  283.8 2.1 shard_map.368
  288.2 4.0 %collective-permute-done.43 = bf16[48,1536]{1,0:T(8,128)(2,1)S(1)} collective-permute-done((bf16[48,1536]{1,0:T(8,128)(2,1)}, bf16[48,1536]{1,0:T(8,128)(2,1)S(1)}, u32[]{:S(2)}, u32[]{:S(2)}) %collective-permute-start.43) | collective-permute-done | bytes 147488 | tf_op jit(solution)/shard_map/ppermute | solution.py:53
  294.5 2.4 shard_map.369
  298.9 2.3 collective-permute-start.39
  301.8 1.7 collective-permute-start.41
  305.3 1.5 gather_fusion.1
  307.5 7.3 %collective-permute-done.40 = bf16[48,1536]{1,0:T(8,128)(2,1)S(1)} collective-permute-done((bf16[48,1536]{1,0:T(8,128)(2,1)S(1)}, bf16[48,1536]{1,0:T(8,128)(2,1)S(1)}, u32[]{:S(2)}, u32[]{:S(2)}) %collective-permute-start.40) | collective-permute-done | bytes 147488 | tf_op jit(solution)/shard_map/ppermute | solution.py:53
  (225 shorter events, 53.0 us)
Async XLA Ops:
  2.7 22.0 %collective-permute-start = (bf16[48,3072]{1,0:T(8,128)(2,1)}, bf16[48,3072]{1,0:T(8,128)(2,1)S(1)}, u32[]{:S(2)}, u32[]{:S(2)}) collective-permute-start(bf16[48,3072]{1,0:T(8,128)(2,1)} %shard_map.350.refs_0_), channel_id=1, source_target_pairs={{0,8},{2,10},{4,12},{6,14},{8,0},{10,2},{12,4},{14,6},{16,24},{18,... | collective-permute-start | bytes 884744 | tf_op jit(solution)/shard_map/ppermute | solution.py:53
  5.7 23.7 %collective-permute-start.1 = (bf16[48,3072]{1,0:T(8,128)(2,1)}, bf16[48,3072]{1,0:T(8,128)(2,1)S(1)}, u32[]{:S(2)}, u32[]{:S(2)}) collective-permute-start(bf16[48,3072]{1,0:T(8,128)(2,1)} %shard_map.350.refs_0_), channel_id=1, source_target_pairs={{0,16},{2,18},{4,20},{6,22},{8,24},{10,26},{12,28},{14,30},{16,0},... | collective-permute-start | bytes 884744 | tf_op jit(solution)/shard_map/ppermute | solution.py:53
  8.3 21.1 %collective-permute-start.2 = (bf16[48,3072]{1,0:T(8,128)(2,1)}, bf16[48,3072]{1,0:T(8,128)(2,1)S(1)}, u32[]{:S(2)}, u32[]{:S(2)}) collective-permute-start(bf16[48,3072]{1,0:T(8,128)(2,1)} %shard_map.350.refs_0_), channel_id=1, source_target_pairs={{0,24},{2,26},{4,28},{6,30},{8,16},{10,18},{12,20},{14,22},{16,8},... | collective-permute-start | bytes 884744 | tf_op jit(solution)/shard_map/ppermute | solution.py:53
  11.3 24.3 %copy-start.2 = (s32[512,128]{1,0:T(8,128)}, s32[512,128]{1,0:T(8,128)S(1)}, u32[]{:S(2)}) copy-start(s32[512,128]{1,0:T(8,128)S(1)} %slice.66.labels_ref) | copy-start | bytes 786436
  32.6 13.5 %collective-permute-start.3 = (bf16[192,1536]{1,0:T(8,128)(2,1)}, bf16[192,1536]{1,0:T(8,128)(2,1)S(1)}, u32[]{:S(2)}, u32[]{:S(2)}) collective-permute-start(bf16[192,1536]{1,0:T(8,128)(2,1)} %get-tuple-element.255.left_ref), channel_id=1, source_target_pairs={{0,4},{2,6},{4,0},{6,2},{8,12},{10,14},{12,8},{14,10},{16,20},{18,... | collective-permute-start | bytes 1769480 | tf_op jit(solution)/shard_map/ppermute | solution.py:53
  34.1 12.9 %collective-permute-start.4 = (bf16[192,1536]{1,0:T(8,128)(2,1)}, bf16[192,1536]{1,0:T(8,128)(2,1)S(1)}, u32[]{:S(2)}, u32[]{:S(2)}) collective-permute-start(bf16[192,1536]{1,0:T(8,128)(2,1)} %get-tuple-element.257.right_ref), channel_id=1, source_target_pairs={{0,2},{2,0},{4,6},{6,4},{8,10},{10,8},{12,14},{14,12},{16,18},{18,... | collective-permute-start | bytes 1769480 | tf_op jit(solution)/shard_map/ppermute | solution.py:53
  37.2 28.6 %all-to-all-start = ((bf16[16,64,384]{2,1,0:T(8,128)(2,1)}), bf16[16,64,384]{2,1,0:T(8,128)(2,1)S(1)}, u32[]{:S(2)}, u32[]{:S(2)}) async-start(bf16[16,64,384]{2,1,0:T(8,128)(2,1)} %gather_fusion), calls=%async_computation | async-start | bytes 1572864 | tf_op jit(solution)/shard_map/all_to_all | solution.py:1115
  51.2 33.2 %collective-permute-start.5 = (bf16[384,1536]{1,0:T(8,128)(2,1)}, bf16[384,1536]{1,0:T(8,128)(2,1)S(1)}, u32[]{:S(2)}, u32[]{:S(2)}) collective-permute-start(bf16[384,1536]{1,0:T(8,128)(2,1)} %get-tuple-element.282.refs_0_), channel_id=1, source_target_pairs={{0,2},{2,0},{4,6},{6,4},{8,10},{10,8},{12,14},{14,12},{16,18},{18,... | collective-permute-start | bytes 3538952 | tf_op jit(solution)/shard_map/ppermute | solution.py:53
  53.3 31.1 %collective-permute-start.6 = (bf16[384,1536]{1,0:T(8,128)(2,1)}, bf16[384,1536]{1,0:T(8,128)(2,1)}, u32[]{:S(2)}, u32[]{:S(2)}) collective-permute-start(bf16[384,1536]{1,0:T(8,128)(2,1)} %get-tuple-element.302.refs_0_), channel_id=1, source_target_pairs={{0,4},{2,6},{4,0},{6,2},{8,12},{10,14},{12,8},{14,10},{16,20},{18,... | collective-permute-start | bytes 3538952 | tf_op jit(solution)/shard_map/ppermute | solution.py:53
  54.0 21.8 %collective-permute-start.7 = (bf16[48,3072]{1,0:T(8,128)(2,1)S(1)}, bf16[48,3072]{1,0:T(8,128)(2,1)S(1)}, u32[]{:S(2)}, u32[]{:S(2)}) collective-permute-start(bf16[48,3072]{1,0:T(8,128)(2,1)S(1)} %copy-done.40), channel_id=1, source_target_pairs={{0,8},{2,10},{4,12},{6,14},{8,0},{10,2},{12,4},{14,6},{16,24},{18,... | collective-permute-start | bytes 884744 | tf_op jit(solution)/shard_map/ppermute | solution.py:53
  64.8 19.6 %collective-permute-start.8 = (bf16[48,3072]{1,0:T(8,128)(2,1)S(1)}, bf16[48,3072]{1,0:T(8,128)(2,1)S(1)}, u32[]{:S(2)}, u32[]{:S(2)}) collective-permute-start(bf16[48,3072]{1,0:T(8,128)(2,1)S(1)} %copy-done.40), channel_id=1, source_target_pairs={{0,16},{2,18},{4,20},{6,22},{8,24},{10,26},{12,28},{14,30},{16,0},... | collective-permute-start | bytes 884744 | tf_op jit(solution)/shard_map/ppermute | solution.py:53
  65.8 18.6 %collective-permute-start.9 = (bf16[48,3072]{1,0:T(8,128)(2,1)S(1)}, bf16[48,3072]{1,0:T(8,128)(2,1)S(1)}, u32[]{:S(2)}, u32[]{:S(2)}) collective-permute-start(bf16[48,3072]{1,0:T(8,128)(2,1)S(1)} %copy-done.40), channel_id=1, source_target_pairs={{0,24},{2,26},{4,28},{6,30},{8,16},{10,18},{12,20},{14,22},{16,8},... | collective-permute-start | bytes 884744 | tf_op jit(solution)/shard_map/ppermute | solution.py:53
  87.5 17.1 %collective-permute-start.12 = (bf16[1024,384]{1,0:T(8,128)(2,1)S(1)}, bf16[1024,384]{1,0:T(8,128)(2,1)S(1)}, u32[]{:S(2)}, u32[]{:S(2)}) collective-permute-start(bf16[1024,384]{1,0:T(8,128)(2,1)S(1)} %bitcast.25), channel_id=1, source_target_pairs={{0,1},{1,0},{2,3},{3,2},{4,5},{5,4},{6,7},{7,6},{8,9},{9,8},{10,11... | collective-permute-start | bytes 2359304 | tf_op jit(solution)/shard_map/ppermute | solution.py:57
  87.5 16.0 %collective-permute-start.10 = (bf16[192,1536]{1,0:T(8,128)(2,1)}, bf16[192,1536]{1,0:T(8,128)(2,1)S(1)}, u32[]{:S(2)}, u32[]{:S(2)}) collective-permute-start(bf16[192,1536]{1,0:T(8,128)(2,1)} %get-tuple-element.289.left_ref), channel_id=1, source_target_pairs={{0,4},{2,6},{4,0},{6,2},{8,12},{10,14},{12,8},{14,10},{16,20},{18,... | collective-permute-start | bytes 1769480 | tf_op jit(solution)/shard_map/ppermute | solution.py:53
  89.0 15.6 %collective-permute-start.11 = (bf16[192,1536]{1,0:T(8,128)(2,1)}, bf16[192,1536]{1,0:T(8,128)(2,1)S(1)}, u32[]{:S(2)}, u32[]{:S(2)}) collective-permute-start(bf16[192,1536]{1,0:T(8,128)(2,1)} %get-tuple-element.291.right_ref), channel_id=1, source_target_pairs={{0,2},{2,0},{4,6},{6,4},{8,10},{10,8},{12,14},{14,12},{16,18},{18,... | collective-permute-start | bytes 1769480 | tf_op jit(solution)/shard_map/ppermute | solution.py:53
  108.7 9.7 %collective-permute-start.13 = (f32[512,768]{1,0:T(8,128)S(1)}, f32[512,768]{1,0:T(8,128)S(1)}, u32[]{:S(2)}, u32[]{:S(2)}) collective-permute-start(f32[512,768]{1,0:T(8,128)S(1)} %copy-done.17), channel_id=1, source_target_pairs={{0,1},{1,0},{2,3},{3,2},{4,5},{5,4},{6,7},{7,6},{8,9},{9,8},{10,11... | collective-permute-start | bytes 4718600 | tf_op jit(solution)/shard_map/ppermute | solution.py:57
  108.7 28.6 %collective-permute-start.16 = (bf16[384,1536]{1,0:T(8,128)(2,1)}, bf16[384,1536]{1,0:T(8,128)(2,1)S(1)}, u32[]{:S(2)}, u32[]{:S(2)}) collective-permute-start(bf16[384,1536]{1,0:T(8,128)(2,1)} %get-tuple-element.311.refs_0_), channel_id=1, source_target_pairs={{0,2},{2,0},{4,6},{6,4},{8,10},{10,8},{12,14},{14,12},{16,18},{18,... | collective-permute-start | bytes 3538952 | tf_op jit(solution)/shard_map/ppermute | solution.py:53
  110.2 28.2 %collective-permute-start.17 = (bf16[384,1536]{1,0:T(8,128)(2,1)}, bf16[384,1536]{1,0:T(8,128)(2,1)S(1)}, u32[]{:S(2)}, u32[]{:S(2)}) collective-permute-start(bf16[384,1536]{1,0:T(8,128)(2,1)} %get-tuple-element.312.refs_2_), channel_id=1, source_target_pairs={{0,4},{2,6},{4,0},{6,2},{8,12},{10,14},{12,8},{14,10},{16,20},{18,... | collective-permute-start | bytes 3538952 | tf_op jit(solution)/shard_map/ppermute | solution.py:53
  136.1 2.6 collective-permute-start.14
  136.2 3.6 %collective-permute-start.15 = (f32[256,768]{1,0:T(8,128)}, f32[256,768]{1,0:T(8,128)S(1)}, u32[]{:S(2)}, u32[]{:S(2)}) collective-permute-start(f32[256,768]{1,0:T(8,128)} %get-tuple-element.308.second_ref), channel_id=1, source_target_pairs={{0,1},{1,0},{2,3},{3,2},{4,5},{5,4},{6,7},{7,6},{8,9},{9,8},{10,11... | collective-permute-start | bytes 2359304 | tf_op jit(solution)/shard_map/ppermute | solution.py:57
  156.4 3.7 %collective-permute-start.20 = (f32[512,768]{1,0:T(8,128)}, f32[512,768]{1,0:T(8,128)S(1)}, u32[]{:S(2)}, u32[]{:S(2)}) collective-permute-start(f32[512,768]{1,0:T(8,128)} %get-tuple-element.317.partial_ref), channel_id=1, source_target_pairs={{0,1},{1,0},{2,3},{3,2},{4,5},{5,4},{6,7},{7,6},{8,9},{9,8},{10,11... | collective-permute-start | bytes 4718600 | tf_op jit(solution)/shard_map/ppermute | solution.py:57
  156.6 29.1 %collective-permute-start.21 = (f32[512,768]{1,0:T(8,128)}, f32[512,768]{1,0:T(8,128)S(1)}, u32[]{:S(2)}, u32[]{:S(2)}) collective-permute-start(f32[512,768]{1,0:T(8,128)} %get-tuple-element.325.down_ref), channel_id=1, source_target_pairs={{0,1},{1,0},{2,3},{3,2},{4,5},{5,4},{6,7},{7,6},{8,9},{9,8},{10,11... | collective-permute-start | bytes 4718600 | tf_op jit(solution)/shard_map/ppermute | solution.py:57
  157.0 28.2 %collective-permute-start.18 = (bf16[384,1536]{1,0:T(8,128)(2,1)}, bf16[384,1536]{1,0:T(8,128)(2,1)S(1)}, u32[]{:S(2)}, u32[]{:S(2)}) collective-permute-start(bf16[384,1536]{1,0:T(8,128)(2,1)} %get-tuple-element.315), channel_id=1, source_target_pairs={{0,2},{2,0},{4,6},{6,4},{8,10},{10,8},{12,14},{14,12},{16,18},{18,... | collective-permute-start | bytes 3538952 | tf_op jit(solution)/shard_map/ppermute | solution.py:53
  157.8 27.9 %collective-permute-start.19 = (bf16[384,1536]{1,0:T(8,128)(2,1)}, bf16[384,1536]{1,0:T(8,128)(2,1)S(1)}, u32[]{:S(2)}, u32[]{:S(2)}) collective-permute-start(bf16[384,1536]{1,0:T(8,128)(2,1)} %get-tuple-element.316), channel_id=1, source_target_pairs={{0,4},{2,6},{4,0},{6,2},{8,12},{10,14},{12,8},{14,10},{16,20},{18,... | collective-permute-start | bytes 3538952 | tf_op jit(solution)/shard_map/ppermute | solution.py:53
  189.6 17.2 %collective-permute-start.24 = (f32[512,768]{1,0:T(8,128)S(1)}, f32[512,768]{1,0:T(8,128)S(1)}, u32[]{:S(2)}, u32[]{:S(2)}) collective-permute-start(f32[512,768]{1,0:T(8,128)S(1)} %copy-done.15), channel_id=1, source_target_pairs={{0,1},{1,0},{2,3},{3,2},{4,5},{5,4},{6,7},{7,6},{8,9},{9,8},{10,11... | collective-permute-start | bytes 4718600 | tf_op jit(solution)/shard_map/ppermute | solution.py:57
  189.6 16.0 %collective-permute-start.22 = (bf16[192,1536]{1,0:T(8,128)(2,1)}, bf16[192,1536]{1,0:T(8,128)(2,1)S(1)}, u32[]{:S(2)}, u32[]{:S(2)}) collective-permute-start(bf16[192,1536]{1,0:T(8,128)(2,1)} %get-tuple-element.340), channel_id=1, source_target_pairs={{0,4},{2,6},{4,0},{6,2},{8,12},{10,14},{12,8},{14,10},{16,20},{18,... | collective-permute-start | bytes 1769480 | tf_op jit(solution)/shard_map/ppermute | solution.py:53
  191.2 15.6 %collective-permute-start.23 = (bf16[192,1536]{1,0:T(8,128)(2,1)}, bf16[192,1536]{1,0:T(8,128)(2,1)S(1)}, u32[]{:S(2)}, u32[]{:S(2)}) collective-permute-start(bf16[192,1536]{1,0:T(8,128)(2,1)} %get-tuple-element.341), channel_id=1, source_target_pairs={{0,2},{2,0},{4,6},{6,4},{8,10},{10,8},{12,14},{14,12},{16,18},{18,... | collective-permute-start | bytes 1769480 | tf_op jit(solution)/shard_map/ppermute | solution.py:53
  211.0 31.6 %collective-permute-start.28 = (bf16[384,768]{1,0:T(8,128)(2,1)S(1)}, bf16[384,768]{1,0:T(8,128)(2,1)S(1)}, u32[]{:S(2)}, u32[]{:S(2)}) collective-permute-start(bf16[384,768]{1,0:T(8,128)(2,1)S(1)} %copy-done.33), channel_id=1, source_target_pairs={{0,2},{2,0},{4,6},{6,4},{8,10},{10,8},{12,14},{14,12},{16,18},{18,... | collective-permute-start | bytes 1769480 | tf_op jit(solution)/shard_map/ppermute | solution.py:53
  212.4 30.2 %collective-permute-start.29 = (bf16[384,768]{1,0:T(8,128)(2,1)S(1)}, bf16[384,768]{1,0:T(8,128)(2,1)S(1)}, u32[]{:S(2)}, u32[]{:S(2)}) collective-permute-start(bf16[384,768]{1,0:T(8,128)(2,1)S(1)} %copy-done.32), channel_id=1, source_target_pairs={{0,4},{2,6},{4,0},{6,2},{8,12},{10,14},{12,8},{14,10},{16,20},{18,... | collective-permute-start | bytes 1769480 | tf_op jit(solution)/shard_map/ppermute | solution.py:53
  212.9 29.7 %collective-permute-start.25 = (bf16[48,3072]{1,0:T(8,128)(2,1)}, bf16[48,3072]{1,0:T(8,128)(2,1)S(1)}, u32[]{:S(2)}, u32[]{:S(2)}) collective-permute-start(bf16[48,3072]{1,0:T(8,128)(2,1)} %get-tuple-element.374), channel_id=1, source_target_pairs={{0,8},{2,10},{4,12},{6,14},{8,0},{10,2},{12,4},{14,6},{16,24},{18,... | collective-permute-start | bytes 884744 | tf_op jit(solution)/shard_map/ppermute | solution.py:53
  218.2 24.3 %collective-permute-start.26 = (bf16[48,3072]{1,0:T(8,128)(2,1)}, bf16[48,3072]{1,0:T(8,128)(2,1)S(1)}, u32[]{:S(2)}, u32[]{:S(2)}) collective-permute-start(bf16[48,3072]{1,0:T(8,128)(2,1)} %get-tuple-element.375), channel_id=1, source_target_pairs={{0,16},{2,18},{4,20},{6,22},{8,24},{10,26},{12,28},{14,30},{16,0},... | collective-permute-start | bytes 884744 | tf_op jit(solution)/shard_map/ppermute | solution.py:53
  218.2 24.3 %collective-permute-start.27 = (bf16[48,3072]{1,0:T(8,128)(2,1)}, bf16[48,3072]{1,0:T(8,128)(2,1)S(1)}, u32[]{:S(2)}, u32[]{:S(2)}) collective-permute-start(bf16[48,3072]{1,0:T(8,128)(2,1)} %get-tuple-element.376), channel_id=1, source_target_pairs={{0,24},{2,26},{4,28},{6,30},{8,16},{10,18},{12,20},{14,22},{16,8},... | collective-permute-start | bytes 884744 | tf_op jit(solution)/shard_map/ppermute | solution.py:53
  242.6 15.3 %collective-permute-start.32 = (f32[512,768]{1,0:T(8,128)}, f32[512,768]{1,0:T(8,128)}, u32[]{:S(2)}, u32[]{:S(2)}) collective-permute-start(f32[512,768]{1,0:T(8,128)} %get-tuple-element.401.partial_ref), channel_id=1, source_target_pairs={{0,1},{1,0},{2,3},{3,2},{4,5},{5,4},{6,7},{7,6},{8,9},{9,8},{10,11... | collective-permute-start | bytes 4718600 | tf_op jit(solution)/shard_map/ppermute | solution.py:57
  242.7 7.2 %collective-permute-start.37 = (bf16[1024,384]{1,0:T(8,128)(2,1)S(1)}, bf16[1024,384]{1,0:T(8,128)(2,1)S(1)}, u32[]{:S(2)}, u32[]{:S(2)}) collective-permute-start(bf16[1024,384]{1,0:T(8,128)(2,1)S(1)} %copy-done.25), channel_id=1, source_target_pairs={{0,1},{1,0},{2,3},{3,2},{4,5},{5,4},{6,7},{7,6},{8,9},{9,8},{10,11... | collective-permute-start | bytes 2359304 | tf_op jit(solution)/shard_map/ppermute | solution.py:57
  246.5 18.6 %collective-permute-start.30 = (bf16[192,768]{1,0:T(8,128)(2,1)}, bf16[192,768]{1,0:T(8,128)(2,1)S(1)}, u32[]{:S(2)}, u32[]{:S(2)}) collective-permute-start(bf16[192,768]{1,0:T(8,128)(2,1)} %get-tuple-element.398), channel_id=1, source_target_pairs={{0,4},{2,6},{4,0},{6,2},{8,12},{10,14},{12,8},{14,10},{16,20},{18,... | collective-permute-start | bytes 884744 | tf_op jit(solution)/shard_map/ppermute | solution.py:53
  247.9 17.2 %collective-permute-start.31 = (bf16[192,768]{1,0:T(8,128)(2,1)}, bf16[192,768]{1,0:T(8,128)(2,1)}, u32[]{:S(2)}, u32[]{:S(2)}) collective-permute-start(bf16[192,768]{1,0:T(8,128)(2,1)} %get-tuple-element.399), channel_id=1, source_target_pairs={{0,2},{2,0},{4,6},{6,4},{8,10},{10,8},{12,14},{14,12},{16,18},{18,... | collective-permute-start | bytes 884744 | tf_op jit(solution)/shard_map/ppermute | solution.py:53
  248.6 27.6 %collective-permute-start.33 = (bf16[384,768]{1,0:T(8,128)(2,1)}, bf16[384,768]{1,0:T(8,128)(2,1)}, u32[]{:S(2)}, u32[]{:S(2)}) collective-permute-start(bf16[384,768]{1,0:T(8,128)(2,1)} %get-tuple-element.418), channel_id=1, source_target_pairs={{0,2},{2,0},{4,6},{6,4},{8,10},{10,8},{12,14},{14,12},{16,18},{18,... | collective-permute-start | bytes 1769480 | tf_op jit(solution)/shard_map/ppermute | solution.py:53
  249.9 26.3 %collective-permute-start.34 = (bf16[384,768]{1,0:T(8,128)(2,1)}, bf16[384,768]{1,0:T(8,128)(2,1)S(1)}, u32[]{:S(2)}, u32[]{:S(2)}) collective-permute-start(bf16[384,768]{1,0:T(8,128)(2,1)} %get-tuple-element.419), channel_id=1, source_target_pairs={{0,4},{2,6},{4,0},{6,2},{8,12},{10,14},{12,8},{14,10},{16,20},{18,... | collective-permute-start | bytes 1769480 | tf_op jit(solution)/shard_map/ppermute | solution.py:53
  251.9 45.0 %all-to-all-start.1 = ((bf16[16,80,384]{2,1,0:T(8,128)(2,1)}), bf16[16,80,384]{2,1,0:T(8,128)(2,1)S(1)}, u32[]{:S(2)}, u32[]{:S(2)}) async-start(bf16[16,80,384]{2,1,0:T(8,128)(2,1)} %pad_maximum_fusion), calls=%async_computation.1 | async-start | bytes 1966080 | tf_op jit(solution)/shard_map/all_to_all | solution.py:1193
  276.2 12.0 %collective-permute-start.42 = (bf16[48,1536]{1,0:T(8,128)(2,1)}, bf16[48,1536]{1,0:T(8,128)(2,1)S(1)}, u32[]{:S(2)}, u32[]{:S(2)}) collective-permute-start(bf16[48,1536]{1,0:T(8,128)(2,1)} %get-tuple-element.453), channel_id=1, source_target_pairs={{0,8},{2,10},{4,12},{6,14},{8,0},{10,2},{12,4},{14,6},{16,24},{18,... | collective-permute-start | bytes 442376 | tf_op jit(solution)/shard_map/ppermute | solution.py:53
  281.2 11.1 %collective-permute-start.43 = (bf16[48,1536]{1,0:T(8,128)(2,1)}, bf16[48,1536]{1,0:T(8,128)(2,1)S(1)}, u32[]{:S(2)}, u32[]{:S(2)}) collective-permute-start(bf16[48,1536]{1,0:T(8,128)(2,1)} %get-tuple-element.454), channel_id=1, source_target_pairs={{0,16},{2,18},{4,20},{6,22},{8,24},{10,26},{12,28},{14,30},{16,0},... | collective-permute-start | bytes 442376 | tf_op jit(solution)/shard_map/ppermute | solution.py:53
  282.4 9.8 %collective-permute-start.44 = (bf16[48,1536]{1,0:T(8,128)(2,1)}, bf16[48,1536]{1,0:T(8,128)(2,1)S(1)}, u32[]{:S(2)}, u32[]{:S(2)}) collective-permute-start(bf16[48,1536]{1,0:T(8,128)(2,1)} %get-tuple-element.455), channel_id=1, source_target_pairs={{0,24},{2,26},{4,28},{6,30},{8,16},{10,18},{12,20},{14,22},{16,8},... | collective-permute-start | bytes 442376 | tf_op jit(solution)/shard_map/ppermute | solution.py:53
  285.9 7.1 %collective-permute-start.35 = (bf16[192,768]{1,0:T(8,128)(2,1)}, bf16[192,768]{1,0:T(8,128)(2,1)S(1)}, u32[]{:S(2)}, u32[]{:S(2)}) collective-permute-start(bf16[192,768]{1,0:T(8,128)(2,1)} %get-tuple-element.424), channel_id=1, source_target_pairs={{0,4},{2,6},{4,0},{6,2},{8,12},{10,14},{12,8},{14,10},{16,20},{18,... | collective-permute-start | bytes 884744 | tf_op jit(solution)/shard_map/ppermute | solution.py:53
  286.7 6.9 %collective-permute-start.36 = (bf16[192,768]{1,0:T(8,128)(2,1)}, bf16[192,768]{1,0:T(8,128)(2,1)S(1)}, u32[]{:S(2)}, u32[]{:S(2)}) collective-permute-start(bf16[192,768]{1,0:T(8,128)(2,1)} %get-tuple-element.425), channel_id=1, source_target_pairs={{0,2},{2,0},{4,6},{6,4},{8,10},{10,8},{12,14},{14,12},{16,18},{18,... | collective-permute-start | bytes 884744 | tf_op jit(solution)/shard_map/ppermute | solution.py:53
  297.0 9.8 %collective-permute-start.38 = (f32[8,384]{1,0:T(8,128)S(1)}, f32[8,384]{1,0:T(8,128)S(1)}, u32[]{:S(2)}, u32[]{:S(2)}) collective-permute-start(f32[8,384]{1,0:T(8,128)S(1)} %slice_add_fusion), channel_id=1, source_target_pairs={{0,1},{1,0},{2,3},{3,2},{4,5},{5,4},{6,7},{7,6},{8,9},{9,8},{10,11... | collective-permute-start | bytes 36872 | tf_op jit(solution)/shard_map/ppermute | solution.py:57
  298.9 8.6 %collective-permute-start.39 = (bf16[48,1536]{1,0:T(8,128)(2,1)}, bf16[48,1536]{1,0:T(8,128)(2,1)S(1)}, u32[]{:S(2)}, u32[]{:S(2)}) collective-permute-start(bf16[48,1536]{1,0:T(8,128)(2,1)} %get-tuple-element.449), channel_id=1, source_target_pairs={{0,8},{2,10},{4,12},{6,14},{8,0},{10,2},{12,4},{14,6},{16,24},{18,... | collective-permute-start | bytes 442376 | tf_op jit(solution)/shard_map/ppermute | solution.py:53
  301.2 13.6 %collective-permute-start.40 = (bf16[48,1536]{1,0:T(8,128)(2,1)S(1)}, bf16[48,1536]{1,0:T(8,128)(2,1)S(1)}, u32[]{:S(2)}, u32[]{:S(2)}) collective-permute-start(bf16[48,1536]{1,0:T(8,128)(2,1)S(1)} %copy-done.51), channel_id=1, source_target_pairs={{0,16},{2,18},{4,20},{6,22},{8,24},{10,26},{12,28},{14,30},{16,0},... | collective-permute-start | bytes 442376 | tf_op jit(solution)/shard_map/ppermute | solution.py:53
  301.8 13.0 %collective-permute-start.41 = (bf16[48,1536]{1,0:T(8,128)(2,1)S(1)}, bf16[48,1536]{1,0:T(8,128)(2,1)S(1)}, u32[]{:S(2)}, u32[]{:S(2)}) collective-permute-start(bf16[48,1536]{1,0:T(8,128)(2,1)S(1)} %copy-done.50), channel_id=1, source_target_pairs={{0,24},{2,26},{4,28},{6,30},{8,16},{10,18},{12,20},{14,22},{16,8},... | collective-permute-start | bytes 442376 | tf_op jit(solution)/shard_map/ppermute | solution.py:53
  (53 other events, 248.5 us)

commit v4 on v3

--- a/solution.py
+++ b/solution.py
@@ -62,10 +62,9 @@
 
 
 def gather_outer(shard, size, late=()):
-    if size <= 16:
-        held = after(shard, late)
-        ins = [swap(held if mask + 4 == size else shard, mask, size) for mask in range(4, size, 4)]
-        return [shard] + ins
+    if size == 16:
+        far, near = swap(shard, 8, size), swap(shard, 4, size)
+        return [shard, near, far, swap(after(far, late), 4, size)]
     shard = after(shard, late)
     mask = 4
     while mask < size:
@@ -134,6 +133,26 @@
         in_specs=[pl.BlockSpec((rows, half), lambda i: (0, 0))] * len(ins),
         out_specs=[pl.BlockSpec((rows // 4, width), lambda i: (0, 0))] * 4,
     )
+
+
+def scatter_pair_parts(state):
+    rows, half = state[-1].shape
+    outs = [struct((rows // 2, 2 * half), dtype) for dtype in (F32, BF16)]
+    return kernel_call(
+        scatter_pair_kernel,
+        state[0::2] + state[1::2],
+        outs,
+        [],
+        grid=(1,),
+        in_specs=[pl.BlockSpec((rows, half), lambda i: (0, 0))] * 6,
+        out_specs=[pl.BlockSpec((rows // 2, 2 * half), lambda i: (0, 0))] * 2,
+    )
+
+
+def scatter_pair_send(keep, taken, size):
+    count = keep.shape[0] // 2
+    rows = keep + taken.astype(F32)
+    return [rows[:count], swap(rows[count:].astype(BF16), 8, size)]
 
 
 def scatter_outer_send(parts, size):
@@ -212,6 +231,21 @@
             rows = slice(k * count, (k + 1) * count)
             total = own_ref[rows, :].astype(F32) + in_ref[rows, :].astype(F32)
             out_ref[:, cols] = (total + more_ref[rows, :].astype(F32)).astype(out_ref.dtype)
+
+
+def scatter_pair_kernel(*refs):
+    *in_refs, keep_ref, out_ref = refs
+    count = keep_ref.shape[0] // 2
+    for side in range(2):
+        own_ref, in_ref, more_ref = in_refs[3 * side : 3 * side + 3]
+        half = own_ref.shape[1]
+        cols = slice(side * half, (side + 1) * half)
+        for k in range(4):
+            rows = slice(k * count, (k + 1) * count)
+            total = own_ref[rows, :].astype(F32) + in_ref[rows, :].astype(F32)
+            target = out_ref if k % 2 else keep_ref
+            spot = slice(k // 2 * count, (k // 2 + 1) * count)
+            target[spot, cols] = (total + more_ref[rows, :].astype(F32)).astype(target.dtype)
 
 
 def cast_kernel(*refs):
@@ -284,8 +318,6 @@
                 sems.at[first + len(copies)],
             )
         )
-    for copy in copies:
-        copy.start()
     return copies
 
 
@@ -293,6 +325,8 @@
     half = out_refs[0].shape[1]
     copies = deliver(grads_ref, out_refs, sems, slice(0, half))
     copies += deliver(grads_ref, out_refs, sems, slice(half, 2 * half), 2)
+    for copy in copies:
+        copy.start()
     for copy in copies:
         copy.wait()
 
@@ -354,6 +388,11 @@
         body(pair, lambda which: pl.ds(pl.multiple_of((which * pairs + pair) * PAIR, PAIR), PAIR))
 
 
+def row_of(value, head):
+    line = lax.broadcasted_iota(jnp.int32, value.shape, 0)
+    return jnp.sum(jnp.where(line == head, value, 0.0), axis=0, keepdims=True)
+
+
 def of_head(value, head):
     lane = lax.broadcasted_iota(jnp.int32, value.shape, 1)
     return jnp.where(lane // HEAD_DIM == head, value, jnp.zeros_like(value))
@@ -415,13 +454,15 @@
     queries = p_ref.shape[1]
     dk_acc[...] = jnp.zeros_like(dk_acc)
     dv_acc[...] = jnp.zeros_like(dv_acc)
-    for head in range(2):
-        rows = slice(head * HEAD_DIM, (head + 1) * HEAD_DIM)
+    dqt_ref[...] = jnp.zeros_like(dqt_ref)
+
+    @pl.loop(0, 2)
+    def each_head(head):
         for start in range(0, targets, queries):
             cols = slice(start, start + queries)
             query = of_head(q_ref[cols, :], head)
             grad = of_head(go_ref[cols, :], head)
-            lse = lse_ref[head : head + 1, cols]
+            lse = row_of(lse_ref[:, cols], head)
             delta_ref[...] = jnp.zeros_like(delta_ref)
 
             def first(base):
@@ -434,7 +475,6 @@
 
             each_chunk(count, size, first)
             delta = delta_ref[...]
-            dqt_ref[rows, cols] = jnp.zeros((HEAD_DIM, queries), F32)
 
             def second(base):
                 keys = pl.ds(base, size)
@@ -442,7 +482,7 @@
                 dv_acc[keys, :] += nn(probs.astype(BF16), grad)
                 low = (probs * (dp_ref[keys, :] - delta)).astype(BF16)
                 dk_acc[keys, :] += nn(low, query)
-                dqt_ref[rows, cols] += tn(k_ref[keys, :], low)[rows]
+                dqt_ref[:, cols] += tn(of_head(k_ref[keys, :], head), low)
 
             each_chunk(count, size, second)
     dq_ref[...] = dqt_ref[...].T.astype(BF16)
@@ -508,9 +548,11 @@
     dk_acc[...] = jnp.zeros_like(dk_acc)
     dv_acc[...] = jnp.zeros_like(dv_acc)
     blocks = targets // TILE
-    for head in range(2):
-        rows = slice(head * HEAD_DIM, (head + 1) * HEAD_DIM)
-        row = bias_ref[head : head + 1, :]
+    dqt_ref[...] = jnp.zeros_like(dqt_ref)
+
+    @pl.loop(0, 2)
+    def each_head(head):
+        row = row_of(bias_ref[...], head)
         tiles = [skewed(row, block) for block in range(blocks)]
         sums = [jnp.zeros((TILE, TILE), F32) for block in range(blocks)]
         for start in range(0, targets, QUERIES):
@@ -519,7 +561,7 @@
             query = of_head(q_ref[cols, :], head)
             grad = of_head(go_ref[cols, :], head)
             score = self_scores(k_ref, query, tiles, start)
-            probs = jnp.exp(score - lse_ref[head : head + 1, cols])
+            probs = jnp.exp(score - row_of(lse_ref[:, cols], head))
             grad_probs = nt(v_ref[:keys, :], grad)
             delta = jnp.sum(probs * grad_probs, axis=0, keepdims=True)
             dv_acc[:keys, :] += nn(probs.astype(BF16), grad)
@@ -531,7 +573,7 @@
                     ]
             low_scores = grad_scores.astype(BF16)
             dk_acc[:keys, :] += nn(low_scores, query)
-            dqt_ref[rows, cols] = tn(k_ref[:keys, :], low_scores)[rows]
+            dqt_ref[:, cols] += tn(of_head(k_ref[:keys, :], head), low_scores)
         lines = [unskewed(tile) for tile in sums]
         parts = []
         for block in range(blocks):
@@ -539,7 +581,9 @@
             if block + 1 < blocks:
                 part = part + lines[block + 1][:, :TILE]
             parts.append(part)
-        dbias_ref[head : head + 1, :] = jnp.concatenate(parts, axis=1)
+        row = jnp.concatenate(parts, axis=1)
+        line = lax.broadcasted_iota(jnp.int32, dbias_ref.shape, 0)
+        dbias_ref[...] = jnp.where(line == head, row, dbias_ref[...])
     dq_ref[...] = dqt_ref[...].T.astype(BF16)
     dk_ref[...] = dk_acc[...].astype(BF16)
     dv_ref[...] = dv_acc[...].astype(BF16)
@@ -713,7 +757,7 @@
             normed_ref[own, :] = (value * root_of(value) * gain).astype(BF16)
 
         each_rows(count, norm)
-    h_copy = pltpu.make_async_copy(h_ref, h_out, out_sems.at[18])
+    h_copy = pltpu.make_async_copy(h_ref, h_out, out_sems.at[36])
     h_copy.start()
     normed_t[...] = normed_ref[...].T
     down_ref[...] = jnp.zeros_like(down_ref)
@@ -721,12 +765,20 @@
     for copy in copies:
         copy.wait()
     hidden = weights_ref.shape[1] // 3
-    half = outs[0].shape[1]
-    sent = []
-
-    def tile(start):
+    tiles = hidden // HIDDEN
+
+    def sends(i):
+        copies = []
+        for k in range(3):
+            columns = slice(k * hidden + i * HIDDEN, k * hidden + (i + 1) * HIDDEN)
+            first = 6 * (i * 3 + k)
+            copies += deliver(grads_ref, outs, out_sems, columns, first)
+        return copies
+
+    @pl.loop(0, tiles)
+    def tile(i):
         gates, ups, downs = (
-            slice(k * hidden + start, k * hidden + start + HIDDEN) for k in range(3)
+            pl.ds(pl.multiple_of(k * hidden + i * HIDDEN, HIDDEN), HIDDEN) for k in range(3)
         )
         normed = normed_ref[...]
         gate = nn(normed, weights_ref[:, gates])
@@ -745,15 +797,19 @@
         grads_ref[:, gates] = nn(normed_t[...], grad_gate).astype(BF16)
         grads_ref[:, ups] = nn(normed_t[...], grad_up).astype(BF16)
         grads_ref[:, downs] = nn(cot_t_ref[...], act).astype(BF16)
-        for columns in (gates, ups, downs):
-            sent.extend(deliver(grads_ref, outs, out_sems, columns, len(sent)))
+        for each in range(tiles):
+
+            @pl.when(i == each)
+            def send():
+                for copy in sends(each):
+                    copy.start()
+
         back_ref[...] += nt(grad_gate, weights_ref[:, gates]) + nt(grad_up, weights_ref[:, ups])
         down_ref[...] += nt(act, weights_ref[:, downs])
 
-    for start in range(0, hidden, HIDDEN):
-        tile(start)
-    for copy in sent:
-        copy.wait()
+    for i in range(tiles):
+        for copy in sends(i):
+            copy.wait()
     h_copy.wait()
 
 
@@ -771,7 +827,7 @@
             pltpu.VMEM((targets, width), BF16),
             pltpu.VMEM((width, targets), BF16),
             pltpu.SemaphoreType.DMA((6,)),
-            pltpu.SemaphoreType.DMA((19,)),
+            pltpu.SemaphoreType.DMA((37,)),
         ],
         time=20,
         in_specs=[IN_VMEM] * 8 + [IN_PLACE] * 4,
@@ -1195,15 +1251,20 @@
         g_one, partial_five, peer_five, tokens, h_two, partial_down, peer_down, gains, turned
     )
     cross, layer_out = after((cross, layer_out))
-    cross = scatter_outer_parts(cross, 0, 1)
-    cross, last = after((cross, last))
-    cross = scatter_outer_send(cross, size)
-    last = scatter_second_parts(last, time=40)
-    last = scatter_second_send(last, size)
-    last, ffn = after((last, ffn))
-    last = scatter_outer_parts(last, 0, 1)
-    last, back, ffn = after((last, back, ffn))
-    last = scatter_outer_send(last, size)
+    if size == 16:
+        cross_keep, cross_out = scatter_pair_parts(cross)
+        cross_out, last = after((cross_out, last))
+        last = scatter_second_send(scatter_second_parts(last, time=40), size)
+        cross_in = swap(cross_out, 4, size)
+        last, ffn = after((last, ffn))
+        last = scatter_outer_parts(last, 0, 1)
+        last, cross_in, back, ffn = after((last, cross_in, back, ffn))
+        last = scatter_outer_send(last, size)
+        cross = scatter_pair_send(cross_keep, cross_in, size)
+    else:
+        cross = scatter_outer_send(scatter_outer_parts(cross, 0, 1), size)
+        last = scatter_second_send(scatter_second_parts(last), size)
+        last = scatter_outer_send(scatter_outer_parts(last, 0, 1), size)
     inverse = jnp.zeros_like(assign).at[assign].set(jnp.arange(size, dtype=jnp.int32))
     encoder_grad = back[:, :count][inverse]
     small = jnp.sum(back[:, count:].astype(F32), axis=0)

time: 320 us -> 315 us (0.984)
  starting transfers between devices: 78.2 us -> 62.8 us
  waiting for transfers between devices: 57.1 us -> 62.9 us
  Pallas kernels: 149 us -> 154 us
    ppermute x35 -> x34, starting transfers between devices: 62 us -> 49.9 us  [swap(): return lax.ppermute(value, 'dp', [(i, i ^ mask) for i in range(size)])]
    pallas_call x21, Pallas kernels: 149 us -> 154 us  [kernel_call(): pl.pallas_call(kernel, out_shape=outs, in_specs=in_specs or [everywhere]...]
    ppermute x35 -> x34, waiting for transfers between devices: 54.8 us -> 58.8 us  [swap(): return lax.ppermute(value, 'dp', [(i, i ^ mask) for i in range(size)])]
    unnamed x108 -> x106, local copies, waits for them, and re-layouts: 10.2 us -> 10.5 us
  transfers between devices with their start and end apart: 47 -> 46, of which waited for: 20 -> 23; matrix products, arithmetic and copies ran while one was open for 5% -> 6% of each run, Pallas kernels for 37% -> 39%
where the time goes in v4:
time: 315 us; the launch traced here: 313 us
  Pallas kernels  154 us (49%)
  waiting for transfers between devices  62.9 us (20%)
  starting transfers between devices  62.8 us (20%)
  local copies, waits for them, and re-layouts  23.8 us (8%)
  other arithmetic  5.82 us (2%)
  between operations  3.25 us (1%)
    pallas_call x21, Pallas kernels, kernel_call(): pl.pallas_call(kernel, out_shape=outs, in_specs=in_specs or [everywhere]...  154 us
    ppermute x34, waiting for transfers between devices, swap(): return lax.ppermute(value, 'dp', [(i, i ^ mask) for i in range(size)])  58.8 us
    ppermute x34, starting transfers between devices, swap(): return lax.ppermute(value, 'dp', [(i, i ^ mask) for i in range(size)])  49.9 us
    unnamed x106, local copies, waits for them, and re-layouts  10.5 us
  transfers between devices with their start and end apart: 46, of which 23 were waited for; matrix products, arithmetic and copies ran while one was open for 6% of the time, Pallas kernels for 39%

profile of v4, /device:TPU:0, one launch (start us, length us, event | category | flops | bytes accessed | tf_op | source)
XLA Modules:
  0.0 313.0 jit_solution(16594450482328574577)
XLA Ops:
  0.7 2.0 shard_map.350.refs_0_
  2.7 4.0 %collective-permute-start.1 = (bf16[48,3072]{1,0:T(8,128)(2,1)}, bf16[48,3072]{1,0:T(8,128)(2,1)S(1)}, u32[]{:S(2)}, u32[]{:S(2)}) collective-permute-start(bf16[48,3072]{1,0:T(8,128)(2,1)} %shard_map.350.refs_0_), channel_id=1, source_target_pairs={{0,16},{2,18},{4,20},{6,22},{8,24},{10,26},{12,28},{14,30},{16,0},... | collective-permute-start | bytes 884744 | tf_op jit(solution)/shard_map/ppermute | solution.py:53
  6.7 1.6 collective-permute-start
  11.4 1.9 shard_map.351.refs_0_
  13.2 1.5 gather_fusion
  17.0 3.4 %collective-permute-done.1.refs_2_ = bf16[48,3072]{1,0:T(8,128)(2,1)S(1)} collective-permute-done((bf16[48,3072]{1,0:T(8,128)(2,1)}, bf16[48,3072]{1,0:T(8,128)(2,1)S(1)}, u32[]{:S(2)}, u32[]{:S(2)}) %collective-permute-start.1) | collective-permute-done | bytes 294944 | tf_op jit(solution)/shard_map/ppermute | solution.py:53
  21.8 7.0 %shard_map.349 = (f32[512,768]{1,0:T(8,128)}, bf16[512,768]{1,0:T(8,128)(2,1)}, bf16[768,512]{1,0:T(8,128)(2,1)}, f32[8,768]{1,0:T(8,128)}, bf16[768,768]{1,0:T(...) custom-call(bf16[512,768]{1,0:T(8,128)(2,1)} %bitcast.29, bf16[512,768]{1,0:T(8,128)(2,1)} %bitcast.30, ...), custom_call_target="tpu_custom_call" | custom-call | flops 2000000000 | bytes 1 | tf_op jit(solution)/shard_map/pallas_call | solution.py:180
  29.6 2.4 shard_map.352
  32.0 1.5 collective-permute-start.3
  36.6 5.2 %all-to-all-start = ((bf16[16,64,384]{2,1,0:T(8,128)(2,1)}), bf16[16,64,384]{2,1,0:T(8,128)(2,1)S(1)}, u32[]{:S(2)}, u32[]{:S(2)}) async-start(bf16[16,64,384]{2,1,0:T(8,128)(2,1)} %gather_fusion), calls=%async_computation | async-start | bytes 1572864 | tf_op jit(solution)/shard_map/all_to_all | solution.py:1171
  42.5 8.9 %collective-permute-done.3.left_in_ref = bf16[192,1536]{1,0:T(8,128)(2,1)S(1)} collective-permute-done((bf16[192,1536]{1,0:T(8,128)(2,1)}, bf16[192,1536]{1,0:T(8,128)(2,1)S(1)}, u32[]{:S(2)}, u32[]{:S(2)}) %collective-permute-start.3) | collective-permute-done | bytes 589856 | tf_op jit(solution)/shard_map/ppermute | solution.py:53
  52.8 3.2 %shard_map.353 = (bf16[384,1536]{1,0:T(8,128)(2,1)}, bf16[384,1536]{1,0:T(8,128)(2,1)}) custom-call(bf16[192,1536]{1,0:T(8,128)(2,1)} %get-tuple-element.251.left_ref, bf16[192,1536]{1,0:T(8,128)(2,1)} %copy-done.37, bf16[192,1536]{1,0:T(8,128)(2,1)} %get-tuple-element.253.right_ref, bf16[192,1536]{1,0:T(8,128)(2,1)} %copy-done.38), custom_call_target="tpu_custom_call" | custom-call | flops 40000000000 | bytes 1 | tf_op jit(solution)/shard_map/pallas_call | solution.py:180
  56.0 2.3 collective-permute-start.5
  58.3 1.9 collective-permute-start.6
  60.2 3.5 %collective-permute-start.8 = (bf16[48,3072]{1,0:T(8,128)(2,1)S(1)}, bf16[48,3072]{1,0:T(8,128)(2,1)}, u32[]{:S(2)}, u32[]{:S(2)}) collective-permute-start(bf16[48,3072]{1,0:T(8,128)(2,1)S(1)} %copy-done.41), channel_id=1, source_target_pairs={{0,16},{2,18},{4,20},{6,22},{8,24},{10,26},{12,28},{14,30},{16,0},... | collective-permute-start | bytes 884744 | tf_op jit(solution)/shard_map/ppermute | solution.py:53
  63.7 9.8 %collective-permute-done.8.refs_2_ = bf16[48,3072]{1,0:T(8,128)(2,1)} collective-permute-done((bf16[48,3072]{1,0:T(8,128)(2,1)S(1)}, bf16[48,3072]{1,0:T(8,128)(2,1)}, u32[]{:S(2)}, u32[]{:S(2)}) %collective-permute-start.8) | collective-permute-done | bytes 294944 | tf_op jit(solution)/shard_map/ppermute | solution.py:53
  74.6 6.9 %collective-permute-done.9.refs_3_ = bf16[48,3072]{1,0:T(8,128)(2,1)S(1)} collective-permute-done((bf16[48,3072]{1,0:T(8,128)(2,1)}, bf16[48,3072]{1,0:T(8,128)(2,1)S(1)}, u32[]{:S(2)}, u32[]{:S(2)}) %collective-permute-start.9) | collective-permute-done | bytes 294944 | tf_op jit(solution)/shard_map/ppermute | solution.py:53
  81.4 1.8 collective-permute-done.5.refs_1_
  83.6 2.8 shard_map.354
  88.2 12.7 %shard_map.355 = (bf16[512,1152]{1,0:T(8,128)(2,1)}, bf16[512,384]{1,0:T(8,128)(2,1)}, f32[3,8,512]{2,1,0:T(8,128)}, f32[512,768]{1,0:T(8,128)}) custom-call(bf16[512,768]{1,0:T(8,128)(2,1)} %get-tuple-element.276.normed_ref, f32[3,8,512]{2,1,0:T(8,128)} %pad.4.bias_ref, bf16[384,1536]{1,0:T(8,128)(2,1)} %get-tuple-element.278.refs_0_, ...), custom_call_target="tpu_custom_call" | custom-call | flops 12000000000 | bytes 1 | tf_op jit(solution)/shard_map/pallas_call | solution.py:180
  100.9 1.6 collective-permute-done.10.left_in_ref
  103.8 3.2 %shard_map.356 = (bf16[384,1536]{1,0:T(8,128)(2,1)}, bf16[384,1536]{1,0:T(8,128)(2,1)}) custom-call(bf16[192,1536]{1,0:T(8,128)(2,1)} %get-tuple-element.285.left_ref, bf16[192,1536]{1,0:T(8,128)(2,1)} %copy-done.39, bf16[192,1536]{1,0:T(8,128)(2,1)} %get-tuple-element.287.right_ref, bf16[192,1536]{1,0:T(8,128)(2,1)} %copy-done.40), custom_call_target="tpu_custom_call" | custom-call | flops 2000000000 | bytes 1 | tf_op jit(solution)/shard_map/pallas_call | solution.py:180
  109.7 7.7 %shard_map.357 = (bf16[1024,768]{1,0:T(8,128)(2,1)}, bf16[1024,768]{1,0:T(8,128)(2,1)}) custom-call(s32[1]{0:T(128)} %bitcast.9.core_ref, bf16[1024,384]{1,0:T(8,128)(2,1)} %bitcast.26, bf16[1024,384]{1,0:T(8,128)(2,1)} %copy-done.28, bf16[768,768]{1,0:T(8,128)(2,1)} %get-tuple-element.297.order_ref, bf16[384,1536]{1,0:T(8,128)(2,1)} %get-tuple-element.298.refs_0_, ...), custom_call_target="tpu_custom_call" | custom-call | flops 8000000000 | bytes 1 | tf_op jit(solution)/shard_map/pallas_call | solution.py:180
  118.7 16.5 %shard_map.358 = (f32[512,768]{1,0:T(8,128)}, bf16[512,768]{1,0:T(8,128)(2,1)}, bf16[512,384]{1,0:T(8,128)(2,1)}, bf16[512,384]{1,0:T(8,128)(2,1)}, f32[3,8,512]...) custom-call(f32[512,768]{1,0:T(8,128)} %get-tuple-element.235.tokens_ref, ...), custom_call_target="tpu_custom_call" | custom-call | flops 16000000000 | bytes 1 | tf_op jit(solution)/shard_map/pallas_call | solution.py:180
  139.8 17.1 %shard_map.359 = (f32[512,768]{1,0:T(8,128)}, f32[512,768]{1,0:T(8,128)}, f32[512,768]{1,0:T(8,128)}, bf16[384,1536]{1,0:T(8,128)(2,1)}, bf16[384,1536]{1,0:T(8,...) custom-call(f32[512,768]{1,0:T(8,128)} %get-tuple-element.302.before_ref.h_ref, ...), custom_call_target="tpu_custom_call" | custom-call | flops 20000000000 | bytes 1 | tf_op jit(solution)/shard_map/pallas_call | solution.py:180
  158.9 1.7 collective-permute-done.20.peer_ref
  161.7 19.9 %shard_map.360 = (f32[512,768]{1,0:T(8,128)}, bf16[512,768]{1,0:T(8,128)(2,1)}, bf16[512,384]{1,0:T(8,128)(2,1)}, bf16[1024,768]{1,0:T(8,128)(2,1)}, f32[512,768]{1,0:T(8,128)}, /*index=5*/f32[8,768]{1,0:T(8,128)}) custom-call(bf16[512,768]{1,0:T(8,128)(2,1)} %get-tuple-element.305.cot_ref, f32[512,768]{1,0:T(8,128)} %get-tuple-element.313.partial_ref, ...), custom_call_target="tpu_custom_call" | custom-call | flops 17999998976 | bytes 1 | tf_op jit(solution)/shard_map/pallas_call | solution.py:180
  181.6 4.0 %collective-permute-done.18.left_in_ref.refs_1_ = bf16[384,1536]{1,0:T(8,128)(2,1)S(1)} collective-permute-done((bf16[384,1536]{1,0:T(8,128)(2,1)}, bf16[384,1536]{1,0:T(8,128)(2,1)S(1)}, u32[]{:S(2)}, u32[]{:S(2)}) %collective-permute-start.18) | collective-permute-done | bytes 1179680 | tf_op jit(solution)/shard_map/ppermute | solution.py:53
  187.2 2.9 shard_map.361
  191.9 12.5 %shard_map.362 = (bf16[1024,384]{1,0:T(8,128)(2,1)}, bf16[1024,384]{1,0:T(8,128)(2,1)}, bf16[384,768]{1,0:T(8,128)(2,1)}, bf16[384,768]{1,0:T(8,128)(2,1)}, bf16...) custom-call(s32[1]{0:T(128)} %bitcast.9.core_ref, bf16[512,768]{1,0:T(8,128)(2,1)} %get-tuple-element.338.normed_ref, ...), custom_call_target="tpu_custom_call" | custom-call | flops 12000000000 | bytes 1 | tf_op jit(solution)/shard_map/pallas_call | solution.py:180
  204.4 1.7 collective-permute-done.22.refs_2_
  207.2 3.4 %shard_map.363 = (f32[48,3072]{1,0:T(8,128)}, bf16[48,3072]{1,0:T(8,128)(2,1)}, bf16[48,3072]{1,0:T(8,128)(2,1)}, bf16[48,3072]{1,0:T(8,128)(2,1)}) custom-call(bf16[384,1536]{1,0:T(8,128)(2,1)} %get-tuple-element.352.left_ref.refs_0_, bf16[384,1536]{1,0:T(8,128)(2,1)} %copy-done.23, bf16[192,1536]{1,0:T(8,128)(2,1)} %copy-done.35, ...), custom_call_target="tpu_custom_call" | custom-call | flops 2000000000 | bytes 1 | tf_op jit(solution)/shard_map/pallas_call | solution.py:180
  211.8 1.5 collective-permute-start.29
  213.3 3.8 %collective-permute-start.26 = (bf16[48,3072]{1,0:T(8,128)(2,1)}, bf16[48,3072]{1,0:T(8,128)(2,1)S(1)}, u32[]{:S(2)}, u32[]{:S(2)}) collective-permute-start(bf16[48,3072]{1,0:T(8,128)(2,1)} %get-tuple-element.371), channel_id=1, source_target_pairs={{0,16},{2,18},{4,20},{6,22},{8,24},{10,26},{12,28},{14,30},{16,0},... | collective-permute-start | bytes 884744 | tf_op jit(solution)/shard_map/ppermute | solution.py:53
  217.7 23.1 %shard_map.364 = (f32[512,768]{1,0:T(8,128)}, f32[512,768]{1,0:T(8,128)}, bf16[16,384]{1,0:T(8,128)(2,1)}, bf16[384,768]{1,0:T(8,128)(2,1)}, bf16[384,768]{1,0:T...) custom-call(f32[512,768]{1,0:T(8,128)} %get-tuple-element.378.g_in_ref, ...), custom_call_target="tpu_custom_call" | custom-call | flops 22000001024 | bytes 1 | tf_op jit(solution)/shard_map/pallas_call | solution.py:180
  242.7 2.2 shard_map.365
  250.2 5.8 %all-to-all-start.1 = ((bf16[16,80,384]{2,1,0:T(8,128)(2,1)}), bf16[16,80,384]{2,1,0:T(8,128)(2,1)S(1)}, u32[]{:S(2)}, u32[]{:S(2)}) async-start(bf16[16,80,384]{2,1,0:T(8,128)(2,1)} %pad_maximum_fusion), calls=%async_computation.1 | async-start | bytes 1966080 | tf_op jit(solution)/shard_map/all_to_all | solution.py:1249
  256.0 7.1 %shard_map.366 = (f32[512,768]{1,0:T(8,128)}, bf16[512,768]{1,0:T(8,128)(2,1)}) custom-call(f32[512,768]{1,0:T(8,128)} %get-tuple-element.396.g_ref, f32[512,768]{1,0:T(8,128)} %get-tuple-element.397.partial_ref, f32[512,768]{1,0:T(8,128)} %collective-permute-done.32.peer_ref, f32[512,768]{1,0:T(8,128)} %get-tuple-element.235.tokens_ref, ...), custom_call_target="tpu_custom_call" | custom-call | flops 8000000000 | bytes 1 | tf_op jit(solution)/shard_map/pallas_call | solution.py:180
  264.0 2.5 shard_map.367
  266.5 7.4 %collective-permute-done.33.left_in_ref.refs_1_ = bf16[384,768]{1,0:T(8,128)(2,1)} collective-permute-done((bf16[384,768]{1,0:T(8,128)(2,1)}, bf16[384,768]{1,0:T(8,128)(2,1)}, u32[]{:S(2)}, u32[]{:S(2)}) %collective-permute-start.33) | collective-permute-done | bytes 589856 | tf_op jit(solution)/shard_map/ppermute | solution.py:53
  274.0 2.2 shard_map.368
  277.3 1.7 collective-permute-start.36
  280.2 2.9 collective-permute-done.35.refs_2_
  285.0 2.4 shard_map.369
  290.0 5.7 %collective-permute-start.43 = (bf16[48,1536]{1,0:T(8,128)(2,1)S(1)}, bf16[48,1536]{1,0:T(8,128)(2,1)}, u32[]{:S(2)}, u32[]{:S(2)}) collective-permute-start(bf16[48,1536]{1,0:T(8,128)(2,1)S(1)} %slice.129), channel_id=1, source_target_pairs={{0,16},{2,18},{4,20},{6,22},{8,24},{10,26},{12,28},{14,30},{16,0},... | collective-permute-start | bytes 442376 | tf_op jit(solution)/shard_map/ppermute | solution.py:53
  295.9 4.2 %collective-permute-start.42 = (bf16[48,1536]{1,0:T(8,128)(2,1)}, bf16[48,1536]{1,0:T(8,128)(2,1)}, u32[]{:S(2)}, u32[]{:S(2)}) collective-permute-start(bf16[48,1536]{1,0:T(8,128)(2,1)} %get-tuple-element.445), channel_id=1, source_target_pairs={{0,24},{2,26},{4,28},{6,30},{8,16},{10,18},{12,20},{14,22},{16,8},... | collective-permute-start | bytes 442376 | tf_op jit(solution)/shard_map/ppermute | solution.py:53
  301.9 1.5 gather_fusion.1
  305.7 5.4 %collective-permute-done.41 = bf16[48,1536]{1,0:T(8,128)(2,1)} collective-permute-done((bf16[48,1536]{1,0:T(8,128)(2,1)}, bf16[48,1536]{1,0:T(8,128)(2,1)}, u32[]{:S(2)}, u32[]{:S(2)}) %collective-permute-start.41) | collective-permute-done | bytes 147488 | tf_op jit(solution)/shard_map/ppermute | solution.py:53
  (224 shorter events, 54.0 us)
Async XLA Ops:
  2.7 17.7 %collective-permute-start.1 = (bf16[48,3072]{1,0:T(8,128)(2,1)}, bf16[48,3072]{1,0:T(8,128)(2,1)S(1)}, u32[]{:S(2)}, u32[]{:S(2)}) collective-permute-start(bf16[48,3072]{1,0:T(8,128)(2,1)} %shard_map.350.refs_0_), channel_id=1, source_target_pairs={{0,16},{2,18},{4,20},{6,22},{8,24},{10,26},{12,28},{14,30},{16,0},... | collective-permute-start | bytes 884744 | tf_op jit(solution)/shard_map/ppermute | solution.py:53
  6.7 22.1 %collective-permute-start = (bf16[48,3072]{1,0:T(8,128)(2,1)}, bf16[48,3072]{1,0:T(8,128)(2,1)S(1)}, u32[]{:S(2)}, u32[]{:S(2)}) collective-permute-start(bf16[48,3072]{1,0:T(8,128)(2,1)} %shard_map.350.refs_0_), channel_id=1, source_target_pairs={{0,8},{2,10},{4,12},{6,14},{8,0},{10,2},{12,4},{14,6},{16,24},{18,... | collective-permute-start | bytes 884744 | tf_op jit(solution)/shard_map/ppermute | solution.py:53
  11.3 23.8 %copy-start.3 = (s32[512,128]{1,0:T(8,128)}, s32[512,128]{1,0:T(8,128)S(1)}, u32[]{:S(2)}) copy-start(s32[512,128]{1,0:T(8,128)S(1)} %slice.73.labels_ref) | copy-start | bytes 786436
  20.4 8.4 %collective-permute-start.2 = (bf16[48,3072]{1,0:T(8,128)(2,1)S(1)}, bf16[48,3072]{1,0:T(8,128)(2,1)S(1)}, u32[]{:S(2)}, u32[]{:S(2)}) collective-permute-start(bf16[48,3072]{1,0:T(8,128)(2,1)S(1)} %collective-permute-done.1.refs_2_), channel_id=1, source_target_pairs={{0,8},{2,10},{4,12},{6,14},{8,0},{10,2},{12,4},{14,6},{16,24},{18,... | collective-permute-start | bytes 884744 | tf_op jit(solution)/shard_map/ppermute | solution.py:53
  32.0 19.4 %collective-permute-start.3 = (bf16[192,1536]{1,0:T(8,128)(2,1)}, bf16[192,1536]{1,0:T(8,128)(2,1)S(1)}, u32[]{:S(2)}, u32[]{:S(2)}) collective-permute-start(bf16[192,1536]{1,0:T(8,128)(2,1)} %get-tuple-element.251.left_ref), channel_id=1, source_target_pairs={{0,4},{2,6},{4,0},{6,2},{8,12},{10,14},{12,8},{14,10},{16,20},{18,... | collective-permute-start | bytes 1769480 | tf_op jit(solution)/shard_map/ppermute | solution.py:53
  33.5 18.3 %collective-permute-start.4 = (bf16[192,1536]{1,0:T(8,128)(2,1)}, bf16[192,1536]{1,0:T(8,128)(2,1)S(1)}, u32[]{:S(2)}, u32[]{:S(2)}) collective-permute-start(bf16[192,1536]{1,0:T(8,128)(2,1)} %get-tuple-element.253.right_ref), channel_id=1, source_target_pairs={{0,2},{2,0},{4,6},{6,4},{8,10},{10,8},{12,14},{14,12},{16,18},{18,... | collective-permute-start | bytes 1769480 | tf_op jit(solution)/shard_map/ppermute | solution.py:53
  36.6 36.9 %all-to-all-start = ((bf16[16,64,384]{2,1,0:T(8,128)(2,1)}), bf16[16,64,384]{2,1,0:T(8,128)(2,1)S(1)}, u32[]{:S(2)}, u32[]{:S(2)}) async-start(bf16[16,64,384]{2,1,0:T(8,128)(2,1)} %gather_fusion), calls=%async_computation | async-start | bytes 1572864 | tf_op jit(solution)/shard_map/all_to_all | solution.py:1171
  56.0 27.2 %collective-permute-start.5 = (bf16[384,1536]{1,0:T(8,128)(2,1)}, bf16[384,1536]{1,0:T(8,128)(2,1)S(1)}, u32[]{:S(2)}, u32[]{:S(2)}) collective-permute-start(bf16[384,1536]{1,0:T(8,128)(2,1)} %get-tuple-element.278.refs_0_), channel_id=1, source_target_pairs={{0,2},{2,0},{4,6},{6,4},{8,10},{10,8},{12,14},{14,12},{16,18},{18,... | collective-permute-start | bytes 3538952 | tf_op jit(solution)/shard_map/ppermute | solution.py:53
  58.3 25.3 %collective-permute-start.6 = (bf16[384,1536]{1,0:T(8,128)(2,1)}, bf16[384,1536]{1,0:T(8,128)(2,1)S(1)}, u32[]{:S(2)}, u32[]{:S(2)}) collective-permute-start(bf16[384,1536]{1,0:T(8,128)(2,1)} %get-tuple-element.298.refs_0_), channel_id=1, source_target_pairs={{0,4},{2,6},{4,0},{6,2},{8,12},{10,14},{12,8},{14,10},{16,20},{18,... | collective-permute-start | bytes 3538952 | tf_op jit(solution)/shard_map/ppermute | solution.py:53
  60.2 13.3 %collective-permute-start.8 = (bf16[48,3072]{1,0:T(8,128)(2,1)S(1)}, bf16[48,3072]{1,0:T(8,128)(2,1)}, u32[]{:S(2)}, u32[]{:S(2)}) collective-permute-start(bf16[48,3072]{1,0:T(8,128)(2,1)S(1)} %copy-done.41), channel_id=1, source_target_pairs={{0,16},{2,18},{4,20},{6,22},{8,24},{10,26},{12,28},{14,30},{16,0},... | collective-permute-start | bytes 884744 | tf_op jit(solution)/shard_map/ppermute | solution.py:53
  63.6 10.9 %collective-permute-start.7 = (bf16[48,3072]{1,0:T(8,128)(2,1)S(1)}, bf16[48,3072]{1,0:T(8,128)(2,1)}, u32[]{:S(2)}, u32[]{:S(2)}) collective-permute-start(bf16[48,3072]{1,0:T(8,128)(2,1)S(1)} %copy-done.41), channel_id=1, source_target_pairs={{0,8},{2,10},{4,12},{6,14},{8,0},{10,2},{12,4},{14,6},{16,24},{18,... | collective-permute-start | bytes 884744 | tf_op jit(solution)/shard_map/ppermute | solution.py:53
  73.5 7.9 %collective-permute-start.9 = (bf16[48,3072]{1,0:T(8,128)(2,1)}, bf16[48,3072]{1,0:T(8,128)(2,1)S(1)}, u32[]{:S(2)}, u32[]{:S(2)}) collective-permute-start(bf16[48,3072]{1,0:T(8,128)(2,1)} %collective-permute-done.8.refs_2_), channel_id=1, source_target_pairs={{0,8},{2,10},{4,12},{6,14},{8,0},{10,2},{12,4},{14,6},{16,24},{18,... | collective-permute-start | bytes 884744 | tf_op jit(solution)/shard_map/ppermute | solution.py:53
  86.4 16.4 %collective-permute-start.12 = (bf16[1024,384]{1,0:T(8,128)(2,1)S(1)}, bf16[1024,384]{1,0:T(8,128)(2,1)S(1)}, u32[]{:S(2)}, u32[]{:S(2)}) collective-permute-start(bf16[1024,384]{1,0:T(8,128)(2,1)S(1)} %bitcast.25), channel_id=1, source_target_pairs={{0,1},{1,0},{2,3},{3,2},{4,5},{5,4},{6,7},{7,6},{8,9},{9,8},{10,11... | collective-permute-start | bytes 2359304 | tf_op jit(solution)/shard_map/ppermute | solution.py:57
  86.5 16.0 %collective-permute-start.10 = (bf16[192,1536]{1,0:T(8,128)(2,1)}, bf16[192,1536]{1,0:T(8,128)(2,1)S(1)}, u32[]{:S(2)}, u32[]{:S(2)}) collective-permute-start(bf16[192,1536]{1,0:T(8,128)(2,1)} %get-tuple-element.285.left_ref), channel_id=1, source_target_pairs={{0,4},{2,6},{4,0},{6,2},{8,12},{10,14},{12,8},{14,10},{16,20},{18,... | collective-permute-start | bytes 1769480 | tf_op jit(solution)/shard_map/ppermute | solution.py:53
  87.1 15.6 %collective-permute-start.11 = (bf16[192,1536]{1,0:T(8,128)(2,1)}, bf16[192,1536]{1,0:T(8,128)(2,1)S(1)}, u32[]{:S(2)}, u32[]{:S(2)}) collective-permute-start(bf16[192,1536]{1,0:T(8,128)(2,1)} %get-tuple-element.287.right_ref), channel_id=1, source_target_pairs={{0,2},{2,0},{4,6},{6,4},{8,10},{10,8},{12,14},{14,12},{16,18},{18,... | collective-permute-start | bytes 1769480 | tf_op jit(solution)/shard_map/ppermute | solution.py:53
  107.0 10.4 %collective-permute-start.13 = (f32[512,768]{1,0:T(8,128)S(1)}, f32[512,768]{1,0:T(8,128)S(1)}, u32[]{:S(2)}, u32[]{:S(2)}) collective-permute-start(f32[512,768]{1,0:T(8,128)S(1)} %copy-done.18), channel_id=1, source_target_pairs={{0,1},{1,0},{2,3},{3,2},{4,5},{5,4},{6,7},{7,6},{8,9},{9,8},{10,11... | collective-permute-start | bytes 4718600 | tf_op jit(solution)/shard_map/ppermute | solution.py:57
  107.0 28.7 %collective-permute-start.16 = (bf16[384,1536]{1,0:T(8,128)(2,1)}, bf16[384,1536]{1,0:T(8,128)(2,1)S(1)}, u32[]{:S(2)}, u32[]{:S(2)}) collective-permute-start(bf16[384,1536]{1,0:T(8,128)(2,1)} %get-tuple-element.307.refs_0_), channel_id=1, source_target_pairs={{0,2},{2,0},{4,6},{6,4},{8,10},{10,8},{12,14},{14,12},{16,18},{18,... | collective-permute-start | bytes 3538952 | tf_op jit(solution)/shard_map/ppermute | solution.py:53
  108.2 28.3 %collective-permute-start.17 = (bf16[384,1536]{1,0:T(8,128)(2,1)}, bf16[384,1536]{1,0:T(8,128)(2,1)S(1)}, u32[]{:S(2)}, u32[]{:S(2)}) collective-permute-start(bf16[384,1536]{1,0:T(8,128)(2,1)} %get-tuple-element.308.refs_2_), channel_id=1, source_target_pairs={{0,4},{2,6},{4,0},{6,2},{8,12},{10,14},{12,8},{14,10},{16,20},{18,... | collective-permute-start | bytes 3538952 | tf_op jit(solution)/shard_map/ppermute | solution.py:53
  135.2 2.6 collective-permute-start.14
  135.3 3.6 %collective-permute-start.15 = (f32[256,768]{1,0:T(8,128)}, f32[256,768]{1,0:T(8,128)S(1)}, u32[]{:S(2)}, u32[]{:S(2)}) collective-permute-start(f32[256,768]{1,0:T(8,128)} %get-tuple-element.304.second_ref), channel_id=1, source_target_pairs={{0,1},{1,0},{2,3},{3,2},{4,5},{5,4},{6,7},{7,6},{8,9},{9,8},{10,11... | collective-permute-start | bytes 2359304 | tf_op jit(solution)/shard_map/ppermute | solution.py:57
  156.9 3.7 %collective-permute-start.20 = (f32[512,768]{1,0:T(8,128)}, f32[512,768]{1,0:T(8,128)S(1)}, u32[]{:S(2)}, u32[]{:S(2)}) collective-permute-start(f32[512,768]{1,0:T(8,128)} %get-tuple-element.313.partial_ref), channel_id=1, source_target_pairs={{0,1},{1,0},{2,3},{3,2},{4,5},{5,4},{6,7},{7,6},{8,9},{9,8},{10,11... | collective-permute-start | bytes 4718600 | tf_op jit(solution)/shard_map/ppermute | solution.py:57
  157.1 29.2 %collective-permute-start.21 = (f32[512,768]{1,0:T(8,128)}, f32[512,768]{1,0:T(8,128)S(1)}, u32[]{:S(2)}, u32[]{:S(2)}) collective-permute-start(f32[512,768]{1,0:T(8,128)} %get-tuple-element.321.down_ref), channel_id=1, source_target_pairs={{0,1},{1,0},{2,3},{3,2},{4,5},{5,4},{6,7},{7,6},{8,9},{9,8},{10,11... | collective-permute-start | bytes 4718600 | tf_op jit(solution)/shard_map/ppermute | solution.py:57
  157.4 28.2 %collective-permute-start.18 = (bf16[384,1536]{1,0:T(8,128)(2,1)}, bf16[384,1536]{1,0:T(8,128)(2,1)S(1)}, u32[]{:S(2)}, u32[]{:S(2)}) collective-permute-start(bf16[384,1536]{1,0:T(8,128)(2,1)} %get-tuple-element.311), channel_id=1, source_target_pairs={{0,2},{2,0},{4,6},{6,4},{8,10},{10,8},{12,14},{14,12},{16,18},{18,... | collective-permute-start | bytes 3538952 | tf_op jit(solution)/shard_map/ppermute | solution.py:53
  158.3 27.9 %collective-permute-start.19 = (bf16[384,1536]{1,0:T(8,128)(2,1)}, bf16[384,1536]{1,0:T(8,128)(2,1)S(1)}, u32[]{:S(2)}, u32[]{:S(2)}) collective-permute-start(bf16[384,1536]{1,0:T(8,128)(2,1)} %get-tuple-element.312), channel_id=1, source_target_pairs={{0,4},{2,6},{4,0},{6,2},{8,12},{10,14},{12,8},{14,10},{16,20},{18,... | collective-permute-start | bytes 3538952 | tf_op jit(solution)/shard_map/ppermute | solution.py:53
  190.1 16.3 %collective-permute-start.24 = (f32[512,768]{1,0:T(8,128)S(1)}, f32[512,768]{1,0:T(8,128)S(1)}, u32[]{:S(2)}, u32[]{:S(2)}) collective-permute-start(f32[512,768]{1,0:T(8,128)S(1)} %copy-done.16), channel_id=1, source_target_pairs={{0,1},{1,0},{2,3},{3,2},{4,5},{5,4},{6,7},{7,6},{8,9},{9,8},{10,11... | collective-permute-start | bytes 4718600 | tf_op jit(solution)/shard_map/ppermute | solution.py:57
  190.1 16.0 %collective-permute-start.22 = (bf16[192,1536]{1,0:T(8,128)(2,1)}, bf16[192,1536]{1,0:T(8,128)(2,1)S(1)}, u32[]{:S(2)}, u32[]{:S(2)}) collective-permute-start(bf16[192,1536]{1,0:T(8,128)(2,1)} %get-tuple-element.336), channel_id=1, source_target_pairs={{0,4},{2,6},{4,0},{6,2},{8,12},{10,14},{12,8},{14,10},{16,20},{18,... | collective-permute-start | bytes 1769480 | tf_op jit(solution)/shard_map/ppermute | solution.py:53
  190.8 15.6 %collective-permute-start.23 = (bf16[192,1536]{1,0:T(8,128)(2,1)}, bf16[192,1536]{1,0:T(8,128)(2,1)S(1)}, u32[]{:S(2)}, u32[]{:S(2)}) collective-permute-start(bf16[192,1536]{1,0:T(8,128)(2,1)} %get-tuple-element.337), channel_id=1, source_target_pairs={{0,2},{2,0},{4,6},{6,4},{8,10},{10,8},{12,14},{14,12},{16,18},{18,... | collective-permute-start | bytes 1769480 | tf_op jit(solution)/shard_map/ppermute | solution.py:53
  210.6 30.3 %collective-permute-start.28 = (bf16[384,768]{1,0:T(8,128)(2,1)S(1)}, bf16[384,768]{1,0:T(8,128)(2,1)S(1)}, u32[]{:S(2)}, u32[]{:S(2)}) collective-permute-start(bf16[384,768]{1,0:T(8,128)(2,1)S(1)} %copy-done.34), channel_id=1, source_target_pairs={{0,2},{2,0},{4,6},{6,4},{8,10},{10,8},{12,14},{14,12},{16,18},{18,... | collective-permute-start | bytes 1769480 | tf_op jit(solution)/shard_map/ppermute | solution.py:53
  211.8 29.1 %collective-permute-start.29 = (bf16[384,768]{1,0:T(8,128)(2,1)S(1)}, bf16[384,768]{1,0:T(8,128)(2,1)S(1)}, u32[]{:S(2)}, u32[]{:S(2)}) collective-permute-start(bf16[384,768]{1,0:T(8,128)(2,1)S(1)} %copy-done.33), channel_id=1, source_target_pairs={{0,4},{2,6},{4,0},{6,2},{8,12},{10,14},{12,8},{14,10},{16,20},{18,... | collective-permute-start | bytes 1769480 | tf_op jit(solution)/shard_map/ppermute | solution.py:53
  213.3 27.5 %collective-permute-start.25 = (bf16[48,3072]{1,0:T(8,128)(2,1)}, bf16[48,3072]{1,0:T(8,128)(2,1)S(1)}, u32[]{:S(2)}, u32[]{:S(2)}) collective-permute-start(bf16[48,3072]{1,0:T(8,128)(2,1)} %get-tuple-element.370), channel_id=1, source_target_pairs={{0,8},{2,10},{4,12},{6,14},{8,0},{10,2},{12,4},{14,6},{16,24},{18,... | collective-permute-start | bytes 884744 | tf_op jit(solution)/shard_map/ppermute | solution.py:53
  213.3 27.6 %collective-permute-start.26 = (bf16[48,3072]{1,0:T(8,128)(2,1)}, bf16[48,3072]{1,0:T(8,128)(2,1)S(1)}, u32[]{:S(2)}, u32[]{:S(2)}) collective-permute-start(bf16[48,3072]{1,0:T(8,128)(2,1)} %get-tuple-element.371), channel_id=1, source_target_pairs={{0,16},{2,18},{4,20},{6,22},{8,24},{10,26},{12,28},{14,30},{16,0},... | collective-permute-start | bytes 884744 | tf_op jit(solution)/shard_map/ppermute | solution.py:53
  217.1 23.7 %collective-permute-start.27 = (bf16[48,3072]{1,0:T(8,128)(2,1)}, bf16[48,3072]{1,0:T(8,128)(2,1)S(1)}, u32[]{:S(2)}, u32[]{:S(2)}) collective-permute-start(bf16[48,3072]{1,0:T(8,128)(2,1)} %get-tuple-element.372), channel_id=1, source_target_pairs={{0,24},{2,26},{4,28},{6,30},{8,16},{10,18},{12,20},{14,22},{16,8},... | collective-permute-start | bytes 884744 | tf_op jit(solution)/shard_map/ppermute | solution.py:53
  217.7 23.3 %copy-start.27 = (bf16[1024,384]{1,0:T(8,128)(2,1)S(1)}, bf16[1024,384]{1,0:T(8,128)(2,1)}, u32[]{:S(2)}) copy-start(bf16[1024,384]{1,0:T(8,128)(2,1)} %get-tuple-element.435) | copy-start | bytes 2359300
  240.9 15.1 %collective-permute-start.32 = (f32[512,768]{1,0:T(8,128)}, f32[512,768]{1,0:T(8,128)}, u32[]{:S(2)}, u32[]{:S(2)}) collective-permute-start(f32[512,768]{1,0:T(8,128)} %get-tuple-element.397.partial_ref), channel_id=1, source_target_pairs={{0,1},{1,0},{2,3},{3,2},{4,5},{5,4},{6,7},{7,6},{8,9},{9,8},{10,11... | collective-permute-start | bytes 4718600 | tf_op jit(solution)/shard_map/ppermute | solution.py:57
  241.0 6.8 %collective-permute-start.38 = (bf16[1024,384]{1,0:T(8,128)(2,1)S(1)}, bf16[1024,384]{1,0:T(8,128)(2,1)S(1)}, u32[]{:S(2)}, u32[]{:S(2)}) collective-permute-start(bf16[1024,384]{1,0:T(8,128)(2,1)S(1)} %copy-done.27), channel_id=1, source_target_pairs={{0,1},{1,0},{2,3},{3,2},{4,5},{5,4},{6,7},{7,6},{8,9},{9,8},{10,11... | collective-permute-start | bytes 2359304 | tf_op jit(solution)/shard_map/ppermute | solution.py:57
  244.9 18.3 %collective-permute-start.30 = (bf16[192,768]{1,0:T(8,128)(2,1)}, bf16[192,768]{1,0:T(8,128)(2,1)S(1)}, u32[]{:S(2)}, u32[]{:S(2)}) collective-permute-start(bf16[192,768]{1,0:T(8,128)(2,1)} %get-tuple-element.394), channel_id=1, source_target_pairs={{0,4},{2,6},{4,0},{6,2},{8,12},{10,14},{12,8},{14,10},{16,20},{18,... | collective-permute-start | bytes 884744 | tf_op jit(solution)/shard_map/ppermute | solution.py:53
  245.7 17.4 %collective-permute-start.31 = (bf16[192,768]{1,0:T(8,128)(2,1)}, bf16[192,768]{1,0:T(8,128)(2,1)S(1)}, u32[]{:S(2)}, u32[]{:S(2)}) collective-permute-start(bf16[192,768]{1,0:T(8,128)(2,1)} %get-tuple-element.395), channel_id=1, source_target_pairs={{0,2},{2,0},{4,6},{6,4},{8,10},{10,8},{12,14},{14,12},{16,18},{18,... | collective-permute-start | bytes 884744 | tf_op jit(solution)/shard_map/ppermute | solution.py:53
  247.0 26.9 %collective-permute-start.33 = (bf16[384,768]{1,0:T(8,128)(2,1)}, bf16[384,768]{1,0:T(8,128)(2,1)}, u32[]{:S(2)}, u32[]{:S(2)}) collective-permute-start(bf16[384,768]{1,0:T(8,128)(2,1)} %get-tuple-element.411), channel_id=1, source_target_pairs={{0,2},{2,0},{4,6},{6,4},{8,10},{10,8},{12,14},{14,12},{16,18},{18,... | collective-permute-start | bytes 1769480 | tf_op jit(solution)/shard_map/ppermute | solution.py:53
  247.8 26.3 %collective-permute-start.34 = (bf16[384,768]{1,0:T(8,128)(2,1)}, bf16[384,768]{1,0:T(8,128)(2,1)}, u32[]{:S(2)}, u32[]{:S(2)}) collective-permute-start(bf16[384,768]{1,0:T(8,128)(2,1)} %get-tuple-element.412), channel_id=1, source_target_pairs={{0,4},{2,6},{4,0},{6,2},{8,12},{10,14},{12,8},{14,10},{16,20},{18,... | collective-permute-start | bytes 1769480 | tf_op jit(solution)/shard_map/ppermute | solution.py:53
  250.2 37.2 %all-to-all-start.1 = ((bf16[16,80,384]{2,1,0:T(8,128)(2,1)}), bf16[16,80,384]{2,1,0:T(8,128)(2,1)S(1)}, u32[]{:S(2)}, u32[]{:S(2)}) async-start(bf16[16,80,384]{2,1,0:T(8,128)(2,1)} %pad_maximum_fusion), calls=%async_computation.1 | async-start | bytes 1966080 | tf_op jit(solution)/shard_map/all_to_all | solution.py:1249
  276.2 7.0 %collective-permute-start.35 = (bf16[192,768]{1,0:T(8,128)(2,1)}, bf16[192,768]{1,0:T(8,128)(2,1)S(1)}, u32[]{:S(2)}, u32[]{:S(2)}) collective-permute-start(bf16[192,768]{1,0:T(8,128)(2,1)} %get-tuple-element.417), channel_id=1, source_target_pairs={{0,4},{2,6},{4,0},{6,2},{8,12},{10,14},{12,8},{14,10},{16,20},{18,... | collective-permute-start | bytes 884744 | tf_op jit(solution)/shard_map/ppermute | solution.py:53
  277.3 6.9 %collective-permute-start.36 = (bf16[192,768]{1,0:T(8,128)(2,1)}, bf16[192,768]{1,0:T(8,128)(2,1)S(1)}, u32[]{:S(2)}, u32[]{:S(2)}) collective-permute-start(bf16[192,768]{1,0:T(8,128)(2,1)} %get-tuple-element.418), channel_id=1, source_target_pairs={{0,2},{2,0},{4,6},{6,4},{8,10},{10,8},{12,14},{14,12},{16,18},{18,... | collective-permute-start | bytes 884744 | tf_op jit(solution)/shard_map/ppermute | solution.py:53
  279.0 8.4 %collective-permute-start.37 = (bf16[96,1536]{1,0:T(8,128)(2,1)S(1)}, bf16[96,1536]{1,0:T(8,128)(2,1)S(1)}, u32[]{:S(2)}, u32[]{:S(2)}) collective-permute-start(bf16[96,1536]{1,0:T(8,128)(2,1)S(1)} %copy-done.46), channel_id=1, source_target_pairs={{0,8},{2,10},{4,12},{6,14},{8,0},{10,2},{12,4},{14,6},{16,24},{18,... | collective-permute-start | bytes 884744 | tf_op jit(solution)/shard_map/ppermute | solution.py:53
  287.5 16.0 %collective-permute-start.39 = (f32[8,384]{1,0:T(8,128)S(1)}, f32[8,384]{1,0:T(8,128)S(1)}, u32[]{:S(2)}, u32[]{:S(2)}) collective-permute-start(f32[8,384]{1,0:T(8,128)S(1)} %slice_add_fusion.1), channel_id=1, source_target_pairs={{0,1},{1,0},{2,3},{3,2},{4,5},{5,4},{6,7},{7,6},{8,9},{9,8},{10,11... | collective-permute-start | bytes 36872 | tf_op jit(solution)/shard_map/ppermute | solution.py:57
  290.0 14.1 %collective-permute-start.43 = (bf16[48,1536]{1,0:T(8,128)(2,1)S(1)}, bf16[48,1536]{1,0:T(8,128)(2,1)}, u32[]{:S(2)}, u32[]{:S(2)}) collective-permute-start(bf16[48,1536]{1,0:T(8,128)(2,1)S(1)} %slice.129), channel_id=1, source_target_pairs={{0,16},{2,18},{4,20},{6,22},{8,24},{10,26},{12,28},{14,30},{16,0},... | collective-permute-start | bytes 442376 | tf_op jit(solution)/shard_map/ppermute | solution.py:53
  295.7 10.0 %collective-permute-start.40 = (bf16[48,1536]{1,0:T(8,128)(2,1)}, bf16[48,1536]{1,0:T(8,128)(2,1)}, u32[]{:S(2)}, u32[]{:S(2)}) collective-permute-start(bf16[48,1536]{1,0:T(8,128)(2,1)} %get-tuple-element.443), channel_id=1, source_target_pairs={{0,8},{2,10},{4,12},{6,14},{8,0},{10,2},{12,4},{14,6},{16,24},{18,... | collective-permute-start | bytes 442376 | tf_op jit(solution)/shard_map/ppermute | solution.py:53
  295.7 15.4 %collective-permute-start.41 = (bf16[48,1536]{1,0:T(8,128)(2,1)}, bf16[48,1536]{1,0:T(8,128)(2,1)}, u32[]{:S(2)}, u32[]{:S(2)}) collective-permute-start(bf16[48,1536]{1,0:T(8,128)(2,1)} %get-tuple-element.444), channel_id=1, source_target_pairs={{0,16},{2,18},{4,20},{6,22},{8,24},{10,26},{12,28},{14,30},{16,0},... | collective-permute-start | bytes 442376 | tf_op jit(solution)/shard_map/ppermute | solution.py:53
  295.9 15.3 %collective-permute-start.42 = (bf16[48,1536]{1,0:T(8,128)(2,1)}, bf16[48,1536]{1,0:T(8,128)(2,1)}, u32[]{:S(2)}, u32[]{:S(2)}) collective-permute-start(bf16[48,1536]{1,0:T(8,128)(2,1)} %get-tuple-element.445), channel_id=1, source_target_pairs={{0,24},{2,26},{4,28},{6,30},{8,16},{10,18},{12,20},{14,22},{16,8},... | collective-permute-start | bytes 442376 | tf_op jit(solution)/shard_map/ppermute | solution.py:53
  (52 other events, 212.5 us)

commit v5 on v4

--- a/solution.py
+++ b/solution.py
@@ -14,6 +14,7 @@
 TILE = 128
 WIDE = 256
 HIDDEN = 512
+CHUNKS = 4
 ROWS = 64
 
 EPS = 1e-06
@@ -79,8 +80,8 @@
 
 
 def gather_second(state, size, time=2):
-    rows, half = state[0].shape
-    outs = [struct((2 * rows, half), BF16)] * 2
+    rows = sum(value.shape[0] for value in state) // 2
+    outs = [struct((rows, state[0].shape[1]), BF16)] * 2
     return kernel_call(join_kernel, list(state), outs, [], time=time)
 
 
@@ -92,6 +93,14 @@
 def send_second(halves, size):
     left, right = halves
     return [left, swap(left, 1, size)], [right, swap(right, 2, size)]
+
+
+def send_apart(state, size):
+    left, left_in, right, right_in = state
+    return (
+        [left, left_in, swap(left, 1, size), swap(left_in, 1, size)],
+        [right, right_in, swap(right, 2, size), swap(right_in, 2, size)],
+    )
 
 
 def scatter_first(grads, size):
@@ -207,12 +216,16 @@
         start += ref.shape[0]
 
 
-def join_kernel(left_ref, left_in_ref, right_ref, right_in_ref, left_out, right_out):
-    count = left_ref.shape[0]
-    left_out[:count, :] = left_ref[...]
-    left_out[count:, :] = left_in_ref[...]
-    right_out[:count, :] = right_ref[...]
-    right_out[count:, :] = right_in_ref[...]
+def join_kernel(*refs):
+    *in_refs, left_out, right_out = refs
+    for out_ref, pieces in (
+        (left_out, in_refs[: len(in_refs) // 2]),
+        (right_out, in_refs[len(in_refs) // 2 :]),
+    ):
+        start = 0
+        for ref in pieces:
+            out_ref[start : start + ref.shape[0], :] = ref[...]
+            start += ref.shape[0]
 
 
 def scatter_second_kernel(left_ref, right_ref, left_in_ref, right_in_ref, left_out, right_out):
@@ -263,10 +276,10 @@
     )[0]
 
 
-def each_rows(count, body):
-    @pl.loop(0, count // ROWS)
+def each_rows(count, body, rows=ROWS):
+    @pl.loop(0, count // rows)
     def step(i):
-        body(pl.ds(pl.multiple_of(i * ROWS, ROWS), ROWS))
+        body(pl.ds(pl.multiple_of(i * rows, rows), rows))
 
 
 def each_tile(start, width, body):
@@ -276,20 +289,21 @@
 
 
 def fetch(left, right, weights_ref, sems, first=0):
+    start = left[0].shape[1] if left else 0
+    columns = weights_ref.shape[1] - start
+    quarter = weights_ref.shape[0] // 4
     moves = []
-    start = left[0].shape[1] if left else 0
     for i, ref in enumerate(left):
         count = ref.shape[0]
         moves.append((ref, weights_ref.at[i * count : (i + 1) * count, :start]))
-    columns = weights_ref.shape[1] - start
-    for i, ref in enumerate(right):
-        count = ref.shape[0] // 2
-        for x in range(2):
-            place = (2 * x + i) * count
+    places = [0, 2, 1, 3]
+    for ref in right:
+        for x in range(ref.shape[0] // quarter):
+            place = places.pop(0) * quarter
             moves.append(
                 (
-                    ref.at[x * count : (x + 1) * count, first : first + columns],
-                    weights_ref.at[place : place + count, start:],
+                    ref.at[x * quarter : (x + 1) * quarter, first : first + columns],
+                    weights_ref.at[place : place + quarter, start:],
                 )
             )
     copies = [pltpu.make_async_copy(*move, sems.at[i]) for i, move in enumerate(moves)]
@@ -680,7 +694,7 @@
 
 def cross_forward_kernel(tokens_ref, partial_ref, peer_ref, gains_ref, kv_ref, dead_ref, *refs):
     (
-        h_ref, normed_ref, query_ref, att_ref, lse_ref, out_ref, more_ref,
+        h_ref, normed_ref, query_ref, att_ref, lse_ref, *out_refs,
         weights_ref, s_ref, acc_ref, sems,
     ) = refs[2:]
     copies = fetch([], refs[:2], weights_ref, sems)
@@ -705,9 +719,9 @@
         )
 
     each_pair(pairs, attend)
-    count = out_ref.shape[0]
-    out_ref[...] = nt(att_ref[:count, :], weights_ref[:, part:])
-    more_ref[...] = nt(att_ref[count:, :], weights_ref[:, part:])
+    count = out_refs[0].shape[0]
+    for i, out_ref in enumerate(out_refs):
+        out_ref[...] = nt(att_ref[i * count : (i + 1) * count, :], weights_ref[:, part:])
 
 
 def cross_forward(tokens, partial, peer, gains, key_value, dead, quarters):
@@ -724,8 +738,7 @@
             struct((targets, part), BF16),
             struct((targets, part), BF16),
             struct((pairs, 8, targets), F32),
-            struct((targets // 2, width), F32),
-            struct((targets // 2, width), F32),
+            *[struct((targets // CHUNKS, width), F32)] * CHUNKS,
         ],
         [
             pltpu.VMEM((width, columns), BF16),
@@ -738,25 +751,22 @@
     )
 
 
-def ffn_kernel(
-    before_ref, first_ref, second_ref, first_in_ref, second_in_ref, gains_ref, cot_ref, cot_t_ref,
-    *refs
-):
-    h_out, down_ref, back_ref, *outs = refs[4:11]
-    weights_ref, grads_ref, h_ref, normed_ref, normed_t, in_sems, out_sems = refs[11:]
-    copies = fetch(refs[:2], refs[2:4], weights_ref, in_sems)
+def ffn_kernel(before_ref, gains_ref, cot_ref, cot_t_ref, *refs):
+    chunks, refs = refs[: 2 * CHUNKS], refs[2 * CHUNKS :]
+    h_out, down_ref, back_ref, *outs = refs[8:15]
+    weights_ref, grads_ref, h_ref, normed_ref, normed_t, in_sems, out_sems = refs[15:]
+    copies = fetch(refs[:4], refs[4:8], weights_ref, in_sems)
     gain = gains_ref[2:3, :]
-    count = first_ref.shape[0]
-    halves = ((first_ref, first_in_ref), (second_ref, second_in_ref))
-    for i, (partial_ref, peer_ref) in enumerate(halves):
+    count = chunks[0].shape[0]
+    for i, (partial_ref, peer_ref) in enumerate(zip(chunks[:CHUNKS], chunks[CHUNKS:])):
 
         def norm(rows):
-            own = pl.ds(pl.multiple_of(rows.start + i * count, ROWS), ROWS)
+            own = pl.ds(pl.multiple_of(rows.start + i * count, rows.size), rows.size)
             value = before_ref[own, :] + (partial_ref[rows, :] + peer_ref[rows, :])
             h_ref[own, :] = value
             normed_ref[own, :] = (value * root_of(value) * gain).astype(BF16)
 
-        each_rows(count, norm)
+        each_rows(count, norm, 32)
     h_copy = pltpu.make_async_copy(h_ref, h_out, out_sems.at[36])
     h_copy.start()
     normed_t[...] = normed_ref[...].T
@@ -818,7 +828,7 @@
     columns = 2 * quarters[0].shape[1]
     return kernel_call(
         ffn_kernel,
-        [before, *partials, *peers, gains, cot, cot_t, *quarters],
+        [before, gains, cot, cot_t, *partials, *peers, *quarters],
         [struct((targets, width), F32)] * 3 + grad_structs(width, columns),
         [
             pltpu.VMEM((width, columns), BF16),
@@ -826,11 +836,11 @@
             pltpu.VMEM((targets, width), F32),
             pltpu.VMEM((targets, width), BF16),
             pltpu.VMEM((width, targets), BF16),
-            pltpu.SemaphoreType.DMA((6,)),
+            pltpu.SemaphoreType.DMA((8,)),
             pltpu.SemaphoreType.DMA((37,)),
         ],
         time=20,
-        in_specs=[IN_VMEM] * 8 + [IN_PLACE] * 4,
+        in_specs=[IN_VMEM] * (4 + 2 * CHUNKS) + [IN_PLACE] * 8,
         out_specs=[IN_PLACE] + [IN_VMEM] * 2 + [IN_PLACE] * 4,
     )
 
@@ -1089,7 +1099,7 @@
         list(ins),
         [struct((targets, width), F32), struct((targets, width), BF16)],
         [],
-        time=8,
+        time=1,
         grid=(targets // WIDE,),
         in_specs=[block] * 7 + [IN_VMEM] * 2,
         out_specs=[block] * 2,
@@ -1137,13 +1147,14 @@
     masks = spot // (2 * outer) + 2 * (spot // outer % 2) + 4 * (spot % outer)
     source = jnp.broadcast_to(((rank ^ masks) * block + spots % block)[None], (8, width))
 
-    weights = gather_outer(
-        low(
-            self_query, self_key, self_value, self_output.T,
-            cross_query, cross_output.T, cross_key, cross_value,
-        ),
-        size,
-    )
+    weights = low(
+        self_query, self_key, self_value, self_output.T,
+        cross_query, cross_output.T, cross_key, cross_value,
+    )
+    if size == 16:
+        pieces = [weights, swap(weights, 4, size), swap(weights, 8, size)]
+    else:
+        pieces = gather_outer(weights, size)
     gains = jnp.concatenate(
         [norm_one[None], norm_two[None], norm_three[None], jnp.zeros((5, width), F32)]
     )
@@ -1161,13 +1172,18 @@
         ],
         [],
     )
-    ffn = low(ffn_gate, ffn_up, ffn_down.T)
+    ffn = low(*after((ffn_gate, ffn_up, ffn_down.T), normed_one))
 
     sent = lax.dynamic_slice_in_dim(encoder_out, core * half, half, 2)[assign]
-    weights, ffn, normed_one, sent = after((weights, ffn, normed_one, sent))
-    weights = gather_first(weights, size)
-    weights, ffn, sent = after((weights, ffn, sent))
-    weights = send_first(weights, size)
+    pieces, normed_one = after((pieces, normed_one))
+    if size == 16:
+        more = swap(pieces[2], 4, size)
+    weights = send_first(gather_first(pieces, size), size)
+    if size == 16:
+        more, ffn, sent = after((more, ffn, sent))
+        more = gather_first([more], size)
+        more, ffn, sent = after((more, ffn, sent))
+        more = send_first(more, size)
     own = lax.all_to_all(sent, "dp", split_axis=0, concat_axis=0, tiled=True)
     own = own.reshape(capacity, half)
     labels, bias_table, lengths = after((buckets[:, :TILE], bias_table, lengths), weights[0])
@@ -1179,6 +1195,9 @@
     bias = jnp.sum(jnp.where(which[None], bias_table.T[:, :, None], 0.0), axis=1)
     bias = jnp.pad(bias.reshape(heads // 2, 2, targets), ((0, 0), (0, 6), (0, 0)))
 
+    if size == 16:
+        weights, more = after((weights, more))
+        weights = [value for both in zip(weights, more) for value in both]
     weights, ffn, bias, dead = after((weights, ffn, bias, dead))
     weights = gather_second(weights, size, time=40)
     weights, ffn = after((weights, ffn))
@@ -1195,9 +1214,7 @@
     ffn, mixed, attended, lse_self, partial_one, own, own_peer = after(
         (ffn, mixed, attended, lse_self, partial_one, own, own_peer)
     )
-    ffn = gather_second(ffn, size)
-    ffn, partial_one, own = after((ffn, partial_one, own))
-    ffn = send_second(ffn, size)
+    ffn = send_apart(ffn, size)
     peer_one = swap_cores(partial_one)
     encoded, key_value = encoder_call(which_core, own, own_peer, order, right)
     h_one, normed_two, cross_q, cross_att, lse_cross, *partial_two = cross_forward(
@@ -1250,16 +1267,18 @@
     decoder_grad, layer_out = last_call(
         g_one, partial_five, peer_five, tokens, h_two, partial_down, peer_down, gains, turned
     )
-    cross, layer_out = after((cross, layer_out))
+    last, layer_out = after((last, layer_out))
     if size == 16:
+        last = scatter_second_parts(last, time=40)
+        cross = after(cross, last[-1])
+        last = scatter_second_send(last, size)
         cross_keep, cross_out = scatter_pair_parts(cross)
-        cross_out, last = after((cross_out, last))
-        last = scatter_second_send(scatter_second_parts(last, time=40), size)
         cross_in = swap(cross_out, 4, size)
-        last, ffn = after((last, ffn))
+        last, ffn = after((last, ffn), cross_out)
         last = scatter_outer_parts(last, 0, 1)
-        last, cross_in, back, ffn = after((last, cross_in, back, ffn))
+        last, back, ffn = after((last, back, ffn))
         last = scatter_outer_send(last, size)
+        back, cross_in = after((back, cross_in), last[1])
         cross = scatter_pair_send(cross_keep, cross_in, size)
     else:
         cross = scatter_outer_send(scatter_outer_parts(cross, 0, 1), size)
@@ -1270,6 +1289,7 @@
     small = jnp.sum(back[:, count:].astype(F32), axis=0)
     small = small[:8] + small[8:]
     both = small + swap_cores(small)
+    last, encoder_grad, small, both = after((last, encoder_grad, small, both))
     sum_ffn, sum_cross, sum_self = scatter_last(ffn), scatter_last(cross), scatter_last(last)
     table = small[6:8].reshape(2, heads // 2, TILE)[:, :, : bias_table.shape[0]]
     grad_table = table.transpose(1, 0, 2).reshape(heads, -1).T

time: 315 us -> 307 us (0.975)
  starting transfers between devices: 62.8 us -> 57.7 us
    ppermute x34 -> x38, starting transfers between devices: 49.9 us -> 47.6 us  [swap(): return lax.ppermute(value, 'dp', [(i, i ^ mask) for i in range(size)])]
    ppermute x34 -> x38, waiting for transfers between devices: 58.8 us -> 59.7 us  [swap(): return lax.ppermute(value, 'dp', [(i, i ^ mask) for i in range(size)])]
  transfers between devices with their start and end apart: 46 -> 52, of which waited for: 23 -> 22; matrix products, arithmetic and copies ran while one was open for 6% -> 6% of each run, Pallas kernels for 39% -> 41%
where the time goes in v5:
time: 307 us; the launch traced here: 306 us
  Pallas kernels  152 us (50%)
  waiting for transfers between devices  62.9 us (20%)
  starting transfers between devices  57.7 us (19%)
  local copies, waits for them, and re-layouts  23.4 us (8%)
  other arithmetic  6.79 us (2%)
  between operations  3.36 us (1%)
    pallas_call x21, Pallas kernels, kernel_call(): pl.pallas_call(kernel, out_shape=outs, in_specs=in_specs or [everywhere]...  152 us
    ppermute x38, waiting for transfers between devices, swap(): return lax.ppermute(value, 'dp', [(i, i ^ mask) for i in range(size)])  59.7 us
    ppermute x38, starting transfers between devices, swap(): return lax.ppermute(value, 'dp', [(i, i ^ mask) for i in range(size)])  47.6 us
    unnamed x106, local copies, waits for them, and re-layouts  9.87 us
  transfers between devices with their start and end apart: 52, of which 22 were waited for; matrix products, arithmetic and copies ran while one was open for 6% of the time, Pallas kernels for 41%

profile of v5, /device:TPU:0, one launch (start us, length us, event | category | flops | bytes accessed | tf_op | source)
XLA Modules:
  0.0 306.3 jit_solution(15370104164762625216)
XLA Ops:
  0.7 2.0 shard_map.350.refs_0_
  2.7 3.0 collective-permute-start
  5.7 2.6 collective-permute-start.1
  11.7 7.0 %shard_map.349 = (f32[512,768]{1,0:T(8,128)}, bf16[512,768]{1,0:T(8,128)(2,1)}, bf16[768,512]{1,0:T(8,128)(2,1)}, f32[8,768]{1,0:T(8,128)}, bf16[768,768]{1,0:T(...) custom-call(bf16[512,768]{1,0:T(8,128)(2,1)} %bitcast.30, bf16[512,768]{1,0:T(8,128)(2,1)} %bitcast.31, ...), custom_call_target="tpu_custom_call" | custom-call | flops 2000000000 | bytes 1 | tf_op jit(solution)/shard_map/pallas_call | solution.py:189
  19.9 1.5 gather_fusion
  22.8 1.9 shard_map.352.refs_0_
  25.6 2.1 shard_map.351
  27.7 1.5 collective-permute-start.2
  29.2 1.5 collective-permute-start.3
  33.7 1.7 shard_map.353
  35.4 1.5 collective-permute-start.5
  36.9 1.5 collective-permute-start.6
  39.1 3.8 %all-to-all-start = ((bf16[16,64,384]{2,1,0:T(8,128)(2,1)}), bf16[16,64,384]{2,1,0:T(8,128)(2,1)S(1)}, u32[]{:S(2)}, u32[]{:S(2)}) async-start(bf16[16,64,384]{2,1,0:T(8,128)(2,1)} %gather_fusion), calls=%async_computation | async-start | bytes 1572864 | tf_op jit(solution)/shard_map/all_to_all | solution.py:1187
  45.3 3.2 %shard_map.354 = (bf16[384,1536]{1,0:T(8,128)(2,1)}, bf16[384,1536]{1,0:T(8,128)(2,1)}) custom-call(bf16[144,1536]{1,0:T(8,128)(2,1)} %get-tuple-element.284.refs_0_, bf16[48,1536]{1,0:T(8,128)(2,1)} %get-tuple-element.285.refs_1_, bf16[144,1536]{1,0:T(8,128)(2,1)} %copy-done.36, bf16[48,1536]{1,0:T(8,128)(2,1)} %copy-done.49, ...), custom_call_target="tpu_custom_call" | custom-call | flops 40000000000 | bytes 1 | tf_op jit(solution)/shard_map/pallas_call | solution.py:189
  48.6 2.0 collective-permute-start.7
  50.6 2.3 collective-permute-start.10
  54.4 19.3 %collective-permute-done.10.refs_2_ = bf16[48,3072]{1,0:T(8,128)(2,1)} collective-permute-done((bf16[48,3072]{1,0:T(8,128)(2,1)S(1)}, bf16[48,3072]{1,0:T(8,128)(2,1)}, u32[]{:S(2)}, u32[]{:S(2)}) %collective-permute-start.10) | collective-permute-done | bytes 294944 | tf_op jit(solution)/shard_map/ppermute | solution.py:54
  73.7 6.1 %collective-permute-done.7.refs_1_ = bf16[384,1536]{1,0:T(8,128)(2,1)S(1)} collective-permute-done((bf16[384,1536]{1,0:T(8,128)(2,1)}, bf16[384,1536]{1,0:T(8,128)(2,1)S(1)}, u32[]{:S(2)}, u32[]{:S(2)}) %collective-permute-start.7) | collective-permute-done | bytes 1179680 | tf_op jit(solution)/shard_map/ppermute | solution.py:54
  79.8 2.0 collective-permute-done.11.refs_3_
  82.5 2.3 shard_map.355
  87.5 12.7 %shard_map.356 = (bf16[512,1152]{1,0:T(8,128)(2,1)}, bf16[512,384]{1,0:T(8,128)(2,1)}, f32[3,8,512]{2,1,0:T(8,128)}, f32[512,768]{1,0:T(8,128)}) custom-call(bf16[512,768]{1,0:T(8,128)(2,1)} %get-tuple-element.313.normed_ref, f32[3,8,512]{2,1,0:T(8,128)} %pad.4.bias_ref, bf16[384,1536]{1,0:T(8,128)(2,1)} %get-tuple-element.315.refs_0_, ...), custom_call_target="tpu_custom_call" | custom-call | flops 12000000000 | bytes 1 | tf_op jit(solution)/shard_map/pallas_call | solution.py:189
  101.7 1.5 collective-permute-start.20
  105.8 7.7 %shard_map.357 = (bf16[1024,768]{1,0:T(8,128)(2,1)}, bf16[1024,768]{1,0:T(8,128)(2,1)}) custom-call(s32[1]{0:T(128)} %bitcast.9.core_ref, bf16[1024,384]{1,0:T(8,128)(2,1)} %bitcast.26, bf16[1024,384]{1,0:T(8,128)(2,1)} %copy-done.24, bf16[768,768]{1,0:T(8,128)(2,1)} %get-tuple-element.326.order_ref, bf16[384,1536]{1,0:T(8,128)(2,1)} %get-tuple-element.327.refs_0_, ...), custom_call_target="tpu_custom_call" | custom-call | flops 8000000000 | bytes 1 | tf_op jit(solution)/shard_map/pallas_call | solution.py:189
  114.8 16.8 %shard_map.358 = (f32[512,768]{1,0:T(8,128)}, bf16[512,768]{1,0:T(8,128)(2,1)}, bf16[512,384]{1,0:T(8,128)(2,1)}, bf16[512,384]{1,0:T(8,128)(2,1)}, f32[3,8,512]...) custom-call(f32[512,768]{1,0:T(8,128)} %get-tuple-element.255.tokens_ref, ...), custom_call_target="tpu_custom_call" | custom-call | flops 16000000000 | bytes 1 | tf_op jit(solution)/shard_map/pallas_call | solution.py:189
  136.0 16.4 %shard_map.359 = (f32[512,768]{1,0:T(8,128)}, f32[512,768]{1,0:T(8,128)}, f32[512,768]{1,0:T(8,128)}, bf16[384,1536]{1,0:T(8,128)(2,1)}, bf16[384,1536]{1,0:T(8,...) custom-call(f32[512,768]{1,0:T(8,128)} %get-tuple-element.331.before_ref.h_ref, ...), custom_call_target="tpu_custom_call" | custom-call | flops 20000000000 | bytes 1 | tf_op jit(solution)/shard_map/pallas_call | solution.py:189
  157.2 19.9 %shard_map.360 = (f32[512,768]{1,0:T(8,128)}, bf16[512,768]{1,0:T(8,128)(2,1)}, bf16[512,384]{1,0:T(8,128)(2,1)}, bf16[1024,768]{1,0:T(8,128)(2,1)}, f32[512,768]{1,0:T(8,128)}, /*index=5*/f32[8,768]{1,0:T(8,128)}) custom-call(bf16[512,768]{1,0:T(8,128)(2,1)} %get-tuple-element.332.cot_ref, f32[512,768]{1,0:T(8,128)} %get-tuple-element.346.partial_ref, ...), custom_call_target="tpu_custom_call" | custom-call | flops 17999998976 | bytes 1 | tf_op jit(solution)/shard_map/pallas_call | solution.py:189
  177.1 4.1 %collective-permute-done.24.left_in_ref.refs_1_ = bf16[384,1536]{1,0:T(8,128)(2,1)S(1)} collective-permute-done((bf16[384,1536]{1,0:T(8,128)(2,1)}, bf16[384,1536]{1,0:T(8,128)(2,1)S(1)}, u32[]{:S(2)}, u32[]{:S(2)}) %collective-permute-start.24) | collective-permute-done | bytes 1179680 | tf_op jit(solution)/shard_map/ppermute | solution.py:54
  182.5 3.4 %shard_map.361 = (bf16[192,1536]{1,0:T(8,128)(2,1)}, bf16[192,1536]{1,0:T(8,128)(2,1)}) custom-call(bf16[384,1536]{1,0:T(8,128)(2,1)} %get-tuple-element.385.left_ref.refs_0_, bf16[384,1536]{1,0:T(8,128)(2,1)} %get-tuple-element.388.right_ref.refs_3_, bf16[384,1536]{1,0:T(8,128)(2,1)} %copy-done.23, ...), custom_call_target="tpu_custom_call" | custom-call | flops 2000000000 | bytes 1 | tf_op jit(solution)/shard_map/pallas_call | solution.py:189
  187.7 12.4 %shard_map.362 = (bf16[1024,384]{1,0:T(8,128)(2,1)}, bf16[1024,384]{1,0:T(8,128)(2,1)}, bf16[384,768]{1,0:T(8,128)(2,1)}, bf16[384,768]{1,0:T(8,128)(2,1)}, bf16...) custom-call(s32[1]{0:T(128)} %bitcast.9.core_ref, bf16[512,768]{1,0:T(8,128)(2,1)} %get-tuple-element.371.normed_ref, ...), custom_call_target="tpu_custom_call" | custom-call | flops 12000000000 | bytes 1 | tf_op jit(solution)/shard_map/pallas_call | solution.py:189
  200.1 1.8 collective-permute-done.28.refs_2_
  203.4 3.4 %shard_map.363 = (f32[48,3072]{1,0:T(8,128)}, bf16[48,3072]{1,0:T(8,128)(2,1)}, bf16[48,3072]{1,0:T(8,128)(2,1)}, bf16[48,3072]{1,0:T(8,128)(2,1)}) custom-call(bf16[384,1536]{1,0:T(8,128)(2,1)} %get-tuple-element.385.left_ref.refs_0_, bf16[384,1536]{1,0:T(8,128)(2,1)} %copy-done.23, bf16[192,1536]{1,0:T(8,128)(2,1)} %copy-done.34, ...), custom_call_target="tpu_custom_call" | custom-call | flops 2000000000 | bytes 1 | tf_op jit(solution)/shard_map/pallas_call | solution.py:189
  208.9 2.2 collective-permute-start.32
  211.2 1.9 collective-permute-start.33
  213.0 23.0 %shard_map.364 = (f32[512,768]{1,0:T(8,128)}, f32[512,768]{1,0:T(8,128)}, bf16[16,384]{1,0:T(8,128)(2,1)}, bf16[384,768]{1,0:T(8,128)(2,1)}, bf16[384,768]{1,0:T...) custom-call(f32[512,768]{1,0:T(8,128)} %get-tuple-element.411.g_in_ref, ...), custom_call_target="tpu_custom_call" | custom-call | flops 22000001024 | bytes 1 | tf_op jit(solution)/shard_map/pallas_call | solution.py:189
  240.6 2.1 shard_map.367
  245.8 4.1 %all-to-all-start.1 = ((bf16[16,80,384]{2,1,0:T(8,128)(2,1)}), bf16[16,80,384]{2,1,0:T(8,128)(2,1)S(1)}, u32[]{:S(2)}, u32[]{:S(2)}) async-start(bf16[16,80,384]{2,1,0:T(8,128)(2,1)} %pad_maximum_fusion), calls=%async_computation.1 | async-start | bytes 1966080 | tf_op jit(solution)/shard_map/all_to_all | solution.py:1266
  251.0 7.1 %shard_map.365 = (f32[512,768]{1,0:T(8,128)}, bf16[512,768]{1,0:T(8,128)(2,1)}) custom-call(f32[512,768]{1,0:T(8,128)} %get-tuple-element.427.g_ref, f32[512,768]{1,0:T(8,128)} %get-tuple-element.428.partial_ref, f32[512,768]{1,0:T(8,128)} %copy-done.3, f32[512,768]{1,0:T(8,128)} %get-tuple-element.255.tokens_ref, f32[512,768]{1,0:T(8,128)} %get-tuple-element.347.h_ref, ...), custom_call_target="tpu_custom_call" | custom-call | flops 1000000000 | bytes 1 | tf_op jit(solution)/shard_map/pallas_call | solution.py:189
  259.3 2.1 shard_map.366
  263.6 7.4 %collective-permute-done.41.refs_2_ = bf16[192,768]{1,0:T(8,128)(2,1)} collective-permute-done((bf16[192,768]{1,0:T(8,128)(2,1)}, bf16[192,768]{1,0:T(8,128)(2,1)}, u32[]{:S(2)}, u32[]{:S(2)}) %collective-permute-start.41) | collective-permute-done | bytes 294944 | tf_op jit(solution)/shard_map/ppermute | solution.py:54
  271.0 2.5 shard_map.368
  273.8 4.4 %collective-permute-done.39.refs_2_ = bf16[192,768]{1,0:T(8,128)(2,1)S(1)} collective-permute-done((bf16[192,768]{1,0:T(8,128)(2,1)}, bf16[192,768]{1,0:T(8,128)(2,1)S(1)}, u32[]{:S(2)}, u32[]{:S(2)}) %collective-permute-start.39) | collective-permute-done | bytes 294944 | tf_op jit(solution)/shard_map/ppermute | solution.py:54
  279.6 2.4 shard_map.369
  283.0 1.6 collective-permute-start.45
  284.6 1.9 collective-permute-start.46
  287.4 1.6 collective-permute-done.44
  290.9 1.5 collective-permute-start.49
  292.4 1.5 gather_fusion.1
  294.0 5.8 %collective-permute-done.45 = bf16[48,1536]{1,0:T(8,128)(2,1)} collective-permute-done((bf16[48,1536]{1,0:T(8,128)(2,1)}, bf16[48,1536]{1,0:T(8,128)(2,1)}, u32[]{:S(2)}, u32[]{:S(2)}) %collective-permute-start.45) | collective-permute-done | bytes 147488 | tf_op jit(solution)/shard_map/ppermute | solution.py:54
  (235 shorter events, 60.9 us)
Async XLA Ops:
  2.7 22.0 %collective-permute-start = (bf16[48,3072]{1,0:T(8,128)(2,1)}, bf16[48,3072]{1,0:T(8,128)(2,1)S(1)}, u32[]{:S(2)}, u32[]{:S(2)}) collective-permute-start(bf16[48,3072]{1,0:T(8,128)(2,1)} %shard_map.350.refs_0_), channel_id=1, source_target_pairs={{0,8},{2,10},{4,12},{6,14},{8,0},{10,2},{12,4},{14,6},{16,24},{18,... | collective-permute-start | bytes 884744 | tf_op jit(solution)/shard_map/ppermute | solution.py:54
  5.7 19.0 %collective-permute-start.1 = (bf16[48,3072]{1,0:T(8,128)(2,1)}, bf16[48,3072]{1,0:T(8,128)(2,1)S(1)}, u32[]{:S(2)}, u32[]{:S(2)}) collective-permute-start(bf16[48,3072]{1,0:T(8,128)(2,1)} %shard_map.350.refs_0_), channel_id=1, source_target_pairs={{0,16},{2,18},{4,20},{6,22},{8,24},{10,26},{12,28},{14,30},{16,0},... | collective-permute-start | bytes 884744 | tf_op jit(solution)/shard_map/ppermute | solution.py:54
  24.7 8.3 %collective-permute-start.4 = (bf16[48,3072]{1,0:T(8,128)(2,1)S(1)}, bf16[48,3072]{1,0:T(8,128)(2,1)S(1)}, u32[]{:S(2)}, u32[]{:S(2)}) collective-permute-start(bf16[48,3072]{1,0:T(8,128)(2,1)S(1)} %collective-permute-done.1.refs_2_), channel_id=1, source_target_pairs={{0,8},{2,10},{4,12},{6,14},{8,0},{10,2},{12,4},{14,6},{16,24},{18,... | collective-permute-start | bytes 884744 | tf_op jit(solution)/shard_map/ppermute | solution.py:54
  27.7 16.5 %collective-permute-start.2 = (bf16[144,1536]{1,0:T(8,128)(2,1)}, bf16[144,1536]{1,0:T(8,128)(2,1)S(1)}, u32[]{:S(2)}, u32[]{:S(2)}) collective-permute-start(bf16[144,1536]{1,0:T(8,128)(2,1)} %get-tuple-element.284.refs_0_), channel_id=1, source_target_pairs={{0,4},{2,6},{4,0},{6,2},{8,12},{10,14},{12,8},{14,10},{16,20},{18,... | collective-permute-start | bytes 1327112 | tf_op jit(solution)/shard_map/ppermute | solution.py:54
  29.2 14.9 %collective-permute-start.3 = (bf16[144,1536]{1,0:T(8,128)(2,1)}, bf16[144,1536]{1,0:T(8,128)(2,1)S(1)}, u32[]{:S(2)}, u32[]{:S(2)}) collective-permute-start(bf16[144,1536]{1,0:T(8,128)(2,1)} %get-tuple-element.288.refs_4_), channel_id=1, source_target_pairs={{0,2},{2,0},{4,6},{6,4},{8,10},{10,8},{12,14},{14,12},{16,18},{18,... | collective-permute-start | bytes 1327112 | tf_op jit(solution)/shard_map/ppermute | solution.py:54
  35.4 7.5 %collective-permute-start.5 = (bf16[48,1536]{1,0:T(8,128)(2,1)}, bf16[48,1536]{1,0:T(8,128)(2,1)S(1)}, u32[]{:S(2)}, u32[]{:S(2)}) collective-permute-start(bf16[48,1536]{1,0:T(8,128)(2,1)} %get-tuple-element.285.refs_1_), channel_id=1, source_target_pairs={{0,4},{2,6},{4,0},{6,2},{8,12},{10,14},{12,8},{14,10},{16,20},{18,... | collective-permute-start | bytes 442376 | tf_op jit(solution)/shard_map/ppermute | solution.py:54
  36.9 7.2 %collective-permute-start.6 = (bf16[48,1536]{1,0:T(8,128)(2,1)}, bf16[48,1536]{1,0:T(8,128)(2,1)S(1)}, u32[]{:S(2)}, u32[]{:S(2)}) collective-permute-start(bf16[48,1536]{1,0:T(8,128)(2,1)} %get-tuple-element.289.refs_5_), channel_id=1, source_target_pairs={{0,2},{2,0},{4,6},{6,4},{8,10},{10,8},{12,14},{14,12},{16,18},{18,... | collective-permute-start | bytes 442376 | tf_op jit(solution)/shard_map/ppermute | solution.py:54
  39.1 34.6 %all-to-all-start = ((bf16[16,64,384]{2,1,0:T(8,128)(2,1)}), bf16[16,64,384]{2,1,0:T(8,128)(2,1)S(1)}, u32[]{:S(2)}, u32[]{:S(2)}) async-start(bf16[16,64,384]{2,1,0:T(8,128)(2,1)} %gather_fusion), calls=%async_computation | async-start | bytes 1572864 | tf_op jit(solution)/shard_map/all_to_all | solution.py:1187
  48.6 31.2 %collective-permute-start.7 = (bf16[384,1536]{1,0:T(8,128)(2,1)}, bf16[384,1536]{1,0:T(8,128)(2,1)S(1)}, u32[]{:S(2)}, u32[]{:S(2)}) collective-permute-start(bf16[384,1536]{1,0:T(8,128)(2,1)} %get-tuple-element.315.refs_0_), channel_id=1, source_target_pairs={{0,2},{2,0},{4,6},{6,4},{8,10},{10,8},{12,14},{14,12},{16,18},{18,... | collective-permute-start | bytes 3538952 | tf_op jit(solution)/shard_map/ppermute | solution.py:54
  50.6 29.2 %collective-permute-start.8 = (bf16[384,1536]{1,0:T(8,128)(2,1)}, bf16[384,1536]{1,0:T(8,128)(2,1)S(1)}, u32[]{:S(2)}, u32[]{:S(2)}) collective-permute-start(bf16[384,1536]{1,0:T(8,128)(2,1)} %get-tuple-element.327.refs_0_), channel_id=1, source_target_pairs={{0,4},{2,6},{4,0},{6,2},{8,12},{10,14},{12,8},{14,10},{16,20},{18,... | collective-permute-start | bytes 3538952 | tf_op jit(solution)/shard_map/ppermute | solution.py:54
  50.6 23.0 %collective-permute-start.10 = (bf16[48,3072]{1,0:T(8,128)(2,1)S(1)}, bf16[48,3072]{1,0:T(8,128)(2,1)}, u32[]{:S(2)}, u32[]{:S(2)}) collective-permute-start(bf16[48,3072]{1,0:T(8,128)(2,1)S(1)} %copy-done.42), channel_id=1, source_target_pairs={{0,16},{2,18},{4,20},{6,22},{8,24},{10,26},{12,28},{14,30},{16,0},... | collective-permute-start | bytes 884744 | tf_op jit(solution)/shard_map/ppermute | solution.py:54
  52.9 20.8 %collective-permute-start.9 = (bf16[48,3072]{1,0:T(8,128)(2,1)S(1)}, bf16[48,3072]{1,0:T(8,128)(2,1)}, u32[]{:S(2)}, u32[]{:S(2)}) collective-permute-start(bf16[48,3072]{1,0:T(8,128)(2,1)S(1)} %copy-done.42), channel_id=1, source_target_pairs={{0,8},{2,10},{4,12},{6,14},{8,0},{10,2},{12,4},{14,6},{16,24},{18,... | collective-permute-start | bytes 884744 | tf_op jit(solution)/shard_map/ppermute | solution.py:54
  73.7 8.1 %collective-permute-start.11 = (bf16[48,3072]{1,0:T(8,128)(2,1)}, bf16[48,3072]{1,0:T(8,128)(2,1)S(1)}, u32[]{:S(2)}, u32[]{:S(2)}) collective-permute-start(bf16[48,3072]{1,0:T(8,128)(2,1)} %collective-permute-done.10.refs_2_), channel_id=1, source_target_pairs={{0,8},{2,10},{4,12},{6,14},{8,0},{10,2},{12,4},{14,6},{16,24},{18,... | collective-permute-start | bytes 884744 | tf_op jit(solution)/shard_map/ppermute | solution.py:54
  84.9 16.8 %collective-permute-start.14 = (bf16[1024,384]{1,0:T(8,128)(2,1)S(1)}, bf16[1024,384]{1,0:T(8,128)(2,1)S(1)}, u32[]{:S(2)}, u32[]{:S(2)}) collective-permute-start(bf16[1024,384]{1,0:T(8,128)(2,1)S(1)} %bitcast.25), channel_id=1, source_target_pairs={{0,1},{1,0},{2,3},{3,2},{4,5},{5,4},{6,7},{7,6},{8,9},{9,8},{10,11... | collective-permute-start | bytes 2359304 | tf_op jit(solution)/shard_map/ppermute | solution.py:58
  84.9 16.0 %collective-permute-start.12 = (bf16[192,1536]{1,0:T(8,128)(2,1)}, bf16[192,1536]{1,0:T(8,128)(2,1)S(1)}, u32[]{:S(2)}, u32[]{:S(2)}) collective-permute-start(bf16[192,1536]{1,0:T(8,128)(2,1)} %get-tuple-element.338.refs_8_), channel_id=1, source_target_pairs={{0,4},{2,6},{4,0},{6,2},{8,12},{10,14},{12,8},{14,10},{16,20},{18,... | collective-permute-start | bytes 1769480 | tf_op jit(solution)/shard_map/ppermute | solution.py:54
  86.0 15.6 %collective-permute-start.13 = (bf16[192,1536]{1,0:T(8,128)(2,1)}, bf16[192,1536]{1,0:T(8,128)(2,1)S(1)}, u32[]{:S(2)}, u32[]{:S(2)}) collective-permute-start(bf16[192,1536]{1,0:T(8,128)(2,1)} %get-tuple-element.340.refs_12_), channel_id=1, source_target_pairs={{0,2},{2,0},{4,6},{6,4},{8,10},{10,8},{12,14},{14,12},{16,18},{18,... | collective-permute-start | bytes 1769480 | tf_op jit(solution)/shard_map/ppermute | solution.py:54
  101.6 12.0 %collective-permute-start.15 = (f32[512,768]{1,0:T(8,128)}, f32[512,768]{1,0:T(8,128)S(1)}, u32[]{:S(2)}, u32[]{:S(2)}) collective-permute-start(f32[512,768]{1,0:T(8,128)} %get-tuple-element.322.partial_ref), channel_id=1, source_target_pairs={{0,1},{1,0},{2,3},{3,2},{4,5},{5,4},{6,7},{7,6},{8,9},{9,8},{10,11... | collective-permute-start | bytes 4718600 | tf_op jit(solution)/shard_map/ppermute | solution.py:58
  101.7 30.0 %collective-permute-start.20 = (bf16[192,1536]{1,0:T(8,128)(2,1)S(1)}, bf16[192,1536]{1,0:T(8,128)(2,1)S(1)}, u32[]{:S(2)}, u32[]{:S(2)}) collective-permute-start(bf16[192,1536]{1,0:T(8,128)(2,1)S(1)} %copy-done.27), channel_id=1, source_target_pairs={{0,2},{2,0},{4,6},{6,4},{8,10},{10,8},{12,14},{14,12},{16,18},{18,... | collective-permute-start | bytes 1769480 | tf_op jit(solution)/shard_map/ppermute | solution.py:54
  103.2 29.0 %collective-permute-start.21 = (bf16[192,1536]{1,0:T(8,128)(2,1)S(1)}, bf16[192,1536]{1,0:T(8,128)(2,1)}, u32[]{:S(2)}, u32[]{:S(2)}) collective-permute-start(bf16[192,1536]{1,0:T(8,128)(2,1)S(1)} %collective-permute-done.12.refs_9_), channel_id=1, source_target_pairs={{0,2},{2,0},{4,6},{6,4},{8,10},{10,8},{12,14},{14,12},{16,18},{18,... | collective-permute-start | bytes 1769480 | tf_op jit(solution)/shard_map/ppermute | solution.py:54
  103.8 28.5 %collective-permute-start.22 = (bf16[192,1536]{1,0:T(8,128)(2,1)S(1)}, bf16[192,1536]{1,0:T(8,128)(2,1)}, u32[]{:S(2)}, u32[]{:S(2)}) collective-permute-start(bf16[192,1536]{1,0:T(8,128)(2,1)S(1)} %copy-done.28), channel_id=1, source_target_pairs={{0,4},{2,6},{4,0},{6,2},{8,12},{10,14},{12,8},{14,10},{16,20},{18,... | collective-permute-start | bytes 1769480 | tf_op jit(solution)/shard_map/ppermute | solution.py:54
  104.8 27.9 %collective-permute-start.23 = (bf16[192,1536]{1,0:T(8,128)(2,1)S(1)}, bf16[192,1536]{1,0:T(8,128)(2,1)}, u32[]{:S(2)}, u32[]{:S(2)}) collective-permute-start(bf16[192,1536]{1,0:T(8,128)(2,1)S(1)} %collective-permute-done.13.refs_13_), channel_id=1, source_target_pairs={{0,4},{2,6},{4,0},{6,2},{8,12},{10,14},{12,8},{14,10},{16,20},{18,... | collective-permute-start | bytes 1769480 | tf_op jit(solution)/shard_map/ppermute | solution.py:54
  152.4 3.7 %collective-permute-start.26 = (f32[512,768]{1,0:T(8,128)}, f32[512,768]{1,0:T(8,128)S(1)}, u32[]{:S(2)}, u32[]{:S(2)}) collective-permute-start(f32[512,768]{1,0:T(8,128)} %get-tuple-element.346.partial_ref), channel_id=1, source_target_pairs={{0,1},{1,0},{2,3},{3,2},{4,5},{5,4},{6,7},{7,6},{8,9},{9,8},{10,11... | collective-permute-start | bytes 4718600 | tf_op jit(solution)/shard_map/ppermute | solution.py:58
  152.6 29.9 %collective-permute-start.27 = (f32[512,768]{1,0:T(8,128)}, f32[512,768]{1,0:T(8,128)S(1)}, u32[]{:S(2)}, u32[]{:S(2)}) collective-permute-start(f32[512,768]{1,0:T(8,128)} %get-tuple-element.354.down_ref), channel_id=1, source_target_pairs={{0,1},{1,0},{2,3},{3,2},{4,5},{5,4},{6,7},{7,6},{8,9},{9,8},{10,11... | collective-permute-start | bytes 4718600 | tf_op jit(solution)/shard_map/ppermute | solution.py:58
  153.0 28.2 %collective-permute-start.24 = (bf16[384,1536]{1,0:T(8,128)(2,1)}, bf16[384,1536]{1,0:T(8,128)(2,1)S(1)}, u32[]{:S(2)}, u32[]{:S(2)}) collective-permute-start(bf16[384,1536]{1,0:T(8,128)(2,1)} %get-tuple-element.344), channel_id=1, source_target_pairs={{0,2},{2,0},{4,6},{6,4},{8,10},{10,8},{12,14},{14,12},{16,18},{18,... | collective-permute-start | bytes 3538952 | tf_op jit(solution)/shard_map/ppermute | solution.py:54
  154.4 28.0 %collective-permute-start.25 = (bf16[384,1536]{1,0:T(8,128)(2,1)}, bf16[384,1536]{1,0:T(8,128)(2,1)}, u32[]{:S(2)}, u32[]{:S(2)}) collective-permute-start(bf16[384,1536]{1,0:T(8,128)(2,1)} %get-tuple-element.345), channel_id=1, source_target_pairs={{0,4},{2,6},{4,0},{6,2},{8,12},{10,14},{12,8},{14,10},{16,20},{18,... | collective-permute-start | bytes 3538952 | tf_op jit(solution)/shard_map/ppermute | solution.py:54
  185.9 16.7 %collective-permute-start.30 = (f32[512,768]{1,0:T(8,128)S(1)}, f32[512,768]{1,0:T(8,128)S(1)}, u32[]{:S(2)}, u32[]{:S(2)}) collective-permute-start(f32[512,768]{1,0:T(8,128)S(1)} %copy-done.17), channel_id=1, source_target_pairs={{0,1},{1,0},{2,3},{3,2},{4,5},{5,4},{6,7},{7,6},{8,9},{9,8},{10,11... | collective-permute-start | bytes 4718600 | tf_op jit(solution)/shard_map/ppermute | solution.py:58
  185.9 16.0 %collective-permute-start.28 = (bf16[192,1536]{1,0:T(8,128)(2,1)}, bf16[192,1536]{1,0:T(8,128)(2,1)S(1)}, u32[]{:S(2)}, u32[]{:S(2)}) collective-permute-start(bf16[192,1536]{1,0:T(8,128)(2,1)} %get-tuple-element.369), channel_id=1, source_target_pairs={{0,4},{2,6},{4,0},{6,2},{8,12},{10,14},{12,8},{14,10},{16,20},{18,... | collective-permute-start | bytes 1769480 | tf_op jit(solution)/shard_map/ppermute | solution.py:54
  187.0 15.6 %collective-permute-start.29 = (bf16[192,1536]{1,0:T(8,128)(2,1)}, bf16[192,1536]{1,0:T(8,128)(2,1)S(1)}, u32[]{:S(2)}, u32[]{:S(2)}) collective-permute-start(bf16[192,1536]{1,0:T(8,128)(2,1)} %get-tuple-element.370), channel_id=1, source_target_pairs={{0,2},{2,0},{4,6},{6,4},{8,10},{10,8},{12,14},{14,12},{16,18},{18,... | collective-permute-start | bytes 1769480 | tf_op jit(solution)/shard_map/ppermute | solution.py:54
  206.9 29.2 %collective-permute-start.34 = (bf16[384,768]{1,0:T(8,128)(2,1)S(1)}, bf16[384,768]{1,0:T(8,128)(2,1)S(1)}, u32[]{:S(2)}, u32[]{:S(2)}) collective-permute-start(bf16[384,768]{1,0:T(8,128)(2,1)S(1)} %copy-done.32), channel_id=1, source_target_pairs={{0,2},{2,0},{4,6},{6,4},{8,10},{10,8},{12,14},{14,12},{16,18},{18,... | collective-permute-start | bytes 1769480 | tf_op jit(solution)/shard_map/ppermute | solution.py:54
  207.6 28.5 %collective-permute-start.35 = (bf16[384,768]{1,0:T(8,128)(2,1)S(1)}, bf16[384,768]{1,0:T(8,128)(2,1)S(1)}, u32[]{:S(2)}, u32[]{:S(2)}) collective-permute-start(bf16[384,768]{1,0:T(8,128)(2,1)S(1)} %copy-done.31), channel_id=1, source_target_pairs={{0,4},{2,6},{4,0},{6,2},{8,12},{10,14},{12,8},{14,10},{16,20},{18,... | collective-permute-start | bytes 1769480 | tf_op jit(solution)/shard_map/ppermute | solution.py:54
  208.6 27.4 %collective-permute-start.31 = (bf16[48,3072]{1,0:T(8,128)(2,1)}, bf16[48,3072]{1,0:T(8,128)(2,1)S(1)}, u32[]{:S(2)}, u32[]{:S(2)}) collective-permute-start(bf16[48,3072]{1,0:T(8,128)(2,1)} %get-tuple-element.403), channel_id=1, source_target_pairs={{0,8},{2,10},{4,12},{6,14},{8,0},{10,2},{12,4},{14,6},{16,24},{18,... | collective-permute-start | bytes 884744 | tf_op jit(solution)/shard_map/ppermute | solution.py:54
  208.9 27.1 %collective-permute-start.32 = (bf16[48,3072]{1,0:T(8,128)(2,1)}, bf16[48,3072]{1,0:T(8,128)(2,1)S(1)}, u32[]{:S(2)}, u32[]{:S(2)}) collective-permute-start(bf16[48,3072]{1,0:T(8,128)(2,1)} %get-tuple-element.404), channel_id=1, source_target_pairs={{0,16},{2,18},{4,20},{6,22},{8,24},{10,26},{12,28},{14,30},{16,0},... | collective-permute-start | bytes 884744 | tf_op jit(solution)/shard_map/ppermute | solution.py:54
  211.2 24.9 %collective-permute-start.33 = (bf16[48,3072]{1,0:T(8,128)(2,1)}, bf16[48,3072]{1,0:T(8,128)(2,1)S(1)}, u32[]{:S(2)}, u32[]{:S(2)}) collective-permute-start(bf16[48,3072]{1,0:T(8,128)(2,1)} %get-tuple-element.405), channel_id=1, source_target_pairs={{0,24},{2,26},{4,28},{6,30},{8,16},{10,18},{12,20},{14,22},{16,8},... | collective-permute-start | bytes 884744 | tf_op jit(solution)/shard_map/ppermute | solution.py:54
  236.9 13.0 %collective-permute-start.38 = (f32[512,768]{1,0:T(8,128)}, f32[512,768]{1,0:T(8,128)S(1)}, u32[]{:S(2)}, u32[]{:S(2)}) collective-permute-start(f32[512,768]{1,0:T(8,128)} %get-tuple-element.428.partial_ref), channel_id=1, source_target_pairs={{0,1},{1,0},{2,3},{3,2},{4,5},{5,4},{6,7},{7,6},{8,9},{9,8},{10,11... | collective-permute-start | bytes 4718600 | tf_op jit(solution)/shard_map/ppermute | solution.py:58
  237.1 6.7 %collective-permute-start.43 = (bf16[1024,384]{1,0:T(8,128)(2,1)}, bf16[1024,384]{1,0:T(8,128)(2,1)S(1)}, u32[]{:S(2)}, u32[]{:S(2)}) collective-permute-start(bf16[1024,384]{1,0:T(8,128)(2,1)} %get-tuple-element.467), channel_id=1, source_target_pairs={{0,1},{1,0},{2,3},{3,2},{4,5},{5,4},{6,7},{7,6},{8,9},{9,8},{10,11... | collective-permute-start | bytes 2359304 | tf_op jit(solution)/shard_map/ppermute | solution.py:58
  238.2 19.9 %collective-permute-start.36 = (bf16[384,768]{1,0:T(8,128)(2,1)}, bf16[384,768]{1,0:T(8,128)(2,1)}, u32[]{:S(2)}, u32[]{:S(2)}) collective-permute-start(bf16[384,768]{1,0:T(8,128)(2,1)} %get-tuple-element.425), channel_id=1, source_target_pairs={{0,2},{2,0},{4,6},{6,4},{8,10},{10,8},{12,14},{14,12},{16,18},{18,... | collective-permute-start | bytes 1769480 | tf_op jit(solution)/shard_map/ppermute | solution.py:54
  239.6 19.7 %collective-permute-start.37 = (bf16[384,768]{1,0:T(8,128)(2,1)}, bf16[384,768]{1,0:T(8,128)(2,1)}, u32[]{:S(2)}, u32[]{:S(2)}) collective-permute-start(bf16[384,768]{1,0:T(8,128)(2,1)} %get-tuple-element.426), channel_id=1, source_target_pairs={{0,4},{2,6},{4,0},{6,2},{8,12},{10,14},{12,8},{14,10},{16,20},{18,... | collective-permute-start | bytes 1769480 | tf_op jit(solution)/shard_map/ppermute | solution.py:54
  242.8 28.2 %collective-permute-start.41 = (bf16[192,768]{1,0:T(8,128)(2,1)}, bf16[192,768]{1,0:T(8,128)(2,1)}, u32[]{:S(2)}, u32[]{:S(2)}) collective-permute-start(bf16[192,768]{1,0:T(8,128)(2,1)} %get-tuple-element.447), channel_id=1, source_target_pairs={{0,4},{2,6},{4,0},{6,2},{8,12},{10,14},{12,8},{14,10},{16,20},{18,... | collective-permute-start | bytes 884744 | tf_op jit(solution)/shard_map/ppermute | solution.py:54
  243.8 27.2 %collective-permute-start.42 = (bf16[192,768]{1,0:T(8,128)(2,1)}, bf16[192,768]{1,0:T(8,128)(2,1)}, u32[]{:S(2)}, u32[]{:S(2)}) collective-permute-start(bf16[192,768]{1,0:T(8,128)(2,1)} %get-tuple-element.448), channel_id=1, source_target_pairs={{0,2},{2,0},{4,6},{6,4},{8,10},{10,8},{12,14},{14,12},{16,18},{18,... | collective-permute-start | bytes 884744 | tf_op jit(solution)/shard_map/ppermute | solution.py:54
  245.8 36.3 %all-to-all-start.1 = ((bf16[16,80,384]{2,1,0:T(8,128)(2,1)}), bf16[16,80,384]{2,1,0:T(8,128)(2,1)S(1)}, u32[]{:S(2)}, u32[]{:S(2)}) async-start(bf16[16,80,384]{2,1,0:T(8,128)(2,1)} %pad_maximum_fusion), calls=%async_computation.1 | async-start | bytes 1966080 | tf_op jit(solution)/shard_map/all_to_all | solution.py:1266
  261.4 16.7 %collective-permute-start.39 = (bf16[192,768]{1,0:T(8,128)(2,1)}, bf16[192,768]{1,0:T(8,128)(2,1)S(1)}, u32[]{:S(2)}, u32[]{:S(2)}) collective-permute-start(bf16[192,768]{1,0:T(8,128)(2,1)} %get-tuple-element.437), channel_id=1, source_target_pairs={{0,4},{2,6},{4,0},{6,2},{8,12},{10,14},{12,8},{14,10},{16,20},{18,... | collective-permute-start | bytes 884744 | tf_op jit(solution)/shard_map/ppermute | solution.py:54
  262.2 16.0 %collective-permute-start.40 = (bf16[192,768]{1,0:T(8,128)(2,1)}, bf16[192,768]{1,0:T(8,128)(2,1)S(1)}, u32[]{:S(2)}, u32[]{:S(2)}) collective-permute-start(bf16[192,768]{1,0:T(8,128)(2,1)} %get-tuple-element.438), channel_id=1, source_target_pairs={{0,2},{2,0},{4,6},{6,4},{8,10},{10,8},{12,14},{14,12},{16,18},{18,... | collective-permute-start | bytes 884744 | tf_op jit(solution)/shard_map/ppermute | solution.py:54
  273.5 13.9 %collective-permute-start.47 = (bf16[96,1536]{1,0:T(8,128)(2,1)}, bf16[96,1536]{1,0:T(8,128)(2,1)}, u32[]{:S(2)}, u32[]{:S(2)}) collective-permute-start(bf16[96,1536]{1,0:T(8,128)(2,1)} %get-tuple-element.455), channel_id=1, source_target_pairs={{0,8},{2,10},{4,12},{6,14},{8,0},{10,2},{12,4},{14,6},{16,24},{18,... | collective-permute-start | bytes 884744 | tf_op jit(solution)/shard_map/ppermute | solution.py:54
  282.0 7.1 %collective-permute-start.44 = (bf16[48,1536]{1,0:T(8,128)(2,1)}, bf16[48,1536]{1,0:T(8,128)(2,1)S(1)}, u32[]{:S(2)}, u32[]{:S(2)}) collective-permute-start(bf16[48,1536]{1,0:T(8,128)(2,1)} %get-tuple-element.474), channel_id=1, source_target_pairs={{0,8},{2,10},{4,12},{6,14},{8,0},{10,2},{12,4},{14,6},{16,24},{18,... | collective-permute-start | bytes 442376 | tf_op jit(solution)/shard_map/ppermute | solution.py:54
  283.0 16.7 %collective-permute-start.45 = (bf16[48,1536]{1,0:T(8,128)(2,1)}, bf16[48,1536]{1,0:T(8,128)(2,1)}, u32[]{:S(2)}, u32[]{:S(2)}) collective-permute-start(bf16[48,1536]{1,0:T(8,128)(2,1)} %get-tuple-element.475), channel_id=1, source_target_pairs={{0,16},{2,18},{4,20},{6,22},{8,24},{10,26},{12,28},{14,30},{16,0},... | collective-permute-start | bytes 442376 | tf_op jit(solution)/shard_map/ppermute | solution.py:54
  284.6 15.1 %collective-permute-start.46 = (bf16[48,1536]{1,0:T(8,128)(2,1)}, bf16[48,1536]{1,0:T(8,128)(2,1)}, u32[]{:S(2)}, u32[]{:S(2)}) collective-permute-start(bf16[48,1536]{1,0:T(8,128)(2,1)} %get-tuple-element.476), channel_id=1, source_target_pairs={{0,24},{2,26},{4,28},{6,30},{8,16},{10,18},{12,20},{14,22},{16,8},... | collective-permute-start | bytes 442376 | tf_op jit(solution)/shard_map/ppermute | solution.py:54
  289.1 4.8 %collective-permute-start.48 = (f32[8,384]{1,0:T(8,128)S(1)}, f32[8,384]{1,0:T(8,128)S(1)}, u32[]{:S(2)}, u32[]{:S(2)}) collective-permute-start(f32[8,384]{1,0:T(8,128)S(1)} %slice_add_fusion.1), channel_id=1, source_target_pairs={{0,1},{1,0},{2,3},{3,2},{4,5},{5,4},{6,7},{7,6},{8,9},{9,8},{10,11... | collective-permute-start | bytes 36872 | tf_op jit(solution)/shard_map/ppermute | solution.py:58
  290.9 13.7 %collective-permute-start.49 = (bf16[48,1536]{1,0:T(8,128)(2,1)S(1)}, bf16[48,1536]{1,0:T(8,128)(2,1)}, u32[]{:S(2)}, u32[]{:S(2)}) collective-permute-start(bf16[48,1536]{1,0:T(8,128)(2,1)S(1)} %slice.128), channel_id=1, source_target_pairs={{0,16},{2,18},{4,20},{6,22},{8,24},{10,26},{12,28},{14,30},{16,0},... | collective-permute-start | bytes 442376 | tf_op jit(solution)/shard_map/ppermute | solution.py:54
  (57 other events, 291.8 us)

commit v6 on v5

--- a/solution.py
+++ b/solution.py
@@ -14,7 +14,7 @@
 TILE = 128
 WIDE = 256
 HIDDEN = 512
-CHUNKS = 4
+CHUNKS = 2
 ROWS = 64
 
 EPS = 1e-06
@@ -347,6 +347,10 @@
 
 def grad_structs(width, columns):
     return [struct((width // 2, columns // 2), BF16)] * 4
+
+
+def both_of(own_ref, peer_ref, rows):
+    return own_ref[rows, :].astype(F32) + peer_ref[rows, :].astype(F32)
 
 
 def root_of(value):
@@ -626,7 +630,7 @@
         )
 
     each_pair(pairs, attend)
-    partial_ref[...] = nt(attended_ref[...], weights_ref[:, 3 * part :])
+    partial_ref[...] = nt(attended_ref[...], weights_ref[:, 3 * part :]).astype(BF16)
 
 
 def self_forward(normed, bias, quarters):
@@ -641,7 +645,7 @@
             struct((targets, 3 * part), BF16),
             struct((targets, part), BF16),
             struct((pairs, 8, targets), F32),
-            struct((targets, width), F32),
+            struct((targets, width), BF16),
         ],
         [
             pltpu.VMEM((width, columns), BF16),
@@ -701,7 +705,7 @@
     gain = gains_ref[1:2, :]
 
     def norm(rows):
-        value = tokens_ref[rows, :] + (partial_ref[rows, :] + peer_ref[rows, :])
+        value = tokens_ref[rows, :] + both_of(partial_ref, peer_ref, rows)
         h_ref[rows, :] = value
         normed_ref[rows, :] = (value * root_of(value) * gain).astype(BF16)
 
@@ -721,7 +725,8 @@
     each_pair(pairs, attend)
     count = out_refs[0].shape[0]
     for i, out_ref in enumerate(out_refs):
-        out_ref[...] = nt(att_ref[i * count : (i + 1) * count, :], weights_ref[:, part:])
+        att = att_ref[i * count : (i + 1) * count, :]
+        out_ref[...] = nt(att, weights_ref[:, part:]).astype(BF16)
 
 
 def cross_forward(tokens, partial, peer, gains, key_value, dead, quarters):
@@ -738,7 +743,7 @@
             struct((targets, part), BF16),
             struct((targets, part), BF16),
             struct((pairs, 8, targets), F32),
-            *[struct((targets // CHUNKS, width), F32)] * CHUNKS,
+            *[struct((targets // CHUNKS, width), BF16)] * CHUNKS,
         ],
         [
             pltpu.VMEM((width, columns), BF16),
@@ -762,7 +767,7 @@
 
         def norm(rows):
             own = pl.ds(pl.multiple_of(rows.start + i * count, rows.size), rows.size)
-            value = before_ref[own, :] + (partial_ref[rows, :] + peer_ref[rows, :])
+            value = before_ref[own, :] + both_of(partial_ref, peer_ref, rows)
             h_ref[own, :] = value
             normed_ref[own, :] = (value * root_of(value) * gain).astype(BF16)
 
@@ -1289,10 +1294,13 @@
     small = jnp.sum(back[:, count:].astype(F32), axis=0)
     small = small[:8] + small[8:]
     both = small + swap_cores(small)
-    last, encoder_grad, small, both = after((last, encoder_grad, small, both))
-    sum_ffn, sum_cross, sum_self = scatter_last(ffn), scatter_last(cross), scatter_last(last)
     table = small[6:8].reshape(2, heads // 2, TILE)[:, :, : bias_table.shape[0]]
     grad_table = table.transpose(1, 0, 2).reshape(heads, -1).T
+    grad_gains = [both[0:4:3].reshape(-1), small[1:5:3].reshape(-1), small[2:6:3].reshape(-1)]
+    last, encoder_grad, grad_gains, grad_table = after(
+        (last, encoder_grad, grad_gains, grad_table)
+    )
+    sum_ffn, sum_cross, sum_self = scatter_last(ffn), scatter_last(cross), scatter_last(last)
 
     def parts(value, count):
         step = value.shape[1] // count
@@ -1305,9 +1313,7 @@
         layer_out[None],
         decoder_grad[None],
         encoder_grad,
-        both[0:4:3].reshape(-1),
-        small[1:5:3].reshape(-1),
-        small[2:6:3].reshape(-1),
+        *grad_gains,
         grad_self_query,
         grad_self_key,
         grad_self_value,

time: 307 us -> 304 us (level)
    unnamed x106 -> x108, local copies, waits for them, and re-layouts: 9.87 us -> 9.42 us
  transfers between devices with their start and end apart: 52 -> 50, of which waited for: 22 -> 21; matrix products, arithmetic and copies ran while one was open for 6% -> 6% of each run, Pallas kernels for 41% -> 41%
where the time goes in v6:
time: 304 us; the launch traced here: 303 us
  Pallas kernels  150 us (49%)
  waiting for transfers between devices  63.3 us (21%)
  starting transfers between devices  57.4 us (19%)
  local copies, waits for them, and re-layouts  22.8 us (8%)
  other arithmetic  5.85 us (2%)
  between operations  3.38 us (1%)
    pallas_call x21, Pallas kernels, kernel_call(): pl.pallas_call(kernel, out_shape=outs, in_specs=in_specs or [everywhere]...  150 us
    ppermute x38, waiting for transfers between devices, swap(): return lax.ppermute(value, 'dp', [(i, i ^ mask) for i in range(size)])  61.4 us
    ppermute x38, starting transfers between devices, swap(): return lax.ppermute(value, 'dp', [(i, i ^ mask) for i in range(size)])  47.9 us
    unnamed x108, local copies, waits for them, and re-layouts  9.42 us
  transfers between devices with their start and end apart: 50, of which 21 were waited for; matrix products, arithmetic and copies ran while one was open for 6% of the time, Pallas kernels for 41%

profile of v6, /device:TPU:0, one launch (start us, length us, event | category | flops | bytes accessed | tf_op | source)
XLA Modules:
  0.0 303.3 jit_solution(7065622657999666031)
XLA Ops:
  0.7 2.0 shard_map.350.refs_0_
  2.7 3.0 collective-permute-start
  5.7 2.6 collective-permute-start.1
  11.7 7.0 %shard_map.349 = (f32[512,768]{1,0:T(8,128)}, bf16[512,768]{1,0:T(8,128)(2,1)}, bf16[768,512]{1,0:T(8,128)(2,1)}, f32[8,768]{1,0:T(8,128)}, bf16[768,768]{1,0:T(...) custom-call(bf16[512,768]{1,0:T(8,128)(2,1)} %bitcast.30, bf16[512,768]{1,0:T(8,128)(2,1)} %bitcast.31, ...), custom_call_target="tpu_custom_call" | custom-call | flops 2000000000 | bytes 1 | tf_op jit(solution)/shard_map/pallas_call | solution.py:189
  19.9 1.5 gather_fusion
  22.8 1.8 shard_map.352.refs_0_
  25.5 2.1 shard_map.351
  27.7 1.5 collective-permute-start.2
  33.7 1.7 shard_map.353
  35.4 1.5 collective-permute-start.5
  36.9 1.5 collective-permute-start.6
  39.1 3.8 %all-to-all-start = ((bf16[16,64,384]{2,1,0:T(8,128)(2,1)}), bf16[16,64,384]{2,1,0:T(8,128)(2,1)S(1)}, u32[]{:S(2)}, u32[]{:S(2)}) async-start(bf16[16,64,384]{2,1,0:T(8,128)(2,1)} %gather_fusion), calls=%async_computation | async-start | bytes 1572864 | tf_op jit(solution)/shard_map/all_to_all | solution.py:1192
  45.3 3.3 %shard_map.354 = (bf16[384,1536]{1,0:T(8,128)(2,1)}, bf16[384,1536]{1,0:T(8,128)(2,1)}) custom-call(bf16[144,1536]{1,0:T(8,128)(2,1)} %get-tuple-element.284.refs_0_, bf16[48,1536]{1,0:T(8,128)(2,1)} %get-tuple-element.285.refs_1_, bf16[144,1536]{1,0:T(8,128)(2,1)} %copy-done.39, bf16[48,1536]{1,0:T(8,128)(2,1)} %copy-done.50, ...), custom_call_target="tpu_custom_call" | custom-call | flops 40000000000 | bytes 1 | tf_op jit(solution)/shard_map/pallas_call | solution.py:189
  48.5 2.0 collective-permute-start.7
  50.6 2.3 collective-permute-start.10
  54.4 19.3 %collective-permute-done.10.refs_2_ = bf16[48,3072]{1,0:T(8,128)(2,1)} collective-permute-done((bf16[48,3072]{1,0:T(8,128)(2,1)S(1)}, bf16[48,3072]{1,0:T(8,128)(2,1)}, u32[]{:S(2)}, u32[]{:S(2)}) %collective-permute-start.10) | collective-permute-done | bytes 294944 | tf_op jit(solution)/shard_map/ppermute | solution.py:54
  73.7 6.1 %collective-permute-done.7.refs_1_ = bf16[384,1536]{1,0:T(8,128)(2,1)S(1)} collective-permute-done((bf16[384,1536]{1,0:T(8,128)(2,1)}, bf16[384,1536]{1,0:T(8,128)(2,1)S(1)}, u32[]{:S(2)}, u32[]{:S(2)}) %collective-permute-start.7) | collective-permute-done | bytes 1179680 | tf_op jit(solution)/shard_map/ppermute | solution.py:54
  79.8 2.0 collective-permute-done.11.refs_3_
  82.5 2.3 shard_map.355
  87.4 12.4 %shard_map.356 = (bf16[512,1152]{1,0:T(8,128)(2,1)}, bf16[512,384]{1,0:T(8,128)(2,1)}, f32[3,8,512]{2,1,0:T(8,128)}, bf16[512,768]{1,0:T(8,128)(2,1)}) custom-call(bf16[512,768]{1,0:T(8,128)(2,1)} %get-tuple-element.313.normed_ref, f32[3,8,512]{2,1,0:T(8,128)} %pad.4.bias_ref, bf16[384,1536]{1,0:T(8,128)(2,1)} %get-tuple-element.315.refs_0_, ...), custom_call_target="tpu_custom_call" | custom-call | flops 12000000000 | bytes 1 | tf_op jit(solution)/shard_map/pallas_call | solution.py:189
  101.7 1.5 collective-permute-start.18
  105.8 7.8 %shard_map.357 = (bf16[1024,768]{1,0:T(8,128)(2,1)}, bf16[1024,768]{1,0:T(8,128)(2,1)}) custom-call(s32[1]{0:T(128)} %bitcast.9.core_ref, bf16[1024,384]{1,0:T(8,128)(2,1)} %bitcast.26, bf16[1024,384]{1,0:T(8,128)(2,1)} %copy-done.24, bf16[768,768]{1,0:T(8,128)(2,1)} %get-tuple-element.326.order_ref, bf16[384,1536]{1,0:T(8,128)(2,1)} %get-tuple-element.327.refs_0_, ...), custom_call_target="tpu_custom_call" | custom-call | flops 8000000000 | bytes 1 | tf_op jit(solution)/shard_map/pallas_call | solution.py:189
  114.6 15.8 %shard_map.358 = (f32[512,768]{1,0:T(8,128)}, bf16[512,768]{1,0:T(8,128)(2,1)}, bf16[512,384]{1,0:T(8,128)(2,1)}, bf16[512,384]{1,0:T(8,128)(2,1)}, f32[3,8,512]...) custom-call(f32[512,768]{1,0:T(8,128)} %get-tuple-element.255.tokens_ref, ...), custom_call_target="tpu_custom_call" | custom-call | flops 16000000000 | bytes 1 | tf_op jit(solution)/shard_map/pallas_call | solution.py:189
  133.7 15.9 %shard_map.359 = (f32[512,768]{1,0:T(8,128)}, f32[512,768]{1,0:T(8,128)}, f32[512,768]{1,0:T(8,128)}, bf16[384,1536]{1,0:T(8,128)(2,1)}, bf16[384,1536]{1,0:T(8,...) custom-call(f32[512,768]{1,0:T(8,128)} %get-tuple-element.331.before_ref.h_ref, ...), custom_call_target="tpu_custom_call" | custom-call | flops 20000000000 | bytes 1 | tf_op jit(solution)/shard_map/pallas_call | solution.py:189
  154.5 19.9 %shard_map.360 = (f32[512,768]{1,0:T(8,128)}, bf16[512,768]{1,0:T(8,128)(2,1)}, bf16[512,384]{1,0:T(8,128)(2,1)}, bf16[1024,768]{1,0:T(8,128)(2,1)}, f32[512,768]{1,0:T(8,128)}, /*index=5*/f32[8,768]{1,0:T(8,128)}) custom-call(bf16[512,768]{1,0:T(8,128)(2,1)} %get-tuple-element.332.cot_ref, f32[512,768]{1,0:T(8,128)} %get-tuple-element.344.partial_ref, ...), custom_call_target="tpu_custom_call" | custom-call | flops 17999998976 | bytes 1 | tf_op jit(solution)/shard_map/pallas_call | solution.py:189
  174.3 4.1 %collective-permute-done.22.left_in_ref.refs_1_ = bf16[384,1536]{1,0:T(8,128)(2,1)S(1)} collective-permute-done((bf16[384,1536]{1,0:T(8,128)(2,1)}, bf16[384,1536]{1,0:T(8,128)(2,1)S(1)}, u32[]{:S(2)}, u32[]{:S(2)}) %collective-permute-start.22) | collective-permute-done | bytes 1179680 | tf_op jit(solution)/shard_map/ppermute | solution.py:54
  179.7 3.4 %shard_map.361 = (bf16[192,1536]{1,0:T(8,128)(2,1)}, bf16[192,1536]{1,0:T(8,128)(2,1)}) custom-call(bf16[384,1536]{1,0:T(8,128)(2,1)} %get-tuple-element.383.left_ref.refs_0_, bf16[384,1536]{1,0:T(8,128)(2,1)} %get-tuple-element.386.right_ref.refs_3_, bf16[384,1536]{1,0:T(8,128)(2,1)} %copy-done.23, ...), custom_call_target="tpu_custom_call" | custom-call | flops 2000000000 | bytes 1 | tf_op jit(solution)/shard_map/pallas_call | solution.py:189
  185.0 12.5 %shard_map.362 = (bf16[1024,384]{1,0:T(8,128)(2,1)}, bf16[1024,384]{1,0:T(8,128)(2,1)}, bf16[384,768]{1,0:T(8,128)(2,1)}, bf16[384,768]{1,0:T(8,128)(2,1)}, bf16...) custom-call(s32[1]{0:T(128)} %bitcast.9.core_ref, bf16[512,768]{1,0:T(8,128)(2,1)} %get-tuple-element.369.normed_ref, ...), custom_call_target="tpu_custom_call" | custom-call | flops 12000000000 | bytes 1 | tf_op jit(solution)/shard_map/pallas_call | solution.py:189
  197.5 1.5 collective-permute-done.26.refs_2_
  200.7 3.4 %shard_map.363 = (f32[48,3072]{1,0:T(8,128)}, bf16[48,3072]{1,0:T(8,128)(2,1)}, bf16[48,3072]{1,0:T(8,128)(2,1)}, bf16[48,3072]{1,0:T(8,128)(2,1)}) custom-call(bf16[384,1536]{1,0:T(8,128)(2,1)} %get-tuple-element.383.left_ref.refs_0_, bf16[384,1536]{1,0:T(8,128)(2,1)} %copy-done.23, bf16[192,1536]{1,0:T(8,128)(2,1)} %copy-done.37, ...), custom_call_target="tpu_custom_call" | custom-call | flops 2000000000 | bytes 1 | tf_op jit(solution)/shard_map/pallas_call | solution.py:189
  206.1 2.2 collective-permute-start.30
  208.4 1.9 collective-permute-start.31
  210.2 23.0 %shard_map.364 = (f32[512,768]{1,0:T(8,128)}, f32[512,768]{1,0:T(8,128)}, bf16[16,384]{1,0:T(8,128)(2,1)}, bf16[384,768]{1,0:T(8,128)(2,1)}, bf16[384,768]{1,0:T...) custom-call(f32[512,768]{1,0:T(8,128)} %get-tuple-element.409.g_in_ref, ...), custom_call_target="tpu_custom_call" | custom-call | flops 22000001024 | bytes 1 | tf_op jit(solution)/shard_map/pallas_call | solution.py:189
  237.7 2.1 shard_map.367
  242.9 4.0 %all-to-all-start.1 = ((bf16[16,80,384]{2,1,0:T(8,128)(2,1)}), bf16[16,80,384]{2,1,0:T(8,128)(2,1)S(1)}, u32[]{:S(2)}, u32[]{:S(2)}) async-start(bf16[16,80,384]{2,1,0:T(8,128)(2,1)} %pad_maximum_fusion), calls=%async_computation.1 | async-start | bytes 1966080 | tf_op jit(solution)/shard_map/all_to_all | solution.py:1271
  248.1 7.1 %shard_map.365 = (f32[512,768]{1,0:T(8,128)}, bf16[512,768]{1,0:T(8,128)(2,1)}) custom-call(f32[512,768]{1,0:T(8,128)} %get-tuple-element.425.g_ref, f32[512,768]{1,0:T(8,128)} %get-tuple-element.426.partial_ref, f32[512,768]{1,0:T(8,128)} %copy-done.4, f32[512,768]{1,0:T(8,128)} %get-tuple-element.255.tokens_ref, f32[512,768]{1,0:T(8,128)} %get-tuple-element.345.h_ref, ...), custom_call_target="tpu_custom_call" | custom-call | flops 1000000000 | bytes 1 | tf_op jit(solution)/shard_map/pallas_call | solution.py:189
  256.4 2.1 shard_map.366
  260.7 7.4 %collective-permute-done.39.refs_2_ = bf16[192,768]{1,0:T(8,128)(2,1)} collective-permute-done((bf16[192,768]{1,0:T(8,128)(2,1)}, bf16[192,768]{1,0:T(8,128)(2,1)}, u32[]{:S(2)}, u32[]{:S(2)}) %collective-permute-start.39) | collective-permute-done | bytes 294944 | tf_op jit(solution)/shard_map/ppermute | solution.py:54
  268.1 2.5 shard_map.368
  270.9 4.3 %collective-permute-done.37.refs_2_ = bf16[192,768]{1,0:T(8,128)(2,1)S(1)} collective-permute-done((bf16[192,768]{1,0:T(8,128)(2,1)}, bf16[192,768]{1,0:T(8,128)(2,1)S(1)}, u32[]{:S(2)}, u32[]{:S(2)}) %collective-permute-start.37) | collective-permute-done | bytes 294944 | tf_op jit(solution)/shard_map/ppermute | solution.py:54
  276.7 2.4 shard_map.369
  280.1 1.5 collective-permute-start.43
  281.6 1.9 collective-permute-start.44
  284.5 1.5 collective-permute-done.42
  286.7 1.6 collective-permute-start.47
  290.2 1.5 gather_fusion.1
  292.3 4.4 %collective-permute-done.43 = bf16[48,1536]{1,0:T(8,128)(2,1)} collective-permute-done((bf16[48,1536]{1,0:T(8,128)(2,1)}, bf16[48,1536]{1,0:T(8,128)(2,1)}, u32[]{:S(2)}, u32[]{:S(2)}) %collective-permute-start.43) | collective-permute-done | bytes 147488 | tf_op jit(solution)/shard_map/ppermute | solution.py:54
  298.6 3.1 %collective-permute-done.47 = bf16[48,1536]{1,0:T(8,128)(2,1)} collective-permute-done((bf16[48,1536]{1,0:T(8,128)(2,1)S(1)}, bf16[48,1536]{1,0:T(8,128)(2,1)}, u32[]{:S(2)}, u32[]{:S(2)}) %collective-permute-start.47) | collective-permute-done | bytes 147488 | tf_op jit(solution)/shard_map/ppermute | solution.py:54
  (234 shorter events, 59.6 us)
Async XLA Ops:
  2.7 22.0 %collective-permute-start = (bf16[48,3072]{1,0:T(8,128)(2,1)}, bf16[48,3072]{1,0:T(8,128)(2,1)S(1)}, u32[]{:S(2)}, u32[]{:S(2)}) collective-permute-start(bf16[48,3072]{1,0:T(8,128)(2,1)} %shard_map.350.refs_0_), channel_id=1, source_target_pairs={{0,8},{2,10},{4,12},{6,14},{8,0},{10,2},{12,4},{14,6},{16,24},{18,... | collective-permute-start | bytes 884744 | tf_op jit(solution)/shard_map/ppermute | solution.py:54
  5.7 19.0 %collective-permute-start.1 = (bf16[48,3072]{1,0:T(8,128)(2,1)}, bf16[48,3072]{1,0:T(8,128)(2,1)S(1)}, u32[]{:S(2)}, u32[]{:S(2)}) collective-permute-start(bf16[48,3072]{1,0:T(8,128)(2,1)} %shard_map.350.refs_0_), channel_id=1, source_target_pairs={{0,16},{2,18},{4,20},{6,22},{8,24},{10,26},{12,28},{14,30},{16,0},... | collective-permute-start | bytes 884744 | tf_op jit(solution)/shard_map/ppermute | solution.py:54
  24.7 8.3 %collective-permute-start.4 = (bf16[48,3072]{1,0:T(8,128)(2,1)S(1)}, bf16[48,3072]{1,0:T(8,128)(2,1)S(1)}, u32[]{:S(2)}, u32[]{:S(2)}) collective-permute-start(bf16[48,3072]{1,0:T(8,128)(2,1)S(1)} %collective-permute-done.1.refs_2_), channel_id=1, source_target_pairs={{0,8},{2,10},{4,12},{6,14},{8,0},{10,2},{12,4},{14,6},{16,24},{18,... | collective-permute-start | bytes 884744 | tf_op jit(solution)/shard_map/ppermute | solution.py:54
  27.7 16.5 %collective-permute-start.2 = (bf16[144,1536]{1,0:T(8,128)(2,1)}, bf16[144,1536]{1,0:T(8,128)(2,1)S(1)}, u32[]{:S(2)}, u32[]{:S(2)}) collective-permute-start(bf16[144,1536]{1,0:T(8,128)(2,1)} %get-tuple-element.284.refs_0_), channel_id=1, source_target_pairs={{0,4},{2,6},{4,0},{6,2},{8,12},{10,14},{12,8},{14,10},{16,20},{18,... | collective-permute-start | bytes 1327112 | tf_op jit(solution)/shard_map/ppermute | solution.py:54
  29.2 14.9 %collective-permute-start.3 = (bf16[144,1536]{1,0:T(8,128)(2,1)}, bf16[144,1536]{1,0:T(8,128)(2,1)S(1)}, u32[]{:S(2)}, u32[]{:S(2)}) collective-permute-start(bf16[144,1536]{1,0:T(8,128)(2,1)} %get-tuple-element.288.refs_4_), channel_id=1, source_target_pairs={{0,2},{2,0},{4,6},{6,4},{8,10},{10,8},{12,14},{14,12},{16,18},{18,... | collective-permute-start | bytes 1327112 | tf_op jit(solution)/shard_map/ppermute | solution.py:54
  35.4 7.5 %collective-permute-start.5 = (bf16[48,1536]{1,0:T(8,128)(2,1)}, bf16[48,1536]{1,0:T(8,128)(2,1)S(1)}, u32[]{:S(2)}, u32[]{:S(2)}) collective-permute-start(bf16[48,1536]{1,0:T(8,128)(2,1)} %get-tuple-element.285.refs_1_), channel_id=1, source_target_pairs={{0,4},{2,6},{4,0},{6,2},{8,12},{10,14},{12,8},{14,10},{16,20},{18,... | collective-permute-start | bytes 442376 | tf_op jit(solution)/shard_map/ppermute | solution.py:54
  36.9 7.2 %collective-permute-start.6 = (bf16[48,1536]{1,0:T(8,128)(2,1)}, bf16[48,1536]{1,0:T(8,128)(2,1)S(1)}, u32[]{:S(2)}, u32[]{:S(2)}) collective-permute-start(bf16[48,1536]{1,0:T(8,128)(2,1)} %get-tuple-element.289.refs_5_), channel_id=1, source_target_pairs={{0,2},{2,0},{4,6},{6,4},{8,10},{10,8},{12,14},{14,12},{16,18},{18,... | collective-permute-start | bytes 442376 | tf_op jit(solution)/shard_map/ppermute | solution.py:54
  39.1 34.6 %all-to-all-start = ((bf16[16,64,384]{2,1,0:T(8,128)(2,1)}), bf16[16,64,384]{2,1,0:T(8,128)(2,1)S(1)}, u32[]{:S(2)}, u32[]{:S(2)}) async-start(bf16[16,64,384]{2,1,0:T(8,128)(2,1)} %gather_fusion), calls=%async_computation | async-start | bytes 1572864 | tf_op jit(solution)/shard_map/all_to_all | solution.py:1192
  48.5 31.2 %collective-permute-start.7 = (bf16[384,1536]{1,0:T(8,128)(2,1)}, bf16[384,1536]{1,0:T(8,128)(2,1)S(1)}, u32[]{:S(2)}, u32[]{:S(2)}) collective-permute-start(bf16[384,1536]{1,0:T(8,128)(2,1)} %get-tuple-element.315.refs_0_), channel_id=1, source_target_pairs={{0,2},{2,0},{4,6},{6,4},{8,10},{10,8},{12,14},{14,12},{16,18},{18,... | collective-permute-start | bytes 3538952 | tf_op jit(solution)/shard_map/ppermute | solution.py:54
  50.6 29.2 %collective-permute-start.8 = (bf16[384,1536]{1,0:T(8,128)(2,1)}, bf16[384,1536]{1,0:T(8,128)(2,1)S(1)}, u32[]{:S(2)}, u32[]{:S(2)}) collective-permute-start(bf16[384,1536]{1,0:T(8,128)(2,1)} %get-tuple-element.327.refs_0_), channel_id=1, source_target_pairs={{0,4},{2,6},{4,0},{6,2},{8,12},{10,14},{12,8},{14,10},{16,20},{18,... | collective-permute-start | bytes 3538952 | tf_op jit(solution)/shard_map/ppermute | solution.py:54
  50.6 23.1 %collective-permute-start.10 = (bf16[48,3072]{1,0:T(8,128)(2,1)S(1)}, bf16[48,3072]{1,0:T(8,128)(2,1)}, u32[]{:S(2)}, u32[]{:S(2)}) collective-permute-start(bf16[48,3072]{1,0:T(8,128)(2,1)S(1)} %copy-done.43), channel_id=1, source_target_pairs={{0,16},{2,18},{4,20},{6,22},{8,24},{10,26},{12,28},{14,30},{16,0},... | collective-permute-start | bytes 884744 | tf_op jit(solution)/shard_map/ppermute | solution.py:54
  52.9 20.8 %collective-permute-start.9 = (bf16[48,3072]{1,0:T(8,128)(2,1)S(1)}, bf16[48,3072]{1,0:T(8,128)(2,1)}, u32[]{:S(2)}, u32[]{:S(2)}) collective-permute-start(bf16[48,3072]{1,0:T(8,128)(2,1)S(1)} %copy-done.43), channel_id=1, source_target_pairs={{0,8},{2,10},{4,12},{6,14},{8,0},{10,2},{12,4},{14,6},{16,24},{18,... | collective-permute-start | bytes 884744 | tf_op jit(solution)/shard_map/ppermute | solution.py:54
  73.6 8.1 %collective-permute-start.11 = (bf16[48,3072]{1,0:T(8,128)(2,1)}, bf16[48,3072]{1,0:T(8,128)(2,1)S(1)}, u32[]{:S(2)}, u32[]{:S(2)}) collective-permute-start(bf16[48,3072]{1,0:T(8,128)(2,1)} %collective-permute-done.10.refs_2_), channel_id=1, source_target_pairs={{0,8},{2,10},{4,12},{6,14},{8,0},{10,2},{12,4},{14,6},{16,24},{18,... | collective-permute-start | bytes 884744 | tf_op jit(solution)/shard_map/ppermute | solution.py:54
  84.8 16.8 %collective-permute-start.14 = (bf16[1024,384]{1,0:T(8,128)(2,1)S(1)}, bf16[1024,384]{1,0:T(8,128)(2,1)S(1)}, u32[]{:S(2)}, u32[]{:S(2)}) collective-permute-start(bf16[1024,384]{1,0:T(8,128)(2,1)S(1)} %bitcast.25), channel_id=1, source_target_pairs={{0,1},{1,0},{2,3},{3,2},{4,5},{5,4},{6,7},{7,6},{8,9},{9,8},{10,11... | collective-permute-start | bytes 2359304 | tf_op jit(solution)/shard_map/ppermute | solution.py:58
  84.9 16.0 %collective-permute-start.12 = (bf16[192,1536]{1,0:T(8,128)(2,1)}, bf16[192,1536]{1,0:T(8,128)(2,1)S(1)}, u32[]{:S(2)}, u32[]{:S(2)}) collective-permute-start(bf16[192,1536]{1,0:T(8,128)(2,1)} %get-tuple-element.336.refs_4_), channel_id=1, source_target_pairs={{0,4},{2,6},{4,0},{6,2},{8,12},{10,14},{12,8},{14,10},{16,20},{18,... | collective-permute-start | bytes 1769480 | tf_op jit(solution)/shard_map/ppermute | solution.py:54
  86.0 15.6 %collective-permute-start.13 = (bf16[192,1536]{1,0:T(8,128)(2,1)}, bf16[192,1536]{1,0:T(8,128)(2,1)S(1)}, u32[]{:S(2)}, u32[]{:S(2)}) collective-permute-start(bf16[192,1536]{1,0:T(8,128)(2,1)} %get-tuple-element.338.refs_8_), channel_id=1, source_target_pairs={{0,2},{2,0},{4,6},{6,4},{8,10},{10,8},{12,14},{14,12},{16,18},{18,... | collective-permute-start | bytes 1769480 | tf_op jit(solution)/shard_map/ppermute | solution.py:54
  101.6 12.1 %collective-permute-start.15 = (bf16[512,768]{1,0:T(8,128)(2,1)}, bf16[512,768]{1,0:T(8,128)(2,1)S(1)}, u32[]{:S(2)}, u32[]{:S(2)}) collective-permute-start(bf16[512,768]{1,0:T(8,128)(2,1)} %get-tuple-element.322.partial_ref), channel_id=1, source_target_pairs={{0,1},{1,0},{2,3},{3,2},{4,5},{5,4},{6,7},{7,6},{8,9},{9,8},{10,11... | collective-permute-start | bytes 2359304 | tf_op jit(solution)/shard_map/ppermute | solution.py:58
  101.7 28.8 %collective-permute-start.18 = (bf16[192,1536]{1,0:T(8,128)(2,1)S(1)}, bf16[192,1536]{1,0:T(8,128)(2,1)S(1)}, u32[]{:S(2)}, u32[]{:S(2)}) collective-permute-start(bf16[192,1536]{1,0:T(8,128)(2,1)S(1)} %copy-done.28), channel_id=1, source_target_pairs={{0,2},{2,0},{4,6},{6,4},{8,10},{10,8},{12,14},{14,12},{16,18},{18,... | collective-permute-start | bytes 1769480 | tf_op jit(solution)/shard_map/ppermute | solution.py:54
  103.2 27.7 %collective-permute-start.19 = (bf16[192,1536]{1,0:T(8,128)(2,1)S(1)}, bf16[192,1536]{1,0:T(8,128)(2,1)S(1)}, u32[]{:S(2)}, u32[]{:S(2)}) collective-permute-start(bf16[192,1536]{1,0:T(8,128)(2,1)S(1)} %collective-permute-done.12.refs_5_), channel_id=1, source_target_pairs={{0,2},{2,0},{4,6},{6,4},{8,10},{10,8},{12,14},{14,12},{16,18},{18,... | collective-permute-start | bytes 1769480 | tf_op jit(solution)/shard_map/ppermute | solution.py:54
  103.8 27.2 %collective-permute-start.20 = (bf16[192,1536]{1,0:T(8,128)(2,1)S(1)}, bf16[192,1536]{1,0:T(8,128)(2,1)S(1)}, u32[]{:S(2)}, u32[]{:S(2)}) collective-permute-start(bf16[192,1536]{1,0:T(8,128)(2,1)S(1)} %copy-done.29), channel_id=1, source_target_pairs={{0,4},{2,6},{4,0},{6,2},{8,12},{10,14},{12,8},{14,10},{16,20},{18,... | collective-permute-start | bytes 1769480 | tf_op jit(solution)/shard_map/ppermute | solution.py:54
  104.8 26.8 %collective-permute-start.21 = (bf16[192,1536]{1,0:T(8,128)(2,1)S(1)}, bf16[192,1536]{1,0:T(8,128)(2,1)}, u32[]{:S(2)}, u32[]{:S(2)}) collective-permute-start(bf16[192,1536]{1,0:T(8,128)(2,1)S(1)} %collective-permute-done.13.refs_9_), channel_id=1, source_target_pairs={{0,4},{2,6},{4,0},{6,2},{8,12},{10,14},{12,8},{14,10},{16,20},{18,... | collective-permute-start | bytes 1769480 | tf_op jit(solution)/shard_map/ppermute | solution.py:54
  149.6 3.7 %collective-permute-start.24 = (f32[512,768]{1,0:T(8,128)}, f32[512,768]{1,0:T(8,128)S(1)}, u32[]{:S(2)}, u32[]{:S(2)}) collective-permute-start(f32[512,768]{1,0:T(8,128)} %get-tuple-element.344.partial_ref), channel_id=1, source_target_pairs={{0,1},{1,0},{2,3},{3,2},{4,5},{5,4},{6,7},{7,6},{8,9},{9,8},{10,11... | collective-permute-start | bytes 4718600 | tf_op jit(solution)/shard_map/ppermute | solution.py:58
  149.8 29.9 %collective-permute-start.25 = (f32[512,768]{1,0:T(8,128)}, f32[512,768]{1,0:T(8,128)S(1)}, u32[]{:S(2)}, u32[]{:S(2)}) collective-permute-start(f32[512,768]{1,0:T(8,128)} %get-tuple-element.352.down_ref), channel_id=1, source_target_pairs={{0,1},{1,0},{2,3},{3,2},{4,5},{5,4},{6,7},{7,6},{8,9},{9,8},{10,11... | collective-permute-start | bytes 4718600 | tf_op jit(solution)/shard_map/ppermute | solution.py:58
  150.2 28.2 %collective-permute-start.22 = (bf16[384,1536]{1,0:T(8,128)(2,1)}, bf16[384,1536]{1,0:T(8,128)(2,1)S(1)}, u32[]{:S(2)}, u32[]{:S(2)}) collective-permute-start(bf16[384,1536]{1,0:T(8,128)(2,1)} %get-tuple-element.342), channel_id=1, source_target_pairs={{0,2},{2,0},{4,6},{6,4},{8,10},{10,8},{12,14},{14,12},{16,18},{18,... | collective-permute-start | bytes 3538952 | tf_op jit(solution)/shard_map/ppermute | solution.py:54
  151.7 28.0 %collective-permute-start.23 = (bf16[384,1536]{1,0:T(8,128)(2,1)}, bf16[384,1536]{1,0:T(8,128)(2,1)}, u32[]{:S(2)}, u32[]{:S(2)}) collective-permute-start(bf16[384,1536]{1,0:T(8,128)(2,1)} %get-tuple-element.343), channel_id=1, source_target_pairs={{0,4},{2,6},{4,0},{6,2},{8,12},{10,14},{12,8},{14,10},{16,20},{18,... | collective-permute-start | bytes 3538952 | tf_op jit(solution)/shard_map/ppermute | solution.py:54
  183.1 16.7 %collective-permute-start.28 = (f32[512,768]{1,0:T(8,128)S(1)}, f32[512,768]{1,0:T(8,128)S(1)}, u32[]{:S(2)}, u32[]{:S(2)}) collective-permute-start(f32[512,768]{1,0:T(8,128)S(1)} %copy-done.18), channel_id=1, source_target_pairs={{0,1},{1,0},{2,3},{3,2},{4,5},{5,4},{6,7},{7,6},{8,9},{9,8},{10,11... | collective-permute-start | bytes 4718600 | tf_op jit(solution)/shard_map/ppermute | solution.py:58
  183.1 16.0 %collective-permute-start.26 = (bf16[192,1536]{1,0:T(8,128)(2,1)}, bf16[192,1536]{1,0:T(8,128)(2,1)S(1)}, u32[]{:S(2)}, u32[]{:S(2)}) collective-permute-start(bf16[192,1536]{1,0:T(8,128)(2,1)} %get-tuple-element.367), channel_id=1, source_target_pairs={{0,4},{2,6},{4,0},{6,2},{8,12},{10,14},{12,8},{14,10},{16,20},{18,... | collective-permute-start | bytes 1769480 | tf_op jit(solution)/shard_map/ppermute | solution.py:54
  184.2 15.6 %collective-permute-start.27 = (bf16[192,1536]{1,0:T(8,128)(2,1)}, bf16[192,1536]{1,0:T(8,128)(2,1)S(1)}, u32[]{:S(2)}, u32[]{:S(2)}) collective-permute-start(bf16[192,1536]{1,0:T(8,128)(2,1)} %get-tuple-element.368), channel_id=1, source_target_pairs={{0,2},{2,0},{4,6},{6,4},{8,10},{10,8},{12,14},{14,12},{16,18},{18,... | collective-permute-start | bytes 1769480 | tf_op jit(solution)/shard_map/ppermute | solution.py:54
  204.0 29.2 %collective-permute-start.32 = (bf16[384,768]{1,0:T(8,128)(2,1)S(1)}, bf16[384,768]{1,0:T(8,128)(2,1)S(1)}, u32[]{:S(2)}, u32[]{:S(2)}) collective-permute-start(bf16[384,768]{1,0:T(8,128)(2,1)S(1)} %copy-done.33), channel_id=1, source_target_pairs={{0,2},{2,0},{4,6},{6,4},{8,10},{10,8},{12,14},{14,12},{16,18},{18,... | collective-permute-start | bytes 1769480 | tf_op jit(solution)/shard_map/ppermute | solution.py:54
  204.8 28.4 %collective-permute-start.33 = (bf16[384,768]{1,0:T(8,128)(2,1)S(1)}, bf16[384,768]{1,0:T(8,128)(2,1)S(1)}, u32[]{:S(2)}, u32[]{:S(2)}) collective-permute-start(bf16[384,768]{1,0:T(8,128)(2,1)S(1)} %copy-done.31), channel_id=1, source_target_pairs={{0,4},{2,6},{4,0},{6,2},{8,12},{10,14},{12,8},{14,10},{16,20},{18,... | collective-permute-start | bytes 1769480 | tf_op jit(solution)/shard_map/ppermute | solution.py:54
  205.8 27.4 %collective-permute-start.29 = (bf16[48,3072]{1,0:T(8,128)(2,1)}, bf16[48,3072]{1,0:T(8,128)(2,1)S(1)}, u32[]{:S(2)}, u32[]{:S(2)}) collective-permute-start(bf16[48,3072]{1,0:T(8,128)(2,1)} %get-tuple-element.401), channel_id=1, source_target_pairs={{0,8},{2,10},{4,12},{6,14},{8,0},{10,2},{12,4},{14,6},{16,24},{18,... | collective-permute-start | bytes 884744 | tf_op jit(solution)/shard_map/ppermute | solution.py:54
  206.1 27.1 %collective-permute-start.30 = (bf16[48,3072]{1,0:T(8,128)(2,1)}, bf16[48,3072]{1,0:T(8,128)(2,1)S(1)}, u32[]{:S(2)}, u32[]{:S(2)}) collective-permute-start(bf16[48,3072]{1,0:T(8,128)(2,1)} %get-tuple-element.402), channel_id=1, source_target_pairs={{0,16},{2,18},{4,20},{6,22},{8,24},{10,26},{12,28},{14,30},{16,0},... | collective-permute-start | bytes 884744 | tf_op jit(solution)/shard_map/ppermute | solution.py:54
  208.4 24.9 %collective-permute-start.31 = (bf16[48,3072]{1,0:T(8,128)(2,1)}, bf16[48,3072]{1,0:T(8,128)(2,1)S(1)}, u32[]{:S(2)}, u32[]{:S(2)}) collective-permute-start(bf16[48,3072]{1,0:T(8,128)(2,1)} %get-tuple-element.403), channel_id=1, source_target_pairs={{0,24},{2,26},{4,28},{6,30},{8,16},{10,18},{12,20},{14,22},{16,8},... | collective-permute-start | bytes 884744 | tf_op jit(solution)/shard_map/ppermute | solution.py:54
  234.1 12.9 %collective-permute-start.36 = (f32[512,768]{1,0:T(8,128)}, f32[512,768]{1,0:T(8,128)S(1)}, u32[]{:S(2)}, u32[]{:S(2)}) collective-permute-start(f32[512,768]{1,0:T(8,128)} %get-tuple-element.426.partial_ref), channel_id=1, source_target_pairs={{0,1},{1,0},{2,3},{3,2},{4,5},{5,4},{6,7},{7,6},{8,9},{9,8},{10,11... | collective-permute-start | bytes 4718600 | tf_op jit(solution)/shard_map/ppermute | solution.py:58
  234.3 6.6 %collective-permute-start.41 = (bf16[1024,384]{1,0:T(8,128)(2,1)}, bf16[1024,384]{1,0:T(8,128)(2,1)S(1)}, u32[]{:S(2)}, u32[]{:S(2)}) collective-permute-start(bf16[1024,384]{1,0:T(8,128)(2,1)} %get-tuple-element.465), channel_id=1, source_target_pairs={{0,1},{1,0},{2,3},{3,2},{4,5},{5,4},{6,7},{7,6},{8,9},{9,8},{10,11... | collective-permute-start | bytes 2359304 | tf_op jit(solution)/shard_map/ppermute | solution.py:58
  235.3 19.8 %collective-permute-start.34 = (bf16[384,768]{1,0:T(8,128)(2,1)}, bf16[384,768]{1,0:T(8,128)(2,1)}, u32[]{:S(2)}, u32[]{:S(2)}) collective-permute-start(bf16[384,768]{1,0:T(8,128)(2,1)} %get-tuple-element.423), channel_id=1, source_target_pairs={{0,2},{2,0},{4,6},{6,4},{8,10},{10,8},{12,14},{14,12},{16,18},{18,... | collective-permute-start | bytes 1769480 | tf_op jit(solution)/shard_map/ppermute | solution.py:54
  236.7 19.7 %collective-permute-start.35 = (bf16[384,768]{1,0:T(8,128)(2,1)}, bf16[384,768]{1,0:T(8,128)(2,1)}, u32[]{:S(2)}, u32[]{:S(2)}) collective-permute-start(bf16[384,768]{1,0:T(8,128)(2,1)} %get-tuple-element.424), channel_id=1, source_target_pairs={{0,4},{2,6},{4,0},{6,2},{8,12},{10,14},{12,8},{14,10},{16,20},{18,... | collective-permute-start | bytes 1769480 | tf_op jit(solution)/shard_map/ppermute | solution.py:54
  239.9 28.2 %collective-permute-start.39 = (bf16[192,768]{1,0:T(8,128)(2,1)}, bf16[192,768]{1,0:T(8,128)(2,1)}, u32[]{:S(2)}, u32[]{:S(2)}) collective-permute-start(bf16[192,768]{1,0:T(8,128)(2,1)} %get-tuple-element.445), channel_id=1, source_target_pairs={{0,4},{2,6},{4,0},{6,2},{8,12},{10,14},{12,8},{14,10},{16,20},{18,... | collective-permute-start | bytes 884744 | tf_op jit(solution)/shard_map/ppermute | solution.py:54
  240.8 27.2 %collective-permute-start.40 = (bf16[192,768]{1,0:T(8,128)(2,1)}, bf16[192,768]{1,0:T(8,128)(2,1)}, u32[]{:S(2)}, u32[]{:S(2)}) collective-permute-start(bf16[192,768]{1,0:T(8,128)(2,1)} %get-tuple-element.446), channel_id=1, source_target_pairs={{0,2},{2,0},{4,6},{6,4},{8,10},{10,8},{12,14},{14,12},{16,18},{18,... | collective-permute-start | bytes 884744 | tf_op jit(solution)/shard_map/ppermute | solution.py:54
  242.9 36.1 %all-to-all-start.1 = ((bf16[16,80,384]{2,1,0:T(8,128)(2,1)}), bf16[16,80,384]{2,1,0:T(8,128)(2,1)S(1)}, u32[]{:S(2)}, u32[]{:S(2)}) async-start(bf16[16,80,384]{2,1,0:T(8,128)(2,1)} %pad_maximum_fusion), calls=%async_computation.1 | async-start | bytes 1966080 | tf_op jit(solution)/shard_map/all_to_all | solution.py:1271
  258.5 16.7 %collective-permute-start.37 = (bf16[192,768]{1,0:T(8,128)(2,1)}, bf16[192,768]{1,0:T(8,128)(2,1)S(1)}, u32[]{:S(2)}, u32[]{:S(2)}) collective-permute-start(bf16[192,768]{1,0:T(8,128)(2,1)} %get-tuple-element.435), channel_id=1, source_target_pairs={{0,4},{2,6},{4,0},{6,2},{8,12},{10,14},{12,8},{14,10},{16,20},{18,... | collective-permute-start | bytes 884744 | tf_op jit(solution)/shard_map/ppermute | solution.py:54
  259.2 16.0 %collective-permute-start.38 = (bf16[192,768]{1,0:T(8,128)(2,1)}, bf16[192,768]{1,0:T(8,128)(2,1)S(1)}, u32[]{:S(2)}, u32[]{:S(2)}) collective-permute-start(bf16[192,768]{1,0:T(8,128)(2,1)} %get-tuple-element.436), channel_id=1, source_target_pairs={{0,2},{2,0},{4,6},{6,4},{8,10},{10,8},{12,14},{14,12},{16,18},{18,... | collective-permute-start | bytes 884744 | tf_op jit(solution)/shard_map/ppermute | solution.py:54
  270.6 13.9 %collective-permute-start.45 = (bf16[96,1536]{1,0:T(8,128)(2,1)}, bf16[96,1536]{1,0:T(8,128)(2,1)S(1)}, u32[]{:S(2)}, u32[]{:S(2)}) collective-permute-start(bf16[96,1536]{1,0:T(8,128)(2,1)} %get-tuple-element.453), channel_id=1, source_target_pairs={{0,8},{2,10},{4,12},{6,14},{8,0},{10,2},{12,4},{14,6},{16,24},{18,... | collective-permute-start | bytes 884744 | tf_op jit(solution)/shard_map/ppermute | solution.py:54
  279.1 7.0 %collective-permute-start.42 = (bf16[48,1536]{1,0:T(8,128)(2,1)}, bf16[48,1536]{1,0:T(8,128)(2,1)S(1)}, u32[]{:S(2)}, u32[]{:S(2)}) collective-permute-start(bf16[48,1536]{1,0:T(8,128)(2,1)} %get-tuple-element.472), channel_id=1, source_target_pairs={{0,8},{2,10},{4,12},{6,14},{8,0},{10,2},{12,4},{14,6},{16,24},{18,... | collective-permute-start | bytes 442376 | tf_op jit(solution)/shard_map/ppermute | solution.py:54
  280.1 16.6 %collective-permute-start.43 = (bf16[48,1536]{1,0:T(8,128)(2,1)}, bf16[48,1536]{1,0:T(8,128)(2,1)}, u32[]{:S(2)}, u32[]{:S(2)}) collective-permute-start(bf16[48,1536]{1,0:T(8,128)(2,1)} %get-tuple-element.473), channel_id=1, source_target_pairs={{0,16},{2,18},{4,20},{6,22},{8,24},{10,26},{12,28},{14,30},{16,0},... | collective-permute-start | bytes 442376 | tf_op jit(solution)/shard_map/ppermute | solution.py:54
  281.6 15.1 %collective-permute-start.44 = (bf16[48,1536]{1,0:T(8,128)(2,1)}, bf16[48,1536]{1,0:T(8,128)(2,1)}, u32[]{:S(2)}, u32[]{:S(2)}) collective-permute-start(bf16[48,1536]{1,0:T(8,128)(2,1)} %get-tuple-element.474), channel_id=1, source_target_pairs={{0,24},{2,26},{4,28},{6,30},{8,16},{10,18},{12,20},{14,22},{16,8},... | collective-permute-start | bytes 442376 | tf_op jit(solution)/shard_map/ppermute | solution.py:54
  286.1 5.6 %collective-permute-start.46 = (f32[8,384]{1,0:T(8,128)S(1)}, f32[8,384]{1,0:T(8,128)S(1)}, u32[]{:S(2)}, u32[]{:S(2)}) collective-permute-start(f32[8,384]{1,0:T(8,128)S(1)} %slice_add_fusion.1), channel_id=1, source_target_pairs={{0,1},{1,0},{2,3},{3,2},{4,5},{5,4},{6,7},{7,6},{8,9},{9,8},{10,11... | collective-permute-start | bytes 36872 | tf_op jit(solution)/shard_map/ppermute | solution.py:58
  286.7 15.0 %collective-permute-start.47 = (bf16[48,1536]{1,0:T(8,128)(2,1)S(1)}, bf16[48,1536]{1,0:T(8,128)(2,1)}, u32[]{:S(2)}, u32[]{:S(2)}) collective-permute-start(bf16[48,1536]{1,0:T(8,128)(2,1)S(1)} %slice.129), channel_id=1, source_target_pairs={{0,16},{2,18},{4,20},{6,22},{8,24},{10,26},{12,28},{14,30},{16,0},... | collective-permute-start | bytes 442376 | tf_op jit(solution)/shard_map/ppermute | solution.py:54
  (57 other events, 290.0 us)

commit v7 on v6

--- a/solution.py
+++ b/solution.py
@@ -756,6 +756,84 @@
     )
 
 
+def cross_whole_kernel(
+    core_ref, own_ref, peer_ref, order_ref, tokens_ref, partial_ref, partial_in_ref, gains_ref,
+    dead_ref, *refs
+):
+    (
+        encoded_ref, kv_ref, h_ref, normed_ref, query_ref, att_ref, lse_ref, *out_refs,
+        weights_ref, s_ref, acc_ref, sems,
+    ) = refs[2:]
+    copies = fetch([], refs[:2], weights_ref, sems)
+    core, half = core_ref[0], own_ref.shape[1]
+    own_rows = pl.ds(pl.multiple_of(core * half, half), half)
+    peer_rows = pl.ds(pl.multiple_of(half - core * half, half), half)
+    encoded = nn(own_ref[...], order_ref[own_rows, :]) + nn(peer_ref[...], order_ref[peer_rows, :])
+    encoded_ref[...] = encoded.astype(BF16)
+    gain = gains_ref[1:2, :]
+
+    def norm(rows):
+        value = tokens_ref[rows, :] + both_of(partial_ref, partial_in_ref, rows)
+        h_ref[rows, :] = value
+        normed_ref[rows, :] = (value * root_of(value) * gain).astype(BF16)
+
+    each_rows(h_ref.shape[0], norm)
+    for copy in copies:
+        copy.wait()
+    part = query_ref.shape[1]
+    pairs = part // PAIR
+
+    @pl.loop(0, 2 * part // WIDE)
+    def project(i):
+        cols = pl.ds(pl.multiple_of(i * WIDE, WIDE), WIDE)
+        source = pl.ds(pl.multiple_of(2 * part + i * WIDE, WIDE), WIDE)
+        kv_ref[:, cols] = nn(encoded_ref[...], weights_ref[:, source]).astype(BF16)
+
+    query_ref[...] = nn(normed_ref[...], weights_ref[:, :part]).astype(BF16)
+
+    def attend(pair, cols):
+        cross_forward_pair(
+            query_ref.at[:, cols(0)], kv_ref.at[:, cols(0)], kv_ref.at[:, cols(1)], dead_ref,
+            att_ref.at[:, cols(0)], lse_ref.at[pair], s_ref, acc_ref,
+        )
+
+    each_pair(pairs, attend)
+    count = out_refs[0].shape[0]
+    for i, out_ref in enumerate(out_refs):
+        att = att_ref[i * count : (i + 1) * count, :]
+        out_ref[...] = nt(att, weights_ref[:, part : 2 * part]).astype(BF16)
+
+
+def cross_whole(core, own, peer, order, tokens, partial, partial_in, gains, dead, quarters):
+    targets, width = tokens.shape
+    capacity = own.shape[0]
+    columns = quarters[0].shape[1]
+    part = columns // 4
+    pairs = part // PAIR
+    return kernel_call(
+        cross_whole_kernel,
+        [core, own, peer, order, tokens, partial, partial_in, gains, dead, *quarters],
+        [
+            struct((capacity, width), BF16),
+            struct((capacity, 2 * part), BF16),
+            struct((targets, width), F32),
+            struct((targets, width), BF16),
+            struct((targets, part), BF16),
+            struct((targets, part), BF16),
+            struct((pairs, 8, targets), F32),
+            *[struct((targets // CHUNKS, width), BF16)] * CHUNKS,
+        ],
+        [
+            pltpu.VMEM((width, columns), BF16),
+            pltpu.VMEM((capacity, queries_of(capacity)), F32),
+            pltpu.VMEM((PAIR, targets), F32),
+            pltpu.SemaphoreType.DMA((4,)),
+        ],
+        in_specs=[IN_SMEM] + [IN_VMEM] * 8 + [IN_PLACE] * 2,
+        time=24,
+    )
+
+
 def ffn_kernel(before_ref, gains_ref, cot_ref, cot_t_ref, *refs):
     chunks, refs = refs[: 2 * CHUNKS], refs[2 * CHUNKS :]
     h_out, down_ref, back_ref, *outs = refs[8:15]
@@ -1221,10 +1299,17 @@
     )
     ffn = send_apart(ffn, size)
     peer_one = swap_cores(partial_one)
-    encoded, key_value = encoder_call(which_core, own, own_peer, order, right)
-    h_one, normed_two, cross_q, cross_att, lse_cross, *partial_two = cross_forward(
-        tokens, partial_one, peer_one, gains, key_value, dead, right
-    )
+    if capacity <= KEYS:
+        (
+            encoded, key_value, h_one, normed_two, cross_q, cross_att, lse_cross, *partial_two
+        ) = cross_whole(
+            which_core, own, own_peer, order, tokens, partial_one, peer_one, gains, dead, right
+        )
+    else:
+        encoded, key_value = encoder_call(which_core, own, own_peer, order, right)
+        h_one, normed_two, cross_q, cross_att, lse_cross, *partial_two = cross_forward(
+            tokens, partial_one, peer_one, gains, key_value, dead, right
+        )
     peer_two = [swap_cores(value) for value in partial_two]
     h_two, partial_down, partial_three, *grads = ffn_call(
         h_one, partial_two, peer_two, gains, cot, cot_t, ffn[0] + ffn[1]

time: 304 us -> 303 us (level)
    pallas_call x21 -> x20, Pallas kernels: 150 us -> 147 us  [kernel_call(): pl.pallas_call(kernel, out_shape=outs, in_specs=in_specs or [everywhere]...]
    ppermute x38, waiting for transfers between devices: 61.4 us -> 64.8 us  [swap(): return lax.ppermute(value, 'dp', [(i, i ^ mask) for i in range(size)])]
  transfers between devices with their start and end apart: 50 -> 50, of which waited for: 21 -> 20; matrix products, arithmetic and copies ran while one was open for 6% -> 6% of each run, Pallas kernels for 41% -> 40%
where the time goes in v7:
time: 303 us; the launch traced here: 302 us
  Pallas kernels  147 us (49%)
  waiting for transfers between devices  65.5 us (22%)
  starting transfers between devices  57.4 us (19%)
  local copies, waits for them, and re-layouts  23 us (8%)
  other arithmetic  5.83 us (2%)
  between operations  3.38 us (1%)
    pallas_call x20, Pallas kernels, kernel_call(): pl.pallas_call(kernel, out_shape=outs, in_specs=in_specs or [everywhere]...  147 us
    ppermute x38, waiting for transfers between devices, swap(): return lax.ppermute(value, 'dp', [(i, i ^ mask) for i in range(size)])  64.8 us
    ppermute x38, starting transfers between devices, swap(): return lax.ppermute(value, 'dp', [(i, i ^ mask) for i in range(size)])  47.9 us
    unnamed x108, local copies, waits for them, and re-layouts  9.59 us
  transfers between devices with their start and end apart: 50, of which 20 were waited for; matrix products, arithmetic and copies ran while one was open for 6% of the time, Pallas kernels for 40%

profile of v7, /device:TPU:0, one launch (start us, length us, event | category | flops | bytes accessed | tf_op | source)
XLA Modules:
  0.0 302.1 jit_solution(6207856385083955105)
XLA Ops:
  0.7 2.0 shard_map.349.refs_0_
  2.7 3.0 %collective-permute-start = (bf16[48,3072]{1,0:T(8,128)(2,1)}, bf16[48,3072]{1,0:T(8,128)(2,1)S(1)}, u32[]{:S(2)}, u32[]{:S(2)}) collective-permute-start(bf16[48,3072]{1,0:T(8,128)(2,1)} %shard_map.349.refs_0_), channel_id=1, source_target_pairs={{0,8},{2,10},{4,12},{6,14},{8,0},{10,2},{12,4},{14,6},{16,24},{18,... | collective-permute-start | bytes 884744 | tf_op jit(solution)/shard_map/ppermute | solution.py:54
  5.7 2.6 collective-permute-start.1
  11.7 7.0 %shard_map.350 = (f32[512,768]{1,0:T(8,128)}, bf16[512,768]{1,0:T(8,128)(2,1)}, bf16[768,512]{1,0:T(8,128)(2,1)}, f32[8,768]{1,0:T(8,128)}, bf16[768,768]{1,0:T(...) custom-call(bf16[512,768]{1,0:T(8,128)(2,1)} %bitcast.30, bf16[512,768]{1,0:T(8,128)(2,1)} %bitcast.31, ...), custom_call_target="tpu_custom_call" | custom-call | flops 2000000000 | bytes 1 | tf_op jit(solution)/shard_map/pallas_call | solution.py:189
  19.9 1.5 gather_fusion
  22.8 1.9 shard_map.352.refs_0_
  25.6 2.1 shard_map.351
  27.7 1.5 collective-permute-start.2
  33.7 1.7 shard_map.353
  35.4 1.5 collective-permute-start.5
  39.1 3.8 %all-to-all-start = ((bf16[16,64,384]{2,1,0:T(8,128)(2,1)}), bf16[16,64,384]{2,1,0:T(8,128)(2,1)S(1)}, u32[]{:S(2)}, u32[]{:S(2)}) async-start(bf16[16,64,384]{2,1,0:T(8,128)(2,1)} %gather_fusion), calls=%async_computation | async-start | bytes 1572864 | tf_op jit(solution)/shard_map/all_to_all | solution.py:1270
  45.3 3.2 %shard_map.354 = (bf16[384,1536]{1,0:T(8,128)(2,1)}, bf16[384,1536]{1,0:T(8,128)(2,1)}) custom-call(bf16[144,1536]{1,0:T(8,128)(2,1)} %get-tuple-element.283.refs_0_, bf16[48,1536]{1,0:T(8,128)(2,1)} %get-tuple-element.284.refs_1_, bf16[144,1536]{1,0:T(8,128)(2,1)} %copy-done.39, bf16[48,1536]{1,0:T(8,128)(2,1)} %copy-done.50, ...), custom_call_target="tpu_custom_call" | custom-call | flops 40000000000 | bytes 1 | tf_op jit(solution)/shard_map/pallas_call | solution.py:189
  48.6 2.0 collective-permute-start.7
  50.6 2.3 collective-permute-start.10
  54.4 19.3 %collective-permute-done.10.refs_2_ = bf16[48,3072]{1,0:T(8,128)(2,1)} collective-permute-done((bf16[48,3072]{1,0:T(8,128)(2,1)S(1)}, bf16[48,3072]{1,0:T(8,128)(2,1)}, u32[]{:S(2)}, u32[]{:S(2)}) %collective-permute-start.10) | collective-permute-done | bytes 294944 | tf_op jit(solution)/shard_map/ppermute | solution.py:54
  73.7 6.1 %collective-permute-done.7.refs_1_ = bf16[384,1536]{1,0:T(8,128)(2,1)S(1)} collective-permute-done((bf16[384,1536]{1,0:T(8,128)(2,1)}, bf16[384,1536]{1,0:T(8,128)(2,1)S(1)}, u32[]{:S(2)}, u32[]{:S(2)}) %collective-permute-start.7) | collective-permute-done | bytes 1179680 | tf_op jit(solution)/shard_map/ppermute | solution.py:54
  79.8 2.0 collective-permute-done.11.refs_3_
  82.5 2.3 shard_map.355
  87.5 12.5 %shard_map.356 = (bf16[512,1152]{1,0:T(8,128)(2,1)}, bf16[512,384]{1,0:T(8,128)(2,1)}, f32[3,8,512]{2,1,0:T(8,128)}, bf16[512,768]{1,0:T(8,128)(2,1)}) custom-call(bf16[512,768]{1,0:T(8,128)(2,1)} %get-tuple-element.312.normed_ref, f32[3,8,512]{2,1,0:T(8,128)} %pad.4.bias_ref, bf16[384,1536]{1,0:T(8,128)(2,1)} %get-tuple-element.314.refs_0_, ...), custom_call_target="tpu_custom_call" | custom-call | flops 12000000000 | bytes 1 | tf_op jit(solution)/shard_map/pallas_call | solution.py:189
  101.7 1.5 collective-permute-start.18
  106.8 20.0 %shard_map.357 = (bf16[1024,768]{1,0:T(8,128)(2,1)}, bf16[1024,768]{1,0:T(8,128)(2,1)}, f32[512,768]{1,0:T(8,128)}, bf16[512,768]{1,0:T(8,128)(2,1)}, bf16[512,3...) custom-call(s32[1]{0:T(128)} %bitcast.core_ref, ...), custom_call_target="tpu_custom_call" | custom-call | flops 24000000000 | bytes 1 | tf_op jit(solution)/shard_map/pallas_call | solution.py:189
  127.4 2.6 collective-permute-done.19.refs_7_
  130.1 1.6 collective-permute-done.21.refs_11_
  132.6 15.9 %shard_map.358 = (f32[512,768]{1,0:T(8,128)}, f32[512,768]{1,0:T(8,128)}, f32[512,768]{1,0:T(8,128)}, bf16[384,1536]{1,0:T(8,128)(2,1)}, bf16[384,1536]{1,0:T(8,...) custom-call(f32[512,768]{1,0:T(8,128)} %get-tuple-element.330.before_ref.h_ref, ...), custom_call_target="tpu_custom_call" | custom-call | flops 20000000000 | bytes 1 | tf_op jit(solution)/shard_map/pallas_call | solution.py:189
  153.3 19.9 %shard_map.359 = (f32[512,768]{1,0:T(8,128)}, bf16[512,768]{1,0:T(8,128)(2,1)}, bf16[512,384]{1,0:T(8,128)(2,1)}, bf16[1024,768]{1,0:T(8,128)(2,1)}, f32[512,768]{1,0:T(8,128)}, /*index=5*/f32[8,768]{1,0:T(8,128)}) custom-call(bf16[512,768]{1,0:T(8,128)(2,1)} %get-tuple-element.331.cot_ref, f32[512,768]{1,0:T(8,128)} %get-tuple-element.343.partial_ref, ...), custom_call_target="tpu_custom_call" | custom-call | flops 17999998976 | bytes 1 | tf_op jit(solution)/shard_map/pallas_call | solution.py:189
  173.2 4.0 %collective-permute-done.22.left_in_ref.refs_1_ = bf16[384,1536]{1,0:T(8,128)(2,1)S(1)} collective-permute-done((bf16[384,1536]{1,0:T(8,128)(2,1)}, bf16[384,1536]{1,0:T(8,128)(2,1)S(1)}, u32[]{:S(2)}, u32[]{:S(2)}) %collective-permute-start.22) | collective-permute-done | bytes 1179680 | tf_op jit(solution)/shard_map/ppermute | solution.py:54
  178.5 3.4 %shard_map.360 = (bf16[192,1536]{1,0:T(8,128)(2,1)}, bf16[192,1536]{1,0:T(8,128)(2,1)}) custom-call(bf16[384,1536]{1,0:T(8,128)(2,1)} %get-tuple-element.383.left_ref.refs_0_, bf16[384,1536]{1,0:T(8,128)(2,1)} %get-tuple-element.386.right_ref.refs_3_, bf16[384,1536]{1,0:T(8,128)(2,1)} %copy-done.23, ...), custom_call_target="tpu_custom_call" | custom-call | flops 2000000000 | bytes 1 | tf_op jit(solution)/shard_map/pallas_call | solution.py:189
  183.8 12.5 %shard_map.361 = (bf16[1024,384]{1,0:T(8,128)(2,1)}, bf16[1024,384]{1,0:T(8,128)(2,1)}, bf16[384,768]{1,0:T(8,128)(2,1)}, bf16[384,768]{1,0:T(8,128)(2,1)}, bf16...) custom-call(s32[1]{0:T(128)} %bitcast.core_ref, bf16[512,768]{1,0:T(8,128)(2,1)} %get-tuple-element.369.normed_ref, ...), custom_call_target="tpu_custom_call" | custom-call | flops 12000000000 | bytes 1 | tf_op jit(solution)/shard_map/pallas_call | solution.py:189
  196.3 1.6 collective-permute-done.26.refs_2_
  199.5 3.4 %shard_map.362 = (f32[48,3072]{1,0:T(8,128)}, bf16[48,3072]{1,0:T(8,128)(2,1)}, bf16[48,3072]{1,0:T(8,128)(2,1)}, bf16[48,3072]{1,0:T(8,128)(2,1)}) custom-call(bf16[384,1536]{1,0:T(8,128)(2,1)} %get-tuple-element.383.left_ref.refs_0_, bf16[384,1536]{1,0:T(8,128)(2,1)} %copy-done.23, bf16[192,1536]{1,0:T(8,128)(2,1)} %copy-done.37, ...), custom_call_target="tpu_custom_call" | custom-call | flops 2000000000 | bytes 1 | tf_op jit(solution)/shard_map/pallas_call | solution.py:189
  205.0 2.2 collective-permute-start.30
  207.2 1.9 collective-permute-start.31
  209.1 23.0 %shard_map.363 = (f32[512,768]{1,0:T(8,128)}, f32[512,768]{1,0:T(8,128)}, bf16[16,384]{1,0:T(8,128)(2,1)}, bf16[384,768]{1,0:T(8,128)(2,1)}, bf16[384,768]{1,0:T...) custom-call(f32[512,768]{1,0:T(8,128)} %get-tuple-element.409.g_in_ref, ...), custom_call_target="tpu_custom_call" | custom-call | flops 22000001024 | bytes 1 | tf_op jit(solution)/shard_map/pallas_call | solution.py:189
  236.6 2.1 shard_map.366
  241.8 4.1 %all-to-all-start.1 = ((bf16[16,80,384]{2,1,0:T(8,128)(2,1)}), bf16[16,80,384]{2,1,0:T(8,128)(2,1)S(1)}, u32[]{:S(2)}, u32[]{:S(2)}) async-start(bf16[16,80,384]{2,1,0:T(8,128)(2,1)} %pad_maximum_fusion), calls=%async_computation.1 | async-start | bytes 1966080 | tf_op jit(solution)/shard_map/all_to_all | solution.py:1356
  247.0 7.1 %shard_map.364 = (f32[512,768]{1,0:T(8,128)}, bf16[512,768]{1,0:T(8,128)(2,1)}) custom-call(f32[512,768]{1,0:T(8,128)} %get-tuple-element.425.g_ref, f32[512,768]{1,0:T(8,128)} %get-tuple-element.426.partial_ref, f32[512,768]{1,0:T(8,128)} %copy-done.4, f32[512,768]{1,0:T(8,128)} %get-tuple-element.324.tokens_ref, f32[512,768]{1,0:T(8,128)} %get-tuple-element.344.h_ref, ...), custom_call_target="tpu_custom_call" | custom-call | flops 1000000000 | bytes 1 | tf_op jit(solution)/shard_map/pallas_call | solution.py:189
  255.3 2.1 shard_map.365
  259.6 7.4 %collective-permute-done.39.refs_2_ = bf16[192,768]{1,0:T(8,128)(2,1)} collective-permute-done((bf16[192,768]{1,0:T(8,128)(2,1)}, bf16[192,768]{1,0:T(8,128)(2,1)}, u32[]{:S(2)}, u32[]{:S(2)}) %collective-permute-start.39) | collective-permute-done | bytes 294944 | tf_op jit(solution)/shard_map/ppermute | solution.py:54
  266.9 2.5 shard_map.367
  269.8 4.3 %collective-permute-done.37.refs_2_ = bf16[192,768]{1,0:T(8,128)(2,1)S(1)} collective-permute-done((bf16[192,768]{1,0:T(8,128)(2,1)}, bf16[192,768]{1,0:T(8,128)(2,1)S(1)}, u32[]{:S(2)}, u32[]{:S(2)}) %collective-permute-start.37) | collective-permute-done | bytes 294944 | tf_op jit(solution)/shard_map/ppermute | solution.py:54
  275.5 2.4 shard_map.368
  278.9 1.6 collective-permute-start.43
  280.5 1.9 collective-permute-start.44
  283.3 1.5 collective-permute-done.42
  285.5 1.7 collective-permute-start.47
  289.0 1.5 gather_fusion.1
  291.1 4.4 %collective-permute-done.43 = bf16[48,1536]{1,0:T(8,128)(2,1)} collective-permute-done((bf16[48,1536]{1,0:T(8,128)(2,1)}, bf16[48,1536]{1,0:T(8,128)(2,1)}, u32[]{:S(2)}, u32[]{:S(2)}) %collective-permute-start.43) | collective-permute-done | bytes 147488 | tf_op jit(solution)/shard_map/ppermute | solution.py:54
  297.4 3.1 %collective-permute-done.47 = bf16[48,1536]{1,0:T(8,128)(2,1)} collective-permute-done((bf16[48,1536]{1,0:T(8,128)(2,1)S(1)}, bf16[48,1536]{1,0:T(8,128)(2,1)}, u32[]{:S(2)}, u32[]{:S(2)}) %collective-permute-start.47) | collective-permute-done | bytes 147488 | tf_op jit(solution)/shard_map/ppermute | solution.py:54
  (233 shorter events, 59.3 us)
Async XLA Ops:
  2.7 22.0 %collective-permute-start = (bf16[48,3072]{1,0:T(8,128)(2,1)}, bf16[48,3072]{1,0:T(8,128)(2,1)S(1)}, u32[]{:S(2)}, u32[]{:S(2)}) collective-permute-start(bf16[48,3072]{1,0:T(8,128)(2,1)} %shard_map.349.refs_0_), channel_id=1, source_target_pairs={{0,8},{2,10},{4,12},{6,14},{8,0},{10,2},{12,4},{14,6},{16,24},{18,... | collective-permute-start | bytes 884744 | tf_op jit(solution)/shard_map/ppermute | solution.py:54
  5.7 19.0 %collective-permute-start.1 = (bf16[48,3072]{1,0:T(8,128)(2,1)}, bf16[48,3072]{1,0:T(8,128)(2,1)S(1)}, u32[]{:S(2)}, u32[]{:S(2)}) collective-permute-start(bf16[48,3072]{1,0:T(8,128)(2,1)} %shard_map.349.refs_0_), channel_id=1, source_target_pairs={{0,16},{2,18},{4,20},{6,22},{8,24},{10,26},{12,28},{14,30},{16,0},... | collective-permute-start | bytes 884744 | tf_op jit(solution)/shard_map/ppermute | solution.py:54
  24.7 8.3 %collective-permute-start.4 = (bf16[48,3072]{1,0:T(8,128)(2,1)S(1)}, bf16[48,3072]{1,0:T(8,128)(2,1)S(1)}, u32[]{:S(2)}, u32[]{:S(2)}) collective-permute-start(bf16[48,3072]{1,0:T(8,128)(2,1)S(1)} %collective-permute-done.1.refs_2_), channel_id=1, source_target_pairs={{0,8},{2,10},{4,12},{6,14},{8,0},{10,2},{12,4},{14,6},{16,24},{18,... | collective-permute-start | bytes 884744 | tf_op jit(solution)/shard_map/ppermute | solution.py:54
  27.7 16.5 %collective-permute-start.2 = (bf16[144,1536]{1,0:T(8,128)(2,1)}, bf16[144,1536]{1,0:T(8,128)(2,1)S(1)}, u32[]{:S(2)}, u32[]{:S(2)}) collective-permute-start(bf16[144,1536]{1,0:T(8,128)(2,1)} %get-tuple-element.283.refs_0_), channel_id=1, source_target_pairs={{0,4},{2,6},{4,0},{6,2},{8,12},{10,14},{12,8},{14,10},{16,20},{18,... | collective-permute-start | bytes 1327112 | tf_op jit(solution)/shard_map/ppermute | solution.py:54
  29.2 14.9 %collective-permute-start.3 = (bf16[144,1536]{1,0:T(8,128)(2,1)}, bf16[144,1536]{1,0:T(8,128)(2,1)S(1)}, u32[]{:S(2)}, u32[]{:S(2)}) collective-permute-start(bf16[144,1536]{1,0:T(8,128)(2,1)} %get-tuple-element.287.refs_4_), channel_id=1, source_target_pairs={{0,2},{2,0},{4,6},{6,4},{8,10},{10,8},{12,14},{14,12},{16,18},{18,... | collective-permute-start | bytes 1327112 | tf_op jit(solution)/shard_map/ppermute | solution.py:54
  35.4 7.5 %collective-permute-start.5 = (bf16[48,1536]{1,0:T(8,128)(2,1)}, bf16[48,1536]{1,0:T(8,128)(2,1)S(1)}, u32[]{:S(2)}, u32[]{:S(2)}) collective-permute-start(bf16[48,1536]{1,0:T(8,128)(2,1)} %get-tuple-element.284.refs_1_), channel_id=1, source_target_pairs={{0,4},{2,6},{4,0},{6,2},{8,12},{10,14},{12,8},{14,10},{16,20},{18,... | collective-permute-start | bytes 442376 | tf_op jit(solution)/shard_map/ppermute | solution.py:54
  36.9 7.2 %collective-permute-start.6 = (bf16[48,1536]{1,0:T(8,128)(2,1)}, bf16[48,1536]{1,0:T(8,128)(2,1)S(1)}, u32[]{:S(2)}, u32[]{:S(2)}) collective-permute-start(bf16[48,1536]{1,0:T(8,128)(2,1)} %get-tuple-element.288.refs_5_), channel_id=1, source_target_pairs={{0,2},{2,0},{4,6},{6,4},{8,10},{10,8},{12,14},{14,12},{16,18},{18,... | collective-permute-start | bytes 442376 | tf_op jit(solution)/shard_map/ppermute | solution.py:54
  39.1 34.6 %all-to-all-start = ((bf16[16,64,384]{2,1,0:T(8,128)(2,1)}), bf16[16,64,384]{2,1,0:T(8,128)(2,1)S(1)}, u32[]{:S(2)}, u32[]{:S(2)}) async-start(bf16[16,64,384]{2,1,0:T(8,128)(2,1)} %gather_fusion), calls=%async_computation | async-start | bytes 1572864 | tf_op jit(solution)/shard_map/all_to_all | solution.py:1270
  48.6 31.2 %collective-permute-start.7 = (bf16[384,1536]{1,0:T(8,128)(2,1)}, bf16[384,1536]{1,0:T(8,128)(2,1)S(1)}, u32[]{:S(2)}, u32[]{:S(2)}) collective-permute-start(bf16[384,1536]{1,0:T(8,128)(2,1)} %get-tuple-element.314.refs_0_), channel_id=1, source_target_pairs={{0,2},{2,0},{4,6},{6,4},{8,10},{10,8},{12,14},{14,12},{16,18},{18,... | collective-permute-start | bytes 3538952 | tf_op jit(solution)/shard_map/ppermute | solution.py:54
  50.6 29.2 %collective-permute-start.8 = (bf16[384,1536]{1,0:T(8,128)(2,1)}, bf16[384,1536]{1,0:T(8,128)(2,1)S(1)}, u32[]{:S(2)}, u32[]{:S(2)}) collective-permute-start(bf16[384,1536]{1,0:T(8,128)(2,1)} %get-tuple-element.328.refs_0_), channel_id=1, source_target_pairs={{0,4},{2,6},{4,0},{6,2},{8,12},{10,14},{12,8},{14,10},{16,20},{18,... | collective-permute-start | bytes 3538952 | tf_op jit(solution)/shard_map/ppermute | solution.py:54
  50.6 23.0 %collective-permute-start.10 = (bf16[48,3072]{1,0:T(8,128)(2,1)S(1)}, bf16[48,3072]{1,0:T(8,128)(2,1)}, u32[]{:S(2)}, u32[]{:S(2)}) collective-permute-start(bf16[48,3072]{1,0:T(8,128)(2,1)S(1)} %copy-done.43), channel_id=1, source_target_pairs={{0,16},{2,18},{4,20},{6,22},{8,24},{10,26},{12,28},{14,30},{16,0},... | collective-permute-start | bytes 884744 | tf_op jit(solution)/shard_map/ppermute | solution.py:54
  52.9 20.8 %collective-permute-start.9 = (bf16[48,3072]{1,0:T(8,128)(2,1)S(1)}, bf16[48,3072]{1,0:T(8,128)(2,1)}, u32[]{:S(2)}, u32[]{:S(2)}) collective-permute-start(bf16[48,3072]{1,0:T(8,128)(2,1)S(1)} %copy-done.43), channel_id=1, source_target_pairs={{0,8},{2,10},{4,12},{6,14},{8,0},{10,2},{12,4},{14,6},{16,24},{18,... | collective-permute-start | bytes 884744 | tf_op jit(solution)/shard_map/ppermute | solution.py:54
  73.7 8.1 %collective-permute-start.11 = (bf16[48,3072]{1,0:T(8,128)(2,1)}, bf16[48,3072]{1,0:T(8,128)(2,1)S(1)}, u32[]{:S(2)}, u32[]{:S(2)}) collective-permute-start(bf16[48,3072]{1,0:T(8,128)(2,1)} %collective-permute-done.10.refs_2_), channel_id=1, source_target_pairs={{0,8},{2,10},{4,12},{6,14},{8,0},{10,2},{12,4},{14,6},{16,24},{18,... | collective-permute-start | bytes 884744 | tf_op jit(solution)/shard_map/ppermute | solution.py:54
  84.9 16.8 %collective-permute-start.14 = (bf16[1024,384]{1,0:T(8,128)(2,1)S(1)}, bf16[1024,384]{1,0:T(8,128)(2,1)S(1)}, u32[]{:S(2)}, u32[]{:S(2)}) collective-permute-start(bf16[1024,384]{1,0:T(8,128)(2,1)S(1)} %bitcast.25), channel_id=1, source_target_pairs={{0,1},{1,0},{2,3},{3,2},{4,5},{5,4},{6,7},{7,6},{8,9},{9,8},{10,11... | collective-permute-start | bytes 2359304 | tf_op jit(solution)/shard_map/ppermute | solution.py:58
  84.9 16.0 %collective-permute-start.12 = (bf16[192,1536]{1,0:T(8,128)(2,1)}, bf16[192,1536]{1,0:T(8,128)(2,1)S(1)}, u32[]{:S(2)}, u32[]{:S(2)}) collective-permute-start(bf16[192,1536]{1,0:T(8,128)(2,1)} %get-tuple-element.335.refs_4_), channel_id=1, source_target_pairs={{0,4},{2,6},{4,0},{6,2},{8,12},{10,14},{12,8},{14,10},{16,20},{18,... | collective-permute-start | bytes 1769480 | tf_op jit(solution)/shard_map/ppermute | solution.py:54
  86.0 15.6 %collective-permute-start.13 = (bf16[192,1536]{1,0:T(8,128)(2,1)}, bf16[192,1536]{1,0:T(8,128)(2,1)S(1)}, u32[]{:S(2)}, u32[]{:S(2)}) collective-permute-start(bf16[192,1536]{1,0:T(8,128)(2,1)} %get-tuple-element.337.refs_8_), channel_id=1, source_target_pairs={{0,2},{2,0},{4,6},{6,4},{8,10},{10,8},{12,14},{14,12},{16,18},{18,... | collective-permute-start | bytes 1769480 | tf_op jit(solution)/shard_map/ppermute | solution.py:54
  101.7 25.2 %collective-permute-start.18 = (bf16[192,1536]{1,0:T(8,128)(2,1)S(1)}, bf16[192,1536]{1,0:T(8,128)(2,1)S(1)}, u32[]{:S(2)}, u32[]{:S(2)}) collective-permute-start(bf16[192,1536]{1,0:T(8,128)(2,1)S(1)} %copy-done.28), channel_id=1, source_target_pairs={{0,2},{2,0},{4,6},{6,4},{8,10},{10,8},{12,14},{14,12},{16,18},{18,... | collective-permute-start | bytes 1769480 | tf_op jit(solution)/shard_map/ppermute | solution.py:54
  103.2 26.8 %collective-permute-start.19 = (bf16[192,1536]{1,0:T(8,128)(2,1)S(1)}, bf16[192,1536]{1,0:T(8,128)(2,1)S(1)}, u32[]{:S(2)}, u32[]{:S(2)}) collective-permute-start(bf16[192,1536]{1,0:T(8,128)(2,1)S(1)} %collective-permute-done.12.refs_5_), channel_id=1, source_target_pairs={{0,2},{2,0},{4,6},{6,4},{8,10},{10,8},{12,14},{14,12},{16,18},{18,... | collective-permute-start | bytes 1769480 | tf_op jit(solution)/shard_map/ppermute | solution.py:54
  103.8 26.3 %collective-permute-start.20 = (bf16[192,1536]{1,0:T(8,128)(2,1)S(1)}, bf16[192,1536]{1,0:T(8,128)(2,1)S(1)}, u32[]{:S(2)}, u32[]{:S(2)}) collective-permute-start(bf16[192,1536]{1,0:T(8,128)(2,1)S(1)} %copy-done.29), channel_id=1, source_target_pairs={{0,4},{2,6},{4,0},{6,2},{8,12},{10,14},{12,8},{14,10},{16,20},{18,... | collective-permute-start | bytes 1769480 | tf_op jit(solution)/shard_map/ppermute | solution.py:54
  104.8 26.8 %collective-permute-start.21 = (bf16[192,1536]{1,0:T(8,128)(2,1)S(1)}, bf16[192,1536]{1,0:T(8,128)(2,1)}, u32[]{:S(2)}, u32[]{:S(2)}) collective-permute-start(bf16[192,1536]{1,0:T(8,128)(2,1)S(1)} %collective-permute-done.13.refs_9_), channel_id=1, source_target_pairs={{0,4},{2,6},{4,0},{6,2},{8,12},{10,14},{12,8},{14,10},{16,20},{18,... | collective-permute-start | bytes 1769480 | tf_op jit(solution)/shard_map/ppermute | solution.py:54
  126.8 4.8 %collective-permute-start.16 = (bf16[256,768]{1,0:T(8,128)(2,1)}, bf16[256,768]{1,0:T(8,128)(2,1)S(1)}, u32[]{:S(2)}, u32[]{:S(2)}) collective-permute-start(bf16[256,768]{1,0:T(8,128)(2,1)} %get-tuple-element.333.refs_0_), channel_id=1, source_target_pairs={{0,1},{1,0},{2,3},{3,2},{4,5},{5,4},{6,7},{7,6},{8,9},{9,8},{10,11... | collective-permute-start | bytes 1179656 | tf_op jit(solution)/shard_map/ppermute | solution.py:58
  126.9 4.7 %collective-permute-start.17 = (bf16[256,768]{1,0:T(8,128)(2,1)}, bf16[256,768]{1,0:T(8,128)(2,1)S(1)}, u32[]{:S(2)}, u32[]{:S(2)}) collective-permute-start(bf16[256,768]{1,0:T(8,128)(2,1)} %get-tuple-element.334.refs_1_), channel_id=1, source_target_pairs={{0,1},{1,0},{2,3},{3,2},{4,5},{5,4},{6,7},{7,6},{8,9},{9,8},{10,11... | collective-permute-start | bytes 1179656 | tf_op jit(solution)/shard_map/ppermute | solution.py:58
  148.6 30.0 %collective-permute-start.25 = (f32[512,768]{1,0:T(8,128)}, f32[512,768]{1,0:T(8,128)S(1)}, u32[]{:S(2)}, u32[]{:S(2)}) collective-permute-start(f32[512,768]{1,0:T(8,128)} %get-tuple-element.352.down_ref), channel_id=1, source_target_pairs={{0,1},{1,0},{2,3},{3,2},{4,5},{5,4},{6,7},{7,6},{8,9},{9,8},{10,11... | collective-permute-start | bytes 4718600 | tf_op jit(solution)/shard_map/ppermute | solution.py:58
  149.1 28.2 %collective-permute-start.22 = (bf16[384,1536]{1,0:T(8,128)(2,1)}, bf16[384,1536]{1,0:T(8,128)(2,1)S(1)}, u32[]{:S(2)}, u32[]{:S(2)}) collective-permute-start(bf16[384,1536]{1,0:T(8,128)(2,1)} %get-tuple-element.341), channel_id=1, source_target_pairs={{0,2},{2,0},{4,6},{6,4},{8,10},{10,8},{12,14},{14,12},{16,18},{18,... | collective-permute-start | bytes 3538952 | tf_op jit(solution)/shard_map/ppermute | solution.py:54
  150.5 28.0 %collective-permute-start.23 = (bf16[384,1536]{1,0:T(8,128)(2,1)}, bf16[384,1536]{1,0:T(8,128)(2,1)}, u32[]{:S(2)}, u32[]{:S(2)}) collective-permute-start(bf16[384,1536]{1,0:T(8,128)(2,1)} %get-tuple-element.342), channel_id=1, source_target_pairs={{0,4},{2,6},{4,0},{6,2},{8,12},{10,14},{12,8},{14,10},{16,20},{18,... | collective-permute-start | bytes 3538952 | tf_op jit(solution)/shard_map/ppermute | solution.py:54
  181.9 16.7 %collective-permute-start.28 = (f32[512,768]{1,0:T(8,128)S(1)}, f32[512,768]{1,0:T(8,128)S(1)}, u32[]{:S(2)}, u32[]{:S(2)}) collective-permute-start(f32[512,768]{1,0:T(8,128)S(1)} %copy-done.18), channel_id=1, source_target_pairs={{0,1},{1,0},{2,3},{3,2},{4,5},{5,4},{6,7},{7,6},{8,9},{9,8},{10,11... | collective-permute-start | bytes 4718600 | tf_op jit(solution)/shard_map/ppermute | solution.py:58
  181.9 16.0 %collective-permute-start.26 = (bf16[192,1536]{1,0:T(8,128)(2,1)}, bf16[192,1536]{1,0:T(8,128)(2,1)S(1)}, u32[]{:S(2)}, u32[]{:S(2)}) collective-permute-start(bf16[192,1536]{1,0:T(8,128)(2,1)} %get-tuple-element.367), channel_id=1, source_target_pairs={{0,4},{2,6},{4,0},{6,2},{8,12},{10,14},{12,8},{14,10},{16,20},{18,... | collective-permute-start | bytes 1769480 | tf_op jit(solution)/shard_map/ppermute | solution.py:54
  183.0 15.6 %collective-permute-start.27 = (bf16[192,1536]{1,0:T(8,128)(2,1)}, bf16[192,1536]{1,0:T(8,128)(2,1)S(1)}, u32[]{:S(2)}, u32[]{:S(2)}) collective-permute-start(bf16[192,1536]{1,0:T(8,128)(2,1)} %get-tuple-element.368), channel_id=1, source_target_pairs={{0,2},{2,0},{4,6},{6,4},{8,10},{10,8},{12,14},{14,12},{16,18},{18,... | collective-permute-start | bytes 1769480 | tf_op jit(solution)/shard_map/ppermute | solution.py:54
  202.9 29.2 %collective-permute-start.32 = (bf16[384,768]{1,0:T(8,128)(2,1)S(1)}, bf16[384,768]{1,0:T(8,128)(2,1)S(1)}, u32[]{:S(2)}, u32[]{:S(2)}) collective-permute-start(bf16[384,768]{1,0:T(8,128)(2,1)S(1)} %copy-done.32), channel_id=1, source_target_pairs={{0,2},{2,0},{4,6},{6,4},{8,10},{10,8},{12,14},{14,12},{16,18},{18,... | collective-permute-start | bytes 1769480 | tf_op jit(solution)/shard_map/ppermute | solution.py:54
  203.7 28.4 %collective-permute-start.33 = (bf16[384,768]{1,0:T(8,128)(2,1)S(1)}, bf16[384,768]{1,0:T(8,128)(2,1)S(1)}, u32[]{:S(2)}, u32[]{:S(2)}) collective-permute-start(bf16[384,768]{1,0:T(8,128)(2,1)S(1)} %copy-done.30), channel_id=1, source_target_pairs={{0,4},{2,6},{4,0},{6,2},{8,12},{10,14},{12,8},{14,10},{16,20},{18,... | collective-permute-start | bytes 1769480 | tf_op jit(solution)/shard_map/ppermute | solution.py:54
  204.7 27.4 %collective-permute-start.29 = (bf16[48,3072]{1,0:T(8,128)(2,1)}, bf16[48,3072]{1,0:T(8,128)(2,1)S(1)}, u32[]{:S(2)}, u32[]{:S(2)}) collective-permute-start(bf16[48,3072]{1,0:T(8,128)(2,1)} %get-tuple-element.401), channel_id=1, source_target_pairs={{0,8},{2,10},{4,12},{6,14},{8,0},{10,2},{12,4},{14,6},{16,24},{18,... | collective-permute-start | bytes 884744 | tf_op jit(solution)/shard_map/ppermute | solution.py:54
  205.0 27.1 %collective-permute-start.30 = (bf16[48,3072]{1,0:T(8,128)(2,1)}, bf16[48,3072]{1,0:T(8,128)(2,1)S(1)}, u32[]{:S(2)}, u32[]{:S(2)}) collective-permute-start(bf16[48,3072]{1,0:T(8,128)(2,1)} %get-tuple-element.402), channel_id=1, source_target_pairs={{0,16},{2,18},{4,20},{6,22},{8,24},{10,26},{12,28},{14,30},{16,0},... | collective-permute-start | bytes 884744 | tf_op jit(solution)/shard_map/ppermute | solution.py:54
  207.2 24.9 %collective-permute-start.31 = (bf16[48,3072]{1,0:T(8,128)(2,1)}, bf16[48,3072]{1,0:T(8,128)(2,1)S(1)}, u32[]{:S(2)}, u32[]{:S(2)}) collective-permute-start(bf16[48,3072]{1,0:T(8,128)(2,1)} %get-tuple-element.403), channel_id=1, source_target_pairs={{0,24},{2,26},{4,28},{6,30},{8,16},{10,18},{12,20},{14,22},{16,8},... | collective-permute-start | bytes 884744 | tf_op jit(solution)/shard_map/ppermute | solution.py:54
  232.9 12.9 %collective-permute-start.36 = (f32[512,768]{1,0:T(8,128)}, f32[512,768]{1,0:T(8,128)S(1)}, u32[]{:S(2)}, u32[]{:S(2)}) collective-permute-start(f32[512,768]{1,0:T(8,128)} %get-tuple-element.426.partial_ref), channel_id=1, source_target_pairs={{0,1},{1,0},{2,3},{3,2},{4,5},{5,4},{6,7},{7,6},{8,9},{9,8},{10,11... | collective-permute-start | bytes 4718600 | tf_op jit(solution)/shard_map/ppermute | solution.py:58
  233.1 6.6 %collective-permute-start.41 = (bf16[1024,384]{1,0:T(8,128)(2,1)}, bf16[1024,384]{1,0:T(8,128)(2,1)S(1)}, u32[]{:S(2)}, u32[]{:S(2)}) collective-permute-start(bf16[1024,384]{1,0:T(8,128)(2,1)} %get-tuple-element.465), channel_id=1, source_target_pairs={{0,1},{1,0},{2,3},{3,2},{4,5},{5,4},{6,7},{7,6},{8,9},{9,8},{10,11... | collective-permute-start | bytes 2359304 | tf_op jit(solution)/shard_map/ppermute | solution.py:58
  234.2 19.8 %collective-permute-start.34 = (bf16[384,768]{1,0:T(8,128)(2,1)}, bf16[384,768]{1,0:T(8,128)(2,1)}, u32[]{:S(2)}, u32[]{:S(2)}) collective-permute-start(bf16[384,768]{1,0:T(8,128)(2,1)} %get-tuple-element.423), channel_id=1, source_target_pairs={{0,2},{2,0},{4,6},{6,4},{8,10},{10,8},{12,14},{14,12},{16,18},{18,... | collective-permute-start | bytes 1769480 | tf_op jit(solution)/shard_map/ppermute | solution.py:54
  235.5 19.7 %collective-permute-start.35 = (bf16[384,768]{1,0:T(8,128)(2,1)}, bf16[384,768]{1,0:T(8,128)(2,1)}, u32[]{:S(2)}, u32[]{:S(2)}) collective-permute-start(bf16[384,768]{1,0:T(8,128)(2,1)} %get-tuple-element.424), channel_id=1, source_target_pairs={{0,4},{2,6},{4,0},{6,2},{8,12},{10,14},{12,8},{14,10},{16,20},{18,... | collective-permute-start | bytes 1769480 | tf_op jit(solution)/shard_map/ppermute | solution.py:54
  238.7 28.2 %collective-permute-start.39 = (bf16[192,768]{1,0:T(8,128)(2,1)}, bf16[192,768]{1,0:T(8,128)(2,1)}, u32[]{:S(2)}, u32[]{:S(2)}) collective-permute-start(bf16[192,768]{1,0:T(8,128)(2,1)} %get-tuple-element.445), channel_id=1, source_target_pairs={{0,4},{2,6},{4,0},{6,2},{8,12},{10,14},{12,8},{14,10},{16,20},{18,... | collective-permute-start | bytes 884744 | tf_op jit(solution)/shard_map/ppermute | solution.py:54
  239.7 27.3 %collective-permute-start.40 = (bf16[192,768]{1,0:T(8,128)(2,1)}, bf16[192,768]{1,0:T(8,128)(2,1)}, u32[]{:S(2)}, u32[]{:S(2)}) collective-permute-start(bf16[192,768]{1,0:T(8,128)(2,1)} %get-tuple-element.446), channel_id=1, source_target_pairs={{0,2},{2,0},{4,6},{6,4},{8,10},{10,8},{12,14},{14,12},{16,18},{18,... | collective-permute-start | bytes 884744 | tf_op jit(solution)/shard_map/ppermute | solution.py:54
  241.8 36.1 %all-to-all-start.1 = ((bf16[16,80,384]{2,1,0:T(8,128)(2,1)}), bf16[16,80,384]{2,1,0:T(8,128)(2,1)S(1)}, u32[]{:S(2)}, u32[]{:S(2)}) async-start(bf16[16,80,384]{2,1,0:T(8,128)(2,1)} %pad_maximum_fusion), calls=%async_computation.1 | async-start | bytes 1966080 | tf_op jit(solution)/shard_map/all_to_all | solution.py:1356
  257.4 16.7 %collective-permute-start.37 = (bf16[192,768]{1,0:T(8,128)(2,1)}, bf16[192,768]{1,0:T(8,128)(2,1)S(1)}, u32[]{:S(2)}, u32[]{:S(2)}) collective-permute-start(bf16[192,768]{1,0:T(8,128)(2,1)} %get-tuple-element.435), channel_id=1, source_target_pairs={{0,4},{2,6},{4,0},{6,2},{8,12},{10,14},{12,8},{14,10},{16,20},{18,... | collective-permute-start | bytes 884744 | tf_op jit(solution)/shard_map/ppermute | solution.py:54
  258.1 16.0 %collective-permute-start.38 = (bf16[192,768]{1,0:T(8,128)(2,1)}, bf16[192,768]{1,0:T(8,128)(2,1)S(1)}, u32[]{:S(2)}, u32[]{:S(2)}) collective-permute-start(bf16[192,768]{1,0:T(8,128)(2,1)} %get-tuple-element.436), channel_id=1, source_target_pairs={{0,2},{2,0},{4,6},{6,4},{8,10},{10,8},{12,14},{14,12},{16,18},{18,... | collective-permute-start | bytes 884744 | tf_op jit(solution)/shard_map/ppermute | solution.py:54
  269.4 13.9 %collective-permute-start.45 = (bf16[96,1536]{1,0:T(8,128)(2,1)}, bf16[96,1536]{1,0:T(8,128)(2,1)S(1)}, u32[]{:S(2)}, u32[]{:S(2)}) collective-permute-start(bf16[96,1536]{1,0:T(8,128)(2,1)} %get-tuple-element.453), channel_id=1, source_target_pairs={{0,8},{2,10},{4,12},{6,14},{8,0},{10,2},{12,4},{14,6},{16,24},{18,... | collective-permute-start | bytes 884744 | tf_op jit(solution)/shard_map/ppermute | solution.py:54
  277.9 6.9 %collective-permute-start.42 = (bf16[48,1536]{1,0:T(8,128)(2,1)}, bf16[48,1536]{1,0:T(8,128)(2,1)S(1)}, u32[]{:S(2)}, u32[]{:S(2)}) collective-permute-start(bf16[48,1536]{1,0:T(8,128)(2,1)} %get-tuple-element.472), channel_id=1, source_target_pairs={{0,8},{2,10},{4,12},{6,14},{8,0},{10,2},{12,4},{14,6},{16,24},{18,... | collective-permute-start | bytes 442376 | tf_op jit(solution)/shard_map/ppermute | solution.py:54
  278.9 16.6 %collective-permute-start.43 = (bf16[48,1536]{1,0:T(8,128)(2,1)}, bf16[48,1536]{1,0:T(8,128)(2,1)}, u32[]{:S(2)}, u32[]{:S(2)}) collective-permute-start(bf16[48,1536]{1,0:T(8,128)(2,1)} %get-tuple-element.473), channel_id=1, source_target_pairs={{0,16},{2,18},{4,20},{6,22},{8,24},{10,26},{12,28},{14,30},{16,0},... | collective-permute-start | bytes 442376 | tf_op jit(solution)/shard_map/ppermute | solution.py:54
  280.5 15.1 %collective-permute-start.44 = (bf16[48,1536]{1,0:T(8,128)(2,1)}, bf16[48,1536]{1,0:T(8,128)(2,1)}, u32[]{:S(2)}, u32[]{:S(2)}) collective-permute-start(bf16[48,1536]{1,0:T(8,128)(2,1)} %get-tuple-element.474), channel_id=1, source_target_pairs={{0,24},{2,26},{4,28},{6,30},{8,16},{10,18},{12,20},{14,22},{16,8},... | collective-permute-start | bytes 442376 | tf_op jit(solution)/shard_map/ppermute | solution.py:54
  284.9 5.6 %collective-permute-start.46 = (f32[8,384]{1,0:T(8,128)S(1)}, f32[8,384]{1,0:T(8,128)S(1)}, u32[]{:S(2)}, u32[]{:S(2)}) collective-permute-start(f32[8,384]{1,0:T(8,128)S(1)} %slice_add_fusion.1), channel_id=1, source_target_pairs={{0,1},{1,0},{2,3},{3,2},{4,5},{5,4},{6,7},{7,6},{8,9},{9,8},{10,11... | collective-permute-start | bytes 36872 | tf_op jit(solution)/shard_map/ppermute | solution.py:58
  285.5 15.0 %collective-permute-start.47 = (bf16[48,1536]{1,0:T(8,128)(2,1)S(1)}, bf16[48,1536]{1,0:T(8,128)(2,1)}, u32[]{:S(2)}, u32[]{:S(2)}) collective-permute-start(bf16[48,1536]{1,0:T(8,128)(2,1)S(1)} %slice.129), channel_id=1, source_target_pairs={{0,16},{2,18},{4,20},{6,22},{8,24},{10,26},{12,28},{14,30},{16,0},... | collective-permute-start | bytes 442376 | tf_op jit(solution)/shard_map/ppermute | solution.py:54
  (57 other events, 321.7 us)

commit v8 on v7

--- a/solution.py
+++ b/solution.py
@@ -836,8 +836,10 @@
 
 def ffn_kernel(before_ref, gains_ref, cot_ref, cot_t_ref, *refs):
     chunks, refs = refs[: 2 * CHUNKS], refs[2 * CHUNKS :]
-    h_out, down_ref, back_ref, *outs = refs[8:15]
-    weights_ref, grads_ref, h_ref, normed_ref, normed_t, in_sems, out_sems = refs[15:]
+    h_out, down_out, back_out, *outs = refs[8:15]
+    (
+        weights_ref, grads_ref, h_ref, down_ref, back_ref, normed_ref, normed_t, in_sems, out_sems,
+    ) = refs[15:]
     copies = fetch(refs[:4], refs[4:8], weights_ref, in_sems)
     gain = gains_ref[2:3, :]
     count = chunks[0].shape[0]
@@ -859,6 +861,7 @@
         copy.wait()
     hidden = weights_ref.shape[1] // 3
     tiles = hidden // HIDDEN
+    back_copy = pltpu.make_async_copy(back_ref, back_out, out_sems.at[37])
 
     def sends(i):
         copies = []
@@ -898,8 +901,17 @@
                     copy.start()
 
         back_ref[...] += nt(grad_gate, weights_ref[:, gates]) + nt(grad_up, weights_ref[:, ups])
+
+        @pl.when(i == tiles - 1)
+        def send_back():
+            back_copy.start()
+
         down_ref[...] += nt(act, weights_ref[:, downs])
 
+    down_copy = pltpu.make_async_copy(down_ref, down_out, out_sems.at[38])
+    down_copy.start()
+    back_copy.wait()
+    down_copy.wait()
     for i in range(tiles):
         for copy in sends(i):
             copy.wait()
@@ -917,14 +929,16 @@
             pltpu.VMEM((width, columns), BF16),
             pltpu.VMEM((width, columns), BF16),
             pltpu.VMEM((targets, width), F32),
+            pltpu.VMEM((targets, width), F32),
+            pltpu.VMEM((targets, width), F32),
             pltpu.VMEM((targets, width), BF16),
             pltpu.VMEM((width, targets), BF16),
             pltpu.SemaphoreType.DMA((8,)),
-            pltpu.SemaphoreType.DMA((37,)),
+            pltpu.SemaphoreType.DMA((39,)),
         ],
         time=20,
         in_specs=[IN_VMEM] * (4 + 2 * CHUNKS) + [IN_PLACE] * 8,
-        out_specs=[IN_PLACE] + [IN_VMEM] * 2 + [IN_PLACE] * 4,
+        out_specs=[IN_PLACE] * 7,
     )
 
 

time: 303 us -> 303 us (level)
  no operation moved by 1% of the time
where the time goes in v8:
time: 303 us; the launch traced here: 302 us
  Pallas kernels  147 us (49%)
  waiting for transfers between devices  65.5 us (22%)
  starting transfers between devices  57.4 us (19%)
  local copies, waits for them, and re-layouts  23 us (8%)
  other arithmetic  5.83 us (2%)
  between operations  3.38 us (1%)
    pallas_call x20, Pallas kernels, kernel_call(): pl.pallas_call(kernel, out_shape=outs, in_specs=in_specs or [everywhere]...  147 us
    ppermute x38, waiting for transfers between devices, swap(): return lax.ppermute(value, 'dp', [(i, i ^ mask) for i in range(size)])  64.8 us
    ppermute x38, starting transfers between devices, swap(): return lax.ppermute(value, 'dp', [(i, i ^ mask) for i in range(size)])  47.9 us
    unnamed x108, local copies, waits for them, and re-layouts  9.59 us
  transfers between devices with their start and end apart: 50, of which 20 were waited for; matrix products, arithmetic and copies ran while one was open for 6% of the time, Pallas kernels for 40%

profile of v8, /device:TPU:0, one launch (start us, length us, event | category | flops | bytes accessed | tf_op | source)
XLA Modules:
  0.0 301.7 jit_solution(13668127551465169537)
XLA Ops:
  0.7 2.0 shard_map.349.refs_0_
  2.7 3.0 %collective-permute-start = (bf16[48,3072]{1,0:T(8,128)(2,1)}, bf16[48,3072]{1,0:T(8,128)(2,1)S(1)}, u32[]{:S(2)}, u32[]{:S(2)}) collective-permute-start(bf16[48,3072]{1,0:T(8,128)(2,1)} %shard_map.349.refs_0_), channel_id=1, source_target_pairs={{0,8},{2,10},{4,12},{6,14},{8,0},{10,2},{12,4},{14,6},{16,24},{18,... | collective-permute-start | bytes 884744 | tf_op jit(solution)/shard_map/ppermute | solution.py:54
  5.7 2.6 collective-permute-start.1
  11.7 7.0 %shard_map.350 = (f32[512,768]{1,0:T(8,128)}, bf16[512,768]{1,0:T(8,128)(2,1)}, bf16[768,512]{1,0:T(8,128)(2,1)}, f32[8,768]{1,0:T(8,128)}, bf16[768,768]{1,0:T(...) custom-call(bf16[512,768]{1,0:T(8,128)(2,1)} %bitcast.30, bf16[512,768]{1,0:T(8,128)(2,1)} %bitcast.31, ...), custom_call_target="tpu_custom_call" | custom-call | flops 2000000000 | bytes 1 | tf_op jit(solution)/shard_map/pallas_call | solution.py:189
  19.9 1.5 gather_fusion
  22.8 1.9 shard_map.352.refs_0_
  25.6 2.1 shard_map.351
  27.7 1.5 collective-permute-start.2
  33.7 1.7 shard_map.353
  35.4 1.5 collective-permute-start.5
  39.1 3.8 %all-to-all-start = ((bf16[16,64,384]{2,1,0:T(8,128)(2,1)}), bf16[16,64,384]{2,1,0:T(8,128)(2,1)S(1)}, u32[]{:S(2)}, u32[]{:S(2)}) async-start(bf16[16,64,384]{2,1,0:T(8,128)(2,1)} %gather_fusion), calls=%async_computation | async-start | bytes 1572864 | tf_op jit(solution)/shard_map/all_to_all | solution.py:1284
  45.3 3.2 %shard_map.354 = (bf16[384,1536]{1,0:T(8,128)(2,1)}, bf16[384,1536]{1,0:T(8,128)(2,1)}) custom-call(bf16[144,1536]{1,0:T(8,128)(2,1)} %get-tuple-element.283.refs_0_, bf16[48,1536]{1,0:T(8,128)(2,1)} %get-tuple-element.284.refs_1_, bf16[144,1536]{1,0:T(8,128)(2,1)} %copy-done.39, bf16[48,1536]{1,0:T(8,128)(2,1)} %copy-done.50, ...), custom_call_target="tpu_custom_call" | custom-call | flops 40000000000 | bytes 1 | tf_op jit(solution)/shard_map/pallas_call | solution.py:189
  48.6 2.0 collective-permute-start.7
  50.6 2.3 collective-permute-start.10
  54.4 19.3 %collective-permute-done.10.refs_2_ = bf16[48,3072]{1,0:T(8,128)(2,1)} collective-permute-done((bf16[48,3072]{1,0:T(8,128)(2,1)S(1)}, bf16[48,3072]{1,0:T(8,128)(2,1)}, u32[]{:S(2)}, u32[]{:S(2)}) %collective-permute-start.10) | collective-permute-done | bytes 294944 | tf_op jit(solution)/shard_map/ppermute | solution.py:54
  73.7 6.1 %collective-permute-done.7.refs_1_ = bf16[384,1536]{1,0:T(8,128)(2,1)S(1)} collective-permute-done((bf16[384,1536]{1,0:T(8,128)(2,1)}, bf16[384,1536]{1,0:T(8,128)(2,1)S(1)}, u32[]{:S(2)}, u32[]{:S(2)}) %collective-permute-start.7) | collective-permute-done | bytes 1179680 | tf_op jit(solution)/shard_map/ppermute | solution.py:54
  79.8 2.0 collective-permute-done.11.refs_3_
  82.5 2.3 shard_map.355
  87.5 12.5 %shard_map.356 = (bf16[512,1152]{1,0:T(8,128)(2,1)}, bf16[512,384]{1,0:T(8,128)(2,1)}, f32[3,8,512]{2,1,0:T(8,128)}, bf16[512,768]{1,0:T(8,128)(2,1)}) custom-call(bf16[512,768]{1,0:T(8,128)(2,1)} %get-tuple-element.312.normed_ref, f32[3,8,512]{2,1,0:T(8,128)} %pad.4.bias_ref, bf16[384,1536]{1,0:T(8,128)(2,1)} %get-tuple-element.314.refs_0_, ...), custom_call_target="tpu_custom_call" | custom-call | flops 12000000000 | bytes 1 | tf_op jit(solution)/shard_map/pallas_call | solution.py:189
  101.7 1.5 collective-permute-start.18
  106.8 20.0 %shard_map.357 = (bf16[1024,768]{1,0:T(8,128)(2,1)}, bf16[1024,768]{1,0:T(8,128)(2,1)}, f32[512,768]{1,0:T(8,128)}, bf16[512,768]{1,0:T(8,128)(2,1)}, bf16[512,3...) custom-call(s32[1]{0:T(128)} %bitcast.core_ref, ...), custom_call_target="tpu_custom_call" | custom-call | flops 24000000000 | bytes 1 | tf_op jit(solution)/shard_map/pallas_call | solution.py:189
  127.4 2.6 collective-permute-done.19.refs_7_
  130.1 1.6 collective-permute-done.21.refs_11_
  132.6 15.6 %shard_map.358 = (f32[512,768]{1,0:T(8,128)}, f32[512,768]{1,0:T(8,128)}, f32[512,768]{1,0:T(8,128)}, bf16[384,1536]{1,0:T(8,128)(2,1)}, bf16[384,1536]{1,0:T(8,...) custom-call(f32[512,768]{1,0:T(8,128)} %get-tuple-element.330.before_ref.h_ref, ...), custom_call_target="tpu_custom_call" | custom-call | flops 20000000000 | bytes 1 | tf_op jit(solution)/shard_map/pallas_call | solution.py:189
  153.0 19.9 %shard_map.359 = (f32[512,768]{1,0:T(8,128)}, bf16[512,768]{1,0:T(8,128)(2,1)}, bf16[512,384]{1,0:T(8,128)(2,1)}, bf16[1024,768]{1,0:T(8,128)(2,1)}, f32[512,768]{1,0:T(8,128)}, /*index=5*/f32[8,768]{1,0:T(8,128)}) custom-call(bf16[512,768]{1,0:T(8,128)(2,1)} %get-tuple-element.331.cot_ref, f32[512,768]{1,0:T(8,128)} %get-tuple-element.343.partial_ref, ...), custom_call_target="tpu_custom_call" | custom-call | flops 17999998976 | bytes 1 | tf_op jit(solution)/shard_map/pallas_call | solution.py:189
  172.8 4.0 %collective-permute-done.22.left_in_ref.refs_1_ = bf16[384,1536]{1,0:T(8,128)(2,1)S(1)} collective-permute-done((bf16[384,1536]{1,0:T(8,128)(2,1)}, bf16[384,1536]{1,0:T(8,128)(2,1)S(1)}, u32[]{:S(2)}, u32[]{:S(2)}) %collective-permute-start.22) | collective-permute-done | bytes 1179680 | tf_op jit(solution)/shard_map/ppermute | solution.py:54
  178.2 3.4 %shard_map.360 = (bf16[192,1536]{1,0:T(8,128)(2,1)}, bf16[192,1536]{1,0:T(8,128)(2,1)}) custom-call(bf16[384,1536]{1,0:T(8,128)(2,1)} %get-tuple-element.383.left_ref.refs_0_, bf16[384,1536]{1,0:T(8,128)(2,1)} %get-tuple-element.386.right_ref.refs_3_, bf16[384,1536]{1,0:T(8,128)(2,1)} %copy-done.23, ...), custom_call_target="tpu_custom_call" | custom-call | flops 2000000000 | bytes 1 | tf_op jit(solution)/shard_map/pallas_call | solution.py:189
  183.4 12.5 %shard_map.361 = (bf16[1024,384]{1,0:T(8,128)(2,1)}, bf16[1024,384]{1,0:T(8,128)(2,1)}, bf16[384,768]{1,0:T(8,128)(2,1)}, bf16[384,768]{1,0:T(8,128)(2,1)}, bf16...) custom-call(s32[1]{0:T(128)} %bitcast.core_ref, bf16[512,768]{1,0:T(8,128)(2,1)} %get-tuple-element.369.normed_ref, ...), custom_call_target="tpu_custom_call" | custom-call | flops 12000000000 | bytes 1 | tf_op jit(solution)/shard_map/pallas_call | solution.py:189
  196.0 1.6 collective-permute-done.26.refs_2_
  199.1 3.4 %shard_map.362 = (f32[48,3072]{1,0:T(8,128)}, bf16[48,3072]{1,0:T(8,128)(2,1)}, bf16[48,3072]{1,0:T(8,128)(2,1)}, bf16[48,3072]{1,0:T(8,128)(2,1)}) custom-call(bf16[384,1536]{1,0:T(8,128)(2,1)} %get-tuple-element.383.left_ref.refs_0_, bf16[384,1536]{1,0:T(8,128)(2,1)} %copy-done.23, bf16[192,1536]{1,0:T(8,128)(2,1)} %copy-done.37, ...), custom_call_target="tpu_custom_call" | custom-call | flops 2000000000 | bytes 1 | tf_op jit(solution)/shard_map/pallas_call | solution.py:189
  204.6 2.2 collective-permute-start.30
  206.9 1.9 collective-permute-start.31
  208.7 23.0 %shard_map.363 = (f32[512,768]{1,0:T(8,128)}, f32[512,768]{1,0:T(8,128)}, bf16[16,384]{1,0:T(8,128)(2,1)}, bf16[384,768]{1,0:T(8,128)(2,1)}, bf16[384,768]{1,0:T...) custom-call(f32[512,768]{1,0:T(8,128)} %get-tuple-element.409.g_in_ref, ...), custom_call_target="tpu_custom_call" | custom-call | flops 22000001024 | bytes 1 | tf_op jit(solution)/shard_map/pallas_call | solution.py:189
  236.2 2.1 shard_map.366
  241.4 4.0 %all-to-all-start.1 = ((bf16[16,80,384]{2,1,0:T(8,128)(2,1)}), bf16[16,80,384]{2,1,0:T(8,128)(2,1)S(1)}, u32[]{:S(2)}, u32[]{:S(2)}) async-start(bf16[16,80,384]{2,1,0:T(8,128)(2,1)} %pad_maximum_fusion), calls=%async_computation.1 | async-start | bytes 1966080 | tf_op jit(solution)/shard_map/all_to_all | solution.py:1370
  246.6 7.1 %shard_map.364 = (f32[512,768]{1,0:T(8,128)}, bf16[512,768]{1,0:T(8,128)(2,1)}) custom-call(f32[512,768]{1,0:T(8,128)} %get-tuple-element.425.g_ref, f32[512,768]{1,0:T(8,128)} %get-tuple-element.426.partial_ref, f32[512,768]{1,0:T(8,128)} %copy-done.4, f32[512,768]{1,0:T(8,128)} %get-tuple-element.324.tokens_ref, f32[512,768]{1,0:T(8,128)} %get-tuple-element.344.h_ref, ...), custom_call_target="tpu_custom_call" | custom-call | flops 1000000000 | bytes 1 | tf_op jit(solution)/shard_map/pallas_call | solution.py:189
  254.9 2.1 shard_map.365
  259.2 7.4 %collective-permute-done.39.refs_2_ = bf16[192,768]{1,0:T(8,128)(2,1)} collective-permute-done((bf16[192,768]{1,0:T(8,128)(2,1)}, bf16[192,768]{1,0:T(8,128)(2,1)}, u32[]{:S(2)}, u32[]{:S(2)}) %collective-permute-start.39) | collective-permute-done | bytes 294944 | tf_op jit(solution)/shard_map/ppermute | solution.py:54
  266.6 2.5 shard_map.367
  269.4 4.3 %collective-permute-done.37.refs_2_ = bf16[192,768]{1,0:T(8,128)(2,1)S(1)} collective-permute-done((bf16[192,768]{1,0:T(8,128)(2,1)}, bf16[192,768]{1,0:T(8,128)(2,1)S(1)}, u32[]{:S(2)}, u32[]{:S(2)}) %collective-permute-start.37) | collective-permute-done | bytes 294944 | tf_op jit(solution)/shard_map/ppermute | solution.py:54
  275.1 2.4 shard_map.368
  278.6 1.6 collective-permute-start.43
  280.1 1.9 collective-permute-start.44
  282.9 1.5 collective-permute-done.42
  285.1 1.7 collective-permute-start.47
  288.6 1.5 gather_fusion.1
  290.8 4.4 %collective-permute-done.43 = bf16[48,1536]{1,0:T(8,128)(2,1)} collective-permute-done((bf16[48,1536]{1,0:T(8,128)(2,1)}, bf16[48,1536]{1,0:T(8,128)(2,1)}, u32[]{:S(2)}, u32[]{:S(2)}) %collective-permute-start.43) | collective-permute-done | bytes 147488 | tf_op jit(solution)/shard_map/ppermute | solution.py:54
  297.0 3.1 %collective-permute-done.47 = bf16[48,1536]{1,0:T(8,128)(2,1)} collective-permute-done((bf16[48,1536]{1,0:T(8,128)(2,1)S(1)}, bf16[48,1536]{1,0:T(8,128)(2,1)}, u32[]{:S(2)}, u32[]{:S(2)}) %collective-permute-start.47) | collective-permute-done | bytes 147488 | tf_op jit(solution)/shard_map/ppermute | solution.py:54
  (233 shorter events, 59.3 us)
Async XLA Ops:
  2.7 22.0 %collective-permute-start = (bf16[48,3072]{1,0:T(8,128)(2,1)}, bf16[48,3072]{1,0:T(8,128)(2,1)S(1)}, u32[]{:S(2)}, u32[]{:S(2)}) collective-permute-start(bf16[48,3072]{1,0:T(8,128)(2,1)} %shard_map.349.refs_0_), channel_id=1, source_target_pairs={{0,8},{2,10},{4,12},{6,14},{8,0},{10,2},{12,4},{14,6},{16,24},{18,... | collective-permute-start | bytes 884744 | tf_op jit(solution)/shard_map/ppermute | solution.py:54
  5.7 19.0 %collective-permute-start.1 = (bf16[48,3072]{1,0:T(8,128)(2,1)}, bf16[48,3072]{1,0:T(8,128)(2,1)S(1)}, u32[]{:S(2)}, u32[]{:S(2)}) collective-permute-start(bf16[48,3072]{1,0:T(8,128)(2,1)} %shard_map.349.refs_0_), channel_id=1, source_target_pairs={{0,16},{2,18},{4,20},{6,22},{8,24},{10,26},{12,28},{14,30},{16,0},... | collective-permute-start | bytes 884744 | tf_op jit(solution)/shard_map/ppermute | solution.py:54
  24.7 8.3 %collective-permute-start.4 = (bf16[48,3072]{1,0:T(8,128)(2,1)S(1)}, bf16[48,3072]{1,0:T(8,128)(2,1)S(1)}, u32[]{:S(2)}, u32[]{:S(2)}) collective-permute-start(bf16[48,3072]{1,0:T(8,128)(2,1)S(1)} %collective-permute-done.1.refs_2_), channel_id=1, source_target_pairs={{0,8},{2,10},{4,12},{6,14},{8,0},{10,2},{12,4},{14,6},{16,24},{18,... | collective-permute-start | bytes 884744 | tf_op jit(solution)/shard_map/ppermute | solution.py:54
  27.7 16.5 %collective-permute-start.2 = (bf16[144,1536]{1,0:T(8,128)(2,1)}, bf16[144,1536]{1,0:T(8,128)(2,1)S(1)}, u32[]{:S(2)}, u32[]{:S(2)}) collective-permute-start(bf16[144,1536]{1,0:T(8,128)(2,1)} %get-tuple-element.283.refs_0_), channel_id=1, source_target_pairs={{0,4},{2,6},{4,0},{6,2},{8,12},{10,14},{12,8},{14,10},{16,20},{18,... | collective-permute-start | bytes 1327112 | tf_op jit(solution)/shard_map/ppermute | solution.py:54
  29.2 14.9 %collective-permute-start.3 = (bf16[144,1536]{1,0:T(8,128)(2,1)}, bf16[144,1536]{1,0:T(8,128)(2,1)S(1)}, u32[]{:S(2)}, u32[]{:S(2)}) collective-permute-start(bf16[144,1536]{1,0:T(8,128)(2,1)} %get-tuple-element.287.refs_4_), channel_id=1, source_target_pairs={{0,2},{2,0},{4,6},{6,4},{8,10},{10,8},{12,14},{14,12},{16,18},{18,... | collective-permute-start | bytes 1327112 | tf_op jit(solution)/shard_map/ppermute | solution.py:54
  35.4 7.5 %collective-permute-start.5 = (bf16[48,1536]{1,0:T(8,128)(2,1)}, bf16[48,1536]{1,0:T(8,128)(2,1)S(1)}, u32[]{:S(2)}, u32[]{:S(2)}) collective-permute-start(bf16[48,1536]{1,0:T(8,128)(2,1)} %get-tuple-element.284.refs_1_), channel_id=1, source_target_pairs={{0,4},{2,6},{4,0},{6,2},{8,12},{10,14},{12,8},{14,10},{16,20},{18,... | collective-permute-start | bytes 442376 | tf_op jit(solution)/shard_map/ppermute | solution.py:54
  36.9 7.2 %collective-permute-start.6 = (bf16[48,1536]{1,0:T(8,128)(2,1)}, bf16[48,1536]{1,0:T(8,128)(2,1)S(1)}, u32[]{:S(2)}, u32[]{:S(2)}) collective-permute-start(bf16[48,1536]{1,0:T(8,128)(2,1)} %get-tuple-element.288.refs_5_), channel_id=1, source_target_pairs={{0,2},{2,0},{4,6},{6,4},{8,10},{10,8},{12,14},{14,12},{16,18},{18,... | collective-permute-start | bytes 442376 | tf_op jit(solution)/shard_map/ppermute | solution.py:54
  39.1 34.6 %all-to-all-start = ((bf16[16,64,384]{2,1,0:T(8,128)(2,1)}), bf16[16,64,384]{2,1,0:T(8,128)(2,1)S(1)}, u32[]{:S(2)}, u32[]{:S(2)}) async-start(bf16[16,64,384]{2,1,0:T(8,128)(2,1)} %gather_fusion), calls=%async_computation | async-start | bytes 1572864 | tf_op jit(solution)/shard_map/all_to_all | solution.py:1284
  48.6 31.2 %collective-permute-start.7 = (bf16[384,1536]{1,0:T(8,128)(2,1)}, bf16[384,1536]{1,0:T(8,128)(2,1)S(1)}, u32[]{:S(2)}, u32[]{:S(2)}) collective-permute-start(bf16[384,1536]{1,0:T(8,128)(2,1)} %get-tuple-element.314.refs_0_), channel_id=1, source_target_pairs={{0,2},{2,0},{4,6},{6,4},{8,10},{10,8},{12,14},{14,12},{16,18},{18,... | collective-permute-start | bytes 3538952 | tf_op jit(solution)/shard_map/ppermute | solution.py:54
  50.6 29.2 %collective-permute-start.8 = (bf16[384,1536]{1,0:T(8,128)(2,1)}, bf16[384,1536]{1,0:T(8,128)(2,1)S(1)}, u32[]{:S(2)}, u32[]{:S(2)}) collective-permute-start(bf16[384,1536]{1,0:T(8,128)(2,1)} %get-tuple-element.328.refs_0_), channel_id=1, source_target_pairs={{0,4},{2,6},{4,0},{6,2},{8,12},{10,14},{12,8},{14,10},{16,20},{18,... | collective-permute-start | bytes 3538952 | tf_op jit(solution)/shard_map/ppermute | solution.py:54
  50.6 23.0 %collective-permute-start.10 = (bf16[48,3072]{1,0:T(8,128)(2,1)S(1)}, bf16[48,3072]{1,0:T(8,128)(2,1)}, u32[]{:S(2)}, u32[]{:S(2)}) collective-permute-start(bf16[48,3072]{1,0:T(8,128)(2,1)S(1)} %copy-done.43), channel_id=1, source_target_pairs={{0,16},{2,18},{4,20},{6,22},{8,24},{10,26},{12,28},{14,30},{16,0},... | collective-permute-start | bytes 884744 | tf_op jit(solution)/shard_map/ppermute | solution.py:54
  52.9 20.8 %collective-permute-start.9 = (bf16[48,3072]{1,0:T(8,128)(2,1)S(1)}, bf16[48,3072]{1,0:T(8,128)(2,1)}, u32[]{:S(2)}, u32[]{:S(2)}) collective-permute-start(bf16[48,3072]{1,0:T(8,128)(2,1)S(1)} %copy-done.43), channel_id=1, source_target_pairs={{0,8},{2,10},{4,12},{6,14},{8,0},{10,2},{12,4},{14,6},{16,24},{18,... | collective-permute-start | bytes 884744 | tf_op jit(solution)/shard_map/ppermute | solution.py:54
  73.7 8.1 %collective-permute-start.11 = (bf16[48,3072]{1,0:T(8,128)(2,1)}, bf16[48,3072]{1,0:T(8,128)(2,1)S(1)}, u32[]{:S(2)}, u32[]{:S(2)}) collective-permute-start(bf16[48,3072]{1,0:T(8,128)(2,1)} %collective-permute-done.10.refs_2_), channel_id=1, source_target_pairs={{0,8},{2,10},{4,12},{6,14},{8,0},{10,2},{12,4},{14,6},{16,24},{18,... | collective-permute-start | bytes 884744 | tf_op jit(solution)/shard_map/ppermute | solution.py:54
  84.9 16.8 %collective-permute-start.14 = (bf16[1024,384]{1,0:T(8,128)(2,1)S(1)}, bf16[1024,384]{1,0:T(8,128)(2,1)S(1)}, u32[]{:S(2)}, u32[]{:S(2)}) collective-permute-start(bf16[1024,384]{1,0:T(8,128)(2,1)S(1)} %bitcast.25), channel_id=1, source_target_pairs={{0,1},{1,0},{2,3},{3,2},{4,5},{5,4},{6,7},{7,6},{8,9},{9,8},{10,11... | collective-permute-start | bytes 2359304 | tf_op jit(solution)/shard_map/ppermute | solution.py:58
  84.9 16.0 %collective-permute-start.12 = (bf16[192,1536]{1,0:T(8,128)(2,1)}, bf16[192,1536]{1,0:T(8,128)(2,1)S(1)}, u32[]{:S(2)}, u32[]{:S(2)}) collective-permute-start(bf16[192,1536]{1,0:T(8,128)(2,1)} %get-tuple-element.335.refs_4_), channel_id=1, source_target_pairs={{0,4},{2,6},{4,0},{6,2},{8,12},{10,14},{12,8},{14,10},{16,20},{18,... | collective-permute-start | bytes 1769480 | tf_op jit(solution)/shard_map/ppermute | solution.py:54
  86.0 15.6 %collective-permute-start.13 = (bf16[192,1536]{1,0:T(8,128)(2,1)}, bf16[192,1536]{1,0:T(8,128)(2,1)S(1)}, u32[]{:S(2)}, u32[]{:S(2)}) collective-permute-start(bf16[192,1536]{1,0:T(8,128)(2,1)} %get-tuple-element.337.refs_8_), channel_id=1, source_target_pairs={{0,2},{2,0},{4,6},{6,4},{8,10},{10,8},{12,14},{14,12},{16,18},{18,... | collective-permute-start | bytes 1769480 | tf_op jit(solution)/shard_map/ppermute | solution.py:54
  101.7 25.2 %collective-permute-start.18 = (bf16[192,1536]{1,0:T(8,128)(2,1)S(1)}, bf16[192,1536]{1,0:T(8,128)(2,1)S(1)}, u32[]{:S(2)}, u32[]{:S(2)}) collective-permute-start(bf16[192,1536]{1,0:T(8,128)(2,1)S(1)} %copy-done.28), channel_id=1, source_target_pairs={{0,2},{2,0},{4,6},{6,4},{8,10},{10,8},{12,14},{14,12},{16,18},{18,... | collective-permute-start | bytes 1769480 | tf_op jit(solution)/shard_map/ppermute | solution.py:54
  103.2 26.8 %collective-permute-start.19 = (bf16[192,1536]{1,0:T(8,128)(2,1)S(1)}, bf16[192,1536]{1,0:T(8,128)(2,1)S(1)}, u32[]{:S(2)}, u32[]{:S(2)}) collective-permute-start(bf16[192,1536]{1,0:T(8,128)(2,1)S(1)} %collective-permute-done.12.refs_5_), channel_id=1, source_target_pairs={{0,2},{2,0},{4,6},{6,4},{8,10},{10,8},{12,14},{14,12},{16,18},{18,... | collective-permute-start | bytes 1769480 | tf_op jit(solution)/shard_map/ppermute | solution.py:54
  103.8 26.3 %collective-permute-start.20 = (bf16[192,1536]{1,0:T(8,128)(2,1)S(1)}, bf16[192,1536]{1,0:T(8,128)(2,1)S(1)}, u32[]{:S(2)}, u32[]{:S(2)}) collective-permute-start(bf16[192,1536]{1,0:T(8,128)(2,1)S(1)} %copy-done.29), channel_id=1, source_target_pairs={{0,4},{2,6},{4,0},{6,2},{8,12},{10,14},{12,8},{14,10},{16,20},{18,... | collective-permute-start | bytes 1769480 | tf_op jit(solution)/shard_map/ppermute | solution.py:54
  104.8 26.8 %collective-permute-start.21 = (bf16[192,1536]{1,0:T(8,128)(2,1)S(1)}, bf16[192,1536]{1,0:T(8,128)(2,1)}, u32[]{:S(2)}, u32[]{:S(2)}) collective-permute-start(bf16[192,1536]{1,0:T(8,128)(2,1)S(1)} %collective-permute-done.13.refs_9_), channel_id=1, source_target_pairs={{0,4},{2,6},{4,0},{6,2},{8,12},{10,14},{12,8},{14,10},{16,20},{18,... | collective-permute-start | bytes 1769480 | tf_op jit(solution)/shard_map/ppermute | solution.py:54
  126.8 4.8 %collective-permute-start.16 = (bf16[256,768]{1,0:T(8,128)(2,1)}, bf16[256,768]{1,0:T(8,128)(2,1)S(1)}, u32[]{:S(2)}, u32[]{:S(2)}) collective-permute-start(bf16[256,768]{1,0:T(8,128)(2,1)} %get-tuple-element.333.refs_0_), channel_id=1, source_target_pairs={{0,1},{1,0},{2,3},{3,2},{4,5},{5,4},{6,7},{7,6},{8,9},{9,8},{10,11... | collective-permute-start | bytes 1179656 | tf_op jit(solution)/shard_map/ppermute | solution.py:58
  126.9 4.7 %collective-permute-start.17 = (bf16[256,768]{1,0:T(8,128)(2,1)}, bf16[256,768]{1,0:T(8,128)(2,1)S(1)}, u32[]{:S(2)}, u32[]{:S(2)}) collective-permute-start(bf16[256,768]{1,0:T(8,128)(2,1)} %get-tuple-element.334.refs_1_), channel_id=1, source_target_pairs={{0,1},{1,0},{2,3},{3,2},{4,5},{5,4},{6,7},{7,6},{8,9},{9,8},{10,11... | collective-permute-start | bytes 1179656 | tf_op jit(solution)/shard_map/ppermute | solution.py:58
  148.2 30.0 %collective-permute-start.25 = (f32[512,768]{1,0:T(8,128)}, f32[512,768]{1,0:T(8,128)S(1)}, u32[]{:S(2)}, u32[]{:S(2)}) collective-permute-start(f32[512,768]{1,0:T(8,128)} %get-tuple-element.352.down_ref), channel_id=1, source_target_pairs={{0,1},{1,0},{2,3},{3,2},{4,5},{5,4},{6,7},{7,6},{8,9},{9,8},{10,11... | collective-permute-start | bytes 4718600 | tf_op jit(solution)/shard_map/ppermute | solution.py:58
  148.7 28.2 %collective-permute-start.22 = (bf16[384,1536]{1,0:T(8,128)(2,1)}, bf16[384,1536]{1,0:T(8,128)(2,1)S(1)}, u32[]{:S(2)}, u32[]{:S(2)}) collective-permute-start(bf16[384,1536]{1,0:T(8,128)(2,1)} %get-tuple-element.341), channel_id=1, source_target_pairs={{0,2},{2,0},{4,6},{6,4},{8,10},{10,8},{12,14},{14,12},{16,18},{18,... | collective-permute-start | bytes 3538952 | tf_op jit(solution)/shard_map/ppermute | solution.py:54
  150.2 28.0 %collective-permute-start.23 = (bf16[384,1536]{1,0:T(8,128)(2,1)}, bf16[384,1536]{1,0:T(8,128)(2,1)}, u32[]{:S(2)}, u32[]{:S(2)}) collective-permute-start(bf16[384,1536]{1,0:T(8,128)(2,1)} %get-tuple-element.342), channel_id=1, source_target_pairs={{0,4},{2,6},{4,0},{6,2},{8,12},{10,14},{12,8},{14,10},{16,20},{18,... | collective-permute-start | bytes 3538952 | tf_op jit(solution)/shard_map/ppermute | solution.py:54
  181.6 16.7 %collective-permute-start.28 = (f32[512,768]{1,0:T(8,128)S(1)}, f32[512,768]{1,0:T(8,128)S(1)}, u32[]{:S(2)}, u32[]{:S(2)}) collective-permute-start(f32[512,768]{1,0:T(8,128)S(1)} %copy-done.18), channel_id=1, source_target_pairs={{0,1},{1,0},{2,3},{3,2},{4,5},{5,4},{6,7},{7,6},{8,9},{9,8},{10,11... | collective-permute-start | bytes 4718600 | tf_op jit(solution)/shard_map/ppermute | solution.py:58
  181.6 16.0 %collective-permute-start.26 = (bf16[192,1536]{1,0:T(8,128)(2,1)}, bf16[192,1536]{1,0:T(8,128)(2,1)S(1)}, u32[]{:S(2)}, u32[]{:S(2)}) collective-permute-start(bf16[192,1536]{1,0:T(8,128)(2,1)} %get-tuple-element.367), channel_id=1, source_target_pairs={{0,4},{2,6},{4,0},{6,2},{8,12},{10,14},{12,8},{14,10},{16,20},{18,... | collective-permute-start | bytes 1769480 | tf_op jit(solution)/shard_map/ppermute | solution.py:54
  182.7 15.6 %collective-permute-start.27 = (bf16[192,1536]{1,0:T(8,128)(2,1)}, bf16[192,1536]{1,0:T(8,128)(2,1)S(1)}, u32[]{:S(2)}, u32[]{:S(2)}) collective-permute-start(bf16[192,1536]{1,0:T(8,128)(2,1)} %get-tuple-element.368), channel_id=1, source_target_pairs={{0,2},{2,0},{4,6},{6,4},{8,10},{10,8},{12,14},{14,12},{16,18},{18,... | collective-permute-start | bytes 1769480 | tf_op jit(solution)/shard_map/ppermute | solution.py:54
  202.5 29.2 %collective-permute-start.32 = (bf16[384,768]{1,0:T(8,128)(2,1)S(1)}, bf16[384,768]{1,0:T(8,128)(2,1)S(1)}, u32[]{:S(2)}, u32[]{:S(2)}) collective-permute-start(bf16[384,768]{1,0:T(8,128)(2,1)S(1)} %copy-done.32), channel_id=1, source_target_pairs={{0,2},{2,0},{4,6},{6,4},{8,10},{10,8},{12,14},{14,12},{16,18},{18,... | collective-permute-start | bytes 1769480 | tf_op jit(solution)/shard_map/ppermute | solution.py:54
  203.3 28.4 %collective-permute-start.33 = (bf16[384,768]{1,0:T(8,128)(2,1)S(1)}, bf16[384,768]{1,0:T(8,128)(2,1)S(1)}, u32[]{:S(2)}, u32[]{:S(2)}) collective-permute-start(bf16[384,768]{1,0:T(8,128)(2,1)S(1)} %copy-done.30), channel_id=1, source_target_pairs={{0,4},{2,6},{4,0},{6,2},{8,12},{10,14},{12,8},{14,10},{16,20},{18,... | collective-permute-start | bytes 1769480 | tf_op jit(solution)/shard_map/ppermute | solution.py:54
  204.3 27.4 %collective-permute-start.29 = (bf16[48,3072]{1,0:T(8,128)(2,1)}, bf16[48,3072]{1,0:T(8,128)(2,1)S(1)}, u32[]{:S(2)}, u32[]{:S(2)}) collective-permute-start(bf16[48,3072]{1,0:T(8,128)(2,1)} %get-tuple-element.401), channel_id=1, source_target_pairs={{0,8},{2,10},{4,12},{6,14},{8,0},{10,2},{12,4},{14,6},{16,24},{18,... | collective-permute-start | bytes 884744 | tf_op jit(solution)/shard_map/ppermute | solution.py:54
  204.6 27.1 %collective-permute-start.30 = (bf16[48,3072]{1,0:T(8,128)(2,1)}, bf16[48,3072]{1,0:T(8,128)(2,1)S(1)}, u32[]{:S(2)}, u32[]{:S(2)}) collective-permute-start(bf16[48,3072]{1,0:T(8,128)(2,1)} %get-tuple-element.402), channel_id=1, source_target_pairs={{0,16},{2,18},{4,20},{6,22},{8,24},{10,26},{12,28},{14,30},{16,0},... | collective-permute-start | bytes 884744 | tf_op jit(solution)/shard_map/ppermute | solution.py:54
  206.9 24.9 %collective-permute-start.31 = (bf16[48,3072]{1,0:T(8,128)(2,1)}, bf16[48,3072]{1,0:T(8,128)(2,1)S(1)}, u32[]{:S(2)}, u32[]{:S(2)}) collective-permute-start(bf16[48,3072]{1,0:T(8,128)(2,1)} %get-tuple-element.403), channel_id=1, source_target_pairs={{0,24},{2,26},{4,28},{6,30},{8,16},{10,18},{12,20},{14,22},{16,8},... | collective-permute-start | bytes 884744 | tf_op jit(solution)/shard_map/ppermute | solution.py:54
  232.6 12.9 %collective-permute-start.36 = (f32[512,768]{1,0:T(8,128)}, f32[512,768]{1,0:T(8,128)S(1)}, u32[]{:S(2)}, u32[]{:S(2)}) collective-permute-start(f32[512,768]{1,0:T(8,128)} %get-tuple-element.426.partial_ref), channel_id=1, source_target_pairs={{0,1},{1,0},{2,3},{3,2},{4,5},{5,4},{6,7},{7,6},{8,9},{9,8},{10,11... | collective-permute-start | bytes 4718600 | tf_op jit(solution)/shard_map/ppermute | solution.py:58
  232.7 6.6 %collective-permute-start.41 = (bf16[1024,384]{1,0:T(8,128)(2,1)}, bf16[1024,384]{1,0:T(8,128)(2,1)S(1)}, u32[]{:S(2)}, u32[]{:S(2)}) collective-permute-start(bf16[1024,384]{1,0:T(8,128)(2,1)} %get-tuple-element.465), channel_id=1, source_target_pairs={{0,1},{1,0},{2,3},{3,2},{4,5},{5,4},{6,7},{7,6},{8,9},{9,8},{10,11... | collective-permute-start | bytes 2359304 | tf_op jit(solution)/shard_map/ppermute | solution.py:58
  233.9 19.8 %collective-permute-start.34 = (bf16[384,768]{1,0:T(8,128)(2,1)}, bf16[384,768]{1,0:T(8,128)(2,1)}, u32[]{:S(2)}, u32[]{:S(2)}) collective-permute-start(bf16[384,768]{1,0:T(8,128)(2,1)} %get-tuple-element.423), channel_id=1, source_target_pairs={{0,2},{2,0},{4,6},{6,4},{8,10},{10,8},{12,14},{14,12},{16,18},{18,... | collective-permute-start | bytes 1769480 | tf_op jit(solution)/shard_map/ppermute | solution.py:54
  235.2 19.7 %collective-permute-start.35 = (bf16[384,768]{1,0:T(8,128)(2,1)}, bf16[384,768]{1,0:T(8,128)(2,1)}, u32[]{:S(2)}, u32[]{:S(2)}) collective-permute-start(bf16[384,768]{1,0:T(8,128)(2,1)} %get-tuple-element.424), channel_id=1, source_target_pairs={{0,4},{2,6},{4,0},{6,2},{8,12},{10,14},{12,8},{14,10},{16,20},{18,... | collective-permute-start | bytes 1769480 | tf_op jit(solution)/shard_map/ppermute | solution.py:54
  238.3 28.3 %collective-permute-start.39 = (bf16[192,768]{1,0:T(8,128)(2,1)}, bf16[192,768]{1,0:T(8,128)(2,1)}, u32[]{:S(2)}, u32[]{:S(2)}) collective-permute-start(bf16[192,768]{1,0:T(8,128)(2,1)} %get-tuple-element.445), channel_id=1, source_target_pairs={{0,4},{2,6},{4,0},{6,2},{8,12},{10,14},{12,8},{14,10},{16,20},{18,... | collective-permute-start | bytes 884744 | tf_op jit(solution)/shard_map/ppermute | solution.py:54
  239.3 27.3 %collective-permute-start.40 = (bf16[192,768]{1,0:T(8,128)(2,1)}, bf16[192,768]{1,0:T(8,128)(2,1)}, u32[]{:S(2)}, u32[]{:S(2)}) collective-permute-start(bf16[192,768]{1,0:T(8,128)(2,1)} %get-tuple-element.446), channel_id=1, source_target_pairs={{0,2},{2,0},{4,6},{6,4},{8,10},{10,8},{12,14},{14,12},{16,18},{18,... | collective-permute-start | bytes 884744 | tf_op jit(solution)/shard_map/ppermute | solution.py:54
  241.4 36.1 %all-to-all-start.1 = ((bf16[16,80,384]{2,1,0:T(8,128)(2,1)}), bf16[16,80,384]{2,1,0:T(8,128)(2,1)S(1)}, u32[]{:S(2)}, u32[]{:S(2)}) async-start(bf16[16,80,384]{2,1,0:T(8,128)(2,1)} %pad_maximum_fusion), calls=%async_computation.1 | async-start | bytes 1966080 | tf_op jit(solution)/shard_map/all_to_all | solution.py:1370
  257.0 16.7 %collective-permute-start.37 = (bf16[192,768]{1,0:T(8,128)(2,1)}, bf16[192,768]{1,0:T(8,128)(2,1)S(1)}, u32[]{:S(2)}, u32[]{:S(2)}) collective-permute-start(bf16[192,768]{1,0:T(8,128)(2,1)} %get-tuple-element.435), channel_id=1, source_target_pairs={{0,4},{2,6},{4,0},{6,2},{8,12},{10,14},{12,8},{14,10},{16,20},{18,... | collective-permute-start | bytes 884744 | tf_op jit(solution)/shard_map/ppermute | solution.py:54
  257.7 16.0 %collective-permute-start.38 = (bf16[192,768]{1,0:T(8,128)(2,1)}, bf16[192,768]{1,0:T(8,128)(2,1)S(1)}, u32[]{:S(2)}, u32[]{:S(2)}) collective-permute-start(bf16[192,768]{1,0:T(8,128)(2,1)} %get-tuple-element.436), channel_id=1, source_target_pairs={{0,2},{2,0},{4,6},{6,4},{8,10},{10,8},{12,14},{14,12},{16,18},{18,... | collective-permute-start | bytes 884744 | tf_op jit(solution)/shard_map/ppermute | solution.py:54
  269.1 13.9 %collective-permute-start.45 = (bf16[96,1536]{1,0:T(8,128)(2,1)}, bf16[96,1536]{1,0:T(8,128)(2,1)S(1)}, u32[]{:S(2)}, u32[]{:S(2)}) collective-permute-start(bf16[96,1536]{1,0:T(8,128)(2,1)} %get-tuple-element.453), channel_id=1, source_target_pairs={{0,8},{2,10},{4,12},{6,14},{8,0},{10,2},{12,4},{14,6},{16,24},{18,... | collective-permute-start | bytes 884744 | tf_op jit(solution)/shard_map/ppermute | solution.py:54
  277.5 6.9 %collective-permute-start.42 = (bf16[48,1536]{1,0:T(8,128)(2,1)}, bf16[48,1536]{1,0:T(8,128)(2,1)S(1)}, u32[]{:S(2)}, u32[]{:S(2)}) collective-permute-start(bf16[48,1536]{1,0:T(8,128)(2,1)} %get-tuple-element.472), channel_id=1, source_target_pairs={{0,8},{2,10},{4,12},{6,14},{8,0},{10,2},{12,4},{14,6},{16,24},{18,... | collective-permute-start | bytes 442376 | tf_op jit(solution)/shard_map/ppermute | solution.py:54
  278.6 16.6 %collective-permute-start.43 = (bf16[48,1536]{1,0:T(8,128)(2,1)}, bf16[48,1536]{1,0:T(8,128)(2,1)}, u32[]{:S(2)}, u32[]{:S(2)}) collective-permute-start(bf16[48,1536]{1,0:T(8,128)(2,1)} %get-tuple-element.473), channel_id=1, source_target_pairs={{0,16},{2,18},{4,20},{6,22},{8,24},{10,26},{12,28},{14,30},{16,0},... | collective-permute-start | bytes 442376 | tf_op jit(solution)/shard_map/ppermute | solution.py:54
  280.1 15.1 %collective-permute-start.44 = (bf16[48,1536]{1,0:T(8,128)(2,1)}, bf16[48,1536]{1,0:T(8,128)(2,1)}, u32[]{:S(2)}, u32[]{:S(2)}) collective-permute-start(bf16[48,1536]{1,0:T(8,128)(2,1)} %get-tuple-element.474), channel_id=1, source_target_pairs={{0,24},{2,26},{4,28},{6,30},{8,16},{10,18},{12,20},{14,22},{16,8},... | collective-permute-start | bytes 442376 | tf_op jit(solution)/shard_map/ppermute | solution.py:54
  284.5 5.6 %collective-permute-start.46 = (f32[8,384]{1,0:T(8,128)S(1)}, f32[8,384]{1,0:T(8,128)S(1)}, u32[]{:S(2)}, u32[]{:S(2)}) collective-permute-start(f32[8,384]{1,0:T(8,128)S(1)} %slice_add_fusion.1), channel_id=1, source_target_pairs={{0,1},{1,0},{2,3},{3,2},{4,5},{5,4},{6,7},{7,6},{8,9},{9,8},{10,11... | collective-permute-start | bytes 36872 | tf_op jit(solution)/shard_map/ppermute | solution.py:58
  285.1 15.0 %collective-permute-start.47 = (bf16[48,1536]{1,0:T(8,128)(2,1)S(1)}, bf16[48,1536]{1,0:T(8,128)(2,1)}, u32[]{:S(2)}, u32[]{:S(2)}) collective-permute-start(bf16[48,1536]{1,0:T(8,128)(2,1)S(1)} %slice.129), channel_id=1, source_target_pairs={{0,16},{2,18},{4,20},{6,22},{8,24},{10,26},{12,28},{14,30},{16,0},... | collective-permute-start | bytes 442376 | tf_op jit(solution)/shard_map/ppermute | solution.py:54
  (57 other events, 321.7 us)
